TPU v7x, 32 devices: a whole 2x2x4 slice. The times are simulated.
32 devices in a mesh: ctx: 8 (over z, y), hv: 4 (over x, core).
Axes of the slice: x: 2, y: 2, z: 4, core: 2. Of those that a mesh axis runs over, the one named last changes fastest.
Arguments:
- queries: bfloat16 [8192, 8, 256], P(('ctx', 'hv')), may hold values from -6 to 6
- key_vectors: bfloat16 [8192, 8, 256], P(('ctx', 'hv')), may hold values from -6 to 6
- value_vectors: bfloat16 [8192, 8, 512], P(('ctx', 'hv')), may hold values from -6 to 6
- input_gate: bfloat16 [8192, 8], P(('ctx', 'hv')), may hold values from -10 to 240
- forget_gate: bfloat16 [8192, 8], P(('ctx', 'hv')), may hold values from -2 to 16
- doc_ids: int32 [8192], P('ctx'), may hold values from 0 to 3, never falling along the last dimension, each value on 1 to 4096 neighbouring positions
Outputs:
- hidden_states: bfloat16 [8192, 8, 512], P(('ctx', 'hv'))
Inputs may be any that keep to these rules, and one draw needn't show every extreme that they name: `doc_ids`: document numbers never fall along the sequence; each of the 4 documents has 1 to 4096 tokens and one has exactly 4096.
All inputs are finite; a program needn't handle non-finite values.
Results may differ from a plain program's by a relative error of at most 0.0034.
Values may be sent and summed in bfloat16 or wider, within the bound.
No kernel may reach another device: no remote copies, remote signals or barrier semaphores. Data moves between devices by JAX's collectives and lax.ppermute only.
A program may use at most 128 MiB of HBM per device.

v0:
```python
import math

import jax
import jax.numpy as jnp
from jax import lax
from jax.sharding import PartitionSpec as P

TOK_DEV = 256


FLOOR_NEG = -1e30
TOP_PRECISION = lax.Precision.HIGHEST


def entering(value, axis, join, neutral):
    count, mine = (lax.axis_size(axis), lax.axis_index(axis))
    pieces = jax.tree.map(lambda part: lax.all_gather(part, axis), value)
    total = jax.tree.map(
        lambda part, zero: jnp.full_like(part, 0) + jnp.asarray(zero, part.dtype), value, neutral
    )

    def hop(position, total):
        longer = join(total, jax.tree.map(lambda part: part[position], pieces))
        return jax.tree.map(lambda new, old: jnp.where(position < mine, new, old), longer, total)

    return lax.fori_loop(0, count - 1, hop, total)


def passed_along(value, axis, steps):
    count = lax.axis_size(axis)
    leading, last = (max(0, -steps), min(count, count - steps))
    return lax.ppermute(value, axis, [(source, source + steps) for source in range(leading, last)])


def as_sent(x):
    return jax.tree.map(lambda a: a.astype(jnp.bfloat16) if a.dtype == jnp.float32 else a, x)


def combine_memory(earlier, later):
    severed_e, decay_e, memory_e, normalizer_e, top_e = earlier
    severed_l, decay_l, memory_l, normalizer_l, top_l = later
    keeping = 1.0 - severed_l
    reached = top_e + decay_l
    stabilizer = jnp.where(severed_l > 0.5, top_l, jnp.maximum(reached, top_l))
    old_factor = keeping * jnp.exp(jnp.minimum(reached - stabilizer, 0.0))
    new_factor = jnp.exp(top_l - stabilizer)
    memory_matrix = old_factor[:, None, None] * memory_e + new_factor[:, None, None] * memory_l
    normalizer = old_factor[:, None] * normalizer_e + new_factor[:, None] * normalizer_l
    return (
        jnp.maximum(severed_e, severed_l),
        decay_e + decay_l,
        memory_matrix,
        normalizer,
        stabilizer,
    )


def empty_memory(head_count, key_width, value_width):
    zero_heads = jnp.zeros((head_count,), jnp.float32)
    return (
        zero_heads,
        zero_heads,
        jnp.zeros((head_count, key_width, value_width), jnp.float32),
        jnp.zeros((head_count, key_width), jnp.float32),
        jnp.full((head_count,), FLOOR_NEG, jnp.float32),
    )


def group_summary(k_group, value_group, gate_in, decay_sum, id_group, alive):
    last_doc = id_group == id_group[-1]
    exponent = decay_sum[-1][None, :] - decay_sum + gate_in
    exponent = jnp.where(last_doc[:, None], exponent, FLOOR_NEG)
    stabilizer = jnp.max(exponent, axis=0)
    factor = jnp.exp(exponent - stabilizer[None, :])
    rescaled_values = k_group.astype(jnp.float32) * factor[:, :, None]
    memory_matrix = jnp.einsum(
        "lfj,lfm->fjm", rescaled_values, value_group.astype(jnp.float32), precision=TOP_PRECISION
    )
    normalizer = jnp.sum(rescaled_values, axis=0)
    severed = (1.0 - alive[-1]) * jnp.ones_like(stabilizer)
    return (severed, decay_sum[-1], memory_matrix, normalizer, stabilizer)


def group_output(
    q_group,
    k_group,
    value_group,
    gate_in,
    decay_sum,
    id_group,
    alive,
    memory_matrix,
    normalizer,
    carried_top,
):
    length = q_group.shape[0]
    key_scaling = 1.0 / math.sqrt(q_group.shape[2])
    block_len = min(512, length)
    scores = (
        jnp.einsum("bhd,shd->hbs", q_group, k_group, preferred_element_type=jnp.float32)
        * key_scaling
    )
    query_decay = decay_sum.T
    source_term = (gate_in - decay_sum).T
    exponent = query_decay[:, :, None] + source_term[:, None, :]
    query_pos = 0 + jnp.arange(block_len)
    source_pos = jnp.arange(block_len)
    allowed = (source_pos[None, :] <= query_pos[:, None]) & (id_group[:, None] == id_group[None, :])
    exponent = jnp.where(allowed[None], exponent, FLOOR_NEG)
    carried = jnp.where(alive[None, :] > 0.5, query_decay + carried_top[:, None], FLOOR_NEG)
    stabilizer = jnp.maximum(jnp.max(exponent, axis=2), carried)
    weights = scores * jnp.exp(exponent - stabilizer[:, :, None])
    denominator = jnp.sum(weights, axis=2)
    upper_term = jnp.einsum(
        "hbs,shv->hbv",
        weights.astype(jnp.bfloat16),
        value_group,
        preferred_element_type=jnp.float32,
    )
    retained_factor = jnp.exp(carried - stabilizer)
    query_single = q_group.astype(jnp.float32)
    upper_term = upper_term + retained_factor[:, :, None] * key_scaling * jnp.einsum(
        "zsj,sjf->szf", query_single, memory_matrix, precision=TOP_PRECISION
    )
    denominator = denominator + retained_factor * key_scaling * jnp.einsum(
        "bhk,hk->hb", query_single, normalizer, precision=TOP_PRECISION
    )
    ratio = upper_term / jnp.maximum(jnp.abs(denominator), 1.0)[:, :, None]
    pieces = [jnp.transpose(ratio, (1, 0, 2)).astype(jnp.bfloat16)]
    return jnp.concatenate(pieces, axis=0)


def run_layer(
    queries, key_vectors, value_vectors, input_gate, forget_gate, own_ids, prev_last, cross_fn
):
    row_count, head_count, key_width = queries.shape
    value_width = value_vectors.shape[2]
    group_len = min(TOK_DEV, row_count)
    count = row_count // group_len

    def shape_groups(array_in):
        return array_in.reshape((count, group_len) + array_in.shape[1:])

    log_forget = jax.nn.log_sigmoid(forget_gate.astype(jnp.float32))
    before_ids = jnp.concatenate([prev_last, own_ids[:-1]])
    q_groups = shape_groups(queries)
    k_groups = shape_groups(key_vectors)
    v_groups = shape_groups(value_vectors)
    gate_groups = shape_groups(input_gate.astype(jnp.float32))
    decay_groups = jnp.cumsum(shape_groups(log_forget), axis=1)
    id_groups = shape_groups(own_ids)
    alive = (id_groups == shape_groups(before_ids)[:, :1]).astype(jnp.float32)
    summaries = jax.vmap(group_summary)(
        k_groups, v_groups, gate_groups, decay_groups, id_groups, alive
    )
    identity = empty_memory(head_count, key_width, value_width)

    def advance(running, element):
        return (combine_memory(running, element), running)

    shard_total, local_prefix = lax.scan(advance, identity, summaries)
    outer = cross_fn(shard_total, identity)
    prefix = jax.vmap(lambda inner_state: combine_memory(outer, inner_state))(local_prefix)
    produced = lax.map(
        lambda element: group_output(*element),
        (
            q_groups,
            k_groups,
            v_groups,
            gate_groups,
            decay_groups,
            id_groups,
            alive,
            prefix[2],
            prefix[3],
            prefix[4],
        ),
    )
    return produced.reshape((row_count, head_count, value_width))


def across_scan(shard_total, identity):
    return entering(shard_total, "ctx", combine_memory, identity)


def local(queries, key_vectors, value_vectors, input_gate, forget_gate, doc_ids):
    shifted_up = passed_along(doc_ids[-1:] + 1, "ctx", 1)
    prev_last = shifted_up - 1
    head_q, head_k, head_v, head_in, head_forget = (
        lax.all_to_all(queries, "hv", split_axis=1, concat_axis=0, tiled=True),
        lax.all_to_all(key_vectors, "hv", split_axis=1, concat_axis=0, tiled=True),
        lax.all_to_all(value_vectors, "hv", split_axis=1, concat_axis=0, tiled=True),
        lax.all_to_all(input_gate, "hv", split_axis=1, concat_axis=0, tiled=True),
        lax.all_to_all(forget_gate, "hv", split_axis=1, concat_axis=0, tiled=True),
    )
    mixed = run_layer(head_q, head_k, head_v, head_in, head_forget, doc_ids, prev_last, across_scan)
    return lax.all_to_all(as_sent(mixed), "hv", split_axis=0, concat_axis=1, tiled=True).astype(
        mixed.dtype
    )


def solution(mesh):
    return jax.shard_map(
        local,
        mesh=mesh,
        in_specs=(
            P(("ctx", "hv"), None, None),
            P(("ctx", "hv"), None, None),
            P(("ctx", "hv"), None, None),
            P(("ctx", "hv"), None),
            P(("ctx", "hv"), None),
            P("ctx"),
        ),
        out_specs=P(("ctx", "hv"), None, None),
        check_vma=False,
    )
```

profile of v0, /device:TPU:25, one launch (start us, length us, event | category | flops | bytes accessed | tf_op | source)
XLA Modules:
  0.0 296.9 jit_solution(15793944097224547715)
XLA Ops:
  6.5 1.3 all_to_all.72
  7.8 3.9 %all-to-all-start.2 = ((bf16[256,4,2]{0,2,1:T(2,128)(2,1)}), bf16[256,4,2]{0,2,1:T(2,128)(2,1)S(1)}, u32[]{:S(2)}, u32[]{:S(2)}) async-start(bf16[256,4,2]{0,2,1:T(2,128)(2,1)} %all_to_all.72), calls=%async_computation.2 | async-start | bytes 8192 | tf_op jit(solution)/shard_map/all_to_all | solution.py:194
  11.7 1.3 all_to_all.74
  13.0 1.8 all-to-all-done.2
  14.8 3.9 %all-to-all-start.3 = ((bf16[256,4,2]{0,2,1:T(2,128)(2,1)}), bf16[256,4,2]{0,2,1:T(2,128)(2,1)S(1)}, u32[]{:S(2)}, u32[]{:S(2)}) async-start(bf16[256,4,2]{0,2,1:T(2,128)(2,1)} %all_to_all.74), calls=%async_computation.3 | async-start | bytes 8192 | tf_op jit(solution)/shard_map/all_to_all | solution.py:193
  18.7 2.4 copy.43
  21.2 0.7 all-to-all-done.3
  21.8 4.2 %all-to-all-start.1 = ((bf16[256,8,256]{2,0,1:T(8,128)(2,1)}), bf16[256,8,256]{2,0,1:T(8,128)(2,1)S(1)}, u32[]{:S(2)}, u32[]{:S(2)}) async-start(bf16[256,8,256]{2,0,1:T(8,128)(2,1)} %copy.43), calls=%async_computation.1 | async-start | bytes 2097152 | tf_op jit(solution)/shard_map/all_to_all | solution.py:191
  26.0 0.6 slice.29
  27.2 3.9 %collective-permute-start = (s32[1]{0:T(128)}, s32[1]{0:T(128)}, u32[]{:S(2)}, u32[]{:S(2)}) collective-permute-start(s32[1]{0:T(128)} %add.130), channel_id=1, source_target_pairs={{0,4},{4,8},{8,12},{12,16},{16,20},{20,24},{24,28},{1,5},{5,9},{9,... | collective-permute-start | bytes 20 | tf_op jit(solution)/shard_map/ppermute | solution.py:32
  31.1 3.6 %copy.48 = bf16[256,8,512]{2,0,1:T(8,128)(2,1)} copy(bf16[256,8,512]{2,1,0:T(8,128)(2,1)} %param.14) | data formatting | bytes 4194304 | tf_op args[2]
  34.7 4.8 %all-to-all-done.1 = bf16[256,8,256]{2,0,1:T(8,128)(2,1)S(1)} async-done(((bf16[256,8,256]{2,0,1:T(8,128)(2,1)}), bf16[256,8,256]{2,0,1:T(8,128)(2,1)S(1)}, u32[]{:S(2)}, u32[]{:S(2)}) %all-to-all-start.1) | async-done | bytes 1048608 | tf_op jit(solution)/shard_map/all_to_all | solution.py:191
  39.5 1.0 copy-done.1
  40.5 4.5 %all-to-all-start.4 = ((bf16[256,8,512]{2,0,1:T(8,128)(2,1)}), bf16[256,8,512]{2,0,1:T(8,128)(2,1)S(1)}, u32[]{:S(2)}, u32[]{:S(2)}) async-start(bf16[256,8,512]{2,0,1:T(8,128)(2,1)} %copy.48), calls=%async_computation.4 | async-start | bytes 4194304 | tf_op jit(solution)/shard_map/all_to_all | solution.py:192
  46.4 2.4 reduce-window.6
  49.8 1.6 fusion.58
  51.4 18.3 %all-to-all-done.4 = bf16[256,8,512]{2,0,1:T(8,128)(2,1)S(1)} async-done(((bf16[256,8,512]{2,0,1:T(8,128)(2,1)}), bf16[256,8,512]{2,0,1:T(8,128)(2,1)S(1)}, u32[]{:S(2)}, u32[]{:S(2)}) %all-to-all-start.4) | async-done | bytes 2097184 | tf_op jit(solution)/shard_map/all_to_all | solution.py:192
  69.8 5.4 %fusion.59 = f32[4,2,256,512]{3,2,1,0:T(8,128)} fusion(bf16[4,256,2,512]{3,1,2,0:T(8,128)(2,1)S(1)} %bitcast.311, bf16[4,256,2,256]{3,1,2,0:T(8,128)(2,1)} %bitcast.314, f32[4,256,2]{1,2,0:T(2,128)S(1)} %subtract_exponential_fusion.2), kind=kOutput, calls=%fused_computation.101 | convolution fusion | flops 3222274048 | bytes 7348224 | tf_op jit(solution)/shard_map/vmap(lfj,lfm->fjm)/dot_general | solution.py:76
  75.3 11.6 %while.61 = (s32[]{:T(128)}, f32[2]{0:T(128)S(1)}, f32[2]{0:T(128)S(1)}, f32[2,256,512]{2,1,0:T(8,128)S(1)}, f32[2,256]{1,0:T(2,128)S(1)}, /*index=5*/f32[2]{0:T...) while((s32[]{:T(128)}, f32[2]{0:T(128)S(1)}, ...), condition=%wide.region_5.6_spmd.clone.clone, body=%wide.region_4.5_spmd.clone.sunk.clone | while | flops 1313311 | bytes 5254035 | solution.py:161
  75.3 1.2 bitcast_dynamic-update-slice_fusion.6
  76.5 1.6 fusion.131
  78.3 1.1 bitcast_dynamic-update-slice_fusion.6
  79.4 1.6 fusion.131
  81.2 1.1 bitcast_dynamic-update-slice_fusion.6
  82.3 1.6 fusion.131
  84.1 1.1 bitcast_dynamic-update-slice_fusion.6
  85.1 1.6 fusion.131
  86.9 1.0 copy-done
  87.9 2.4 copy.42
  90.3 5.2 %all-to-all-start = ((bf16[256,8,256]{2,0,1:T(8,128)(2,1)}), bf16[256,8,256]{2,0,1:T(8,128)(2,1)}, u32[]{:S(2)}, u32[]{:S(2)}) async-start(bf16[256,8,256]{2,0,1:T(8,128)(2,1)} %copy.42), calls=%async_computation | async-start | bytes 2097152 | tf_op jit(solution)/shard_map/all_to_all | solution.py:190
  95.5 0.6 dynamic-slice
  97.4 15.2 %all-reduce.3 = (f32[16]{0:T(128)S(1)}, f32[16]{0:T(128)S(1)}, f32[16]{0:T(128)S(1)}) all-reduce(f32[16]{0:T(128)S(1)} %dynamic-update-slice, f32[16]{0:T(128)S(1)} %dynamic-update-slice.1, f32[16]{0:T(128)S(1)} %dynamic-update-slice.2), channel_id=2, replica_groups=mesh['ctx'=8,'hv'=4] {'ctx'}, use_global_device_ids=true, to_apply=%add | all-reduce | flops 48 | bytes 384
  112.9 23.2 %all-gather.5 = f32[8,2,256]{2,1,0:T(2,128)S(1)} all-gather(f32[1,2,256]{2,1,0:T(2,128)S(1)} %bitcast.321), channel_id=6, replica_groups=mesh['ctx'=8,'hv'=4] {'ctx'}, dimensions={0}, use_global_device_ids=true | all-gather | bytes 18432 | tf_op jit(solution)/shard_map/all_gather | solution.py:17
  136.1 75.5 %all-gather.8.cloned.1.call-done = f32[16,256,512]{2,1,0:T(8,128)} async-done(((f32[2,256,512]{2,1,0:T(8,128)}), f32[16,256,512]{2,1,0:T(8,128)}) %all-gather.8.cloned.1.call-update) | async-done | bytes 8388624 | tf_op jit(solution)/shard_map/all_gather | solution.py:17
  211.6 13.7 %while.62 = (s32[]{:T(128)}, f32[2,256,512]{2,1,0:T(8,128)S(1)}, f32[2,256]{1,0:T(2,128)S(1)}, f32[2]{0:T(128)S(1)}, s32[]{:T(128)}, /*index=5*/f32[8,2]{1,0:T(8...) while((s32[]{:T(128)}, f32[2,256,512]{2,1,0:T(8,128)S(1)}, ...), condition=%wide.region_7.8_spmd.clone.clone, body=%wide.region_6.7_spmd.clone.sunk.clone | while | flops 1313310 | bytes 3152166 | solution.py:26
  211.7 1.8 fusion.133
  213.6 1.8 fusion.133
  215.6 1.8 fusion.133
  217.5 1.8 fusion.133
  219.5 1.8 fusion.133
  221.4 1.8 fusion.133
  223.4 1.8 fusion.133
  225.4 5.0 %multiply_add_fusion = f32[4,2,256,512]{3,2,1,0:T(8,128)} fusion(f32[4,2,256,512]{3,2,1,0:T(8,128)} %get-tuple-element.339, f32[4,2]{1,0:T(4,128)S(1)} %subtract_exponential_fusion.3, f32[2,256,512]{2,1,0:T(8,128)S(1)} %get-tuple-element.338, f32[4,2]{1,0:T(4,128)S(1)} %get-tuple-element.576), kind=kLoop, calls=%fused_computation.98 | loop fusion | flops 3145728 | bytes 9437248 | tf_op jit(solution)/shard_map/vmap()/add | solution.py:47
  230.4 25.1 %while.60 = (s32[]{:T(128)}, bf16[4,256,2,512]{3,1,0,2:T(8,128)(2,1)}, bf16[4,256,2,256]{3,1,2,0:T(8,128)(2,1)}, bf16[4,256,2,256]{3,1,2,0:T(8,128)(2,1)}, s32[4...) while((s32[]{:T(128)}, ...), condition=%wide.region_11.12_spmd.clone, body=%wide.region_8.11_spmd.sunk.clone | while | flops 1010767616 | bytes 6027701 | solution.py:164
  230.8 1.3 fusion.125
  232.2 1.3 fusion.127
  233.6 2.0 fusion.129
  235.6 1.2 fusion.130
  237.1 1.3 fusion.125
  238.5 1.3 fusion.127
  239.8 2.0 fusion.129
  241.8 1.2 fusion.130
  243.4 1.3 fusion.125
  244.7 1.3 fusion.127
  246.1 2.0 fusion.129
  248.1 1.2 fusion.130
  249.6 1.3 fusion.125
  251.0 1.3 fusion.127
  252.4 2.0 fusion.129
  254.3 1.2 fusion.130
  255.5 3.7 %copy.52 = bf16[1024,2,512]{2,1,0:T(2,128)(2,1)S(1)} copy(bf16[1024,2,512]{2,0,1:T(8,128)(2,1)} %bitcast.35) | data formatting | bytes 4194304 | tf_op jit(solution)/shard_map/reshape | solution.py:179
  259.3 27.7 %all_to_all.89 = bf16[1024,2,512]{2,1,0:T(2,128)(2,1)S(1)} all-to-all(bf16[1024,2,512]{2,1,0:T(2,128)(2,1)S(1)} %copy.52), channel_id=1, replica_groups=mesh['ctx'=8,'hv'=4] {'hv'}, dimensions={0} | all-to-all | bytes 4194304 | tf_op jit(solution)/shard_map/all_to_all | solution.py:197
  287.0 0.3 copy.53
  287.6 2.5 copy.55
  (156 shorter events, 6.7 us)
Async XLA Ops:
  7.8 7.0 %all-to-all-start.2 = ((bf16[256,4,2]{0,2,1:T(2,128)(2,1)}), bf16[256,4,2]{0,2,1:T(2,128)(2,1)S(1)}, u32[]{:S(2)}, u32[]{:S(2)}) async-start(bf16[256,4,2]{0,2,1:T(2,128)(2,1)} %all_to_all.72), calls=%async_computation.2 | async-start | bytes 8192 | tf_op jit(solution)/shard_map/all_to_all | solution.py:194
  14.8 7.0 %all-to-all-start.3 = ((bf16[256,4,2]{0,2,1:T(2,128)(2,1)}), bf16[256,4,2]{0,2,1:T(2,128)(2,1)S(1)}, u32[]{:S(2)}, u32[]{:S(2)}) async-start(bf16[256,4,2]{0,2,1:T(2,128)(2,1)} %all_to_all.74), calls=%async_computation.3 | async-start | bytes 8192 | tf_op jit(solution)/shard_map/all_to_all | solution.py:193
  18.7 7.3 %copy-start.2 = (s32[1024]{0:T(1024)S(1)}, s32[1024]{0:T(1024)}, u32[]{:S(2)}) copy-start(s32[1024]{0:T(1024)} %param.17) | copy-start | bytes 12292
  21.8 17.7 %all-to-all-start.1 = ((bf16[256,8,256]{2,0,1:T(8,128)(2,1)}), bf16[256,8,256]{2,0,1:T(8,128)(2,1)S(1)}, u32[]{:S(2)}, u32[]{:S(2)}) async-start(bf16[256,8,256]{2,0,1:T(8,128)(2,1)} %copy.43), calls=%async_computation.1 | async-start | bytes 2097152 | tf_op jit(solution)/shard_map/all_to_all | solution.py:191
  27.2 18.1 %collective-permute-start = (s32[1]{0:T(128)}, s32[1]{0:T(128)}, u32[]{:S(2)}, u32[]{:S(2)}) collective-permute-start(s32[1]{0:T(128)} %add.130), channel_id=1, source_target_pairs={{0,4},{4,8},{8,12},{12,16},{16,20},{20,24},{24,28},{1,5},{5,9},{9,... | collective-permute-start | bytes 20 | tf_op jit(solution)/shard_map/ppermute | solution.py:32
  39.5 1.1 copy-start.1
  40.5 29.3 %all-to-all-start.4 = ((bf16[256,8,512]{2,0,1:T(8,128)(2,1)}), bf16[256,8,512]{2,0,1:T(8,128)(2,1)S(1)}, u32[]{:S(2)}, u32[]{:S(2)}) async-start(bf16[256,8,512]{2,0,1:T(8,128)(2,1)} %copy.48), calls=%async_computation.4 | async-start | bytes 4194304 | tf_op jit(solution)/shard_map/all_to_all | solution.py:192
  45.1 166.6 %all-gather.8.cloned.1.call-start = ((), (), s32[]{:S(2)}) async-start(), calls=%async_computation.6 | async-start | bytes 9437184 | tf_op jit(solution)/shard_map/all_gather | solution.py:17
  86.9 1.0 copy-start
  87.9 7.6 %copy-start.3 = (u32[32]{0:T(128)S(1)}, u32[32]{0:T(128)}, u32[]{:S(2)}) copy-start(u32[32]{0:T(128)} %constant.143) | copy-start | bytes 388
  90.3 140.1 %all-to-all-start = ((bf16[256,8,256]{2,0,1:T(8,128)(2,1)}), bf16[256,8,256]{2,0,1:T(8,128)(2,1)}, u32[]{:S(2)}, u32[]{:S(2)}) async-start(bf16[256,8,256]{2,0,1:T(8,128)(2,1)} %copy.42), calls=%async_computation | async-start | bytes 2097152 | tf_op jit(solution)/shard_map/all_to_all | solution.py:190
Sparse Core Ops, SparseCore 0:
  88.0 123.5 all-gather.7
where the time goes:
time: 303 us; the launch traced here: 297 us
  waiting for transfers between devices  101 us (33%)
  blocking collectives  66.2 us (22%)
  other arithmetic  36.4 us (12%)
  matrix products  28.4 us (9%)
  starting transfers between devices  25.5 us (8%)
  local copies, waits for them, and re-layouts  23.4 us (8%)
  between operations  15.4 us (5%)
    all_gather x1, waiting for transfers between devices, entering(): pieces = jax.tree.map(lambda part: lax.all_gather(part, axis), value)  75.5 us
    all_to_all x1, blocking collectives, local(): lax.all_to_all(as_sent(mixed), 'hv', split_axis=0, concat_axis=1, tiled=T...  27.7 us
    all_gather x1, blocking collectives, entering(): pieces = jax.tree.map(lambda part: lax.all_gather(part, axis), value)  23.2 us
    all_to_all x1, waiting for transfers between devices, local(): lax.all_to_all(value_vectors, 'hv', split_axis=1, concat_axis=0, tiled=True)  18.3 us
    unnamed x1, blocking collectives  15.2 us
    select_n x21, other arithmetic, hop(): jnp.where(position < mine, new, old)  13.4 us
    unnamed x19, local copies, waits for them, and re-layouts  11.8 us
    add x5, other arithmetic, combine_memory(): old_factor[:, None, None] * memory_e + new_factor[:, None, None] * memory_l  11.2 us
  transfers between devices with their start and end apart: 7, of which 5 were waited for; matrix products, arithmetic and copies ran while one was open for 12% of the time, Pallas kernels for 0%

commit v1 on v0

v1 whole, which is shorter than its diff:
```python
import functools

import jax
import jax.numpy as jnp
from jax import lax
from jax.experimental import pallas as pl
from jax.experimental.pallas import tpu as pltpu
from jax.sharding import PartitionSpec as P

AXES = ("ctx", "hv")
FLOOR_NEG = -1e30
META = 16
LANES = 128
F32, BF16 = jnp.float32, jnp.bfloat16

NN = (((1,), (0,)), ((), ()))
NT = (((1,), (1,)), ((), ()))


def dot(a, b, dims=NN):
    return lax.dot_general(a, b, dims, preferred_element_type=F32)


def split3(x):
    hi = x.astype(BF16).astype(F32)
    mid = (x - hi).astype(BF16).astype(F32)
    return hi, mid, (x - hi - mid).astype(BF16).astype(F32)


def iota(shape, dim):
    return lax.broadcasted_iota(jnp.int32, shape, dim)


def meta_rows(normalizer, top, decay, doc):
    line = jnp.concatenate([normalizer, top, decay], axis=1)
    hi, mid, low = split3(line)
    width = line.shape[1]
    doc_line = jnp.concatenate([doc] * (width // LANES), axis=1)
    row = iota((META, width), 0)
    rows = jnp.where(row == 0, hi, jnp.where(row == 1, mid, jnp.where(row == 2, low, 0.0)))
    return jnp.where(row == 3, doc_line, rows).astype(BF16)


def read_meta(ref):
    key_width = ref.shape[0] - META
    rows = ref[key_width:, :].astype(F32)
    line = (rows[2:3] + rows[1:2]) + rows[0:1]
    return (
        line[:, :key_width],
        line[:, key_width : key_width + LANES],
        line[:, key_width + LANES : key_width + 2 * LANES],
        rows[3:4, :LANES],
    )


def weighted(refs, coefs):
    key_width, value_width = refs[0].shape[0] - META, refs[0].shape[1]
    total = None
    for ref, coef in zip(refs, coefs, strict=True):
        wide = jnp.concatenate([coef] * (value_width // LANES), axis=1)
        term = wide * ref[:key_width, :].astype(F32)
        total = term if total is None else total + term
    return total


def gate_rows(core, own_ref, other_ref, heads):
    own, other = own_ref[...].astype(F32), other_ref[...].astype(F32)
    both = jnp.concatenate(
        [jnp.where(core == 0, own, other), jnp.where(core == 0, other, own)], axis=1
    )
    gate_in, forget = both[:heads], both[heads:]
    log_forget = jnp.minimum(forget, 0.0) - jnp.log1p(jnp.exp(-jnp.abs(forget)))
    length = both.shape[1]
    upto = (iota((length, length), 0) <= iota((length, length), 1)).astype(BF16)
    pieces = dot(jnp.concatenate(split3(log_forget), axis=0).astype(BF16), upto)
    decay = (pieces[2 * heads :] + pieces[heads : 2 * heads]) + pieces[:heads]
    return gate_in, decay


def relayout_kernel(half, q_ref, k_ref, v_ref, in_ref, forget_ref, scalars, *outs):
    core = scalars[1]
    q_keep, k_keep, v_keep, q_send, k_send, v_send, gates = outs
    heads = in_ref.shape[0]
    gates[:heads, :] = in_ref[...]
    gates[heads:, :] = forget_ref[...]

    def body(first, second):
        for source, low, high in zip((q_ref, k_ref, v_ref), first, second, strict=True):
            for h in range(half):
                low[h] = source[:, h, :]
                high[h] = source[:, half + h, :]

    keep, send = (q_keep, k_keep, v_keep), (q_send, k_send, v_send)

    @pl.when(core == 0)
    def _():
        body(keep, send)

    @pl.when(core != 0)
    def _():
        body(send, keep)


def state_kernel(
    heads, scalars, k_own, v_own, k_oth, v_oth, g_own, g_oth, ids_ref, *rest
):
    outs, (factors, tops, decays, payload) = rest[:-4], rest[-4:]
    step = pl.program_id(0)
    core = scalars[1]
    half = heads // 2
    tokens = k_own.shape[1]
    key_width, value_width = k_own.shape[2], v_own.shape[2]
    length = 2 * tokens

    @pl.when(step == 0)
    def _():
        gate_in, decay = gate_rows(core, g_own, g_oth, heads)
        ids = ids_ref[...]
        exponent = decay[:, length - 1 :] - decay + gate_in
        exponent = jnp.where(ids == ids[:, length - 1 :], exponent, FLOOR_NEG)
        top = jnp.max(exponent, axis=1, keepdims=True)
        factors[...] = jnp.exp(exponent - top)
        tops[...] = jnp.broadcast_to(top, tops.shape)
        decays[...] = jnp.broadcast_to(decay[:, length - 1 :], decays.shape)

    head = half * core + jnp.bitwise_xor(scalars[0], step)
    row = factors[pl.ds(head, 1), :]
    first, last = row[:, :tokens], row[:, tokens:]
    total, normal = None, None
    for k_ref, v_ref, f in (
        (k_own, v_own, jnp.where(core == 0, first, last)),
        (k_oth, v_oth, jnp.where(core == 0, last, first)),
    ):
        keys, values = k_ref[0], v_ref[0]
        scaled = keys.astype(F32).T * f
        high = scaled.astype(BF16)
        low = (scaled - high.astype(F32)).astype(BF16)
        part = dot(low, values) + dot(high, values)
        pieces = jnp.concatenate(split3(f) + (jnp.zeros((META - 3, tokens), F32),), axis=0)
        sums = dot(pieces.astype(BF16), keys)
        line = (sums[2:3] + sums[1:2]) + sums[0:1]
        total = part if total is None else total + part
        normal = line if normal is None else normal + line
    doc = jnp.broadcast_to(ids_ref[:, length - 1 :].astype(F32) + 1.0, (1, LANES))
    payload[:key_width, :] = total.astype(BF16)
    payload[key_width:, :] = meta_rows(
        normal, tops[pl.ds(head, 1), :], decays[pl.ds(head, 1), :], doc
    )
    for i, out in enumerate(outs):

        @pl.when(step == i)
        def _(out=out):
            out[...] = payload[...]


def total_kernel(group, scalars, *refs):
    states, out = refs[:group], refs[group]
    place = [jnp.bitwise_xor(scalars[0], r) for r in range(group)]
    metas = [read_meta(ref) for ref in states]
    zero = jnp.zeros((1, LANES), F32)
    doc = sum((jnp.where(place[r] == group - 1, metas[r][3], zero) for r in range(group)), zero)
    reached = []
    for r in range(group):
        after = sum(
            (jnp.where(place[i] > place[r], metas[i][2], zero) for i in range(group)), zero
        )
        reached.append(jnp.where(metas[r][3] == doc, metas[r][1] + after, FLOOR_NEG))
    top = functools.reduce(jnp.maximum, reached)
    coefs = [
        jnp.where(metas[r][3] == doc, jnp.exp(reached[r] - top), 0.0) for r in range(group)
    ]
    key_width = out.shape[0] - META
    out[:key_width, :] = weighted(states, coefs).astype(BF16)
    normal = sum(
        jnp.concatenate([coefs[r]] * (key_width // LANES), axis=1) * metas[r][0]
        for r in range(group)
    )
    decay = sum((metas[r][2] for r in range(group)), zero)
    out[key_width:, :] = meta_rows(normal, top, decay, doc)


def entering_kernel(group, reach, scalars, *refs):
    states, totals, outs = refs[:group], refs[group : group + reach], refs[group + reach :]
    place = [jnp.bitwise_xor(scalars[0], r) for r in range(group)]
    metas = [read_meta(ref) for ref in states]
    far = [read_meta(ref) for ref in totals]
    zero = jnp.zeros((1, LANES), F32)
    key_width = outs[0].shape[0] - META
    for r in range(group):
        mine = place[r]
        doc = jnp.where(mine == 0, far[0][3], zero)
        for i in range(group):
            doc = doc + jnp.where(place[i] == mine - 1, metas[i][3], zero)
        passed = sum(
            (jnp.where(place[i] < mine, metas[i][2], zero) for i in range(group)), zero
        )
        sources, reached, normals = [], [], []
        for i in range(group):
            if i == r:
                continue
            between = sum(
                (
                    jnp.where((place[n] < mine) & (place[n] > place[i]), metas[n][2], zero)
                    for n in range(group)
                ),
                zero,
            )
            there = jnp.where(place[i] < mine, metas[i][3], -1.0)
            alive = there == doc
            sources.append(states[i])
            normals.append(metas[i][0])
            reached.append((alive, jnp.where(alive, metas[i][1] + between, FLOOR_NEG)))
        for d in range(reach):
            alive = (far[d][3] == doc) & (far[d][3] > 0.5)
            sources.append(totals[d])
            normals.append(far[d][0])
            reached.append((alive, jnp.where(alive, far[d][1] + passed, FLOOR_NEG)))
            passed = passed + far[d][2]
        top = functools.reduce(jnp.maximum, [value for _, value in reached])
        coefs = [jnp.where(alive, jnp.exp(value - top), 0.0) for alive, value in reached]
        outs[r][:key_width, :] = weighted(sources, coefs).astype(BF16)
        normal = sum(
            jnp.concatenate([coef] * (key_width // LANES), axis=1) * line
            for coef, line in zip(coefs, normals, strict=True)
        )
        outs[r][key_width:, :] = meta_rows(normal, top, zero, doc)


def output_kernel(heads, group, scalars, *refs):
    q_own, k_own, v_own, q_oth, k_oth, v_oth, g_own, g_oth, ids_ref = refs[:9]
    entering = refs[9 : 9 + group]
    keep, send, source_rows, columns, bias, payload = refs[9 + group :]
    step = pl.program_id(0)
    core = scalars[1]
    half = heads // 2
    tokens, key_width = q_own.shape[1], q_own.shape[2]
    length = 2 * tokens
    scaling = key_width**-0.5

    @pl.when(step == 0)
    def _():
        gate_in, decay = gate_rows(core, g_own, g_oth, heads)
        source_rows[...] = gate_in - decay
        docs = ids_ref[...].astype(F32) + 1.0
        filler = jnp.zeros((LANES - heads - 1, length), F32)
        turned = jnp.concatenate([decay, docs, filler], axis=0).T
        columns[...] = turned
        same = turned[:, heads : heads + 1] == docs
        causal = iota((length, length), 0) >= iota((length, length), 1)
        bias[...] = jnp.where(same & causal, 0.0, FLOOR_NEG)

    for i, ref in enumerate(entering):

        @pl.when(step == i)
        def _(ref=ref):
            payload[...] = ref[...]

    head = half * core + jnp.bitwise_xor(scalars[0], step)
    is_first = core == 0
    source = source_rows[pl.ds(head, 1), :]
    lane = iota((length, LANES), 1)
    turned = columns[...]
    decay = jnp.sum(jnp.where(lane == head, turned, 0.0), axis=1, keepdims=True)
    docs = turned[:, heads : heads + 1]
    normal, top, _, doc = read_meta(payload)
    carried = jnp.where(docs == doc[:, :1], decay + top[:, :1], FLOOR_NEG)
    pieces = jnp.concatenate(split3(normal) + (jnp.zeros((META - 3, key_width), F32),), axis=0)
    pieces = pieces.astype(BF16)
    memory = payload[:key_width, :]

    def ordered(own, other):
        own, other = own[0], other[0]
        return jnp.where(is_first, own, other), jnp.where(is_first, other, own)

    queries, keys, values = ordered(q_own, q_oth), ordered(k_own, k_oth), ordered(v_own, v_oth)
    results = []
    for block in range(2):
        rows = slice(block * tokens, (block + 1) * tokens)
        query = queries[block]
        stabilizer = carried[rows]
        exponents = []
        for s in range(block + 1):
            cols = slice(s * tokens, (s + 1) * tokens)
            exponent = (decay[rows] + source[:, cols]) + bias[rows, cols]
            exponents.append(exponent)
            stabilizer = jnp.maximum(stabilizer, jnp.max(exponent, axis=1, keepdims=True))
        retained = jnp.exp(carried[rows] - stabilizer) * scaling
        seen = dot(query, pieces, NT)
        denominator = retained * ((seen[:, 2:3] + seen[:, 1:2]) + seen[:, 0:1])
        numerator = retained * dot(query, memory)
        for s in range(block + 1):
            weights = dot(query, keys[s], NT) * scaling * jnp.exp(exponents[s] - stabilizer)
            denominator = denominator + jnp.sum(weights, axis=1, keepdims=True)
            high = weights.astype(BF16)
            numerator = numerator + dot(high, values[s])
            if s < block:
                low = (weights - high.astype(F32)).astype(BF16)
                numerator = numerator + dot(low, values[s])
        results.append((numerator / jnp.maximum(jnp.abs(denominator), 1.0)).astype(BF16))
    keep[0] = jnp.where(is_first, results[0], results[1])
    send[0] = jnp.where(is_first, results[1], results[0])


def merge_kernel(scalars, own_ref, other_ref, out_ref):
    half = own_ref.shape[0]

    def body(low, high):
        for h in range(half):
            out_ref[:, h, :] = low[h]
            out_ref[:, half + h, :] = high[h]

    @pl.when(scalars[1] == 0)
    def _():
        body(own_ref, other_ref)

    @pl.when(scalars[1] != 0)
    def _():
        body(other_ref, own_ref)


def whole(shape):
    return pl.BlockSpec(shape, lambda *_: (0,) * len(shape))


def params():
    return pltpu.CompilerParams(vmem_limit_bytes=56 * 2**20)


SMEM = pl.BlockSpec(memory_space=pltpu.SMEM)


def shape_of(*dims, dtype=BF16):
    return jax.ShapeDtypeStruct(dims, dtype)


def local(devices, queries, key_vectors, value_vectors, input_gate, forget_gate, doc_ids):
    tokens, heads, key_width = queries.shape
    value_width = value_vectors.shape[2]
    half = heads // 2
    group = half
    chips = devices // 2
    levels = chips // group
    reach = max(1, levels // 2)
    ctx, hv = lax.axis_index("ctx"), lax.axis_index("hv")
    chip = ctx * (lax.axis_size("hv") // 2) + hv // 2
    scalars = jnp.stack([chip % group, hv % 2]).astype(jnp.int32)
    ids = lax.dynamic_slice(doc_ids, ((hv // 2) * 2 * tokens,), (2 * tokens,))[None, :]

    def swap_cores(x):
        return lax.ppermute(x, AXES, [(d, d ^ 1) for d in range(devices)])

    def in_group(x, r):
        pairs = [(d, d ^ (2 * r)) for d in range(devices)]
        return lax.ppermute(x, AXES, pairs)

    def to_later(x, levels_on):
        jump = 2 * group * levels_on
        return lax.ppermute(x, AXES, [(d, d + jump) for d in range(devices - jump)])

    rows = key_width + META
    narrow, wide = (half, tokens, key_width), (half, tokens, value_width)
    q_keep, k_keep, v_keep, q_send, k_send, v_send, gates = pl.pallas_call(
        functools.partial(relayout_kernel, half),
        in_specs=[
            whole(queries.shape),
            whole(key_vectors.shape),
            whole(value_vectors.shape),
            whole((heads, tokens)),
            whole((heads, tokens)),
            SMEM,
        ],
        out_specs=[whole(s) for s in (narrow, narrow, wide) * 2 + ((2 * heads, tokens),)],
        out_shape=[shape_of(*s) for s in (narrow, narrow, wide) * 2 + ((2 * heads, tokens),)],
        compiler_params=params(),
        name="relayout",
    )(queries, key_vectors, value_vectors, input_gate.T, forget_gate.T, scalars)
    gates_oth = swap_cores(gates)
    k_oth = swap_cores(k_send)
    v_oth = swap_cores(v_send)
    q_oth = swap_cores(q_send)

    def by_head(width):
        return pl.BlockSpec(
            (1, tokens, width), lambda i, s: (jnp.bitwise_xor(s[0], i), 0, 0)
        )

    small = [
        whole((2 * heads, tokens)),
        whole((2 * heads, tokens)),
        whole((1, 2 * tokens)),
    ]
    state = (rows, value_width)
    states = pl.pallas_call(
        functools.partial(state_kernel, heads),
        grid_spec=pltpu.PrefetchScalarGridSpec(
            num_scalar_prefetch=1,
            grid=(group,),
            in_specs=[by_head(key_width), by_head(value_width)] * 2 + small,
            out_specs=[whole(state)] * group,
            scratch_shapes=[
                pltpu.VMEM((heads, 2 * tokens), F32),
                pltpu.VMEM((heads, LANES), F32),
                pltpu.VMEM((heads, LANES), F32),
                pltpu.VMEM(state, BF16),
            ],
        ),
        out_shape=[shape_of(*state)] * group,
        compiler_params=params(),
        name="states",
    )(scalars, k_keep, v_keep, k_oth, v_oth, gates, gates_oth, ids)
    gathered = [states[0]] + [in_group(states[r], r) for r in range(1, group)]

    total = pl.pallas_call(
        functools.partial(total_kernel, group),
        in_specs=[SMEM] + [whole(state)] * group,
        out_specs=whole(state),
        out_shape=shape_of(*state),
        compiler_params=params(),
        name="group_total",
    )(scalars, *gathered)
    totals = [to_later(total, d) for d in range(1, reach + 1)]

    outgoing = pl.pallas_call(
        functools.partial(entering_kernel, group, reach),
        in_specs=[SMEM] + [whole(state)] * (group + reach),
        out_specs=[whole(state)] * group,
        out_shape=[shape_of(*state)] * group,
        compiler_params=params(),
        name="entering",
    )(scalars, *gathered, *totals)
    entering = [outgoing[0]] + [in_group(outgoing[r], r) for r in range(1, group)]

    length = 2 * tokens
    keep, send = pl.pallas_call(
        functools.partial(output_kernel, heads, group),
        grid_spec=pltpu.PrefetchScalarGridSpec(
            num_scalar_prefetch=1,
            grid=(group,),
            in_specs=[by_head(key_width), by_head(key_width), by_head(value_width)] * 2
            + small
            + [whole(state)] * group,
            out_specs=[by_head(value_width)] * 2,
            scratch_shapes=[
                pltpu.VMEM((heads, length), F32),
                pltpu.VMEM((length, LANES), F32),
                pltpu.VMEM((length, length), F32),
                pltpu.VMEM(state, BF16),
            ],
        ),
        out_shape=[shape_of(*wide)] * 2,
        compiler_params=params(),
        name="outputs",
    )(scalars, q_keep, k_keep, v_keep, q_oth, k_oth, v_oth, gates, gates_oth, ids, *entering)
    received = swap_cores(send)
    return pl.pallas_call(
        merge_kernel,
        in_specs=[SMEM, whole(wide), whole(wide)],
        out_specs=whole(value_vectors.shape),
        out_shape=shape_of(*value_vectors.shape),
        compiler_params=params(),
        name="merge",
    )(scalars, keep, received)


def solution(mesh):
    return jax.shard_map(
        functools.partial(local, mesh.size),
        mesh=mesh,
        in_specs=(
            P(AXES, None, None),
            P(AXES, None, None),
            P(AXES, None, None),
            P(AXES, None),
            P(AXES, None),
            P("ctx"),
        ),
        out_specs=P(AXES, None, None),
        check_vma=False,
    )
```

time: 303 us -> 105 us (0.35)
  the two profiles are of different devices: /device:TPU:25 before, /device:TPU:17 now
where the time goes in v1:
time: 105 us; the launch traced here: 104 us
  waiting for transfers between devices  46.4 us (44%)
  Pallas kernels  37.7 us (36%)
  starting transfers between devices  14.5 us (14%)
  local copies, waits for them, and re-layouts  4.94 us (5%)
    ppermute x6, waiting for transfers between devices, in_group(): return lax.ppermute(x, AXES, pairs)  24.7 us
    ppermute x2, waiting for transfers between devices, to_later(): return lax.ppermute(x, AXES, [(d, d + jump) for d in range(devices - jump)])  17.2 us
    pallas_call x1, Pallas kernels, local(): pl.pallas_call(functools.partial(relayout_kernel, half), in_specs=[whole(...  10.5 us
    pallas_call x1, Pallas kernels, local(): pl.pallas_call(functools.partial(output_kernel, heads, group), grid_spec=...  9.67 us
    pallas_call x1, Pallas kernels, local(): pl.pallas_call(functools.partial(state_kernel, heads), grid_spec=pltpu.Pr...  6.28 us
    pallas_call x1, Pallas kernels, local(): pl.pallas_call(merge_kernel, in_specs=[SMEM, whole(wide), whole(wide)], o...  5.75 us
    ppermute x6, starting transfers between devices, in_group(): return lax.ppermute(x, AXES, pairs)  5.3 us
    ppermute x5, starting transfers between devices, swap_cores(): return lax.ppermute(x, AXES, [(d, d ^ 1) for d in range(devices)])  4.73 us
  transfers between devices with their start and end apart: 13, of which 10 were waited for; matrix products, arithmetic and copies ran while one was open for 1% of the time, Pallas kernels for 3%

profile of v1, /device:TPU:17, one launch (start us, length us, event | category | flops | bytes accessed | tf_op | source)
XLA Modules:
  0.0 104.2 jit_solution(9704133284783773117)
XLA Ops:
  0.0 0.6 pad_add_fusion.scalars
  0.6 0.0 copy-start.13
  0.6 10.5 %relayout.1 = (bf16[4,256,256]{2,1,0:T(8,128)(2,1)}, bf16[4,256,256]{2,1,0:T(8,128)(2,1)}, bf16[4,256,512]{2,1,0:T(8,128)(2,1)}, bf16[4,256,256]{2,1,0:T(8,128)(...) custom-call(bf16[256,8,256]{2,1,0:T(8,128)(2,1)} %q_ref.1, ...), custom_call_target="tpu_custom_call" | custom-call | tf_op jit(solution)/shard_map/relayout/pallas_call | solution.py:362
  11.2 0.7 collective-permute-start.2
  11.8 0.1 collective-permute-start.1
  11.9 0.4 collective-permute-start.3
  12.3 0.0 copy-done.13
  12.3 0.7 dynamic_slice.3
  13.0 2.1 %collective-permute-done.3.g_oth.refs_7_ = bf16[16,256]{1,0:T(8,128)(2,1)S(1)} collective-permute-done((bf16[16,256]{1,0:T(8,128)(2,1)}, bf16[16,256]{1,0:T(8,128)(2,1)S(1)}, u32[]{:S(2)}, u32[]{:S(2)}) %collective-permute-start.3) | collective-permute-done | bytes 8224 | tf_op jit(solution)/shard_map/ppermute | solution.py:350
  15.1 0.0 copy-start.12
  15.1 0.0 collective-permute-done.1.k_oth.refs_4_
  15.1 0.0 copy-start.1
  15.1 0.0 collective-permute-done.2.v_oth.refs_5_
  15.1 0.0 copy-start
  15.1 0.6 copy-done.12
  15.7 0.2 copy-done.1
  15.9 0.3 copy-done
  16.2 0.0 copy-start.14
  16.2 6.3 %states.1 = (bf16[272,512]{1,0:T(8,128)(2,1)}, bf16[272,512]{1,0:T(8,128)(2,1)}, bf16[272,512]{1,0:T(8,128)(2,1)}, bf16[272,512]{1,0:T(8,128)(2,1)}) custom-call(s32[2]{0:T(128)} %pad_add_fusion.scalars, bf16[4,256,256]{2,1,0:T(8,128)(2,1)} %get-tuple-element.23.k_own.refs_1_, bf16[4,256,512]{2,1,0:T(8,128)(2,1)} %get-tuple-element.24.v_own.refs_2_, ...), custom_call_target="tpu_custom_call" | custom-call | tf_op jit(solution)/shard_map/states/pallas_call | solution.py:393
  22.5 1.2 %collective-permute-start.4 = (bf16[272,512]{1,0:T(8,128)(2,1)}, bf16[272,512]{1,0:T(8,128)(2,1)S(1)}, u32[]{:S(2)}, u32[]{:S(2)}) collective-permute-start(bf16[272,512]{1,0:T(8,128)(2,1)} %get-tuple-element.30), channel_id=1, source_target_pairs={{0,2},{1,3},{2,0},{3,1},{4,6},{5,7},{6,4},{7,5},{8,10},{9,11},{10,... | collective-permute-start | bytes 835592 | tf_op jit(solution)/shard_map/ppermute | solution.py:354
  23.7 1.2 %collective-permute-start.5 = (bf16[272,512]{1,0:T(8,128)(2,1)}, bf16[272,512]{1,0:T(8,128)(2,1)S(1)}, u32[]{:S(2)}, u32[]{:S(2)}) collective-permute-start(bf16[272,512]{1,0:T(8,128)(2,1)} %get-tuple-element.31), channel_id=1, source_target_pairs={{0,4},{1,5},{2,6},{3,7},{4,0},{5,1},{6,2},{7,3},{8,12},{9,13},{10,... | collective-permute-start | bytes 835592 | tf_op jit(solution)/shard_map/ppermute | solution.py:354
  25.0 0.2 collective-permute-start.6
  25.2 5.4 %collective-permute-done.4.refs_1_ = bf16[272,512]{1,0:T(8,128)(2,1)S(1)} collective-permute-done((bf16[272,512]{1,0:T(8,128)(2,1)}, bf16[272,512]{1,0:T(8,128)(2,1)S(1)}, u32[]{:S(2)}, u32[]{:S(2)}) %collective-permute-start.4) | collective-permute-done | bytes 278560 | tf_op jit(solution)/shard_map/ppermute | solution.py:354
  30.6 0.0 copy-start.2
  30.6 0.9 collective-permute-done.5.refs_2_
  31.5 0.0 copy-start.3
  31.5 6.0 %collective-permute-done.6.refs_3_ = bf16[272,512]{1,0:T(8,128)(2,1)S(1)} collective-permute-done((bf16[272,512]{1,0:T(8,128)(2,1)}, bf16[272,512]{1,0:T(8,128)(2,1)S(1)}, u32[]{:S(2)}, u32[]{:S(2)}) %collective-permute-start.6) | collective-permute-done | bytes 278560 | tf_op jit(solution)/shard_map/ppermute | solution.py:354
  37.6 0.0 copy-start.4
  37.6 0.0 copy-done.2
  37.6 0.0 copy-done.3
  37.6 0.7 copy-done.4
  38.3 2.2 %group_total.1 = bf16[272,512]{1,0:T(8,128)(2,1)} custom-call(s32[2]{0:T(128)} %pad_add_fusion.scalars, bf16[272,512]{1,0:T(8,128)(2,1)} %get-tuple-element.29.refs_0_, bf16[272,512]{1,0:T(8,128)(2,1)} %copy-done.2, bf16[272,512]{1,0:T(8,128)(2,1)} %copy-done.3, bf16[272,512]{1,0:T(8,128)(2,1)} %copy-done.4), custom_call_target="tpu_custom_call" | custom-call | tf_op jit(solution)/shard_map/group_total/pallas_call | solution.py:413
  40.5 1.3 %collective-permute-start.8 = (bf16[272,512]{1,0:T(8,128)(2,1)}, bf16[272,512]{1,0:T(8,128)(2,1)S(1)}, u32[]{:S(2)}, u32[]{:S(2)}) collective-permute-start(bf16[272,512]{1,0:T(8,128)(2,1)} %group_total.1), channel_id=1, source_target_pairs={{0,16},{1,17},{2,18},{3,19},{4,20},{5,21},{6,22},{7,23},{8,24},{9,... | collective-permute-start | bytes 835592 | tf_op jit(solution)/shard_map/ppermute | solution.py:358
  41.8 3.2 %collective-permute-start.7 = (bf16[272,512]{1,0:T(8,128)(2,1)}, bf16[272,512]{1,0:T(8,128)(2,1)S(1)}, u32[]{:S(2)}, u32[]{:S(2)}) collective-permute-start(bf16[272,512]{1,0:T(8,128)(2,1)} %group_total.1), channel_id=1, source_target_pairs={{0,8},{1,9},{2,10},{3,11},{4,12},{5,13},{6,14},{7,15},{8,16},{9,17... | collective-permute-start | bytes 835592 | tf_op jit(solution)/shard_map/ppermute | solution.py:358
  45.0 0.0 copy-done.14
  45.0 1.9 %collective-permute-start = (bf16[4,256,256]{2,1,0:T(8,128)(2,1)S(1)}, bf16[4,256,256]{2,1,0:T(8,128)(2,1)S(1)}, u32[]{:S(2)}, u32[]{:S(2)}) collective-permute-start(bf16[4,256,256]{2,1,0:T(8,128)(2,1)S(1)} %copy-done.14), channel_id=1, source_target_pairs={{0,1},{1,0},{2,3},{3,2},{4,5},{5,4},{6,7},{7,6},{8,9},{9,8},{10,11... | collective-permute-start | bytes 1572872 | tf_op jit(solution)/shard_map/ppermute | solution.py:350
  46.9 3.4 %collective-permute-done.8.refs_5_ = bf16[272,512]{1,0:T(8,128)(2,1)S(1)} collective-permute-done((bf16[272,512]{1,0:T(8,128)(2,1)}, bf16[272,512]{1,0:T(8,128)(2,1)S(1)}, u32[]{:S(2)}, u32[]{:S(2)}) %collective-permute-start.8) | collective-permute-done | bytes 278560 | tf_op jit(solution)/shard_map/ppermute | solution.py:358
  50.2 0.0 copy-start.10
  50.2 13.8 %collective-permute-done.7.refs_4_ = bf16[272,512]{1,0:T(8,128)(2,1)S(1)} collective-permute-done((bf16[272,512]{1,0:T(8,128)(2,1)}, bf16[272,512]{1,0:T(8,128)(2,1)S(1)}, u32[]{:S(2)}, u32[]{:S(2)}) %collective-permute-start.7) | collective-permute-done | bytes 278560 | tf_op jit(solution)/shard_map/ppermute | solution.py:358
  64.0 0.0 copy-done.10
  64.0 0.0 copy-start.11
  64.0 0.7 copy-done.11
  64.8 3.2 %entering.1 = (bf16[272,512]{1,0:T(8,128)(2,1)}, bf16[272,512]{1,0:T(8,128)(2,1)}, bf16[272,512]{1,0:T(8,128)(2,1)}, bf16[272,512]{1,0:T(8,128)(2,1)}) custom-call(s32[2]{0:T(128)} %pad_add_fusion.scalars, bf16[272,512]{1,0:T(8,128)(2,1)} %get-tuple-element.29.refs_0_, bf16[272,512]{1,0:T(8,128)(2,1)} %copy-done.2, bf16[272,512]{1,0:T(8,128)(2,1)} %copy-done.3, ...), custom_call_target="tpu_custom_call" | custom-call | tf_op jit(solution)/shard_map/entering/pallas_call | solution.py:423
  68.0 1.2 %collective-permute-start.9 = (bf16[272,512]{1,0:T(8,128)(2,1)}, bf16[272,512]{1,0:T(8,128)(2,1)S(1)}, u32[]{:S(2)}, u32[]{:S(2)}) collective-permute-start(bf16[272,512]{1,0:T(8,128)(2,1)} %get-tuple-element.34), channel_id=1, source_target_pairs={{0,2},{1,3},{2,0},{3,1},{4,6},{5,7},{6,4},{7,5},{8,10},{9,11},{10,... | collective-permute-start | bytes 835592 | tf_op jit(solution)/shard_map/ppermute | solution.py:354
  69.2 0.3 collective-permute-start.10
  69.4 1.2 %collective-permute-start.11 = (bf16[272,512]{1,0:T(8,128)(2,1)}, bf16[272,512]{1,0:T(8,128)(2,1)S(1)}, u32[]{:S(2)}, u32[]{:S(2)}) collective-permute-start(bf16[272,512]{1,0:T(8,128)(2,1)} %get-tuple-element.36), channel_id=1, source_target_pairs={{0,6},{1,7},{2,4},{3,5},{4,2},{5,3},{6,0},{7,1},{8,14},{9,15},{10,... | collective-permute-start | bytes 835592 | tf_op jit(solution)/shard_map/ppermute | solution.py:354
  70.6 0.0 collective-permute-done.refs_3_
  70.7 0.0 copy-start.6
  70.7 5.3 %collective-permute-done.9.refs_10_ = bf16[272,512]{1,0:T(8,128)(2,1)S(1)} collective-permute-done((bf16[272,512]{1,0:T(8,128)(2,1)}, bf16[272,512]{1,0:T(8,128)(2,1)S(1)}, u32[]{:S(2)}, u32[]{:S(2)}) %collective-permute-start.9) | collective-permute-done | bytes 278560 | tf_op jit(solution)/shard_map/ppermute | solution.py:354
  75.9 0.0 copy-start.7
  75.9 0.9 collective-permute-done.10.refs_11_
  76.8 0.0 copy-start.8
  76.8 6.1 %collective-permute-done.11.refs_12_ = bf16[272,512]{1,0:T(8,128)(2,1)S(1)} collective-permute-done((bf16[272,512]{1,0:T(8,128)(2,1)}, bf16[272,512]{1,0:T(8,128)(2,1)S(1)}, u32[]{:S(2)}, u32[]{:S(2)}) %collective-permute-start.11) | collective-permute-done | bytes 278560 | tf_op jit(solution)/shard_map/ppermute | solution.py:354
  82.9 0.0 copy-start.9
  82.9 0.0 copy-done.6
  82.9 0.0 copy-done.7
  82.9 0.0 copy-done.8
  82.9 0.7 copy-done.9
  83.6 9.7 %outputs.1 = (bf16[4,256,512]{2,1,0:T(8,128)(2,1)}, bf16[4,256,512]{2,1,0:T(8,128)(2,1)}) custom-call(s32[2]{0:T(128)} %pad_add_fusion.scalars, bf16[4,256,256]{2,1,0:T(8,128)(2,1)} %get-tuple-element.22.refs_0_, bf16[4,256,256]{2,1,0:T(8,128)(2,1)} %get-tuple-element.23.k_own.refs_1_, bf16[4,256,512]{2,1,0:T(8,128)(2,1)} %get-tuple-element.24.v_own.refs_2_, ...), custom_call_target="tpu_custom_call" | custom-call | tf_op jit(solution)/shard_map/outputs/pallas_call | solution.py:434
  93.3 1.6 %collective-permute-start.12 = (bf16[4,256,512]{2,1,0:T(8,128)(2,1)}, bf16[4,256,512]{2,1,0:T(8,128)(2,1)S(1)}, u32[]{:S(2)}, u32[]{:S(2)}) collective-permute-start(bf16[4,256,512]{2,1,0:T(8,128)(2,1)} %get-tuple-element.38), channel_id=1, source_target_pairs={{0,1},{1,0},{2,3},{3,2},{4,5},{5,4},{6,7},{7,6},{8,9},{9,8},{10,11... | collective-permute-start | bytes 3145736 | tf_op jit(solution)/shard_map/ppermute | solution.py:350
  95.0 2.5 %collective-permute-done.12.other_ref = bf16[4,256,512]{2,1,0:T(8,128)(2,1)S(1)} collective-permute-done((bf16[4,256,512]{2,1,0:T(8,128)(2,1)}, bf16[4,256,512]{2,1,0:T(8,128)(2,1)S(1)}, u32[]{:S(2)}, u32[]{:S(2)}) %collective-permute-start.12) | collective-permute-done | bytes 1048608 | tf_op jit(solution)/shard_map/ppermute | solution.py:350
  97.5 0.0 copy-start.5
  97.5 1.0 copy-done.5
  98.4 5.7 %merge.1 = bf16[256,8,512]{2,1,0:T(8,128)(2,1)} custom-call(s32[2]{0:T(128)} %pad_add_fusion.scalars, bf16[4,256,512]{2,1,0:T(8,128)(2,1)} %get-tuple-element.37.own_ref, bf16[4,256,512]{2,1,0:T(8,128)(2,1)} %copy-done.5), custom_call_target="tpu_custom_call" | custom-call | tf_op jit(solution)/shard_map/merge/pallas_call | solution.py:455
Async XLA Ops:
  0.6 11.7 %copy-start.13 = (s32[1024]{0:T(1024)S(1)}, s32[1024]{0:T(1024)}, u32[]{:S(2)}) copy-start(s32[1024]{0:T(1024)} %param.11) | copy-start | bytes 12292
  11.2 3.9 %collective-permute-start.2 = (bf16[4,256,512]{2,1,0:T(8,128)(2,1)}, bf16[4,256,512]{2,1,0:T(8,128)(2,1)S(1)}, u32[]{:S(2)}, u32[]{:S(2)}) collective-permute-start(bf16[4,256,512]{2,1,0:T(8,128)(2,1)} %get-tuple-element.27), channel_id=1, source_target_pairs={{0,1},{1,0},{2,3},{3,2},{4,5},{5,4},{6,7},{7,6},{8,9},{9,8},{10,11... | collective-permute-start | bytes 3145736 | tf_op jit(solution)/shard_map/ppermute | solution.py:350
  11.8 3.3 %collective-permute-start.1 = (bf16[4,256,256]{2,1,0:T(8,128)(2,1)}, bf16[4,256,256]{2,1,0:T(8,128)(2,1)S(1)}, u32[]{:S(2)}, u32[]{:S(2)}) collective-permute-start(bf16[4,256,256]{2,1,0:T(8,128)(2,1)} %get-tuple-element.26), channel_id=1, source_target_pairs={{0,1},{1,0},{2,3},{3,2},{4,5},{5,4},{6,7},{7,6},{8,9},{9,8},{10,11... | collective-permute-start | bytes 1572872 | tf_op jit(solution)/shard_map/ppermute | solution.py:350
  11.9 3.2 %collective-permute-start.3 = (bf16[16,256]{1,0:T(8,128)(2,1)}, bf16[16,256]{1,0:T(8,128)(2,1)S(1)}, u32[]{:S(2)}, u32[]{:S(2)}) collective-permute-start(bf16[16,256]{1,0:T(8,128)(2,1)} %get-tuple-element.28.g_own.refs_6_), channel_id=1, source_target_pairs={{0,1},{1,0},{2,3},{3,2},{4,5},{5,4},{6,7},{7,6},{8,9},{9,8},{10,11... | collective-permute-start | bytes 24584 | tf_op jit(solution)/shard_map/ppermute | solution.py:350
  15.1 0.6 copy-start.12
  15.1 0.8 copy-start.1
  15.1 1.1 %copy-start = (bf16[4,256,512]{2,1,0:T(8,128)(2,1)}, bf16[4,256,512]{2,1,0:T(8,128)(2,1)S(1)}, u32[]{:S(2)}) copy-start(bf16[4,256,512]{2,1,0:T(8,128)(2,1)S(1)} %collective-permute-done.2.v_oth.refs_5_) | copy-start | bytes 3145732
  16.2 28.7 %copy-start.14 = (bf16[4,256,256]{2,1,0:T(8,128)(2,1)S(1)}, bf16[4,256,256]{2,1,0:T(8,128)(2,1)}, u32[]{:S(2)}) copy-start(bf16[4,256,256]{2,1,0:T(8,128)(2,1)} %get-tuple-element.25) | copy-start | bytes 1572868
  22.5 8.0 %collective-permute-start.4 = (bf16[272,512]{1,0:T(8,128)(2,1)}, bf16[272,512]{1,0:T(8,128)(2,1)S(1)}, u32[]{:S(2)}, u32[]{:S(2)}) collective-permute-start(bf16[272,512]{1,0:T(8,128)(2,1)} %get-tuple-element.30), channel_id=1, source_target_pairs={{0,2},{1,3},{2,0},{3,1},{4,6},{5,7},{6,4},{7,5},{8,10},{9,11},{10,... | collective-permute-start | bytes 835592 | tf_op jit(solution)/shard_map/ppermute | solution.py:354
  23.7 7.8 %collective-permute-start.5 = (bf16[272,512]{1,0:T(8,128)(2,1)}, bf16[272,512]{1,0:T(8,128)(2,1)S(1)}, u32[]{:S(2)}, u32[]{:S(2)}) collective-permute-start(bf16[272,512]{1,0:T(8,128)(2,1)} %get-tuple-element.31), channel_id=1, source_target_pairs={{0,4},{1,5},{2,6},{3,7},{4,0},{5,1},{6,2},{7,3},{8,12},{9,13},{10,... | collective-permute-start | bytes 835592 | tf_op jit(solution)/shard_map/ppermute | solution.py:354
  25.0 12.6 %collective-permute-start.6 = (bf16[272,512]{1,0:T(8,128)(2,1)}, bf16[272,512]{1,0:T(8,128)(2,1)S(1)}, u32[]{:S(2)}, u32[]{:S(2)}) collective-permute-start(bf16[272,512]{1,0:T(8,128)(2,1)} %get-tuple-element.32), channel_id=1, source_target_pairs={{0,6},{1,7},{2,4},{3,5},{4,2},{5,3},{6,0},{7,1},{8,14},{9,15},{10,... | collective-permute-start | bytes 835592 | tf_op jit(solution)/shard_map/ppermute | solution.py:354
  30.6 7.0 %copy-start.2 = (bf16[272,512]{1,0:T(8,128)(2,1)}, bf16[272,512]{1,0:T(8,128)(2,1)S(1)}, u32[]{:S(2)}) copy-start(bf16[272,512]{1,0:T(8,128)(2,1)S(1)} %collective-permute-done.4.refs_1_) | copy-start | bytes 835588
  31.5 6.1 %copy-start.3 = (bf16[272,512]{1,0:T(8,128)(2,1)}, bf16[272,512]{1,0:T(8,128)(2,1)S(1)}, u32[]{:S(2)}) copy-start(bf16[272,512]{1,0:T(8,128)(2,1)S(1)} %collective-permute-done.5.refs_2_) | copy-start | bytes 835588
  37.6 0.7 copy-start.4
  40.5 9.8 %collective-permute-start.8 = (bf16[272,512]{1,0:T(8,128)(2,1)}, bf16[272,512]{1,0:T(8,128)(2,1)S(1)}, u32[]{:S(2)}, u32[]{:S(2)}) collective-permute-start(bf16[272,512]{1,0:T(8,128)(2,1)} %group_total.1), channel_id=1, source_target_pairs={{0,16},{1,17},{2,18},{3,19},{4,20},{5,21},{6,22},{7,23},{8,24},{9,... | collective-permute-start | bytes 835592 | tf_op jit(solution)/shard_map/ppermute | solution.py:358
  41.8 22.3 %collective-permute-start.7 = (bf16[272,512]{1,0:T(8,128)(2,1)}, bf16[272,512]{1,0:T(8,128)(2,1)S(1)}, u32[]{:S(2)}, u32[]{:S(2)}) collective-permute-start(bf16[272,512]{1,0:T(8,128)(2,1)} %group_total.1), channel_id=1, source_target_pairs={{0,8},{1,9},{2,10},{3,11},{4,12},{5,13},{6,14},{7,15},{8,16},{9,17... | collective-permute-start | bytes 835592 | tf_op jit(solution)/shard_map/ppermute | solution.py:358
  45.0 25.7 %collective-permute-start = (bf16[4,256,256]{2,1,0:T(8,128)(2,1)S(1)}, bf16[4,256,256]{2,1,0:T(8,128)(2,1)S(1)}, u32[]{:S(2)}, u32[]{:S(2)}) collective-permute-start(bf16[4,256,256]{2,1,0:T(8,128)(2,1)S(1)} %copy-done.14), channel_id=1, source_target_pairs={{0,1},{1,0},{2,3},{3,2},{4,5},{5,4},{6,7},{7,6},{8,9},{9,8},{10,11... | collective-permute-start | bytes 1572872 | tf_op jit(solution)/shard_map/ppermute | solution.py:350
  50.2 13.8 %copy-start.10 = (bf16[272,512]{1,0:T(8,128)(2,1)}, bf16[272,512]{1,0:T(8,128)(2,1)S(1)}, u32[]{:S(2)}) copy-start(bf16[272,512]{1,0:T(8,128)(2,1)S(1)} %collective-permute-done.8.refs_5_) | copy-start | bytes 835588
  64.0 0.7 copy-start.11
  68.0 7.9 %collective-permute-start.9 = (bf16[272,512]{1,0:T(8,128)(2,1)}, bf16[272,512]{1,0:T(8,128)(2,1)S(1)}, u32[]{:S(2)}, u32[]{:S(2)}) collective-permute-start(bf16[272,512]{1,0:T(8,128)(2,1)} %get-tuple-element.34), channel_id=1, source_target_pairs={{0,2},{1,3},{2,0},{3,1},{4,6},{5,7},{6,4},{7,5},{8,10},{9,11},{10,... | collective-permute-start | bytes 835592 | tf_op jit(solution)/shard_map/ppermute | solution.py:354
  69.2 7.7 %collective-permute-start.10 = (bf16[272,512]{1,0:T(8,128)(2,1)}, bf16[272,512]{1,0:T(8,128)(2,1)S(1)}, u32[]{:S(2)}, u32[]{:S(2)}) collective-permute-start(bf16[272,512]{1,0:T(8,128)(2,1)} %get-tuple-element.35), channel_id=1, source_target_pairs={{0,4},{1,5},{2,6},{3,7},{4,0},{5,1},{6,2},{7,3},{8,12},{9,13},{10,... | collective-permute-start | bytes 835592 | tf_op jit(solution)/shard_map/ppermute | solution.py:354
  69.4 13.5 %collective-permute-start.11 = (bf16[272,512]{1,0:T(8,128)(2,1)}, bf16[272,512]{1,0:T(8,128)(2,1)S(1)}, u32[]{:S(2)}, u32[]{:S(2)}) collective-permute-start(bf16[272,512]{1,0:T(8,128)(2,1)} %get-tuple-element.36), channel_id=1, source_target_pairs={{0,6},{1,7},{2,4},{3,5},{4,2},{5,3},{6,0},{7,1},{8,14},{9,15},{10,... | collective-permute-start | bytes 835592 | tf_op jit(solution)/shard_map/ppermute | solution.py:354
  70.7 12.3 %copy-start.6 = (bf16[4,256,256]{2,1,0:T(8,128)(2,1)}, bf16[4,256,256]{2,1,0:T(8,128)(2,1)S(1)}, u32[]{:S(2)}) copy-start(bf16[4,256,256]{2,1,0:T(8,128)(2,1)S(1)} %collective-permute-done.refs_3_) | copy-start | bytes 1572868
  75.9 7.0 %copy-start.7 = (bf16[272,512]{1,0:T(8,128)(2,1)}, bf16[272,512]{1,0:T(8,128)(2,1)S(1)}, u32[]{:S(2)}) copy-start(bf16[272,512]{1,0:T(8,128)(2,1)S(1)} %collective-permute-done.9.refs_10_) | copy-start | bytes 835588
  76.8 6.1 %copy-start.8 = (bf16[272,512]{1,0:T(8,128)(2,1)}, bf16[272,512]{1,0:T(8,128)(2,1)S(1)}, u32[]{:S(2)}) copy-start(bf16[272,512]{1,0:T(8,128)(2,1)S(1)} %collective-permute-done.10.refs_11_) | copy-start | bytes 835588
  82.9 0.7 copy-start.9
  93.3 4.1 %collective-permute-start.12 = (bf16[4,256,512]{2,1,0:T(8,128)(2,1)}, bf16[4,256,512]{2,1,0:T(8,128)(2,1)S(1)}, u32[]{:S(2)}, u32[]{:S(2)}) collective-permute-start(bf16[4,256,512]{2,1,0:T(8,128)(2,1)} %get-tuple-element.38), channel_id=1, source_target_pairs={{0,1},{1,0},{2,3},{3,2},{4,5},{5,4},{6,7},{7,6},{8,9},{9,8},{10,11... | collective-permute-start | bytes 3145736 | tf_op jit(solution)/shard_map/ppermute | solution.py:350
  97.5 1.0 copy-start.5

commit v2 on v1

--- a/solution.py
+++ b/solution.py
@@ -11,6 +11,7 @@
 FLOOR_NEG = -1e30
 META = 16
 LANES = 128
+LAY = 256
 F32, BF16 = jnp.float32, jnp.bfloat16
 
 NN = (((1,), (0,)), ((), ()))
@@ -77,53 +78,52 @@
     return gate_in, decay
 
 
-def relayout_kernel(half, q_ref, k_ref, v_ref, in_ref, forget_ref, scalars, *outs):
+def by_head_order(heads):
+    n = LAY // heads
+    out, inside = iota((LAY, LAY), 0), iota((LAY, LAY), 1)
+    return ((inside % heads == out // n) & (inside // heads == out % n)).astype(BF16)
+
+
+def relayout_kernel(half, count, scalars, *refs):
+    sources, outs = refs[:count], refs[count:]
+    heads = 2 * half
+    n = LAY // heads
     core = scalars[1]
-    q_keep, k_keep, v_keep, q_send, k_send, v_send, gates = outs
-    heads = in_ref.shape[0]
-    gates[:heads, :] = in_ref[...]
-    gates[heads:, :] = forget_ref[...]
-
-    def body(first, second):
-        for source, low, high in zip((q_ref, k_ref, v_ref), first, second, strict=True):
-            for h in range(half):
-                low[h] = source[:, h, :]
-                high[h] = source[:, half + h, :]
-
-    keep, send = (q_keep, k_keep, v_keep), (q_send, k_send, v_send)
-
-    @pl.when(core == 0)
-    def _():
-        body(keep, send)
-
-    @pl.when(core != 0)
-    def _():
-        body(send, keep)
-
-
-def state_kernel(
-    heads, scalars, k_own, v_own, k_oth, v_oth, g_own, g_oth, ids_ref, *rest
-):
-    outs, (factors, tops, decays, payload) = rest[:-4], rest[-4:]
-    step = pl.program_id(0)
+    order = by_head_order(heads)
+    for index, source in enumerate(sources):
+        keep, send = outs[index], outs[count + index]
+        tokens, _, width = source.shape
+        for g in range(tokens // n):
+            span = slice(g * n, (g + 1) * n)
+            rows = dot(order, source[span].reshape(LAY, width)).astype(BF16)
+            rows = rows.reshape(heads, n, width)
+            keep[:, span, :] = jnp.where(core == 0, rows[:half], rows[half:])
+            send[:, span, :] = jnp.where(core == 0, rows[half:], rows[:half])
+
+
+def gates_kernel(heads, scalars, g_own, g_oth, ids_ref, *outs):
+    factors, tops, decays, source_rows, columns = outs
     core = scalars[1]
-    half = heads // 2
-    tokens = k_own.shape[1]
-    key_width, value_width = k_own.shape[2], v_own.shape[2]
+    length = ids_ref.shape[1]
+    gate_in, decay = gate_rows(core, g_own, g_oth, heads)
+    ids = ids_ref[...]
+    exponent = decay[:, length - 1 :] - decay + gate_in
+    exponent = jnp.where(ids == ids[:, length - 1 :], exponent, FLOOR_NEG)
+    top = jnp.max(exponent, axis=1, keepdims=True)
+    factors[...] = jnp.exp(exponent - top)
+    tops[...] = jnp.broadcast_to(top, tops.shape)
+    decays[...] = jnp.broadcast_to(decay[:, length - 1 :], decays.shape)
+    source_rows[...] = gate_in - decay
+    docs = ids.astype(F32) + 1.0
+    filler = jnp.zeros((LANES - heads - 1, length), F32)
+    columns[...] = jnp.concatenate([decay, docs, filler], axis=0).T
+
+
+def state_kernel(slot, heads, scalars, k_own, v_own, k_oth, v_oth, factors, tops, decays, ids_ref, out):
+    core = scalars[1]
+    tokens, key_width = k_own.shape[1:]
     length = 2 * tokens
-
-    @pl.when(step == 0)
-    def _():
-        gate_in, decay = gate_rows(core, g_own, g_oth, heads)
-        ids = ids_ref[...]
-        exponent = decay[:, length - 1 :] - decay + gate_in
-        exponent = jnp.where(ids == ids[:, length - 1 :], exponent, FLOOR_NEG)
-        top = jnp.max(exponent, axis=1, keepdims=True)
-        factors[...] = jnp.exp(exponent - top)
-        tops[...] = jnp.broadcast_to(top, tops.shape)
-        decays[...] = jnp.broadcast_to(decay[:, length - 1 :], decays.shape)
-
-    head = half * core + jnp.bitwise_xor(scalars[0], step)
+    head = (heads // 2) * core + jnp.bitwise_xor(scalars[0], slot)
     row = factors[pl.ds(head, 1), :]
     first, last = row[:, :tokens], row[:, tokens:]
     total, normal = None, None
@@ -142,15 +142,10 @@
         total = part if total is None else total + part
         normal = line if normal is None else normal + line
     doc = jnp.broadcast_to(ids_ref[:, length - 1 :].astype(F32) + 1.0, (1, LANES))
-    payload[:key_width, :] = total.astype(BF16)
-    payload[key_width:, :] = meta_rows(
+    out[:key_width, :] = total.astype(BF16)
+    out[key_width:, :] = meta_rows(
         normal, tops[pl.ds(head, 1), :], decays[pl.ds(head, 1), :], doc
     )
-    for i, out in enumerate(outs):
-
-        @pl.when(step == i)
-        def _(out=out):
-            out[...] = payload[...]
 
 
 def total_kernel(group, scalars, *refs):
@@ -226,42 +221,22 @@
         outs[r][key_width:, :] = meta_rows(normal, top, zero, doc)
 
 
-def output_kernel(heads, group, scalars, *refs):
-    q_own, k_own, v_own, q_oth, k_oth, v_oth, g_own, g_oth, ids_ref = refs[:9]
-    entering = refs[9 : 9 + group]
-    keep, send, source_rows, columns, bias, payload = refs[9 + group :]
-    step = pl.program_id(0)
+def output_kernel(slot, heads, scalars, *refs):
+    q_own, k_own, v_own, q_oth, k_oth, v_oth, source_rows, columns, ids_ref, payload = refs[:10]
+    keep, send = refs[10:]
     core = scalars[1]
-    half = heads // 2
-    tokens, key_width = q_own.shape[1], q_own.shape[2]
+    tokens, key_width = q_own.shape[1:]
     length = 2 * tokens
     scaling = key_width**-0.5
-
-    @pl.when(step == 0)
-    def _():
-        gate_in, decay = gate_rows(core, g_own, g_oth, heads)
-        source_rows[...] = gate_in - decay
-        docs = ids_ref[...].astype(F32) + 1.0
-        filler = jnp.zeros((LANES - heads - 1, length), F32)
-        turned = jnp.concatenate([decay, docs, filler], axis=0).T
-        columns[...] = turned
-        same = turned[:, heads : heads + 1] == docs
-        causal = iota((length, length), 0) >= iota((length, length), 1)
-        bias[...] = jnp.where(same & causal, 0.0, FLOOR_NEG)
-
-    for i, ref in enumerate(entering):
-
-        @pl.when(step == i)
-        def _(ref=ref):
-            payload[...] = ref[...]
-
-    head = half * core + jnp.bitwise_xor(scalars[0], step)
+    head = (heads // 2) * core + jnp.bitwise_xor(scalars[0], slot)
     is_first = core == 0
     source = source_rows[pl.ds(head, 1), :]
     lane = iota((length, LANES), 1)
     turned = columns[...]
     decay = jnp.sum(jnp.where(lane == head, turned, 0.0), axis=1, keepdims=True)
     docs = turned[:, heads : heads + 1]
+    source_docs = ids_ref[...].astype(F32) + 1.0
+    causal = iota((tokens, tokens), 0) >= iota((tokens, tokens), 1)
     normal, top, _, doc = read_meta(payload)
     carried = jnp.where(docs == doc[:, :1], decay + top[:, :1], FLOOR_NEG)
     pieces = jnp.concatenate(split3(normal) + (jnp.zeros((META - 3, key_width), F32),), axis=0)
@@ -281,7 +256,10 @@
         exponents = []
         for s in range(block + 1):
             cols = slice(s * tokens, (s + 1) * tokens)
-            exponent = (decay[rows] + source[:, cols]) + bias[rows, cols]
+            allowed = docs[rows] == source_docs[:, cols]
+            if s == block:
+                allowed = allowed & causal
+            exponent = jnp.where(allowed, decay[rows] + source[:, cols], FLOOR_NEG)
             exponents.append(exponent)
             stabilizer = jnp.maximum(stabilizer, jnp.max(exponent, axis=1, keepdims=True))
         retained = jnp.exp(carried[rows] - stabilizer) * scaling
@@ -297,25 +275,26 @@
                 low = (weights - high.astype(F32)).astype(BF16)
                 numerator = numerator + dot(low, values[s])
         results.append((numerator / jnp.maximum(jnp.abs(denominator), 1.0)).astype(BF16))
-    keep[0] = jnp.where(is_first, results[0], results[1])
-    send[0] = jnp.where(is_first, results[1], results[0])
-
-
-def merge_kernel(scalars, own_ref, other_ref, out_ref):
-    half = own_ref.shape[0]
-
-    def body(low, high):
-        for h in range(half):
-            out_ref[:, h, :] = low[h]
-            out_ref[:, half + h, :] = high[h]
-
-    @pl.when(scalars[1] == 0)
-    def _():
-        body(own_ref, other_ref)
-
-    @pl.when(scalars[1] != 0)
-    def _():
-        body(other_ref, own_ref)
+    keep[...] = jnp.where(is_first, results[0], results[1])
+    send[...] = jnp.where(is_first, results[1], results[0])
+
+
+def merge_kernel(heads, scalars, *refs):
+    pieces, out = refs[:heads], refs[heads]
+    half = heads // 2
+    n = LAY // heads
+    mine, core = scalars[0], scalars[1]
+    into, given = iota((LAY, LAY), 0), iota((LAY, LAY), 1)
+    index = given // n
+    slot = jnp.bitwise_and(index, half - 1)
+    side = jnp.where(index < half, core, 1 - core)
+    head = side * half + jnp.bitwise_xor(slot, mine)
+    order = ((into % heads == head) & (into // heads == given % n)).astype(BF16)
+    tokens, width = pieces[0].shape
+    for g in range(tokens // n):
+        span = slice(g * n, (g + 1) * n)
+        rows = jnp.concatenate([piece[span, :] for piece in pieces], axis=0)
+        out[span] = dot(order, rows).reshape(n, heads, width).astype(BF16)
 
 
 def whole(shape):
@@ -358,57 +337,75 @@
         return lax.ppermute(x, AXES, [(d, d + jump) for d in range(devices - jump)])
 
     rows = key_width + META
-    narrow, wide = (half, tokens, key_width), (half, tokens, value_width)
-    q_keep, k_keep, v_keep, q_send, k_send, v_send, gates = pl.pallas_call(
-        functools.partial(relayout_kernel, half),
-        in_specs=[
-            whole(queries.shape),
-            whole(key_vectors.shape),
-            whole(value_vectors.shape),
-            whole((heads, tokens)),
-            whole((heads, tokens)),
-            SMEM,
-        ],
-        out_specs=[whole(s) for s in (narrow, narrow, wide) * 2 + ((2 * heads, tokens),)],
-        out_shape=[shape_of(*s) for s in (narrow, narrow, wide) * 2 + ((2 * heads, tokens),)],
+    state = (rows, value_width)
+    sizes = {key_width: (half, tokens, key_width), value_width: (half, tokens, value_width)}
+
+    def relayout(*sources):
+        outs = [sizes[x.shape[2]] for x in sources] * 2
+        return pl.pallas_call(
+            functools.partial(relayout_kernel, half, len(sources)),
+            in_specs=[SMEM] + [whole(x.shape) for x in sources],
+            out_specs=[whole(s) for s in outs],
+            out_shape=[shape_of(*s) for s in outs],
+            compiler_params=params(),
+            name="relayout",
+        )(scalars, *sources)
+
+    gates = jnp.concatenate([input_gate.T, forget_gate.T], axis=0)
+    gates_oth = swap_cores(gates)
+    k_keep, v_keep, k_send, v_send = relayout(key_vectors, value_vectors)
+    v_oth = swap_cores(v_send)
+    k_oth = swap_cores(k_send)
+    gate_shapes = [
+        (heads, 2 * tokens),
+        (heads, LANES),
+        (heads, LANES),
+        (heads, 2 * tokens),
+        (2 * tokens, LANES),
+    ]
+    factors, tops, decays, source_rows, columns = pl.pallas_call(
+        functools.partial(gates_kernel, heads),
+        in_specs=[SMEM] + [whole(gates.shape)] * 2 + [whole(ids.shape)],
+        out_specs=[whole(s) for s in gate_shapes],
+        out_shape=[shape_of(*s, dtype=F32) for s in gate_shapes],
         compiler_params=params(),
-        name="relayout",
-    )(queries, key_vectors, value_vectors, input_gate.T, forget_gate.T, scalars)
-    gates_oth = swap_cores(gates)
-    k_oth = swap_cores(k_send)
-    v_oth = swap_cores(v_send)
+        name="gates",
+    )(scalars, gates, gates_oth, ids)
+
+    def of_head(slot, x):
+        return pl.BlockSpec(
+            (1,) + x.shape[1:], lambda i, s: (jnp.bitwise_xor(s[0], slot), 0, 0)
+        )
+
+    def per_head(kernel, slot, by_head, others, out_shapes, name):
+        return pl.pallas_call(
+            functools.partial(kernel, slot, heads),
+            grid_spec=pltpu.PrefetchScalarGridSpec(
+                num_scalar_prefetch=1,
+                grid=(1,),
+                in_specs=[of_head(slot, x) for x in by_head] + [whole(x.shape) for x in others],
+                out_specs=[whole(s) for s in out_shapes],
+            ),
+            out_shape=[shape_of(*s) for s in out_shapes],
+            compiler_params=params(),
+            name=name,
+        )(scalars, *by_head, *others)
+
+    farthest_first = list(range(group - 1, -1, -1))
+    gathered = [None] * group
+    for r in farthest_first:
+        [made] = per_head(
+            state_kernel,
+            r,
+            (k_keep, v_keep, k_oth, v_oth),
+            (factors, tops, decays, ids),
+            [state],
+            "state",
+        )
+        gathered[r] = in_group(made, r) if r else made
+    queries, gathered[0] = lax.optimization_barrier((queries, gathered[0]))
+    q_keep, q_send = relayout(queries)
     q_oth = swap_cores(q_send)
-
-    def by_head(width):
-        return pl.BlockSpec(
-            (1, tokens, width), lambda i, s: (jnp.bitwise_xor(s[0], i), 0, 0)
-        )
-
-    small = [
-        whole((2 * heads, tokens)),
-        whole((2 * heads, tokens)),
-        whole((1, 2 * tokens)),
-    ]
-    state = (rows, value_width)
-    states = pl.pallas_call(
-        functools.partial(state_kernel, heads),
-        grid_spec=pltpu.PrefetchScalarGridSpec(
-            num_scalar_prefetch=1,
-            grid=(group,),
-            in_specs=[by_head(key_width), by_head(value_width)] * 2 + small,
-            out_specs=[whole(state)] * group,
-            scratch_shapes=[
-                pltpu.VMEM((heads, 2 * tokens), F32),
-                pltpu.VMEM((heads, LANES), F32),
-                pltpu.VMEM((heads, LANES), F32),
-                pltpu.VMEM(state, BF16),
-            ],
-        ),
-        out_shape=[shape_of(*state)] * group,
-        compiler_params=params(),
-        name="states",
-    )(scalars, k_keep, v_keep, k_oth, v_oth, gates, gates_oth, ids)
-    gathered = [states[0]] + [in_group(states[r], r) for r in range(1, group)]
 
     total = pl.pallas_call(
         functools.partial(total_kernel, group),
@@ -418,7 +415,7 @@
         compiler_params=params(),
         name="group_total",
     )(scalars, *gathered)
-    totals = [to_later(total, d) for d in range(1, reach + 1)]
+    totals = [to_later(total, d) for d in range(reach, 0, -1)][::-1]
 
     outgoing = pl.pallas_call(
         functools.partial(entering_kernel, group, reach),
@@ -428,38 +425,28 @@
         compiler_params=params(),
         name="entering",
     )(scalars, *gathered, *totals)
-    entering = [outgoing[0]] + [in_group(outgoing[r], r) for r in range(1, group)]
-
-    length = 2 * tokens
-    keep, send = pl.pallas_call(
-        functools.partial(output_kernel, heads, group),
-        grid_spec=pltpu.PrefetchScalarGridSpec(
-            num_scalar_prefetch=1,
-            grid=(group,),
-            in_specs=[by_head(key_width), by_head(key_width), by_head(value_width)] * 2
-            + small
-            + [whole(state)] * group,
-            out_specs=[by_head(value_width)] * 2,
-            scratch_shapes=[
-                pltpu.VMEM((heads, length), F32),
-                pltpu.VMEM((length, LANES), F32),
-                pltpu.VMEM((length, length), F32),
-                pltpu.VMEM(state, BF16),
-            ],
-        ),
-        out_shape=[shape_of(*wide)] * 2,
-        compiler_params=params(),
-        name="outputs",
-    )(scalars, q_keep, k_keep, v_keep, q_oth, k_oth, v_oth, gates, gates_oth, ids, *entering)
-    received = swap_cores(send)
+    entering = [in_group(outgoing[r], r) if r else outgoing[r] for r in farthest_first][::-1]
+
+    kept, received = [], []
+    for r in range(group):
+        keep, send = per_head(
+            output_kernel,
+            r,
+            (q_keep, k_keep, v_keep, q_oth, k_oth, v_oth),
+            (source_rows, columns, ids, entering[r]),
+            [(tokens, value_width)] * 2,
+            "output",
+        )
+        kept.append(keep)
+        received.append(swap_cores(send))
     return pl.pallas_call(
-        merge_kernel,
-        in_specs=[SMEM, whole(wide), whole(wide)],
+        functools.partial(merge_kernel, heads),
+        in_specs=[SMEM] + [whole((tokens, value_width))] * heads,
         out_specs=whole(value_vectors.shape),
         out_shape=shape_of(*value_vectors.shape),
         compiler_params=params(),
         name="merge",
-    )(scalars, keep, received)
+    )(scalars, *kept, *received)
 
 
 def solution(mesh):

time: 105 us -> 95.7 us (0.911)
  the two profiles are of different devices: /device:TPU:17 before, /device:TPU:25 now
where the time goes in v2:
time: 95.7 us; the launch traced here: 95.1 us
  Pallas kernels  49.1 us (51%)
  waiting for transfers between devices  21.6 us (23%)
  starting transfers between devices  15.8 us (17%)
  local copies, waits for them, and re-layouts  7.9 us (8%)
    pallas_call x8, Pallas kernels, per_head(): pl.pallas_call(functools.partial(kernel, slot, heads), grid_spec=pltpu.Pr...  31.1 us
    ppermute x2, waiting for transfers between devices, to_later(): return lax.ppermute(x, AXES, [(d, d + jump) for d in range(devices - jump)])  13.9 us
    unnamed x40, local copies, waits for them, and re-layouts  7.25 us
    pallas_call x2, Pallas kernels, relayout(): pl.pallas_call(functools.partial(relayout_kernel, half, len(sources)), in...  7.12 us
    ppermute x8, starting transfers between devices, swap_cores(): return lax.ppermute(x, AXES, [(d, d ^ 1) for d in range(devices)])  7.09 us
    ppermute x6, starting transfers between devices, in_group(): return lax.ppermute(x, AXES, pairs)  5.98 us
    ppermute x6, waiting for transfers between devices, in_group(): return lax.ppermute(x, AXES, pairs)  4.26 us
    pallas_call x1, Pallas kernels, local(): pl.pallas_call(functools.partial(merge_kernel, heads), in_specs=[SMEM] +...  3.55 us
  transfers between devices with their start and end apart: 16, of which 6 were waited for; matrix products, arithmetic and copies ran while one was open for 1% of the time, Pallas kernels for 38%

profile of v2, /device:TPU:25, one launch (start us, length us, event | category | flops | bytes accessed | tf_op | source)
XLA Modules:
  0.0 95.1 jit_solution(4111880429307302257)
XLA Ops:
  0.0 0.6 pad_add_fusion.scalars
  0.6 4.4 %relayout.2 = (bf16[4,256,256]{2,1,0:T(8,128)(2,1)}, bf16[4,256,512]{2,1,0:T(8,128)(2,1)}, bf16[4,256,256]{2,1,0:T(8,128)(2,1)}, bf16[4,256,512]{2,1,0:T(8,128)(2,1)}) custom-call(s32[2]{0:T(128)} %pad_add_fusion.scalars, bf16[256,8,256]{2,1,0:T(8,128)(2,1)} %refs_0_.1, bf16[256,8,512]{2,1,0:T(8,128)(2,1)} %refs_1_.1), custom_call_target="tpu_custom_call" | custom-call | tf_op jit(solution)/shard_map/relayout/pallas_call | solution.py:345
  5.1 0.7 collective-permute-start.1
  5.7 0.0 collective-permute-start
  5.8 0.0 copy-done.18
  5.8 0.6 collective-permute-start.2
  6.3 0.6 dynamic_slice.3
  7.0 2.0 %collective-permute-done.2.g_oth = bf16[16,256]{1,0:T(8,128)(2,1)S(1)} collective-permute-done((bf16[16,256]{1,0:T(8,128)(2,1)S(1)}, bf16[16,256]{1,0:T(8,128)(2,1)S(1)}, u32[]{:S(2)}, u32[]{:S(2)}) %collective-permute-start.2) | collective-permute-done | bytes 8224 | tf_op jit(solution)/shard_map/ppermute | solution.py:329
  9.0 0.0 copy-done.15
  9.0 0.6 copy-done.16
  9.6 1.9 %gates.1 = (f32[8,512]{1,0:T(8,128)}, f32[8,128]{1,0:T(8,128)}, f32[8,128]{1,0:T(8,128)}, f32[8,512]{1,0:T(8,128)}, f32[512,128]{1,0:T(8,128)}) custom-call(s32[2]{0:T(128)} %pad_add_fusion.scalars, bf16[16,256]{1,0:T(8,128)(2,1)} %copy-done.15, bf16[16,256]{1,0:T(8,128)(2,1)} %copy-done.16, s32[1,512]{1,0:T(1,128)} %bitcast.5), custom_call_target="tpu_custom_call" | custom-call | tf_op jit(solution)/shard_map/gates/pallas_call | solution.py:366
  11.5 0.0 collective-permute-done.k_oth.refs_4_
  11.5 0.0 collective-permute-done.1.v_oth.refs_5_
  11.5 0.8 copy-done.1
  12.3 0.4 copy-done
  12.7 3.0 %state.7 = bf16[272,512]{1,0:T(8,128)(2,1)} custom-call(s32[2]{0:T(128)} %pad_add_fusion.scalars, bf16[4,256,256]{2,1,0:T(8,128)(2,1)} %get-tuple-element.30.k_own.refs_1_, bf16[4,256,512]{2,1,0:T(8,128)(2,1)} %get-tuple-element.31.v_own.refs_2_, bf16[4,256,256]{2,1,0:T(8,128)(2,1)} %copy-done.1, bf16[4,256,512]{2,1,0:T(8,128)(2,1)} %copy-done, ...), custom_call_target="tpu_custom_call" | custom-call | tf_op jit(solution)/shard_map/state/pallas_call | solution.py:381
  15.7 2.2 %collective-permute-start.6 = (bf16[272,512]{1,0:T(8,128)(2,1)}, bf16[272,512]{1,0:T(8,128)(2,1)S(1)}, u32[]{:S(2)}, u32[]{:S(2)}) collective-permute-start(bf16[272,512]{1,0:T(8,128)(2,1)} %state.7), channel_id=1, source_target_pairs={{0,6},{1,7},{2,4},{3,5},{4,2},{5,3},{6,0},{7,1},{8,14},{9,15},{10,... | collective-permute-start | bytes 835592 | tf_op jit(solution)/shard_map/ppermute | solution.py:333
  17.9 3.0 %state.6 = bf16[272,512]{1,0:T(8,128)(2,1)} custom-call(s32[2]{0:T(128)} %pad_add_fusion.scalars, bf16[4,256,256]{2,1,0:T(8,128)(2,1)} %get-tuple-element.30.k_own.refs_1_, bf16[4,256,512]{2,1,0:T(8,128)(2,1)} %get-tuple-element.31.v_own.refs_2_, bf16[4,256,256]{2,1,0:T(8,128)(2,1)} %copy-done.1, bf16[4,256,512]{2,1,0:T(8,128)(2,1)} %copy-done, ...), custom_call_target="tpu_custom_call" | custom-call | tf_op jit(solution)/shard_map/state/pallas_call | solution.py:381
  20.9 0.2 collective-permute-start.5
  21.1 3.0 %state.5 = bf16[272,512]{1,0:T(8,128)(2,1)} custom-call(s32[2]{0:T(128)} %pad_add_fusion.scalars, bf16[4,256,256]{2,1,0:T(8,128)(2,1)} %get-tuple-element.30.k_own.refs_1_, bf16[4,256,512]{2,1,0:T(8,128)(2,1)} %get-tuple-element.31.v_own.refs_2_, bf16[4,256,256]{2,1,0:T(8,128)(2,1)} %copy-done.1, bf16[4,256,512]{2,1,0:T(8,128)(2,1)} %copy-done, ...), custom_call_target="tpu_custom_call" | custom-call | tf_op jit(solution)/shard_map/state/pallas_call | solution.py:381
  24.2 0.2 collective-permute-start.4
  24.4 3.0 %state.4.refs_0_ = bf16[272,512]{1,0:T(8,128)(2,1)} custom-call(s32[2]{0:T(128)} %pad_add_fusion.scalars, bf16[4,256,256]{2,1,0:T(8,128)(2,1)} %get-tuple-element.30.k_own.refs_1_, bf16[4,256,512]{2,1,0:T(8,128)(2,1)} %get-tuple-element.31.v_own.refs_2_, bf16[4,256,256]{2,1,0:T(8,128)(2,1)} %copy-done.1, bf16[4,256,512]{2,1,0:T(8,128)(2,1)} %copy-done, ...), custom_call_target="tpu_custom_call" | custom-call | tf_op jit(solution)/shard_map/state/pallas_call | solution.py:381
  27.4 0.0 collective-permute-done.6.refs_3_
  27.4 4.0 %collective-permute-done.5.refs_2_ = bf16[272,512]{1,0:T(8,128)(2,1)S(1)} collective-permute-done((bf16[272,512]{1,0:T(8,128)(2,1)}, bf16[272,512]{1,0:T(8,128)(2,1)S(1)}, u32[]{:S(2)}, u32[]{:S(2)}) %collective-permute-start.5) | collective-permute-done | bytes 278560 | tf_op jit(solution)/shard_map/ppermute | solution.py:333
  31.4 0.3 collective-permute-done.4.refs_1_
  31.7 0.4 copy-done.4
  32.1 0.7 copy-done.5
  32.8 2.2 %group_total.1 = bf16[272,512]{1,0:T(8,128)(2,1)} custom-call(s32[2]{0:T(128)} %pad_add_fusion.scalars, bf16[272,512]{1,0:T(8,128)(2,1)} %state.4.refs_0_, bf16[272,512]{1,0:T(8,128)(2,1)} %copy-done.5, bf16[272,512]{1,0:T(8,128)(2,1)} %copy-done.4, bf16[272,512]{1,0:T(8,128)(2,1)} %copy-done.3), custom_call_target="tpu_custom_call" | custom-call | tf_op jit(solution)/shard_map/group_total/pallas_call | solution.py:410
  35.0 1.3 %collective-permute-start.7 = (bf16[272,512]{1,0:T(8,128)(2,1)}, bf16[272,512]{1,0:T(8,128)(2,1)S(1)}, u32[]{:S(2)}, u32[]{:S(2)}) collective-permute-start(bf16[272,512]{1,0:T(8,128)(2,1)} %group_total.1), channel_id=1, source_target_pairs={{0,8},{1,9},{2,10},{3,11},{4,12},{5,13},{6,14},{7,15},{8,16},{9,17... | collective-permute-start | bytes 835592 | tf_op jit(solution)/shard_map/ppermute | solution.py:337
  36.3 1.5 %collective-permute-start.8 = (bf16[272,512]{1,0:T(8,128)(2,1)}, bf16[272,512]{1,0:T(8,128)(2,1)S(1)}, u32[]{:S(2)}, u32[]{:S(2)}) collective-permute-start(bf16[272,512]{1,0:T(8,128)(2,1)} %group_total.1), channel_id=1, source_target_pairs={{0,16},{1,17},{2,18},{3,19},{4,20},{5,21},{6,22},{7,23},{8,24},{9,... | collective-permute-start | bytes 835592 | tf_op jit(solution)/shard_map/ppermute | solution.py:337
  37.8 2.7 %relayout.3 = (bf16[4,256,256]{2,1,0:T(8,128)(2,1)}, bf16[4,256,256]{2,1,0:T(8,128)(2,1)}) custom-call(s32[2]{0:T(128)} %pad_add_fusion.scalars, bf16[256,8,256]{2,1,0:T(8,128)(2,1)} %refs_0_.2), custom_call_target="tpu_custom_call" | custom-call | tf_op jit(solution)/shard_map/relayout/pallas_call | solution.py:345
  40.4 1.4 %collective-permute-start.3 = (bf16[4,256,256]{2,1,0:T(8,128)(2,1)}, bf16[4,256,256]{2,1,0:T(8,128)(2,1)S(1)}, u32[]{:S(2)}, u32[]{:S(2)}) collective-permute-start(bf16[4,256,256]{2,1,0:T(8,128)(2,1)} %get-tuple-element.39), channel_id=1, source_target_pairs={{0,1},{1,0},{2,3},{3,2},{4,5},{5,4},{6,7},{7,6},{8,9},{9,8},{10,11... | collective-permute-start | bytes 1572872 | tf_op jit(solution)/shard_map/ppermute | solution.py:329
  41.8 2.2 %collective-permute-done.7.refs_4_ = bf16[272,512]{1,0:T(8,128)(2,1)S(1)} collective-permute-done((bf16[272,512]{1,0:T(8,128)(2,1)}, bf16[272,512]{1,0:T(8,128)(2,1)S(1)}, u32[]{:S(2)}, u32[]{:S(2)}) %collective-permute-start.7) | collective-permute-done | bytes 278560 | tf_op jit(solution)/shard_map/ppermute | solution.py:337
  44.0 11.8 %collective-permute-done.8.refs_5_ = bf16[272,512]{1,0:T(8,128)(2,1)S(1)} collective-permute-done((bf16[272,512]{1,0:T(8,128)(2,1)}, bf16[272,512]{1,0:T(8,128)(2,1)S(1)}, u32[]{:S(2)}, u32[]{:S(2)}) %collective-permute-start.8) | collective-permute-done | bytes 278560 | tf_op jit(solution)/shard_map/ppermute | solution.py:337
  55.8 0.7 copy-done.10
  56.5 3.2 %entering.1 = (bf16[272,512]{1,0:T(8,128)(2,1)}, bf16[272,512]{1,0:T(8,128)(2,1)}, bf16[272,512]{1,0:T(8,128)(2,1)}, bf16[272,512]{1,0:T(8,128)(2,1)}) custom-call(s32[2]{0:T(128)} %pad_add_fusion.scalars, bf16[272,512]{1,0:T(8,128)(2,1)} %state.4.refs_0_, bf16[272,512]{1,0:T(8,128)(2,1)} %copy-done.5, bf16[272,512]{1,0:T(8,128)(2,1)} %copy-done.4, ...), custom_call_target="tpu_custom_call" | custom-call | tf_op jit(solution)/shard_map/entering/pallas_call | solution.py:420
  59.7 3.1 %collective-permute-start.11 = (bf16[272,512]{1,0:T(8,128)(2,1)}, bf16[272,512]{1,0:T(8,128)(2,1)S(1)}, u32[]{:S(2)}, u32[]{:S(2)}) collective-permute-start(bf16[272,512]{1,0:T(8,128)(2,1)} %get-tuple-element.49), channel_id=1, source_target_pairs={{0,6},{1,7},{2,4},{3,5},{4,2},{5,3},{6,0},{7,1},{8,14},{9,15},{10,... | collective-permute-start | bytes 835592 | tf_op jit(solution)/shard_map/ppermute | solution.py:333
  62.8 0.2 collective-permute-start.10
  63.0 0.1 collective-permute-start.9
  63.1 0.0 collective-permute-done.3.refs_3_
  63.1 0.8 copy-done.2
  63.9 4.7 %output.4 = (bf16[256,512]{1,0:T(8,128)(2,1)}, bf16[256,512]{1,0:T(8,128)(2,1)}) custom-call(s32[2]{0:T(128)} %pad_add_fusion.scalars, bf16[4,256,256]{2,1,0:T(8,128)(2,1)} %get-tuple-element.38.refs_0_, bf16[4,256,256]{2,1,0:T(8,128)(2,1)} %get-tuple-element.30.k_own.refs_1_, bf16[4,256,512]{2,1,0:T(8,128)(2,1)} %get-tuple-element.31.v_own.refs_2_, ...), custom_call_target="tpu_custom_call" | custom-call | tf_op jit(solution)/shard_map/output/pallas_call | solution.py:381
  68.6 2.4 %collective-permute-start.12 = (bf16[256,512]{1,0:T(8,128)(2,1)}, bf16[256,512]{1,0:T(8,128)(2,1)S(1)}, u32[]{:S(2)}, u32[]{:S(2)}) collective-permute-start(bf16[256,512]{1,0:T(8,128)(2,1)} %get-tuple-element.51), channel_id=1, source_target_pairs={{0,1},{1,0},{2,3},{3,2},{4,5},{5,4},{6,7},{7,6},{8,9},{9,8},{10,11... | collective-permute-start | bytes 786440 | tf_op jit(solution)/shard_map/ppermute | solution.py:329
  71.0 0.0 collective-permute-done.11.refs_9_
  71.0 0.7 copy-done.8
  71.7 4.8 %output.7 = (bf16[256,512]{1,0:T(8,128)(2,1)}, bf16[256,512]{1,0:T(8,128)(2,1)}) custom-call(s32[2]{0:T(128)} %pad_add_fusion.scalars, bf16[4,256,256]{2,1,0:T(8,128)(2,1)} %get-tuple-element.38.refs_0_, bf16[4,256,256]{2,1,0:T(8,128)(2,1)} %get-tuple-element.30.k_own.refs_1_, bf16[4,256,512]{2,1,0:T(8,128)(2,1)} %get-tuple-element.31.v_own.refs_2_, ...), custom_call_target="tpu_custom_call" | custom-call | tf_op jit(solution)/shard_map/output/pallas_call | solution.py:381
  76.5 1.6 %collective-permute-start.15 = (bf16[256,512]{1,0:T(8,128)(2,1)}, bf16[256,512]{1,0:T(8,128)(2,1)S(1)}, u32[]{:S(2)}, u32[]{:S(2)}) collective-permute-start(bf16[256,512]{1,0:T(8,128)(2,1)} %get-tuple-element.54), channel_id=1, source_target_pairs={{0,1},{1,0},{2,3},{3,2},{4,5},{5,4},{6,7},{7,6},{8,9},{9,8},{10,11... | collective-permute-start | bytes 786440 | tf_op jit(solution)/shard_map/ppermute | solution.py:329
  78.1 0.0 collective-permute-done.10.refs_9_
  78.1 0.7 copy-done.7
  78.8 4.7 %output.6 = (bf16[256,512]{1,0:T(8,128)(2,1)}, bf16[256,512]{1,0:T(8,128)(2,1)}) custom-call(s32[2]{0:T(128)} %pad_add_fusion.scalars, bf16[4,256,256]{2,1,0:T(8,128)(2,1)} %get-tuple-element.38.refs_0_, bf16[4,256,256]{2,1,0:T(8,128)(2,1)} %get-tuple-element.30.k_own.refs_1_, bf16[4,256,512]{2,1,0:T(8,128)(2,1)} %get-tuple-element.31.v_own.refs_2_, ...), custom_call_target="tpu_custom_call" | custom-call | tf_op jit(solution)/shard_map/output/pallas_call | solution.py:381
  83.5 0.0 collective-permute-start.14
  83.5 0.0 collective-permute-done.9.refs_9_
  83.5 0.0 copy-start.6
  83.5 0.7 copy-done.6
  84.2 4.7 %output.5 = (bf16[256,512]{1,0:T(8,128)(2,1)}, bf16[256,512]{1,0:T(8,128)(2,1)}) custom-call(s32[2]{0:T(128)} %pad_add_fusion.scalars, bf16[4,256,256]{2,1,0:T(8,128)(2,1)} %get-tuple-element.38.refs_0_, bf16[4,256,256]{2,1,0:T(8,128)(2,1)} %get-tuple-element.30.k_own.refs_1_, bf16[4,256,512]{2,1,0:T(8,128)(2,1)} %get-tuple-element.31.v_own.refs_2_, ...), custom_call_target="tpu_custom_call" | custom-call | tf_op jit(solution)/shard_map/output/pallas_call | solution.py:381
  89.0 0.5 collective-permute-start.13
  89.5 0.0 collective-permute-done.12.refs_4_
  89.5 0.0 collective-permute-done.15.refs_7_
  89.5 0.0 collective-permute-done.14.refs_6_
  89.5 0.0 copy-start.13
  89.5 1.3 %collective-permute-done.13.refs_5_ = bf16[256,512]{1,0:T(8,128)(2,1)S(1)} collective-permute-done((bf16[256,512]{1,0:T(8,128)(2,1)}, bf16[256,512]{1,0:T(8,128)(2,1)S(1)}, u32[]{:S(2)}, u32[]{:S(2)}) %collective-permute-start.13) | collective-permute-done | bytes 262176 | tf_op jit(solution)/shard_map/ppermute | solution.py:329
  90.9 0.0 copy-done.12
  90.9 0.7 copy-done.14
  91.6 3.6 %merge.1 = bf16[256,8,512]{2,1,0:T(8,128)(2,1)} custom-call(s32[2]{0:T(128)} %pad_add_fusion.scalars, bf16[256,512]{1,0:T(8,128)(2,1)} %get-tuple-element.44.refs_0_, bf16[256,512]{1,0:T(8,128)(2,1)} %get-tuple-element.46.refs_1_, bf16[256,512]{1,0:T(8,128)(2,1)} %get-tuple-element.48.refs_2_, bf16[256,512]{1,0:T(8,128)(2,1)} %get-tuple-element.50.refs_3_, ...), custom_call_target="tpu_custom_call" | custom-call | tf_op jit(solution)/shard_map/merge/pallas_call | solution.py:442
  (25 shorter events, 0.0 us)
Async XLA Ops:
  0.0 5.8 %copy-start.18 = (bf16[256,8]{0,1:T(8,128)(2,1)S(1)}, bf16[256,8]{0,1:T(8,128)(2,1)}, u32[]{:S(2)}) copy-start(bf16[256,8]{0,1:T(8,128)(2,1)} %param.9) | copy-start | bytes 12292
  0.0 5.8 %copy-start.17 = (bf16[256,8]{0,1:T(8,128)(2,1)S(1)}, bf16[256,8]{0,1:T(8,128)(2,1)}, u32[]{:S(2)}) copy-start(bf16[256,8]{0,1:T(8,128)(2,1)} %param.10) | copy-start | bytes 12292
  0.0 6.3 %copy-start.19 = (s32[1024]{0:T(1024)S(1)}, s32[1024]{0:T(1024)}, u32[]{:S(2)}) copy-start(s32[1024]{0:T(1024)} %param.11) | copy-start | bytes 12292
  5.1 6.4 %collective-permute-start.1 = (bf16[4,256,512]{2,1,0:T(8,128)(2,1)}, bf16[4,256,512]{2,1,0:T(8,128)(2,1)S(1)}, u32[]{:S(2)}, u32[]{:S(2)}) collective-permute-start(bf16[4,256,512]{2,1,0:T(8,128)(2,1)} %get-tuple-element.33), channel_id=1, source_target_pairs={{0,1},{1,0},{2,3},{3,2},{4,5},{5,4},{6,7},{7,6},{8,9},{9,8},{10,11... | collective-permute-start | bytes 3145736 | tf_op jit(solution)/shard_map/ppermute | solution.py:329
  5.7 5.8 %collective-permute-start = (bf16[4,256,256]{2,1,0:T(8,128)(2,1)}, bf16[4,256,256]{2,1,0:T(8,128)(2,1)S(1)}, u32[]{:S(2)}, u32[]{:S(2)}) collective-permute-start(bf16[4,256,256]{2,1,0:T(8,128)(2,1)} %get-tuple-element.32), channel_id=1, source_target_pairs={{0,1},{1,0},{2,3},{3,2},{4,5},{5,4},{6,7},{7,6},{8,9},{9,8},{10,11... | collective-permute-start | bytes 1572872 | tf_op jit(solution)/shard_map/ppermute | solution.py:329
  5.8 3.2 %copy-start.15 = (bf16[16,256]{1,0:T(8,128)(2,1)}, bf16[16,256]{1,0:T(8,128)(2,1)S(1)}, u32[]{:S(2)}) copy-start(bf16[16,256]{1,0:T(8,128)(2,1)S(1)} %pad_maximum_fusion.g_own) | copy-start | bytes 24580
  5.8 3.2 %collective-permute-start.2 = (bf16[16,256]{1,0:T(8,128)(2,1)S(1)}, bf16[16,256]{1,0:T(8,128)(2,1)S(1)}, u32[]{:S(2)}, u32[]{:S(2)}) collective-permute-start(bf16[16,256]{1,0:T(8,128)(2,1)S(1)} %pad_maximum_fusion.g_own), channel_id=1, source_target_pairs={{0,1},{1,0},{2,3},{3,2},{4,5},{5,4},{6,7},{7,6},{8,9},{9,8},{10,11... | collective-permute-start | bytes 24584 | tf_op jit(solution)/shard_map/ppermute | solution.py:329
  9.0 0.6 copy-start.16
  11.5 0.8 copy-start.1
  11.5 1.1 %copy-start = (bf16[4,256,512]{2,1,0:T(8,128)(2,1)}, bf16[4,256,512]{2,1,0:T(8,128)(2,1)S(1)}, u32[]{:S(2)}) copy-start(bf16[4,256,512]{2,1,0:T(8,128)(2,1)S(1)} %collective-permute-done.1.v_oth.refs_5_) | copy-start | bytes 3145732
  15.7 11.7 %collective-permute-start.6 = (bf16[272,512]{1,0:T(8,128)(2,1)}, bf16[272,512]{1,0:T(8,128)(2,1)S(1)}, u32[]{:S(2)}, u32[]{:S(2)}) collective-permute-start(bf16[272,512]{1,0:T(8,128)(2,1)} %state.7), channel_id=1, source_target_pairs={{0,6},{1,7},{2,4},{3,5},{4,2},{5,3},{6,0},{7,1},{8,14},{9,15},{10,... | collective-permute-start | bytes 835592 | tf_op jit(solution)/shard_map/ppermute | solution.py:333
  20.9 10.4 %collective-permute-start.5 = (bf16[272,512]{1,0:T(8,128)(2,1)}, bf16[272,512]{1,0:T(8,128)(2,1)S(1)}, u32[]{:S(2)}, u32[]{:S(2)}) collective-permute-start(bf16[272,512]{1,0:T(8,128)(2,1)} %state.6), channel_id=1, source_target_pairs={{0,4},{1,5},{2,6},{3,7},{4,0},{5,1},{6,2},{7,3},{8,12},{9,13},{10,... | collective-permute-start | bytes 835592 | tf_op jit(solution)/shard_map/ppermute | solution.py:333
  24.2 7.5 %collective-permute-start.4 = (bf16[272,512]{1,0:T(8,128)(2,1)}, bf16[272,512]{1,0:T(8,128)(2,1)S(1)}, u32[]{:S(2)}, u32[]{:S(2)}) collective-permute-start(bf16[272,512]{1,0:T(8,128)(2,1)} %state.5), channel_id=1, source_target_pairs={{0,2},{1,3},{2,0},{3,1},{4,6},{5,7},{6,4},{7,5},{8,10},{9,11},{10,... | collective-permute-start | bytes 835592 | tf_op jit(solution)/shard_map/ppermute | solution.py:333
  27.4 4.3 %copy-start.3 = (bf16[272,512]{1,0:T(8,128)(2,1)}, bf16[272,512]{1,0:T(8,128)(2,1)S(1)}, u32[]{:S(2)}) copy-start(bf16[272,512]{1,0:T(8,128)(2,1)S(1)} %collective-permute-done.6.refs_3_) | copy-start | bytes 835588
  31.4 0.7 copy-start.4
  32.1 0.7 copy-start.5
  35.0 9.0 %collective-permute-start.7 = (bf16[272,512]{1,0:T(8,128)(2,1)}, bf16[272,512]{1,0:T(8,128)(2,1)S(1)}, u32[]{:S(2)}, u32[]{:S(2)}) collective-permute-start(bf16[272,512]{1,0:T(8,128)(2,1)} %group_total.1), channel_id=1, source_target_pairs={{0,8},{1,9},{2,10},{3,11},{4,12},{5,13},{6,14},{7,15},{8,16},{9,17... | collective-permute-start | bytes 835592 | tf_op jit(solution)/shard_map/ppermute | solution.py:337
  36.3 19.5 %collective-permute-start.8 = (bf16[272,512]{1,0:T(8,128)(2,1)}, bf16[272,512]{1,0:T(8,128)(2,1)S(1)}, u32[]{:S(2)}, u32[]{:S(2)}) collective-permute-start(bf16[272,512]{1,0:T(8,128)(2,1)} %group_total.1), channel_id=1, source_target_pairs={{0,16},{1,17},{2,18},{3,19},{4,20},{5,21},{6,22},{7,23},{8,24},{9,... | collective-permute-start | bytes 835592 | tf_op jit(solution)/shard_map/ppermute | solution.py:337
  40.4 22.6 %collective-permute-start.3 = (bf16[4,256,256]{2,1,0:T(8,128)(2,1)}, bf16[4,256,256]{2,1,0:T(8,128)(2,1)S(1)}, u32[]{:S(2)}, u32[]{:S(2)}) collective-permute-start(bf16[4,256,256]{2,1,0:T(8,128)(2,1)} %get-tuple-element.39), channel_id=1, source_target_pairs={{0,1},{1,0},{2,3},{3,2},{4,5},{5,4},{6,7},{7,6},{8,9},{9,8},{10,11... | collective-permute-start | bytes 1572872 | tf_op jit(solution)/shard_map/ppermute | solution.py:329
  44.0 11.8 %copy-start.9 = (bf16[272,512]{1,0:T(8,128)(2,1)}, bf16[272,512]{1,0:T(8,128)(2,1)S(1)}, u32[]{:S(2)}) copy-start(bf16[272,512]{1,0:T(8,128)(2,1)S(1)} %collective-permute-done.7.refs_4_) | copy-start | bytes 835588
  55.8 0.7 copy-start.10
  59.7 11.3 %collective-permute-start.11 = (bf16[272,512]{1,0:T(8,128)(2,1)}, bf16[272,512]{1,0:T(8,128)(2,1)S(1)}, u32[]{:S(2)}, u32[]{:S(2)}) collective-permute-start(bf16[272,512]{1,0:T(8,128)(2,1)} %get-tuple-element.49), channel_id=1, source_target_pairs={{0,6},{1,7},{2,4},{3,5},{4,2},{5,3},{6,0},{7,1},{8,14},{9,15},{10,... | collective-permute-start | bytes 835592 | tf_op jit(solution)/shard_map/ppermute | solution.py:333
  62.8 15.3 %collective-permute-start.10 = (bf16[272,512]{1,0:T(8,128)(2,1)}, bf16[272,512]{1,0:T(8,128)(2,1)S(1)}, u32[]{:S(2)}, u32[]{:S(2)}) collective-permute-start(bf16[272,512]{1,0:T(8,128)(2,1)} %get-tuple-element.47), channel_id=1, source_target_pairs={{0,4},{1,5},{2,6},{3,7},{4,0},{5,1},{6,2},{7,3},{8,12},{9,13},{10,... | collective-permute-start | bytes 835592 | tf_op jit(solution)/shard_map/ppermute | solution.py:333
  63.0 20.5 %collective-permute-start.9 = (bf16[272,512]{1,0:T(8,128)(2,1)}, bf16[272,512]{1,0:T(8,128)(2,1)S(1)}, u32[]{:S(2)}, u32[]{:S(2)}) collective-permute-start(bf16[272,512]{1,0:T(8,128)(2,1)} %get-tuple-element.45), channel_id=1, source_target_pairs={{0,2},{1,3},{2,0},{3,1},{4,6},{5,7},{6,4},{7,5},{8,10},{9,11},{10,... | collective-permute-start | bytes 835592 | tf_op jit(solution)/shard_map/ppermute | solution.py:333
  63.1 0.8 copy-start.2
  68.6 20.9 %collective-permute-start.12 = (bf16[256,512]{1,0:T(8,128)(2,1)}, bf16[256,512]{1,0:T(8,128)(2,1)S(1)}, u32[]{:S(2)}, u32[]{:S(2)}) collective-permute-start(bf16[256,512]{1,0:T(8,128)(2,1)} %get-tuple-element.51), channel_id=1, source_target_pairs={{0,1},{1,0},{2,3},{3,2},{4,5},{5,4},{6,7},{7,6},{8,9},{9,8},{10,11... | collective-permute-start | bytes 786440 | tf_op jit(solution)/shard_map/ppermute | solution.py:329
  71.0 0.7 copy-start.8
  76.5 13.0 %collective-permute-start.15 = (bf16[256,512]{1,0:T(8,128)(2,1)}, bf16[256,512]{1,0:T(8,128)(2,1)S(1)}, u32[]{:S(2)}, u32[]{:S(2)}) collective-permute-start(bf16[256,512]{1,0:T(8,128)(2,1)} %get-tuple-element.54), channel_id=1, source_target_pairs={{0,1},{1,0},{2,3},{3,2},{4,5},{5,4},{6,7},{7,6},{8,9},{9,8},{10,11... | collective-permute-start | bytes 786440 | tf_op jit(solution)/shard_map/ppermute | solution.py:329
  78.1 0.7 copy-start.7
  83.5 6.0 %collective-permute-start.14 = (bf16[256,512]{1,0:T(8,128)(2,1)}, bf16[256,512]{1,0:T(8,128)(2,1)S(1)}, u32[]{:S(2)}, u32[]{:S(2)}) collective-permute-start(bf16[256,512]{1,0:T(8,128)(2,1)} %get-tuple-element.53), channel_id=1, source_target_pairs={{0,1},{1,0},{2,3},{3,2},{4,5},{5,4},{6,7},{7,6},{8,9},{9,8},{10,11... | collective-permute-start | bytes 786440 | tf_op jit(solution)/shard_map/ppermute | solution.py:329
  83.5 0.7 copy-start.6
  89.0 1.9 %collective-permute-start.13 = (bf16[256,512]{1,0:T(8,128)(2,1)}, bf16[256,512]{1,0:T(8,128)(2,1)S(1)}, u32[]{:S(2)}, u32[]{:S(2)}) collective-permute-start(bf16[256,512]{1,0:T(8,128)(2,1)} %get-tuple-element.52), channel_id=1, source_target_pairs={{0,1},{1,0},{2,3},{3,2},{4,5},{5,4},{6,7},{7,6},{8,9},{9,8},{10,11... | collective-permute-start | bytes 786440 | tf_op jit(solution)/shard_map/ppermute | solution.py:329
  89.5 1.4 %copy-start.11 = (bf16[256,512]{1,0:T(8,128)(2,1)}, bf16[256,512]{1,0:T(8,128)(2,1)S(1)}, u32[]{:S(2)}) copy-start(bf16[256,512]{1,0:T(8,128)(2,1)S(1)} %collective-permute-done.12.refs_4_) | copy-start | bytes 786436
  89.5 1.4 %copy-start.12 = (bf16[256,512]{1,0:T(8,128)(2,1)}, bf16[256,512]{1,0:T(8,128)(2,1)S(1)}, u32[]{:S(2)}) copy-start(bf16[256,512]{1,0:T(8,128)(2,1)S(1)} %collective-permute-done.15.refs_7_) | copy-start | bytes 786436
  89.5 1.4 %copy-start.13 = (bf16[256,512]{1,0:T(8,128)(2,1)}, bf16[256,512]{1,0:T(8,128)(2,1)S(1)}, u32[]{:S(2)}) copy-start(bf16[256,512]{1,0:T(8,128)(2,1)S(1)} %collective-permute-done.14.refs_6_) | copy-start | bytes 786436
  90.9 0.7 copy-start.14

commit v3 on v2

--- a/solution.py
+++ b/solution.py
@@ -33,33 +33,33 @@
 
 
 def meta_rows(normalizer, top, decay, doc):
-    line = jnp.concatenate([normalizer, top, decay], axis=1)
-    hi, mid, low = split3(line)
-    width = line.shape[1]
-    doc_line = jnp.concatenate([doc] * (width // LANES), axis=1)
+    width = normalizer.shape[1]
     row = iota((META, width), 0)
-    rows = jnp.where(row == 0, hi, jnp.where(row == 1, mid, jnp.where(row == 2, low, 0.0)))
-    return jnp.where(row == 3, doc_line, rows).astype(BF16)
-
-
-def read_meta(ref):
-    key_width = ref.shape[0] - META
-    rows = ref[key_width:, :].astype(F32)
-    line = (rows[2:3] + rows[1:2]) + rows[0:1]
-    return (
-        line[:, :key_width],
-        line[:, key_width : key_width + LANES],
-        line[:, key_width + LANES : key_width + 2 * LANES],
-        rows[3:4, :LANES],
-    )
+    rows = jnp.where(row == 6, jnp.concatenate([doc] * (width // LANES), axis=1), 0.0)
+    lines = split3(normalizer) + split3(jnp.concatenate([top, decay], axis=1))
+    for index, line in enumerate(lines):
+        rows = jnp.where(row == index, line, rows)
+    return rows.astype(BF16)
+
+
+def read_meta(refs):
+    key_width = refs[0].shape[0] - META
+    rows = [ref[key_width:, :].astype(F32) for ref in refs]
+    normals = jnp.concatenate([(x[2:3] + x[1:2]) + x[0:1] for x in rows], axis=0)
+    line = jnp.concatenate([(x[5:6] + x[4:5]) + x[3:4] for x in rows], axis=0)
+    docs = jnp.concatenate([x[6:7, :LANES] for x in rows], axis=0)
+    return normals, line[:, :LANES], line[:, LANES:], docs
+
+
+def wide(x, width):
+    return jnp.concatenate([x] * (width // LANES), axis=1)
 
 
 def weighted(refs, coefs):
-    key_width, value_width = refs[0].shape[0] - META, refs[0].shape[1]
+    key_width, width = refs[0].shape[0] - META, refs[0].shape[1]
     total = None
     for ref, coef in zip(refs, coefs, strict=True):
-        wide = jnp.concatenate([coef] * (value_width // LANES), axis=1)
-        term = wide * ref[:key_width, :].astype(F32)
+        term = wide(coef, width) * ref[:key_width, :].astype(F32)
         total = term if total is None else total + term
     return total
 
@@ -119,11 +119,15 @@
     columns[...] = jnp.concatenate([decay, docs, filler], axis=0).T
 
 
-def state_kernel(slot, heads, scalars, k_own, v_own, k_oth, v_oth, factors, tops, decays, ids_ref, out):
-    core = scalars[1]
+def state_kernel(first_slot, heads, scalars, *refs):
+    k_own, v_own, k_oth, v_oth, factors, tops, decays, ids_ref = refs[:8]
+    outs, halves = refs[8:-1], refs[-1]
+    step = pl.program_id(0)
+    mine, core = scalars[0], scalars[1]
     tokens, key_width = k_own.shape[1:]
+    part = v_own.shape[2] // 2
     length = 2 * tokens
-    head = (heads // 2) * core + jnp.bitwise_xor(scalars[0], slot)
+    head = (heads // 2) * core + jnp.bitwise_xor(mine // 2, first_slot - step)
     row = factors[pl.ds(head, 1), :]
     first, last = row[:, :tokens], row[:, tokens:]
     total, normal = None, None
@@ -135,100 +139,106 @@
         scaled = keys.astype(F32).T * f
         high = scaled.astype(BF16)
         low = (scaled - high.astype(F32)).astype(BF16)
-        part = dot(low, values) + dot(high, values)
+        piece = dot(low, values) + dot(high, values)
         pieces = jnp.concatenate(split3(f) + (jnp.zeros((META - 3, tokens), F32),), axis=0)
         sums = dot(pieces.astype(BF16), keys)
         line = (sums[2:3] + sums[1:2]) + sums[0:1]
-        total = part if total is None else total + part
+        total = piece if total is None else total + piece
         normal = line if normal is None else normal + line
     doc = jnp.broadcast_to(ids_ref[:, length - 1 :].astype(F32) + 1.0, (1, LANES))
-    out[:key_width, :] = total.astype(BF16)
-    out[key_width:, :] = meta_rows(
-        normal, tops[pl.ds(head, 1), :], decays[pl.ds(head, 1), :], doc
-    )
+    rows = meta_rows(normal, tops[pl.ds(head, 1), :], decays[pl.ds(head, 1), :], doc)
+    for half in range(2):
+        halves[half, :key_width, :] = total[:, half * part : (half + 1) * part].astype(BF16)
+        halves[half, key_width:, :] = rows
+    for i, out in enumerate(outs):
+
+        @pl.when(step == i // 2)
+        def _(out=out, i=i):
+            out[...] = halves[jnp.bitwise_xor(mine % 2, i % 2)]
+
+
+def decay_before(mine, place, decays):
+    group = decays.shape[0]
+    before = jnp.zeros_like(decays)
+    for i in range(group):
+        before = before + jnp.where(place > jnp.bitwise_xor(mine, i), decays[i : i + 1], 0.0)
+    return before
 
 
 def total_kernel(group, scalars, *refs):
     states, out = refs[:group], refs[group]
-    place = [jnp.bitwise_xor(scalars[0], r) for r in range(group)]
-    metas = [read_meta(ref) for ref in states]
-    zero = jnp.zeros((1, LANES), F32)
-    doc = sum((jnp.where(place[r] == group - 1, metas[r][3], zero) for r in range(group)), zero)
-    reached = []
-    for r in range(group):
-        after = sum(
-            (jnp.where(place[i] > place[r], metas[i][2], zero) for i in range(group)), zero
-        )
-        reached.append(jnp.where(metas[r][3] == doc, metas[r][1] + after, FLOOR_NEG))
-    top = functools.reduce(jnp.maximum, reached)
-    coefs = [
-        jnp.where(metas[r][3] == doc, jnp.exp(reached[r] - top), 0.0) for r in range(group)
-    ]
-    key_width = out.shape[0] - META
-    out[:key_width, :] = weighted(states, coefs).astype(BF16)
-    normal = sum(
-        jnp.concatenate([coefs[r]] * (key_width // LANES), axis=1) * metas[r][0]
-        for r in range(group)
-    )
-    decay = sum((metas[r][2] for r in range(group)), zero)
-    out[key_width:, :] = meta_rows(normal, top, decay, doc)
+    mine = scalars[0]
+    key_width, width = out.shape[0] - META, out.shape[1]
+    normals, tops, decays, docs = read_meta(states)
+    place = jnp.bitwise_xor(iota((group, LANES), 0), mine)
+    whole_decay = jnp.sum(decays, axis=0, keepdims=True)
+    after = whole_decay - decay_before(mine, place, decays) - decays
+    doc = jnp.sum(jnp.where(place == group - 1, docs, 0.0), axis=0, keepdims=True)
+    alive = docs == doc
+    reached = jnp.where(alive, tops + after, FLOOR_NEG)
+    top = jnp.max(reached, axis=0, keepdims=True)
+    coefs = jnp.where(alive, jnp.exp(reached - top), 0.0)
+    out[:key_width, :] = weighted(
+        states, [coefs[i : i + 1] for i in range(group)]
+    ).astype(BF16)
+    normal = jnp.sum(wide(coefs, width) * normals, axis=0, keepdims=True)
+    out[key_width:, :] = meta_rows(normal, top, whole_decay, doc)
 
 
 def entering_kernel(group, reach, scalars, *refs):
     states, totals, outs = refs[:group], refs[group : group + reach], refs[group + reach :]
-    place = [jnp.bitwise_xor(scalars[0], r) for r in range(group)]
-    metas = [read_meta(ref) for ref in states]
-    far = [read_meta(ref) for ref in totals]
+    mine = scalars[0]
+    key_width, width = outs[0].shape[0] - META, outs[0].shape[1]
+    normals, tops, decays, docs = read_meta(states)
+    far_normals, far_tops, far_decays, far_docs = read_meta(totals)
+    place = jnp.bitwise_xor(iota((group, LANES), 0), mine)
+    before = decay_before(mine, place, decays)
     zero = jnp.zeros((1, LANES), F32)
-    key_width = outs[0].shape[0] - META
+    far_reached, passed = [], zero
+    for d in range(reach):
+        far_reached.append(far_tops[d : d + 1] + passed)
+        passed = passed + far_decays[d : d + 1]
+    far_reached = jnp.concatenate(far_reached, axis=0)
     for r in range(group):
-        mine = place[r]
-        doc = jnp.where(mine == 0, far[0][3], zero)
-        for i in range(group):
-            doc = doc + jnp.where(place[i] == mine - 1, metas[i][3], zero)
-        passed = sum(
-            (jnp.where(place[i] < mine, metas[i][2], zero) for i in range(group)), zero
+        here = jnp.bitwise_xor(mine, r)
+        doc = jnp.sum(jnp.where(place == here - 1, docs, 0.0), axis=0, keepdims=True)
+        doc = jnp.where(here == 0, far_docs[0:1], doc)
+        mark = before[r : r + 1]
+        alive = (place < here) & (docs == doc)
+        reached = jnp.where(alive, tops + (mark - before - decays), FLOOR_NEG)
+        far_alive = (far_docs == doc) & (far_docs > 0.5)
+        far = jnp.where(far_alive, far_reached + mark, FLOOR_NEG)
+        top = jnp.maximum(
+            jnp.max(reached, axis=0, keepdims=True), jnp.max(far, axis=0, keepdims=True)
         )
-        sources, reached, normals = [], [], []
-        for i in range(group):
-            if i == r:
-                continue
-            between = sum(
-                (
-                    jnp.where((place[n] < mine) & (place[n] > place[i]), metas[n][2], zero)
-                    for n in range(group)
-                ),
-                zero,
-            )
-            there = jnp.where(place[i] < mine, metas[i][3], -1.0)
-            alive = there == doc
-            sources.append(states[i])
-            normals.append(metas[i][0])
-            reached.append((alive, jnp.where(alive, metas[i][1] + between, FLOOR_NEG)))
-        for d in range(reach):
-            alive = (far[d][3] == doc) & (far[d][3] > 0.5)
-            sources.append(totals[d])
-            normals.append(far[d][0])
-            reached.append((alive, jnp.where(alive, far[d][1] + passed, FLOOR_NEG)))
-            passed = passed + far[d][2]
-        top = functools.reduce(jnp.maximum, [value for _, value in reached])
-        coefs = [jnp.where(alive, jnp.exp(value - top), 0.0) for alive, value in reached]
-        outs[r][:key_width, :] = weighted(sources, coefs).astype(BF16)
-        normal = sum(
-            jnp.concatenate([coef] * (key_width // LANES), axis=1) * line
-            for coef, line in zip(coefs, normals, strict=True)
-        )
+        coefs = jnp.where(alive, jnp.exp(reached - top), 0.0)
+        far_coefs = jnp.where(far_alive, jnp.exp(far - top), 0.0)
+        others = [i for i in range(group) if i != r]
+        outs[r][:key_width, :] = weighted(
+            [states[i] for i in others] + list(totals),
+            [coefs[i : i + 1] for i in others]
+            + [far_coefs[d : d + 1] for d in range(reach)],
+        ).astype(BF16)
+        normal = jnp.sum(wide(coefs, width) * normals, axis=0, keepdims=True)
+        normal = normal + jnp.sum(wide(far_coefs, width) * far_normals, axis=0, keepdims=True)
         outs[r][key_width:, :] = meta_rows(normal, top, zero, doc)
 
 
-def output_kernel(slot, heads, scalars, *refs):
-    q_own, k_own, v_own, q_oth, k_oth, v_oth, source_rows, columns, ids_ref, payload = refs[:10]
-    keep, send = refs[10:]
-    core = scalars[1]
+def output_kernel(first_slot, heads, scalars, *refs):
+    q_own, k_own, v_own, q_oth, k_oth, v_oth, source_rows, columns, ids_ref = refs[:9]
+    entering, (keep, send, payload) = refs[9:-3], refs[-3:]
+    step = pl.program_id(0)
+    mine, core = scalars[0], scalars[1]
     tokens, key_width = q_own.shape[1:]
     length = 2 * tokens
     scaling = key_width**-0.5
-    head = (heads // 2) * core + jnp.bitwise_xor(scalars[0], slot)
+    for i, ref in enumerate(entering):
+
+        @pl.when(step == i // 2)
+        def _(ref=ref, i=i):
+            payload[jnp.bitwise_xor(mine % 2, i % 2)] = ref[...]
+
+    head = (heads // 2) * core + jnp.bitwise_xor(mine // 2, first_slot + step)
     is_first = core == 0
     source = source_rows[pl.ds(head, 1), :]
     lane = iota((length, LANES), 1)
@@ -237,11 +247,11 @@
     docs = turned[:, heads : heads + 1]
     source_docs = ids_ref[...].astype(F32) + 1.0
     causal = iota((tokens, tokens), 0) >= iota((tokens, tokens), 1)
-    normal, top, _, doc = read_meta(payload)
+    normal, top, _, doc = read_meta([payload.at[0]])
     carried = jnp.where(docs == doc[:, :1], decay + top[:, :1], FLOOR_NEG)
     pieces = jnp.concatenate(split3(normal) + (jnp.zeros((META - 3, key_width), F32),), axis=0)
     pieces = pieces.astype(BF16)
-    memory = payload[:key_width, :]
+    memory = jnp.concatenate([payload[0, :key_width, :], payload[1, :key_width, :]], axis=1)
 
     def ordered(own, other):
         own, other = own[0], other[0]
@@ -275,25 +285,27 @@
                 low = (weights - high.astype(F32)).astype(BF16)
                 numerator = numerator + dot(low, values[s])
         results.append((numerator / jnp.maximum(jnp.abs(denominator), 1.0)).astype(BF16))
-    keep[...] = jnp.where(is_first, results[0], results[1])
-    send[...] = jnp.where(is_first, results[1], results[0])
+    keep[0] = jnp.where(is_first, results[0], results[1])
+    send[0] = jnp.where(is_first, results[1], results[0])
 
 
 def merge_kernel(heads, scalars, *refs):
-    pieces, out = refs[:heads], refs[heads]
+    stacks, out = refs[:-1], refs[-1]
     half = heads // 2
     n = LAY // heads
-    mine, core = scalars[0], scalars[1]
+    mine, core = scalars[0] // 2, scalars[1]
     into, given = iota((LAY, LAY), 0), iota((LAY, LAY), 1)
     index = given // n
     slot = jnp.bitwise_and(index, half - 1)
     side = jnp.where(index < half, core, 1 - core)
     head = side * half + jnp.bitwise_xor(slot, mine)
     order = ((into % heads == head) & (into // heads == given % n)).astype(BF16)
-    tokens, width = pieces[0].shape
+    _, tokens, width = stacks[0].shape
     for g in range(tokens // n):
         span = slice(g * n, (g + 1) * n)
-        rows = jnp.concatenate([piece[span, :] for piece in pieces], axis=0)
+        rows = jnp.concatenate(
+            [stack[i, span, :] for stack in stacks for i in range(stack.shape[0])], axis=0
+        )
         out[span] = dot(order, rows).reshape(n, heads, width).astype(BF16)
 
 
@@ -316,7 +328,8 @@
     tokens, heads, key_width = queries.shape
     value_width = value_vectors.shape[2]
     half = heads // 2
-    group = half
+    group = heads
+    part = value_width // 2
     chips = devices // 2
     levels = chips // group
     reach = max(1, levels // 2)
@@ -337,7 +350,7 @@
         return lax.ppermute(x, AXES, [(d, d + jump) for d in range(devices - jump)])
 
     rows = key_width + META
-    state = (rows, value_width)
+    state = (rows, part)
     sizes = {key_width: (half, tokens, key_width), value_width: (half, tokens, value_width)}
 
     def relayout(*sources):
@@ -372,38 +385,49 @@
         name="gates",
     )(scalars, gates, gates_oth, ids)
 
-    def of_head(slot, x):
-        return pl.BlockSpec(
-            (1,) + x.shape[1:], lambda i, s: (jnp.bitwise_xor(s[0], slot), 0, 0)
-        )
-
-    def per_head(kernel, slot, by_head, others, out_shapes, name):
+    def per_head(kernel, first_slot, steps, down, by_head, others, outs, scratch, name):
+        def block(x):
+            def index(i, s):
+                slot = first_slot - i if down else first_slot + i
+                return (jnp.bitwise_xor(s[0] // 2, slot), 0, 0)
+
+            return pl.BlockSpec((1,) + x.shape[1:], index)
+
         return pl.pallas_call(
-            functools.partial(kernel, slot, heads),
+            functools.partial(kernel, first_slot, heads),
             grid_spec=pltpu.PrefetchScalarGridSpec(
                 num_scalar_prefetch=1,
-                grid=(1,),
-                in_specs=[of_head(slot, x) for x in by_head] + [whole(x.shape) for x in others],
-                out_specs=[whole(s) for s in out_shapes],
+                grid=(steps,),
+                in_specs=[block(x) for x in by_head] + [whole(x.shape) for x in others],
+                out_specs=[spec for spec, _ in outs],
+                scratch_shapes=scratch,
             ),
-            out_shape=[shape_of(*s) for s in out_shapes],
+            out_shape=[shape for _, shape in outs],
             compiler_params=params(),
             name=name,
         )(scalars, *by_head, *others)
 
-    farthest_first = list(range(group - 1, -1, -1))
-    gathered = [None] * group
-    for r in farthest_first:
-        [made] = per_head(
+    made = [None] * group
+    at_once = half // 2
+    for first_slot in range(half - 1, -1, -at_once):
+        lowest = 2 * (first_slot - at_once + 1)
+        pairs = [2 * (first_slot - i) + b for i in range(at_once) for b in range(2)]
+        outs = per_head(
             state_kernel,
-            r,
+            first_slot,
+            at_once,
+            True,
             (k_keep, v_keep, k_oth, v_oth),
             (factors, tops, decays, ids),
-            [state],
-            "state",
+            [(whole(state), shape_of(*state))] * len(pairs),
+            [pltpu.VMEM((2,) + state, BF16)],
+            "states",
         )
-        gathered[r] = in_group(made, r) if r else made
-    queries, gathered[0] = lax.optimization_barrier((queries, gathered[0]))
+        for r, out in zip(pairs, outs, strict=True):
+            made[r] = out
+        if lowest == 0:
+            queries, made[0] = lax.optimization_barrier((queries, made[0]))
+    gathered = [in_group(made[r], r) if r else made[0] for r in range(group - 1, -1, -1)][::-1]
     q_keep, q_send = relayout(queries)
     q_oth = swap_cores(q_send)
 
@@ -425,23 +449,28 @@
         compiler_params=params(),
         name="entering",
     )(scalars, *gathered, *totals)
-    entering = [in_group(outgoing[r], r) if r else outgoing[r] for r in farthest_first][::-1]
+    entering = [in_group(outgoing[r], r) if r else outgoing[0] for r in range(group - 1, -1, -1)]
+    entering = entering[::-1]
 
     kept, received = [], []
-    for r in range(group):
+    for first_slot, count in ((0, 1), (1, half - 1)):
+        spec = pl.BlockSpec((1, tokens, value_width), lambda i, s: (i, 0, 0))
         keep, send = per_head(
             output_kernel,
-            r,
+            first_slot,
+            count,
+            False,
             (q_keep, k_keep, v_keep, q_oth, k_oth, v_oth),
-            (source_rows, columns, ids, entering[r]),
-            [(tokens, value_width)] * 2,
-            "output",
+            (source_rows, columns, ids, *entering[2 * first_slot : 2 * (first_slot + count)]),
+            [(spec, shape_of(count, tokens, value_width))] * 2,
+            [pltpu.VMEM((2,) + state, BF16)],
+            "outputs",
         )
         kept.append(keep)
         received.append(swap_cores(send))
     return pl.pallas_call(
         functools.partial(merge_kernel, heads),
-        in_specs=[SMEM] + [whole((tokens, value_width))] * heads,
+        in_specs=[SMEM] + [whole(x.shape) for x in kept + received],
         out_specs=whole(value_vectors.shape),
         out_shape=shape_of(*value_vectors.shape),
         compiler_params=params(),

time: 95.7 us -> 104 us (1.087)
  waiting for transfers between devices: 21.6 us -> 34.5 us
  Pallas kernels: 49.1 us -> 40.3 us
  starting transfers between devices: 15.8 us -> 19.9 us
  local copies, waits for them, and re-layouts: 7.9 us -> 6.8 us
    ppermute x6 -> x14, waiting for transfers between devices: 4.26 us -> 21.3 us  [in_group(): return lax.ppermute(x, AXES, pairs)]
    pallas_call x8 -> x4, Pallas kernels: 31.1 us -> 21.6 us  [per_head(): pl.pallas_call(functools.partial(kernel, first_slot, heads), grid_spec=pl...]
    ppermute x6 -> x14, starting transfers between devices: 5.98 us -> 11.6 us  [in_group(): return lax.ppermute(x, AXES, pairs)]
    ppermute x2 -> x1, waiting for transfers between devices: 13.9 us -> 9.81 us  [to_later(): return lax.ppermute(x, AXES, [(d, d + jump) for d in range(devices - jump)])]
    ppermute x2 -> x1, starting transfers between devices: 2.75 us -> 1.28 us  [to_later(): return lax.ppermute(x, AXES, [(d, d + jump) for d in range(devices - jump)])]
    unnamed x40 -> x52, local copies, waits for them, and re-layouts: 7.25 us -> 6.15 us
    ppermute x8 -> x6, starting transfers between devices: 7.09 us -> 7.01 us  [swap_cores(): return lax.ppermute(x, AXES, [(d, d ^ 1) for d in range(devices)])]
    ppermute x8 -> x6, waiting for transfers between devices: 3.36 us -> 3.41 us  [swap_cores(): return lax.ppermute(x, AXES, [(d, d ^ 1) for d in range(devices)])]
  transfers between devices with their start and end apart: 16 -> 21, of which waited for: 6 -> 11; matrix products, arithmetic and copies ran while one was open for 1% -> 1% of each run, Pallas kernels for 38% -> 19%
where the time goes in v3:
time: 104 us; the launch traced here: 102 us
  Pallas kernels  40.3 us (39%)
  waiting for transfers between devices  34.5 us (33%)
  starting transfers between devices  19.9 us (19%)
  local copies, waits for them, and re-layouts  6.8 us (7%)
    pallas_call x4, Pallas kernels, per_head(): pl.pallas_call(functools.partial(kernel, first_slot, heads), grid_spec=pl...  21.6 us
    ppermute x14, waiting for transfers between devices, in_group(): return lax.ppermute(x, AXES, pairs)  21.3 us
    ppermute x14, starting transfers between devices, in_group(): return lax.ppermute(x, AXES, pairs)  11.6 us
    ppermute x1, waiting for transfers between devices, to_later(): return lax.ppermute(x, AXES, [(d, d + jump) for d in range(devices - jump)])  9.81 us
    pallas_call x2, Pallas kernels, relayout(): pl.pallas_call(functools.partial(relayout_kernel, half, len(sources)), in...  7.09 us
    ppermute x6, starting transfers between devices, swap_cores(): return lax.ppermute(x, AXES, [(d, d ^ 1) for d in range(devices)])  7.01 us
    unnamed x52, local copies, waits for them, and re-layouts  6.15 us
    pallas_call x1, Pallas kernels, local(): pl.pallas_call(functools.partial(entering_kernel, group, reach), in_specs...  3.89 us
  transfers between devices with their start and end apart: 21, of which 11 were waited for; matrix products, arithmetic and copies ran while one was open for 1% of the time, Pallas kernels for 19%

profile of v3, /device:TPU:25, one launch (start us, length us, event | category | flops | bytes accessed | tf_op | source)
XLA Modules:
  0.0 102.4 jit_solution(9852674880235433795)
XLA Ops:
  0.0 0.7 pad_add_fusion.scalars
  0.7 4.4 %relayout.2 = (bf16[4,256,256]{2,1,0:T(8,128)(2,1)}, bf16[4,256,512]{2,1,0:T(8,128)(2,1)}, bf16[4,256,256]{2,1,0:T(8,128)(2,1)}, bf16[4,256,512]{2,1,0:T(8,128)(2,1)}) custom-call(s32[2]{0:T(128)} %pad_add_fusion.scalars, bf16[256,8,256]{2,1,0:T(8,128)(2,1)} %refs_0_.1, bf16[256,8,512]{2,1,0:T(8,128)(2,1)} %refs_1_.1), custom_call_target="tpu_custom_call" | custom-call | tf_op jit(solution)/shard_map/relayout/pallas_call | solution.py:358
  5.1 0.7 collective-permute-start.1
  5.8 0.0 collective-permute-start
  5.8 0.6 collective-permute-start.2
  6.4 0.6 dynamic_slice.3
  7.0 2.0 %collective-permute-done.2.g_oth = bf16[16,256]{1,0:T(8,128)(2,1)S(1)} collective-permute-done((bf16[16,256]{1,0:T(8,128)(2,1)S(1)}, bf16[16,256]{1,0:T(8,128)(2,1)S(1)}, u32[]{:S(2)}, u32[]{:S(2)}) %collective-permute-start.2) | collective-permute-done | bytes 8224 | tf_op jit(solution)/shard_map/ppermute | solution.py:342
  9.1 0.6 copy-done.21
  9.6 1.9 %gates.1 = (f32[8,512]{1,0:T(8,128)}, f32[8,128]{1,0:T(8,128)}, f32[8,128]{1,0:T(8,128)}, f32[8,512]{1,0:T(8,128)}, f32[512,128]{1,0:T(8,128)}) custom-call(s32[2]{0:T(128)} %pad_add_fusion.scalars, bf16[16,256]{1,0:T(8,128)(2,1)} %copy-done.20, bf16[16,256]{1,0:T(8,128)(2,1)} %copy-done.21, s32[1,512]{1,0:T(1,128)} %bitcast.5), custom_call_target="tpu_custom_call" | custom-call | tf_op jit(solution)/shard_map/gates/pallas_call | solution.py:379
  11.5 0.0 collective-permute-done.refs_2_.refs_4_
  11.5 0.0 collective-permute-done.1.refs_3_.refs_5_
  11.6 0.8 copy-done.1
  12.3 0.4 copy-done
  12.7 3.9 %states.3 = (bf16[272,256]{1,0:T(8,128)(2,1)}, bf16[272,256]{1,0:T(8,128)(2,1)}, bf16[272,256]{1,0:T(8,128)(2,1)}, bf16[272,256]{1,0:T(8,128)(2,1)}) custom-call(s32[2]{0:T(128)} %pad_add_fusion.scalars, bf16[4,256,256]{2,1,0:T(8,128)(2,1)} %get-tuple-element.38.refs_0_.refs_1_, bf16[4,256,512]{2,1,0:T(8,128)(2,1)} %get-tuple-element.39.refs_1_.refs_2_, ...), custom_call_target="tpu_custom_call" | custom-call | tf_op jit(solution)/shard_map/states/pallas_call | solution.py:396
  16.6 2.1 %collective-permute-start.10 = (bf16[272,256]{1,0:T(8,128)(2,1)}, bf16[272,256]{1,0:T(8,128)(2,1)S(1)}, u32[]{:S(2)}, u32[]{:S(2)}) collective-permute-start(bf16[272,256]{1,0:T(8,128)(2,1)} %get-tuple-element.58), channel_id=1, source_target_pairs={{0,14},{1,15},{2,12},{3,13},{4,10},{5,11},{6,8},{7,9},{8,6},{9,7},... | collective-permute-start | bytes 417800 | tf_op jit(solution)/shard_map/ppermute | solution.py:346
  18.6 1.3 %collective-permute-start.7 = (bf16[272,256]{1,0:T(8,128)(2,1)}, bf16[272,256]{1,0:T(8,128)(2,1)S(1)}, u32[]{:S(2)}, u32[]{:S(2)}) collective-permute-start(bf16[272,256]{1,0:T(8,128)(2,1)} %get-tuple-element.55), channel_id=1, source_target_pairs={{0,8},{1,9},{2,10},{3,11},{4,12},{5,13},{6,14},{7,15},{8,0},{9,1},... | collective-permute-start | bytes 417800 | tf_op jit(solution)/shard_map/ppermute | solution.py:346
  19.9 0.1 collective-permute-start.8
  20.1 1.2 %collective-permute-start.9 = (bf16[272,256]{1,0:T(8,128)(2,1)}, bf16[272,256]{1,0:T(8,128)(2,1)S(1)}, u32[]{:S(2)}, u32[]{:S(2)}) collective-permute-start(bf16[272,256]{1,0:T(8,128)(2,1)} %get-tuple-element.57), channel_id=1, source_target_pairs={{0,12},{1,13},{2,14},{3,15},{4,8},{5,9},{6,10},{7,11},{8,4},{9,5},... | collective-permute-start | bytes 417800 | tf_op jit(solution)/shard_map/ppermute | solution.py:346
  21.3 3.9 %states.2 = (bf16[272,256]{1,0:T(8,128)(2,1)}, bf16[272,256]{1,0:T(8,128)(2,1)}, bf16[272,256]{1,0:T(8,128)(2,1)}, bf16[272,256]{1,0:T(8,128)(2,1)}) custom-call(s32[2]{0:T(128)} %pad_add_fusion.scalars, bf16[4,256,256]{2,1,0:T(8,128)(2,1)} %get-tuple-element.38.refs_0_.refs_1_, bf16[4,256,512]{2,1,0:T(8,128)(2,1)} %get-tuple-element.39.refs_1_.refs_2_, ...), custom_call_target="tpu_custom_call" | custom-call | tf_op jit(solution)/shard_map/states/pallas_call | solution.py:396
  25.1 1.2 %collective-permute-start.4 = (bf16[272,256]{1,0:T(8,128)(2,1)}, bf16[272,256]{1,0:T(8,128)(2,1)S(1)}, u32[]{:S(2)}, u32[]{:S(2)}) collective-permute-start(bf16[272,256]{1,0:T(8,128)(2,1)} %get-tuple-element.52), channel_id=1, source_target_pairs={{0,2},{1,3},{2,0},{3,1},{4,6},{5,7},{6,4},{7,5},{8,10},{9,11},{10,... | collective-permute-start | bytes 417800 | tf_op jit(solution)/shard_map/ppermute | solution.py:346
  26.4 0.0 collective-permute-done.10.refs_7_
  26.4 1.2 %collective-permute-start.5 = (bf16[272,256]{1,0:T(8,128)(2,1)}, bf16[272,256]{1,0:T(8,128)(2,1)S(1)}, u32[]{:S(2)}, u32[]{:S(2)}) collective-permute-start(bf16[272,256]{1,0:T(8,128)(2,1)} %get-tuple-element.53), channel_id=1, source_target_pairs={{0,4},{1,5},{2,6},{3,7},{4,0},{5,1},{6,2},{7,3},{8,12},{9,13},{10,... | collective-permute-start | bytes 417800 | tf_op jit(solution)/shard_map/ppermute | solution.py:346
  27.6 0.0 collective-permute-done.7.refs_4_
  27.6 0.2 collective-permute-start.6
  27.8 2.7 %relayout.3 = (bf16[4,256,256]{2,1,0:T(8,128)(2,1)}, bf16[4,256,256]{2,1,0:T(8,128)(2,1)}) custom-call(s32[2]{0:T(128)} %pad_add_fusion.scalars, bf16[256,8,256]{2,1,0:T(8,128)(2,1)} %refs_0_.2), custom_call_target="tpu_custom_call" | custom-call | tf_op jit(solution)/shard_map/relayout/pallas_call | solution.py:358
  30.5 0.0 collective-permute-done.8.refs_5_
  30.5 2.3 %collective-permute-start.3 = (bf16[4,256,256]{2,1,0:T(8,128)(2,1)}, bf16[4,256,256]{2,1,0:T(8,128)(2,1)S(1)}, u32[]{:S(2)}, u32[]{:S(2)}) collective-permute-start(bf16[4,256,256]{2,1,0:T(8,128)(2,1)} %get-tuple-element.48), channel_id=1, source_target_pairs={{0,1},{1,0},{2,3},{3,2},{4,5},{5,4},{6,7},{7,6},{8,9},{9,8},{10,11... | collective-permute-start | bytes 1572872 | tf_op jit(solution)/shard_map/ppermute | solution.py:342
  32.8 0.0 collective-permute-done.9.refs_6_
  32.8 0.1 collective-permute-done.4.refs_1_
  32.9 4.3 %collective-permute-done.5.refs_2_ = bf16[272,256]{1,0:T(8,128)(2,1)S(1)} collective-permute-done((bf16[272,256]{1,0:T(8,128)(2,1)}, bf16[272,256]{1,0:T(8,128)(2,1)S(1)}, u32[]{:S(2)}, u32[]{:S(2)}) %collective-permute-start.5) | collective-permute-done | bytes 139296 | tf_op jit(solution)/shard_map/ppermute | solution.py:346
  37.2 0.0 collective-permute-done.6.refs_3_
  37.2 0.6 copy-done.9
  37.9 0.7 copy-done.10
  38.5 2.2 %group_total.1 = bf16[272,256]{1,0:T(8,128)(2,1)} custom-call(s32[2]{0:T(128)} %pad_add_fusion.scalars, bf16[272,256]{1,0:T(8,128)(2,1)} %get-tuple-element.51.refs_0_, bf16[272,256]{1,0:T(8,128)(2,1)} %copy-done.8, bf16[272,256]{1,0:T(8,128)(2,1)} %copy-done.9, bf16[272,256]{1,0:T(8,128)(2,1)} %copy-done.10, bf16[272,256]{1,0:T(8,128)(2,1)} %copy-done.5, ...), custom_call_target="tpu_custom_call" | custom-call | tf_op jit(solution)/shard_map/group_total/pallas_call | solution.py:434
  40.8 1.3 %collective-permute-start.11 = (bf16[272,256]{1,0:T(8,128)(2,1)}, bf16[272,256]{1,0:T(8,128)(2,1)S(1)}, u32[]{:S(2)}, u32[]{:S(2)}) collective-permute-start(bf16[272,256]{1,0:T(8,128)(2,1)} %group_total.1), channel_id=1, source_target_pairs={{0,16},{1,17},{2,18},{3,19},{4,20},{5,21},{6,22},{7,23},{8,24},{9,... | collective-permute-start | bytes 417800 | tf_op jit(solution)/shard_map/ppermute | solution.py:350
  42.0 9.8 %collective-permute-done.11.refs_8_ = bf16[272,256]{1,0:T(8,128)(2,1)S(1)} collective-permute-done((bf16[272,256]{1,0:T(8,128)(2,1)}, bf16[272,256]{1,0:T(8,128)(2,1)S(1)}, u32[]{:S(2)}, u32[]{:S(2)}) %collective-permute-start.11) | collective-permute-done | bytes 139296 | tf_op jit(solution)/shard_map/ppermute | solution.py:350
  51.9 0.6 copy-done.18
  52.5 3.9 %entering.1 = (bf16[272,256]{1,0:T(8,128)(2,1)}, bf16[272,256]{1,0:T(8,128)(2,1)}, bf16[272,256]{1,0:T(8,128)(2,1)}, bf16[272,256]{1,0:T(8,128)(2,1)}, bf16[272,...) custom-call(s32[2]{0:T(128)} %pad_add_fusion.scalars, ...), custom_call_target="tpu_custom_call" | custom-call | tf_op jit(solution)/shard_map/entering/pallas_call | solution.py:444
  56.4 1.1 %collective-permute-start.13 = (bf16[272,256]{1,0:T(8,128)(2,1)}, bf16[272,256]{1,0:T(8,128)(2,1)S(1)}, u32[]{:S(2)}, u32[]{:S(2)}) collective-permute-start(bf16[272,256]{1,0:T(8,128)(2,1)} %get-tuple-element.62), channel_id=1, source_target_pairs={{0,4},{1,5},{2,6},{3,7},{4,0},{5,1},{6,2},{7,3},{8,12},{9,13},{10,... | collective-permute-start | bytes 417800 | tf_op jit(solution)/shard_map/ppermute | solution.py:346
  57.5 0.0 collective-permute-start.14
  57.5 0.0 collective-permute-start.15
  57.5 2.7 %collective-permute-start.16 = (bf16[272,256]{1,0:T(8,128)(2,1)}, bf16[272,256]{1,0:T(8,128)(2,1)S(1)}, u32[]{:S(2)}, u32[]{:S(2)}) collective-permute-start(bf16[272,256]{1,0:T(8,128)(2,1)} %get-tuple-element.65), channel_id=1, source_target_pairs={{0,10},{1,11},{2,8},{3,9},{4,14},{5,15},{6,12},{7,13},{8,2},{9,3},... | collective-permute-start | bytes 417800 | tf_op jit(solution)/shard_map/ppermute | solution.py:346
  60.2 0.8 collective-permute-done.13.refs_9_
  61.0 0.1 collective-permute-start.17
  61.1 1.6 %collective-permute-done.14.refs_10_ = bf16[272,256]{1,0:T(8,128)(2,1)S(1)} collective-permute-done((bf16[272,256]{1,0:T(8,128)(2,1)}, bf16[272,256]{1,0:T(8,128)(2,1)S(1)}, u32[]{:S(2)}, u32[]{:S(2)}) %collective-permute-start.14) | collective-permute-done | bytes 139296 | tf_op jit(solution)/shard_map/ppermute | solution.py:346
  62.7 0.0 collective-permute-start.18
  62.7 0.0 collective-permute-done.15.refs_11_
  62.7 2.8 %collective-permute-done.16.refs_12_ = bf16[272,256]{1,0:T(8,128)(2,1)S(1)} collective-permute-done((bf16[272,256]{1,0:T(8,128)(2,1)}, bf16[272,256]{1,0:T(8,128)(2,1)S(1)}, u32[]{:S(2)}, u32[]{:S(2)}) %collective-permute-start.16) | collective-permute-done | bytes 139296 | tf_op jit(solution)/shard_map/ppermute | solution.py:346
  65.5 2.9 %collective-permute-done.17.refs_13_ = bf16[272,256]{1,0:T(8,128)(2,1)S(1)} collective-permute-done((bf16[272,256]{1,0:T(8,128)(2,1)}, bf16[272,256]{1,0:T(8,128)(2,1)S(1)}, u32[]{:S(2)}, u32[]{:S(2)}) %collective-permute-start.17) | collective-permute-done | bytes 139296 | tf_op jit(solution)/shard_map/ppermute | solution.py:346
  68.4 4.1 %collective-permute-done.18.refs_14_ = bf16[272,256]{1,0:T(8,128)(2,1)S(1)} collective-permute-done((bf16[272,256]{1,0:T(8,128)(2,1)}, bf16[272,256]{1,0:T(8,128)(2,1)S(1)}, u32[]{:S(2)}, u32[]{:S(2)}) %collective-permute-start.18) | collective-permute-done | bytes 139296 | tf_op jit(solution)/shard_map/ppermute | solution.py:346
  72.5 0.6 copy-done.17
  73.1 0.2 copy-done.2
  73.3 9.2 %outputs.3 = (bf16[3,256,512]{2,1,0:T(8,128)(2,1)}, bf16[3,256,512]{2,1,0:T(8,128)(2,1)}) custom-call(s32[2]{0:T(128)} %pad_add_fusion.scalars, bf16[4,256,256]{2,1,0:T(8,128)(2,1)} %get-tuple-element.47.refs_0_, bf16[4,256,256]{2,1,0:T(8,128)(2,1)} %get-tuple-element.38.refs_0_.refs_1_, bf16[4,256,512]{2,1,0:T(8,128)(2,1)} %get-tuple-element.39.refs_1_.refs_2_, ...), custom_call_target="tpu_custom_call" | custom-call | tf_op jit(solution)/shard_map/outputs/pallas_call | solution.py:396
  82.5 2.5 %collective-permute-start.20 = (bf16[3,256,512]{2,1,0:T(8,128)(2,1)}, bf16[3,256,512]{2,1,0:T(8,128)(2,1)S(1)}, u32[]{:S(2)}, u32[]{:S(2)}) collective-permute-start(bf16[3,256,512]{2,1,0:T(8,128)(2,1)} %get-tuple-element.70), channel_id=1, source_target_pairs={{0,1},{1,0},{2,3},{3,2},{4,5},{5,4},{6,7},{7,6},{8,9},{9,8},{10,11... | collective-permute-start | bytes 2359304 | tf_op jit(solution)/shard_map/ppermute | solution.py:342
  85.0 0.3 collective-permute-start.12
  85.2 4.9 %collective-permute-done.12.refs_10_ = bf16[272,256]{1,0:T(8,128)(2,1)S(1)} collective-permute-done((bf16[272,256]{1,0:T(8,128)(2,1)S(1)}, bf16[272,256]{1,0:T(8,128)(2,1)S(1)}, u32[]{:S(2)}, u32[]{:S(2)}) %collective-permute-start.12) | collective-permute-done | bytes 139296 | tf_op jit(solution)/shard_map/ppermute | solution.py:346
  90.1 0.7 copy-done.19
  90.8 4.7 %outputs.2 = (bf16[1,256,512]{2,1,0:T(8,128)(2,1)}, bf16[1,256,512]{2,1,0:T(8,128)(2,1)}) custom-call(s32[2]{0:T(128)} %pad_add_fusion.scalars, bf16[4,256,256]{2,1,0:T(8,128)(2,1)} %get-tuple-element.47.refs_0_, bf16[4,256,256]{2,1,0:T(8,128)(2,1)} %get-tuple-element.38.refs_0_.refs_1_, bf16[4,256,512]{2,1,0:T(8,128)(2,1)} %get-tuple-element.39.refs_1_.refs_2_, ...), custom_call_target="tpu_custom_call" | custom-call | tf_op jit(solution)/shard_map/outputs/pallas_call | solution.py:396
  95.5 0.9 collective-permute-start.19
  96.4 1.4 %collective-permute-done.19.refs_2_ = bf16[1,256,512]{2,1,0:T(8,128)(2,1)S(1)} collective-permute-done((bf16[1,256,512]{2,1,0:T(8,128)(2,1)}, bf16[1,256,512]{2,1,0:T(8,128)(2,1)S(1)}, u32[]{:S(2)}, u32[]{:S(2)}) %collective-permute-start.19) | collective-permute-done | bytes 262176 | tf_op jit(solution)/shard_map/ppermute | solution.py:342
  97.8 0.0 collective-permute-done.20.refs_3_
  97.8 0.7 copy-done.11
  98.5 0.3 copy-done.3
  98.8 3.6 %merge.1 = bf16[256,8,512]{2,1,0:T(8,128)(2,1)} custom-call(s32[2]{0:T(128)} %pad_add_fusion.scalars, bf16[1,256,512]{2,1,0:T(8,128)(2,1)} %get-tuple-element.61.refs_0_, bf16[3,256,512]{2,1,0:T(8,128)(2,1)} %get-tuple-element.68.refs_1_, bf16[1,256,512]{2,1,0:T(8,128)(2,1)} %copy-done.11, bf16[3,256,512]{2,1,0:T(8,128)(2,1)} %copy-done.3), custom_call_target="tpu_custom_call" | custom-call | tf_op jit(solution)/shard_map/merge/pallas_call | solution.py:471
  (43 shorter events, 0.1 us)
Async XLA Ops:
  0.0 5.8 %copy-start.23 = (bf16[256,8]{0,1:T(8,128)(2,1)S(1)}, bf16[256,8]{0,1:T(8,128)(2,1)}, u32[]{:S(2)}) copy-start(bf16[256,8]{0,1:T(8,128)(2,1)} %param.9) | copy-start | bytes 12292
  0.0 5.8 %copy-start.22 = (bf16[256,8]{0,1:T(8,128)(2,1)S(1)}, bf16[256,8]{0,1:T(8,128)(2,1)}, u32[]{:S(2)}) copy-start(bf16[256,8]{0,1:T(8,128)(2,1)} %param.10) | copy-start | bytes 12292
  0.0 6.4 %copy-start.24 = (s32[1024]{0:T(1024)S(1)}, s32[1024]{0:T(1024)}, u32[]{:S(2)}) copy-start(s32[1024]{0:T(1024)} %param.11) | copy-start | bytes 12292
  5.1 6.4 %collective-permute-start.1 = (bf16[4,256,512]{2,1,0:T(8,128)(2,1)}, bf16[4,256,512]{2,1,0:T(8,128)(2,1)S(1)}, u32[]{:S(2)}, u32[]{:S(2)}) collective-permute-start(bf16[4,256,512]{2,1,0:T(8,128)(2,1)} %get-tuple-element.41), channel_id=1, source_target_pairs={{0,1},{1,0},{2,3},{3,2},{4,5},{5,4},{6,7},{7,6},{8,9},{9,8},{10,11... | collective-permute-start | bytes 3145736 | tf_op jit(solution)/shard_map/ppermute | solution.py:342
  5.8 5.8 %collective-permute-start = (bf16[4,256,256]{2,1,0:T(8,128)(2,1)}, bf16[4,256,256]{2,1,0:T(8,128)(2,1)S(1)}, u32[]{:S(2)}, u32[]{:S(2)}) collective-permute-start(bf16[4,256,256]{2,1,0:T(8,128)(2,1)} %get-tuple-element.40), channel_id=1, source_target_pairs={{0,1},{1,0},{2,3},{3,2},{4,5},{5,4},{6,7},{7,6},{8,9},{9,8},{10,11... | collective-permute-start | bytes 1572872 | tf_op jit(solution)/shard_map/ppermute | solution.py:342
  5.8 3.2 %copy-start.20 = (bf16[16,256]{1,0:T(8,128)(2,1)}, bf16[16,256]{1,0:T(8,128)(2,1)S(1)}, u32[]{:S(2)}) copy-start(bf16[16,256]{1,0:T(8,128)(2,1)S(1)} %pad_maximum_fusion.g_own) | copy-start | bytes 24580
  5.8 3.2 %collective-permute-start.2 = (bf16[16,256]{1,0:T(8,128)(2,1)S(1)}, bf16[16,256]{1,0:T(8,128)(2,1)S(1)}, u32[]{:S(2)}, u32[]{:S(2)}) collective-permute-start(bf16[16,256]{1,0:T(8,128)(2,1)S(1)} %pad_maximum_fusion.g_own), channel_id=1, source_target_pairs={{0,1},{1,0},{2,3},{3,2},{4,5},{5,4},{6,7},{7,6},{8,9},{9,8},{10,11... | collective-permute-start | bytes 24584 | tf_op jit(solution)/shard_map/ppermute | solution.py:342
  9.0 0.6 copy-start.21
  11.5 0.8 copy-start.1
  11.6 1.1 %copy-start = (bf16[4,256,512]{2,1,0:T(8,128)(2,1)}, bf16[4,256,512]{2,1,0:T(8,128)(2,1)S(1)}, u32[]{:S(2)}) copy-start(bf16[4,256,512]{2,1,0:T(8,128)(2,1)S(1)} %collective-permute-done.1.refs_3_.refs_5_) | copy-start | bytes 3145732
  16.6 9.8 %collective-permute-start.10 = (bf16[272,256]{1,0:T(8,128)(2,1)}, bf16[272,256]{1,0:T(8,128)(2,1)S(1)}, u32[]{:S(2)}, u32[]{:S(2)}) collective-permute-start(bf16[272,256]{1,0:T(8,128)(2,1)} %get-tuple-element.58), channel_id=1, source_target_pairs={{0,14},{1,15},{2,12},{3,13},{4,10},{5,11},{6,8},{7,9},{8,6},{9,7},... | collective-permute-start | bytes 417800 | tf_op jit(solution)/shard_map/ppermute | solution.py:346
  18.6 9.0 %collective-permute-start.7 = (bf16[272,256]{1,0:T(8,128)(2,1)}, bf16[272,256]{1,0:T(8,128)(2,1)S(1)}, u32[]{:S(2)}, u32[]{:S(2)}) collective-permute-start(bf16[272,256]{1,0:T(8,128)(2,1)} %get-tuple-element.55), channel_id=1, source_target_pairs={{0,8},{1,9},{2,10},{3,11},{4,12},{5,13},{6,14},{7,15},{8,0},{9,1},... | collective-permute-start | bytes 417800 | tf_op jit(solution)/shard_map/ppermute | solution.py:346
  19.9 10.6 %collective-permute-start.8 = (bf16[272,256]{1,0:T(8,128)(2,1)}, bf16[272,256]{1,0:T(8,128)(2,1)S(1)}, u32[]{:S(2)}, u32[]{:S(2)}) collective-permute-start(bf16[272,256]{1,0:T(8,128)(2,1)} %get-tuple-element.56), channel_id=1, source_target_pairs={{0,10},{1,11},{2,8},{3,9},{4,14},{5,15},{6,12},{7,13},{8,2},{9,3},... | collective-permute-start | bytes 417800 | tf_op jit(solution)/shard_map/ppermute | solution.py:346
  20.1 12.8 %collective-permute-start.9 = (bf16[272,256]{1,0:T(8,128)(2,1)}, bf16[272,256]{1,0:T(8,128)(2,1)S(1)}, u32[]{:S(2)}, u32[]{:S(2)}) collective-permute-start(bf16[272,256]{1,0:T(8,128)(2,1)} %get-tuple-element.57), channel_id=1, source_target_pairs={{0,12},{1,13},{2,14},{3,15},{4,8},{5,9},{6,10},{7,11},{8,4},{9,5},... | collective-permute-start | bytes 417800 | tf_op jit(solution)/shard_map/ppermute | solution.py:346
  25.1 7.7 %collective-permute-start.4 = (bf16[272,256]{1,0:T(8,128)(2,1)}, bf16[272,256]{1,0:T(8,128)(2,1)S(1)}, u32[]{:S(2)}, u32[]{:S(2)}) collective-permute-start(bf16[272,256]{1,0:T(8,128)(2,1)} %get-tuple-element.52), channel_id=1, source_target_pairs={{0,2},{1,3},{2,0},{3,1},{4,6},{5,7},{6,4},{7,5},{8,10},{9,11},{10,... | collective-permute-start | bytes 417800 | tf_op jit(solution)/shard_map/ppermute | solution.py:346
  26.4 10.8 %copy-start.4 = (bf16[272,256]{1,0:T(8,128)(2,1)}, bf16[272,256]{1,0:T(8,128)(2,1)S(1)}, u32[]{:S(2)}) copy-start(bf16[272,256]{1,0:T(8,128)(2,1)S(1)} %collective-permute-done.10.refs_7_) | copy-start | bytes 417796
  26.4 10.8 %collective-permute-start.5 = (bf16[272,256]{1,0:T(8,128)(2,1)}, bf16[272,256]{1,0:T(8,128)(2,1)S(1)}, u32[]{:S(2)}, u32[]{:S(2)}) collective-permute-start(bf16[272,256]{1,0:T(8,128)(2,1)} %get-tuple-element.53), channel_id=1, source_target_pairs={{0,4},{1,5},{2,6},{3,7},{4,0},{5,1},{6,2},{7,3},{8,12},{9,13},{10,... | collective-permute-start | bytes 417800 | tf_op jit(solution)/shard_map/ppermute | solution.py:346
  27.6 9.6 %copy-start.5 = (bf16[272,256]{1,0:T(8,128)(2,1)}, bf16[272,256]{1,0:T(8,128)(2,1)S(1)}, u32[]{:S(2)}) copy-start(bf16[272,256]{1,0:T(8,128)(2,1)S(1)} %collective-permute-done.7.refs_4_) | copy-start | bytes 417796
  27.6 9.6 %collective-permute-start.6 = (bf16[272,256]{1,0:T(8,128)(2,1)}, bf16[272,256]{1,0:T(8,128)(2,1)S(1)}, u32[]{:S(2)}, u32[]{:S(2)}) collective-permute-start(bf16[272,256]{1,0:T(8,128)(2,1)} %get-tuple-element.54), channel_id=1, source_target_pairs={{0,6},{1,7},{2,4},{3,5},{4,2},{5,3},{6,0},{7,1},{8,14},{9,15},{10,... | collective-permute-start | bytes 417800 | tf_op jit(solution)/shard_map/ppermute | solution.py:346
  30.5 6.7 %copy-start.6 = (bf16[272,256]{1,0:T(8,128)(2,1)}, bf16[272,256]{1,0:T(8,128)(2,1)S(1)}, u32[]{:S(2)}) copy-start(bf16[272,256]{1,0:T(8,128)(2,1)S(1)} %collective-permute-done.8.refs_5_) | copy-start | bytes 417796
  30.5 42.0 %collective-permute-start.3 = (bf16[4,256,256]{2,1,0:T(8,128)(2,1)}, bf16[4,256,256]{2,1,0:T(8,128)(2,1)S(1)}, u32[]{:S(2)}, u32[]{:S(2)}) collective-permute-start(bf16[4,256,256]{2,1,0:T(8,128)(2,1)} %get-tuple-element.48), channel_id=1, source_target_pairs={{0,1},{1,0},{2,3},{3,2},{4,5},{5,4},{6,7},{7,6},{8,9},{9,8},{10,11... | collective-permute-start | bytes 1572872 | tf_op jit(solution)/shard_map/ppermute | solution.py:342
  32.8 4.4 %copy-start.7 = (bf16[272,256]{1,0:T(8,128)(2,1)}, bf16[272,256]{1,0:T(8,128)(2,1)S(1)}, u32[]{:S(2)}) copy-start(bf16[272,256]{1,0:T(8,128)(2,1)S(1)} %collective-permute-done.9.refs_6_) | copy-start | bytes 417796
  32.9 4.3 %copy-start.8 = (bf16[272,256]{1,0:T(8,128)(2,1)}, bf16[272,256]{1,0:T(8,128)(2,1)S(1)}, u32[]{:S(2)}) copy-start(bf16[272,256]{1,0:T(8,128)(2,1)S(1)} %collective-permute-done.4.refs_1_) | copy-start | bytes 417796
  37.2 0.7 copy-start.9
  37.9 0.7 copy-start.10
  40.8 11.1 %collective-permute-start.11 = (bf16[272,256]{1,0:T(8,128)(2,1)}, bf16[272,256]{1,0:T(8,128)(2,1)S(1)}, u32[]{:S(2)}, u32[]{:S(2)}) collective-permute-start(bf16[272,256]{1,0:T(8,128)(2,1)} %group_total.1), channel_id=1, source_target_pairs={{0,16},{1,17},{2,18},{3,19},{4,20},{5,21},{6,22},{7,23},{8,24},{9,... | collective-permute-start | bytes 417800 | tf_op jit(solution)/shard_map/ppermute | solution.py:350
  51.9 0.7 copy-start.18
  56.4 4.6 %collective-permute-start.13 = (bf16[272,256]{1,0:T(8,128)(2,1)}, bf16[272,256]{1,0:T(8,128)(2,1)S(1)}, u32[]{:S(2)}, u32[]{:S(2)}) collective-permute-start(bf16[272,256]{1,0:T(8,128)(2,1)} %get-tuple-element.62), channel_id=1, source_target_pairs={{0,4},{1,5},{2,6},{3,7},{4,0},{5,1},{6,2},{7,3},{8,12},{9,13},{10,... | collective-permute-start | bytes 417800 | tf_op jit(solution)/shard_map/ppermute | solution.py:346
  57.5 5.1 %collective-permute-start.14 = (bf16[272,256]{1,0:T(8,128)(2,1)}, bf16[272,256]{1,0:T(8,128)(2,1)S(1)}, u32[]{:S(2)}, u32[]{:S(2)}) collective-permute-start(bf16[272,256]{1,0:T(8,128)(2,1)} %get-tuple-element.63), channel_id=1, source_target_pairs={{0,6},{1,7},{2,4},{3,5},{4,2},{5,3},{6,0},{7,1},{8,14},{9,15},{10,... | collective-permute-start | bytes 417800 | tf_op jit(solution)/shard_map/ppermute | solution.py:346
  57.5 5.1 %collective-permute-start.15 = (bf16[272,256]{1,0:T(8,128)(2,1)}, bf16[272,256]{1,0:T(8,128)(2,1)S(1)}, u32[]{:S(2)}, u32[]{:S(2)}) collective-permute-start(bf16[272,256]{1,0:T(8,128)(2,1)} %get-tuple-element.64), channel_id=1, source_target_pairs={{0,8},{1,9},{2,10},{3,11},{4,12},{5,13},{6,14},{7,15},{8,0},{9,1},... | collective-permute-start | bytes 417800 | tf_op jit(solution)/shard_map/ppermute | solution.py:346
  57.5 7.9 %collective-permute-start.16 = (bf16[272,256]{1,0:T(8,128)(2,1)}, bf16[272,256]{1,0:T(8,128)(2,1)S(1)}, u32[]{:S(2)}, u32[]{:S(2)}) collective-permute-start(bf16[272,256]{1,0:T(8,128)(2,1)} %get-tuple-element.65), channel_id=1, source_target_pairs={{0,10},{1,11},{2,8},{3,9},{4,14},{5,15},{6,12},{7,13},{8,2},{9,3},... | collective-permute-start | bytes 417800 | tf_op jit(solution)/shard_map/ppermute | solution.py:346
  61.0 11.5 %copy-start.12 = (bf16[272,256]{1,0:T(8,128)(2,1)}, bf16[272,256]{1,0:T(8,128)(2,1)S(1)}, u32[]{:S(2)}) copy-start(bf16[272,256]{1,0:T(8,128)(2,1)S(1)} %collective-permute-done.13.refs_9_) | copy-start | bytes 417796
  61.0 7.4 %collective-permute-start.17 = (bf16[272,256]{1,0:T(8,128)(2,1)}, bf16[272,256]{1,0:T(8,128)(2,1)S(1)}, u32[]{:S(2)}, u32[]{:S(2)}) collective-permute-start(bf16[272,256]{1,0:T(8,128)(2,1)} %get-tuple-element.66), channel_id=1, source_target_pairs={{0,12},{1,13},{2,14},{3,15},{4,8},{5,9},{6,10},{7,11},{8,4},{9,5},... | collective-permute-start | bytes 417800 | tf_op jit(solution)/shard_map/ppermute | solution.py:346
  62.6 9.8 %copy-start.13 = (bf16[272,256]{1,0:T(8,128)(2,1)}, bf16[272,256]{1,0:T(8,128)(2,1)S(1)}, u32[]{:S(2)}) copy-start(bf16[272,256]{1,0:T(8,128)(2,1)S(1)} %collective-permute-done.14.refs_10_) | copy-start | bytes 417796
  62.7 9.8 %collective-permute-start.18 = (bf16[272,256]{1,0:T(8,128)(2,1)}, bf16[272,256]{1,0:T(8,128)(2,1)S(1)}, u32[]{:S(2)}, u32[]{:S(2)}) collective-permute-start(bf16[272,256]{1,0:T(8,128)(2,1)} %get-tuple-element.67), channel_id=1, source_target_pairs={{0,14},{1,15},{2,12},{3,13},{4,10},{5,11},{6,8},{7,9},{8,6},{9,7},... | collective-permute-start | bytes 417800 | tf_op jit(solution)/shard_map/ppermute | solution.py:346
  62.7 9.8 %copy-start.14 = (bf16[272,256]{1,0:T(8,128)(2,1)}, bf16[272,256]{1,0:T(8,128)(2,1)S(1)}, u32[]{:S(2)}) copy-start(bf16[272,256]{1,0:T(8,128)(2,1)S(1)} %collective-permute-done.15.refs_11_) | copy-start | bytes 417796
  65.5 7.0 %copy-start.15 = (bf16[272,256]{1,0:T(8,128)(2,1)}, bf16[272,256]{1,0:T(8,128)(2,1)S(1)}, u32[]{:S(2)}) copy-start(bf16[272,256]{1,0:T(8,128)(2,1)S(1)} %collective-permute-done.16.refs_12_) | copy-start | bytes 417796
  68.4 4.1 %copy-start.16 = (bf16[272,256]{1,0:T(8,128)(2,1)}, bf16[272,256]{1,0:T(8,128)(2,1)S(1)}, u32[]{:S(2)}) copy-start(bf16[272,256]{1,0:T(8,128)(2,1)S(1)} %collective-permute-done.17.refs_13_) | copy-start | bytes 417796
  72.4 0.7 copy-start.17
  72.4 0.8 copy-start.2
  73.3 11.7 %copy-start.25 = (bf16[272,256]{1,0:T(8,128)(2,1)S(1)}, bf16[272,256]{1,0:T(8,128)(2,1)}, u32[]{:S(2)}) copy-start(bf16[272,256]{1,0:T(8,128)(2,1)} %get-tuple-element.60) | copy-start | bytes 417796
  82.5 15.3 %collective-permute-start.20 = (bf16[3,256,512]{2,1,0:T(8,128)(2,1)}, bf16[3,256,512]{2,1,0:T(8,128)(2,1)S(1)}, u32[]{:S(2)}, u32[]{:S(2)}) collective-permute-start(bf16[3,256,512]{2,1,0:T(8,128)(2,1)} %get-tuple-element.70), channel_id=1, source_target_pairs={{0,1},{1,0},{2,3},{3,2},{4,5},{5,4},{6,7},{7,6},{8,9},{9,8},{10,11... | collective-permute-start | bytes 2359304 | tf_op jit(solution)/shard_map/ppermute | solution.py:342
  85.0 5.1 %collective-permute-start.12 = (bf16[272,256]{1,0:T(8,128)(2,1)S(1)}, bf16[272,256]{1,0:T(8,128)(2,1)S(1)}, u32[]{:S(2)}, u32[]{:S(2)}) collective-permute-start(bf16[272,256]{1,0:T(8,128)(2,1)S(1)} %copy-done.25), channel_id=1, source_target_pairs={{0,2},{1,3},{2,0},{3,1},{4,6},{5,7},{6,4},{7,5},{8,10},{9,11},{10,... | collective-permute-start | bytes 417800 | tf_op jit(solution)/shard_map/ppermute | solution.py:346
  90.1 0.7 copy-start.19
  95.5 2.3 %collective-permute-start.19 = (bf16[1,256,512]{2,1,0:T(8,128)(2,1)}, bf16[1,256,512]{2,1,0:T(8,128)(2,1)S(1)}, u32[]{:S(2)}, u32[]{:S(2)}) collective-permute-start(bf16[1,256,512]{2,1,0:T(8,128)(2,1)} %get-tuple-element.69), channel_id=1, source_target_pairs={{0,1},{1,0},{2,3},{3,2},{4,5},{5,4},{6,7},{7,6},{8,9},{9,8},{10,11... | collective-permute-start | bytes 786440 | tf_op jit(solution)/shard_map/ppermute | solution.py:342
  97.8 0.7 copy-start.11
  97.8 1.0 copy-start.3

commit v4 on v3

--- a/solution.py
+++ b/solution.py
@@ -119,7 +119,7 @@
     columns[...] = jnp.concatenate([decay, docs, filler], axis=0).T
 
 
-def state_kernel(first_slot, heads, scalars, *refs):
+def state_kernel(heads, scalars, *refs):
     k_own, v_own, k_oth, v_oth, factors, tops, decays, ids_ref = refs[:8]
     outs, halves = refs[8:-1], refs[-1]
     step = pl.program_id(0)
@@ -127,7 +127,7 @@
     tokens, key_width = k_own.shape[1:]
     part = v_own.shape[2] // 2
     length = 2 * tokens
-    head = (heads // 2) * core + jnp.bitwise_xor(mine // 2, first_slot - step)
+    head = (heads // 2) * core + jnp.bitwise_xor(mine, step)
     row = factors[pl.ds(head, 1), :]
     first, last = row[:, :tokens], row[:, tokens:]
     total, normal = None, None
@@ -154,7 +154,7 @@
 
         @pl.when(step == i // 2)
         def _(out=out, i=i):
-            out[...] = halves[jnp.bitwise_xor(mine % 2, i % 2)]
+            out[...] = halves[i % 2]
 
 
 def decay_before(mine, place, decays):
@@ -224,21 +224,15 @@
         outs[r][key_width:, :] = meta_rows(normal, top, zero, doc)
 
 
-def output_kernel(first_slot, heads, scalars, *refs):
+def local_kernel(first_slot, heads, scalars, *refs):
     q_own, k_own, v_own, q_oth, k_oth, v_oth, source_rows, columns, ids_ref = refs[:9]
-    entering, (keep, send, payload) = refs[9:-3], refs[-3:]
+    numerators, stats = refs[-2:]
     step = pl.program_id(0)
     mine, core = scalars[0], scalars[1]
     tokens, key_width = q_own.shape[1:]
     length = 2 * tokens
     scaling = key_width**-0.5
-    for i, ref in enumerate(entering):
-
-        @pl.when(step == i // 2)
-        def _(ref=ref, i=i):
-            payload[jnp.bitwise_xor(mine % 2, i % 2)] = ref[...]
-
-    head = (heads // 2) * core + jnp.bitwise_xor(mine // 2, first_slot + step)
+    head = (heads // 2) * core + jnp.bitwise_xor(mine, first_slot + step)
     is_first = core == 0
     source = source_rows[pl.ds(head, 1), :]
     lane = iota((length, LANES), 1)
@@ -247,66 +241,97 @@
     docs = turned[:, heads : heads + 1]
     source_docs = ids_ref[...].astype(F32) + 1.0
     causal = iota((tokens, tokens), 0) >= iota((tokens, tokens), 1)
-    normal, top, _, doc = read_meta([payload.at[0]])
-    carried = jnp.where(docs == doc[:, :1], decay + top[:, :1], FLOOR_NEG)
-    pieces = jnp.concatenate(split3(normal) + (jnp.zeros((META - 3, key_width), F32),), axis=0)
-    pieces = pieces.astype(BF16)
-    memory = jnp.concatenate([payload[0, :key_width, :], payload[1, :key_width, :]], axis=1)
 
     def ordered(own, other):
         own, other = own[0], other[0]
         return jnp.where(is_first, own, other), jnp.where(is_first, other, own)
 
     queries, keys, values = ordered(q_own, q_oth), ordered(k_own, k_oth), ordered(v_own, v_oth)
-    results = []
     for block in range(2):
         rows = slice(block * tokens, (block + 1) * tokens)
-        query = queries[block]
-        stabilizer = carried[rows]
         exponents = []
         for s in range(block + 1):
             cols = slice(s * tokens, (s + 1) * tokens)
             allowed = docs[rows] == source_docs[:, cols]
             if s == block:
                 allowed = allowed & causal
-            exponent = jnp.where(allowed, decay[rows] + source[:, cols], FLOOR_NEG)
-            exponents.append(exponent)
-            stabilizer = jnp.maximum(stabilizer, jnp.max(exponent, axis=1, keepdims=True))
-        retained = jnp.exp(carried[rows] - stabilizer) * scaling
+            exponents.append(jnp.where(allowed, decay[rows] + source[:, cols], FLOOR_NEG))
+        stabilizer = functools.reduce(
+            jnp.maximum, [jnp.max(x, axis=1, keepdims=True) for x in exponents]
+        )
+        numerator, denominator = None, None
+        for s in range(block + 1):
+            weights = dot(queries[block], keys[s], NT) * scaling
+            weights = weights * jnp.exp(exponents[s] - stabilizer)
+            high = weights.astype(BF16)
+            part = dot(high, values[s])
+            if s < block:
+                part = part + dot((weights - high.astype(F32)).astype(BF16), values[s])
+            numerator = part if s == 0 else numerator + part
+            part = jnp.sum(weights, axis=1, keepdims=True)
+            denominator = part if s == 0 else denominator + part
+        side = core if block == 0 else 1 - core
+        numerators[0, side] = numerator
+        lane = iota((tokens, LANES), 1)
+        stats[0, side] = jnp.where(
+            lane == 0,
+            stabilizer,
+            jnp.where(lane == 1, denominator, jnp.where(lane == 2, decay[rows], docs[rows])),
+        )
+
+
+def output_kernel(scalars, q_own, q_oth, numerators, stats, *refs):
+    entering, (keep, send, payload) = refs[:-3], refs[-3:]
+    step = pl.program_id(0)
+    key_width = q_own.shape[2]
+    scaling = key_width**-0.5
+    for i, ref in enumerate(entering):
+
+        @pl.when(step == i)
+        def _(ref=ref):
+            payload[...] = ref[...]
+
+    normal, top, _, doc = read_meta([payload])
+    pieces = jnp.concatenate(split3(normal) + (jnp.zeros((META - 3, key_width), F32),), axis=0)
+    pieces = pieces.astype(BF16)
+    memory = payload[:key_width, :]
+    for side, (q_ref, out) in enumerate(((q_own, keep), (q_oth, send))):
+        query = q_ref[0]
+        stat = stats[0, side]
+        local, docs = stat[:, 0:1], stat[:, 3:4]
+        carried = jnp.where(docs == doc[:, :1], stat[:, 2:3] + top[:, :1], FLOOR_NEG)
+        stabilizer = jnp.maximum(local, carried)
+        shrink = jnp.exp(local - stabilizer)
+        retained = jnp.exp(carried - stabilizer) * scaling
         seen = dot(query, pieces, NT)
-        denominator = retained * ((seen[:, 2:3] + seen[:, 1:2]) + seen[:, 0:1])
-        numerator = retained * dot(query, memory)
-        for s in range(block + 1):
-            weights = dot(query, keys[s], NT) * scaling * jnp.exp(exponents[s] - stabilizer)
-            denominator = denominator + jnp.sum(weights, axis=1, keepdims=True)
-            high = weights.astype(BF16)
-            numerator = numerator + dot(high, values[s])
-            if s < block:
-                low = (weights - high.astype(F32)).astype(BF16)
-                numerator = numerator + dot(low, values[s])
-        results.append((numerator / jnp.maximum(jnp.abs(denominator), 1.0)).astype(BF16))
-    keep[0] = jnp.where(is_first, results[0], results[1])
-    send[0] = jnp.where(is_first, results[1], results[0])
+        seen = (seen[:, 2:3] + seen[:, 1:2]) + seen[:, 0:1]
+        denominator = shrink * stat[:, 1:2] + retained * seen
+        inverse = 1.0 / jnp.maximum(jnp.abs(denominator), 1.0)
+        result = (shrink * inverse) * numerators[0, side]
+        result = result + (retained * inverse) * dot(query, memory)
+        out[0] = result.astype(BF16)
 
 
 def merge_kernel(heads, scalars, *refs):
-    stacks, out = refs[:-1], refs[-1]
+    kept, received, out = refs[:2], refs[2:4], refs[4]
     half = heads // 2
     n = LAY // heads
-    mine, core = scalars[0] // 2, scalars[1]
+    mine, core = scalars[0], scalars[1]
     into, given = iota((LAY, LAY), 0), iota((LAY, LAY), 1)
     index = given // n
     slot = jnp.bitwise_and(index, half - 1)
     side = jnp.where(index < half, core, 1 - core)
     head = side * half + jnp.bitwise_xor(slot, mine)
     order = ((into % heads == head) & (into // heads == given % n)).astype(BF16)
-    _, tokens, width = stacks[0].shape
+    _, tokens, width = kept[0].shape
     for g in range(tokens // n):
         span = slice(g * n, (g + 1) * n)
-        rows = jnp.concatenate(
-            [stack[i, span, :] for stack in stacks for i in range(stack.shape[0])], axis=0
-        )
-        out[span] = dot(order, rows).reshape(n, heads, width).astype(BF16)
+        for p in range(2):
+            rows = jnp.concatenate([kept[p][:, span, :], received[p][:, span, :]], axis=0)
+            turned = dot(order, rows.reshape(LAY, width))
+            out[span, :, p * width : (p + 1) * width] = turned.reshape(n, heads, width).astype(
+                BF16
+            )
 
 
 def whole(shape):
@@ -328,7 +353,7 @@
     tokens, heads, key_width = queries.shape
     value_width = value_vectors.shape[2]
     half = heads // 2
-    group = heads
+    group = half
     part = value_width // 2
     chips = devices // 2
     levels = chips // group
@@ -365,10 +390,16 @@
         )(scalars, *sources)
 
     gates = jnp.concatenate([input_gate.T, forget_gate.T], axis=0)
+    gates, key_vectors = lax.optimization_barrier((gates, key_vectors))
     gates_oth = swap_cores(gates)
     k_keep, v_keep, k_send, v_send = relayout(key_vectors, value_vectors)
+    gates_oth, k_send, v_send = lax.optimization_barrier((gates_oth, k_send, v_send))
+    k_oth = swap_cores(k_send)
     v_oth = swap_cores(v_send)
-    k_oth = swap_cores(k_send)
+    queries, _ = lax.optimization_barrier((queries, v_send))
+    q_keep, q_send = relayout(queries)
+    k_oth, q_send = lax.optimization_barrier((k_oth, q_send))
+    q_oth = swap_cores(q_send)
     gate_shapes = [
         (heads, 2 * tokens),
         (heads, LANES),
@@ -385,87 +416,111 @@
         name="gates",
     )(scalars, gates, gates_oth, ids)
 
-    def per_head(kernel, first_slot, steps, down, by_head, others, outs, scratch, name):
-        def block(x):
-            def index(i, s):
-                slot = first_slot - i if down else first_slot + i
-                return (jnp.bitwise_xor(s[0] // 2, slot), 0, 0)
-
-            return pl.BlockSpec((1,) + x.shape[1:], index)
-
+    def by_slot(x, first_slot=0):
+        return pl.BlockSpec(
+            (1,) + x.shape[1:], lambda i, s: (jnp.bitwise_xor(s[0], first_slot + i), 0, 0)
+        )
+
+    made = pl.pallas_call(
+        functools.partial(state_kernel, heads),
+        grid_spec=pltpu.PrefetchScalarGridSpec(
+            num_scalar_prefetch=1,
+            grid=(group,),
+            in_specs=[by_slot(x) for x in (k_keep, v_keep, k_oth, v_oth)]
+            + [whole(x.shape) for x in (factors, tops, decays, ids)],
+            out_specs=[whole(state)] * (2 * group),
+            scratch_shapes=[pltpu.VMEM((2,) + state, BF16)],
+        ),
+        out_shape=[shape_of(*state)] * (2 * group),
+        compiler_params=params(),
+        name="states",
+    )(scalars, k_keep, v_keep, k_oth, v_oth, factors, tops, decays, ids)
+    made = [made[p::2] for p in range(2)]
+    gathered = [
+        [made[p][0]] + [in_group(made[p][r], r) for r in range(1, group)] for p in range(2)
+    ]
+    local_shapes = [(half, 2, tokens, value_width), (half, 2, tokens, LANES)]
+
+    def own_terms(first_slot, count, q_own, into):
+        by_head = (q_own, k_keep, v_keep, q_oth, k_oth, v_oth)
+        small = (source_rows, columns, ids)
         return pl.pallas_call(
-            functools.partial(kernel, first_slot, heads),
+            functools.partial(local_kernel, first_slot, heads),
             grid_spec=pltpu.PrefetchScalarGridSpec(
                 num_scalar_prefetch=1,
-                grid=(steps,),
-                in_specs=[block(x) for x in by_head] + [whole(x.shape) for x in others],
-                out_specs=[spec for spec, _ in outs],
-                scratch_shapes=scratch,
+                grid=(count,),
+                in_specs=[by_slot(x, first_slot) for x in by_head]
+                + [whole(x.shape) for x in small]
+                + [pl.BlockSpec(memory_space=pl.ANY)] * len(into),
+                out_specs=[
+                    pl.BlockSpec((1,) + s[1:], lambda i, _: (first_slot + i, 0, 0, 0))
+                    for s in local_shapes
+                ],
             ),
-            out_shape=[shape for _, shape in outs],
+            out_shape=[shape_of(*s, dtype=F32) for s in local_shapes],
+            input_output_aliases={10 + i: i for i in range(len(into))},
             compiler_params=params(),
-            name=name,
-        )(scalars, *by_head, *others)
-
-    made = [None] * group
-    at_once = half // 2
-    for first_slot in range(half - 1, -1, -at_once):
-        lowest = 2 * (first_slot - at_once + 1)
-        pairs = [2 * (first_slot - i) + b for i in range(at_once) for b in range(2)]
-        outs = per_head(
-            state_kernel,
-            first_slot,
-            at_once,
-            True,
-            (k_keep, v_keep, k_oth, v_oth),
-            (factors, tops, decays, ids),
-            [(whole(state), shape_of(*state))] * len(pairs),
-            [pltpu.VMEM((2,) + state, BF16)],
-            "states",
-        )
-        for r, out in zip(pairs, outs, strict=True):
-            made[r] = out
-        if lowest == 0:
-            queries, made[0] = lax.optimization_barrier((queries, made[0]))
-    gathered = [in_group(made[r], r) if r else made[0] for r in range(group - 1, -1, -1)][::-1]
-    q_keep, q_send = relayout(queries)
-    q_oth = swap_cores(q_send)
-
-    total = pl.pallas_call(
-        functools.partial(total_kernel, group),
-        in_specs=[SMEM] + [whole(state)] * group,
-        out_specs=whole(state),
-        out_shape=shape_of(*state),
-        compiler_params=params(),
-        name="group_total",
-    )(scalars, *gathered)
-    totals = [to_later(total, d) for d in range(reach, 0, -1)][::-1]
-
-    outgoing = pl.pallas_call(
-        functools.partial(entering_kernel, group, reach),
-        in_specs=[SMEM] + [whole(state)] * (group + reach),
-        out_specs=[whole(state)] * group,
-        out_shape=[shape_of(*state)] * group,
-        compiler_params=params(),
-        name="entering",
-    )(scalars, *gathered, *totals)
-    entering = [in_group(outgoing[r], r) if r else outgoing[0] for r in range(group - 1, -1, -1)]
-    entering = entering[::-1]
-
+            name="own_terms",
+        )(scalars, *by_head, *small, *into)
+
+    def group_total(states):
+        return pl.pallas_call(
+            functools.partial(total_kernel, group),
+            in_specs=[SMEM] + [whole(state)] * group,
+            out_specs=whole(state),
+            out_shape=shape_of(*state),
+            compiler_params=params(),
+            name="group_total",
+        )(scalars, *states)
+
+    def entering_states(states, total):
+        totals = [to_later(total, d) for d in range(1, reach + 1)]
+        return pl.pallas_call(
+            functools.partial(entering_kernel, group, reach),
+            in_specs=[SMEM] + [whole(state)] * (group + reach),
+            out_specs=[whole(state)] * group,
+            out_shape=[shape_of(*state)] * group,
+            compiler_params=params(),
+            name="entering",
+        )(scalars, *states, *totals)
+
+    def outputs(p, numerators, stats, entering):
+        spec = pl.BlockSpec((1, tokens, part), lambda i, s: (i, 0, 0))
+        return pl.pallas_call(
+            output_kernel,
+            grid_spec=pltpu.PrefetchScalarGridSpec(
+                num_scalar_prefetch=1,
+                grid=(group,),
+                in_specs=[by_slot(q_keep), by_slot(q_oth)]
+                + [
+                    pl.BlockSpec((1, 2, tokens, part), lambda i, s: (i, 0, 0, p)),
+                    pl.BlockSpec((1, 2, tokens, LANES), lambda i, s: (i, 0, 0, 0)),
+                ]
+                + [whole(state)] * group,
+                out_specs=[spec] * 2,
+                scratch_shapes=[pltpu.VMEM(state, BF16)],
+            ),
+            out_shape=[shape_of(half, tokens, part)] * 2,
+            compiler_params=params(),
+            name="outputs",
+        )(scalars, q_keep, q_oth, numerators, stats, *entering)
+
+    early = half // 2
+    first_total = group_total(gathered[0])
+    q_later, _ = lax.optimization_barrier((q_keep, first_total))
+    terms = own_terms(0, early, q_later, ())
+    gathered[1], terms = lax.optimization_barrier((gathered[1], terms))
+    second_total = group_total(gathered[1])
+    q_last, _ = lax.optimization_barrier((q_keep, second_total))
+    terms = own_terms(early, half - early, q_last, terms)
+    leaving = [entering_states(gathered[0], first_total)]
+    gathered[1], leaving[0] = lax.optimization_barrier((gathered[1], leaving[0]))
+    leaving.append(entering_states(gathered[1], second_total))
+    (numerators, stats), _ = lax.optimization_barrier((terms, leaving[1][0]))
     kept, received = [], []
-    for first_slot, count in ((0, 1), (1, half - 1)):
-        spec = pl.BlockSpec((1, tokens, value_width), lambda i, s: (i, 0, 0))
-        keep, send = per_head(
-            output_kernel,
-            first_slot,
-            count,
-            False,
-            (q_keep, k_keep, v_keep, q_oth, k_oth, v_oth),
-            (source_rows, columns, ids, *entering[2 * first_slot : 2 * (first_slot + count)]),
-            [(spec, shape_of(count, tokens, value_width))] * 2,
-            [pltpu.VMEM((2,) + state, BF16)],
-            "outputs",
-        )
+    for p in range(2):
+        entering = [leaving[p][0]] + [in_group(leaving[p][r], r) for r in range(1, group)]
+        keep, send = outputs(p, numerators, stats, entering)
         kept.append(keep)
         received.append(swap_cores(send))
     return pl.pallas_call(

time: 104 us -> 101 us (0.971)
  waiting for transfers between devices: 34.5 us -> 9.84 us
  Pallas kernels: 40.3 us -> 53.3 us
  starting transfers between devices: 19.9 us -> 26 us
  local copies, waits for them, and re-layouts: 6.8 us -> 8.43 us
    ppermute x14 -> x12, waiting for transfers between devices: 21.3 us -> 2.89 us  [in_group(): return lax.ppermute(x, AXES, pairs)]
    pallas_call x6 -> x9, Pallas kernels: 27.8 us -> 40.7 us  [the longest x2 14.9 us: outputs(): pl.pallas_call(output_kernel, grid_spec=pltpu.PrefetchScalarGridSpec(num_...]
    ppermute x1 -> x4, waiting for transfers between devices: 9.81 us -> 4.4 us  [to_later(): return lax.ppermute(x, AXES, [(d, d + jump) for d in range(devices - jump)])]
    ppermute x1 -> x4, starting transfers between devices: 1.28 us -> 5.14 us  [to_later(): return lax.ppermute(x, AXES, [(d, d + jump) for d in range(devices - jump)])]
    ppermute x6, starting transfers between devices: 7.01 us -> 9.15 us  [swap_cores(): return lax.ppermute(x, AXES, [(d, d ^ 1) for d in range(devices)])]
    unnamed x52 -> x48, local copies, waits for them, and re-layouts: 6.15 us -> 7.78 us
    ppermute x14 -> x12, starting transfers between devices: 11.6 us -> 11.7 us  [in_group(): return lax.ppermute(x, AXES, pairs)]
  transfers between devices with their start and end apart: 21 -> 22, of which waited for: 11 -> 6; matrix products, arithmetic and copies ran while one was open for 1% -> 1% of each run, Pallas kernels for 19% -> 48%
where the time goes in v4:
time: 101 us; the launch traced here: 99.1 us
  Pallas kernels  53.3 us (53%)
  starting transfers between devices  26 us (26%)
  waiting for transfers between devices  9.84 us (10%)
  local copies, waits for them, and re-layouts  8.43 us (8%)
  other arithmetic  1.32 us (1%)
    pallas_call x2, Pallas kernels, outputs(): pl.pallas_call(output_kernel, grid_spec=pltpu.PrefetchScalarGridSpec(num_...  14.9 us
    ppermute x12, starting transfers between devices, in_group(): return lax.ppermute(x, AXES, pairs)  11.7 us
    pallas_call x2, Pallas kernels, own_terms(): pl.pallas_call(functools.partial(local_kernel, first_slot, heads), grid_s...  11 us
    ppermute x6, starting transfers between devices, swap_cores(): return lax.ppermute(x, AXES, [(d, d ^ 1) for d in range(devices)])  9.15 us
    unnamed x48, local copies, waits for them, and re-layouts  7.78 us
    pallas_call x2, Pallas kernels, relayout(): pl.pallas_call(functools.partial(relayout_kernel, half, len(sources)), in...  7.11 us
    pallas_call x1, Pallas kernels, local(): pl.pallas_call(functools.partial(state_kernel, heads), grid_spec=pltpu.Pr...  5.88 us
    ppermute x4, starting transfers between devices, to_later(): return lax.ppermute(x, AXES, [(d, d + jump) for d in range(devices - jump)])  5.14 us
  transfers between devices with their start and end apart: 22, of which 6 were waited for; matrix products, arithmetic and copies ran while one was open for 1% of the time, Pallas kernels for 48%

profile of v4, /device:TPU:25, one launch (start us, length us, event | category | flops | bytes accessed | tf_op | source)
XLA Modules:
  0.0 99.1 jit_solution(16721252805989802494)
XLA Ops:
  0.0 0.7 pad_maximum_fusion.g_own
  0.7 0.7 collective-permute-start
  1.4 0.6 pad_add_fusion.scalars
  2.0 4.4 %relayout.2 = (bf16[4,256,256]{2,1,0:T(8,128)(2,1)}, bf16[4,256,512]{2,1,0:T(8,128)(2,1)}, bf16[4,256,256]{2,1,0:T(8,128)(2,1)}, bf16[4,256,512]{2,1,0:T(8,128)(2,1)}) custom-call(s32[2]{0:T(128)} %pad_add_fusion.scalars, bf16[256,8,256]{2,1,0:T(8,128)(2,1)} %refs_0_, bf16[256,8,512]{2,1,0:T(8,128)(2,1)} %refs_1_.1), custom_call_target="tpu_custom_call" | custom-call | tf_op jit(solution)/shard_map/relayout/pallas_call | solution.py:383
  6.5 0.1 collective-permute-start.3
  6.5 0.5 collective-permute-start.1
  7.0 2.7 %relayout.3 = (bf16[4,256,256]{2,1,0:T(8,128)(2,1)}, bf16[4,256,256]{2,1,0:T(8,128)(2,1)}) custom-call(s32[2]{0:T(128)} %pad_add_fusion.scalars, bf16[256,8,256]{2,1,0:T(8,128)(2,1)} %refs_0_.1), custom_call_target="tpu_custom_call" | custom-call | tf_op jit(solution)/shard_map/relayout/pallas_call | solution.py:383
  9.7 0.4 collective-permute-done.1.refs_2_.refs_4_
  10.1 0.1 collective-permute-start.2
  10.3 0.6 dynamic_slice.3
  10.9 1.9 %gates.1 = (f32[8,512]{1,0:T(8,128)}, f32[8,128]{1,0:T(8,128)}, f32[8,128]{1,0:T(8,128)}, f32[8,512]{1,0:T(8,128)}, f32[512,128]{1,0:T(8,128)}) custom-call(s32[2]{0:T(128)} %pad_add_fusion.scalars, bf16[16,256]{1,0:T(8,128)(2,1)} %copy-done.21, bf16[16,256]{1,0:T(8,128)(2,1)} %copy-done.22, s32[1,512]{1,0:T(1,128)} %bitcast.5), custom_call_target="tpu_custom_call" | custom-call | tf_op jit(solution)/shard_map/gates/pallas_call | solution.py:410
  12.8 0.0 collective-permute-done.3.refs_3_.refs_5_
  12.9 1.0 copy-done
  13.8 5.9 %states.1 = (bf16[272,256]{1,0:T(8,128)(2,1)}, bf16[272,256]{1,0:T(8,128)(2,1)}, bf16[272,256]{1,0:T(8,128)(2,1)}, bf16[272,256]{1,0:T(8,128)(2,1)}, bf16[272,25...) custom-call(s32[2]{0:T(128)} %pad_add_fusion.scalars, ...), custom_call_target="tpu_custom_call" | custom-call | tf_op jit(solution)/shard_map/states/pallas_call | solution.py:424
  19.7 1.2 %collective-permute-start.7 = (bf16[272,256]{1,0:T(8,128)(2,1)}, bf16[272,256]{1,0:T(8,128)(2,1)S(1)}, u32[]{:S(2)}, u32[]{:S(2)}) collective-permute-start(bf16[272,256]{1,0:T(8,128)(2,1)} %get-tuple-element.88), channel_id=1, source_target_pairs={{0,2},{1,3},{2,0},{3,1},{4,6},{5,7},{6,4},{7,5},{8,10},{9,11},{10,... | collective-permute-start | bytes 417800 | tf_op jit(solution)/shard_map/ppermute | solution.py:371
  21.0 1.2 %collective-permute-start.8 = (bf16[272,256]{1,0:T(8,128)(2,1)}, bf16[272,256]{1,0:T(8,128)(2,1)S(1)}, u32[]{:S(2)}, u32[]{:S(2)}) collective-permute-start(bf16[272,256]{1,0:T(8,128)(2,1)} %get-tuple-element.89), channel_id=1, source_target_pairs={{0,4},{1,5},{2,6},{3,7},{4,0},{5,1},{6,2},{7,3},{8,12},{9,13},{10,... | collective-permute-start | bytes 417800 | tf_op jit(solution)/shard_map/ppermute | solution.py:371
  22.2 0.2 collective-permute-start.9
  22.4 1.2 %collective-permute-start.4 = (bf16[272,256]{1,0:T(8,128)(2,1)}, bf16[272,256]{1,0:T(8,128)(2,1)S(1)}, u32[]{:S(2)}, u32[]{:S(2)}) collective-permute-start(bf16[272,256]{1,0:T(8,128)(2,1)} %get-tuple-element.84), channel_id=1, source_target_pairs={{0,2},{1,3},{2,0},{3,1},{4,6},{5,7},{6,4},{7,5},{8,10},{9,11},{10,... | collective-permute-start | bytes 417800 | tf_op jit(solution)/shard_map/ppermute | solution.py:371
  23.6 1.2 %collective-permute-done.7.refs_1_ = bf16[272,256]{1,0:T(8,128)(2,1)S(1)} collective-permute-done((bf16[272,256]{1,0:T(8,128)(2,1)}, bf16[272,256]{1,0:T(8,128)(2,1)S(1)}, u32[]{:S(2)}, u32[]{:S(2)}) %collective-permute-start.7) | collective-permute-done | bytes 139296 | tf_op jit(solution)/shard_map/ppermute | solution.py:371
  24.8 1.3 %collective-permute-start.5 = (bf16[272,256]{1,0:T(8,128)(2,1)}, bf16[272,256]{1,0:T(8,128)(2,1)S(1)}, u32[]{:S(2)}, u32[]{:S(2)}) collective-permute-start(bf16[272,256]{1,0:T(8,128)(2,1)} %get-tuple-element.85), channel_id=1, source_target_pairs={{0,4},{1,5},{2,6},{3,7},{4,0},{5,1},{6,2},{7,3},{8,12},{9,13},{10,... | collective-permute-start | bytes 417800 | tf_op jit(solution)/shard_map/ppermute | solution.py:371
  26.1 1.1 %collective-permute-start.6 = (bf16[272,256]{1,0:T(8,128)(2,1)}, bf16[272,256]{1,0:T(8,128)(2,1)S(1)}, u32[]{:S(2)}, u32[]{:S(2)}) collective-permute-start(bf16[272,256]{1,0:T(8,128)(2,1)} %get-tuple-element.86), channel_id=1, source_target_pairs={{0,6},{1,7},{2,4},{3,5},{4,2},{5,3},{6,0},{7,1},{8,14},{9,15},{10,... | collective-permute-start | bytes 417800 | tf_op jit(solution)/shard_map/ppermute | solution.py:371
  27.2 1.6 %collective-permute-done.9.refs_3_ = bf16[272,256]{1,0:T(8,128)(2,1)S(1)} collective-permute-done((bf16[272,256]{1,0:T(8,128)(2,1)}, bf16[272,256]{1,0:T(8,128)(2,1)S(1)}, u32[]{:S(2)}, u32[]{:S(2)}) %collective-permute-start.9) | collective-permute-done | bytes 139296 | tf_op jit(solution)/shard_map/ppermute | solution.py:371
  28.9 0.6 copy-done.7
  29.5 1.9 %group_total.2 = bf16[272,256]{1,0:T(8,128)(2,1)} custom-call(s32[2]{0:T(128)} %pad_add_fusion.scalars, bf16[272,256]{1,0:T(8,128)(2,1)} %get-tuple-element.87.refs_0_, bf16[272,256]{1,0:T(8,128)(2,1)} %copy-done.4, bf16[272,256]{1,0:T(8,128)(2,1)} %copy-done.6, bf16[272,256]{1,0:T(8,128)(2,1)} %copy-done.7), custom_call_target="tpu_custom_call" | custom-call | tf_op jit(solution)/shard_map/group_total/pallas_call | solution.py:467
  31.4 1.3 %collective-permute-start.10 = (bf16[272,256]{1,0:T(8,128)(2,1)}, bf16[272,256]{1,0:T(8,128)(2,1)S(1)}, u32[]{:S(2)}, u32[]{:S(2)}) collective-permute-start(bf16[272,256]{1,0:T(8,128)(2,1)} %group_total.2), channel_id=1, source_target_pairs={{0,8},{1,9},{2,10},{3,11},{4,12},{5,13},{6,14},{7,15},{8,16},{9,17... | collective-permute-start | bytes 417800 | tf_op jit(solution)/shard_map/ppermute | solution.py:375
  32.7 0.0 collective-permute-done.2.refs_3_.q_oth
  32.7 1.3 %collective-permute-start.11 = (bf16[272,256]{1,0:T(8,128)(2,1)}, bf16[272,256]{1,0:T(8,128)(2,1)S(1)}, u32[]{:S(2)}, u32[]{:S(2)}) collective-permute-start(bf16[272,256]{1,0:T(8,128)(2,1)} %group_total.2), channel_id=1, source_target_pairs={{0,16},{1,17},{2,18},{3,19},{4,20},{5,21},{6,22},{7,23},{8,24},{9,... | collective-permute-start | bytes 417800 | tf_op jit(solution)/shard_map/ppermute | solution.py:375
  34.1 5.5 %own_terms.2 = (f32[4,2,256,512]{3,2,1,0:T(8,128)}, f32[4,2,256,128]{3,2,1,0:T(8,128)}) custom-call(s32[2]{0:T(128)} %pad_add_fusion.scalars, bf16[4,256,256]{2,1,0:T(8,128)(2,1)} %get-tuple-element.100.refs_0_.q_own, bf16[4,256,256]{2,1,0:T(8,128)(2,1)} %get-tuple-element.76.refs_0_.refs_1_, bf16[4,256,512]{2,1,0:T(8,128)(2,1)} %get-tuple-element.77.refs_1_.refs_2_, ...), custom_call_target="tpu_custom_call" | custom-call | tf_op jit(solution)/shard_map/own_terms/pallas_call | solution.py:447
  39.6 0.0 collective-permute-done.5.refs_2_
  39.6 0.6 copy-done.3
  40.2 0.0 copy-done.5
  40.3 0.1 copy-done.8
  40.3 1.9 %group_total.3 = bf16[272,256]{1,0:T(8,128)(2,1)} custom-call(s32[2]{0:T(128)} %pad_add_fusion.scalars, bf16[272,256]{1,0:T(8,128)(2,1)} %get-tuple-element.109.refs_0_, bf16[272,256]{1,0:T(8,128)(2,1)} %copy-done.3, bf16[272,256]{1,0:T(8,128)(2,1)} %copy-done.5, bf16[272,256]{1,0:T(8,128)(2,1)} %copy-done.8), custom_call_target="tpu_custom_call" | custom-call | tf_op jit(solution)/shard_map/group_total/pallas_call | solution.py:467
  42.2 1.3 %collective-permute-start.12 = (bf16[272,256]{1,0:T(8,128)(2,1)}, bf16[272,256]{1,0:T(8,128)(2,1)S(1)}, u32[]{:S(2)}, u32[]{:S(2)}) collective-permute-start(bf16[272,256]{1,0:T(8,128)(2,1)} %group_total.3), channel_id=1, source_target_pairs={{0,8},{1,9},{2,10},{3,11},{4,12},{5,13},{6,14},{7,15},{8,16},{9,17... | collective-permute-start | bytes 417800 | tf_op jit(solution)/shard_map/ppermute | solution.py:375
  43.5 1.3 %collective-permute-start.13 = (bf16[272,256]{1,0:T(8,128)(2,1)}, bf16[272,256]{1,0:T(8,128)(2,1)S(1)}, u32[]{:S(2)}, u32[]{:S(2)}) collective-permute-start(bf16[272,256]{1,0:T(8,128)(2,1)} %group_total.3), channel_id=1, source_target_pairs={{0,16},{1,17},{2,18},{3,19},{4,20},{5,21},{6,22},{7,23},{8,24},{9,... | collective-permute-start | bytes 417800 | tf_op jit(solution)/shard_map/ppermute | solution.py:375
  44.9 0.0 collective-permute-done.11.refs_5_
  44.9 0.6 copy-done.17
  45.5 0.6 copy-done.18
  46.1 2.5 %entering.2 = (bf16[272,256]{1,0:T(8,128)(2,1)}, bf16[272,256]{1,0:T(8,128)(2,1)}, bf16[272,256]{1,0:T(8,128)(2,1)}, bf16[272,256]{1,0:T(8,128)(2,1)}) custom-call(s32[2]{0:T(128)} %pad_add_fusion.scalars, bf16[272,256]{1,0:T(8,128)(2,1)} %get-tuple-element.87.refs_0_, bf16[272,256]{1,0:T(8,128)(2,1)} %copy-done.4, bf16[272,256]{1,0:T(8,128)(2,1)} %copy-done.6, ...), custom_call_target="tpu_custom_call" | custom-call | tf_op jit(solution)/shard_map/entering/pallas_call | solution.py:478
  48.7 0.2 collective-permute-done.12.refs_4_
  48.9 4.2 %collective-permute-done.13.refs_5_ = bf16[272,256]{1,0:T(8,128)(2,1)S(1)} collective-permute-done((bf16[272,256]{1,0:T(8,128)(2,1)}, bf16[272,256]{1,0:T(8,128)(2,1)S(1)}, u32[]{:S(2)}, u32[]{:S(2)}) %collective-permute-start.13) | collective-permute-done | bytes 139296 | tf_op jit(solution)/shard_map/ppermute | solution.py:375
  53.1 0.6 copy-done.20
  53.7 2.5 %entering.3 = (bf16[272,256]{1,0:T(8,128)(2,1)}, bf16[272,256]{1,0:T(8,128)(2,1)}, bf16[272,256]{1,0:T(8,128)(2,1)}, bf16[272,256]{1,0:T(8,128)(2,1)}) custom-call(s32[2]{0:T(128)} %pad_add_fusion.scalars, bf16[272,256]{1,0:T(8,128)(2,1)} %get-tuple-element.109.refs_0_, bf16[272,256]{1,0:T(8,128)(2,1)} %copy-done.3, bf16[272,256]{1,0:T(8,128)(2,1)} %copy-done.5, ...), custom_call_target="tpu_custom_call" | custom-call | tf_op jit(solution)/shard_map/entering/pallas_call | solution.py:478
  56.3 1.6 %collective-permute-start.17 = (bf16[272,256]{1,0:T(8,128)(2,1)}, bf16[272,256]{1,0:T(8,128)(2,1)S(1)}, u32[]{:S(2)}, u32[]{:S(2)}) collective-permute-start(bf16[272,256]{1,0:T(8,128)(2,1)} %get-tuple-element.121), channel_id=1, source_target_pairs={{0,2},{1,3},{2,0},{3,1},{4,6},{5,7},{6,4},{7,5},{8,10},{9,11},{10,... | collective-permute-start | bytes 417800 | tf_op jit(solution)/shard_map/ppermute | solution.py:371
  57.9 0.0 collective-permute-start.18
  57.9 1.2 %collective-permute-start.19 = (bf16[272,256]{1,0:T(8,128)(2,1)}, bf16[272,256]{1,0:T(8,128)(2,1)S(1)}, u32[]{:S(2)}, u32[]{:S(2)}) collective-permute-start(bf16[272,256]{1,0:T(8,128)(2,1)} %get-tuple-element.123), channel_id=1, source_target_pairs={{0,6},{1,7},{2,4},{3,5},{4,2},{5,3},{6,0},{7,1},{8,14},{9,15},{10,... | collective-permute-start | bytes 417800 | tf_op jit(solution)/shard_map/ppermute | solution.py:371
  59.1 1.5 %collective-permute-start.14 = (bf16[272,256]{1,0:T(8,128)(2,1)}, bf16[272,256]{1,0:T(8,128)(2,1)S(1)}, u32[]{:S(2)}, u32[]{:S(2)}) collective-permute-start(bf16[272,256]{1,0:T(8,128)(2,1)} %get-tuple-element.117), channel_id=1, source_target_pairs={{0,2},{1,3},{2,0},{3,1},{4,6},{5,7},{6,4},{7,5},{8,10},{9,11},{10,... | collective-permute-start | bytes 417800 | tf_op jit(solution)/shard_map/ppermute | solution.py:371
  60.5 0.0 collective-permute-start.15
  60.5 0.0 collective-permute-done.17.refs_1_
  60.5 1.2 %collective-permute-start.16 = (bf16[272,256]{1,0:T(8,128)(2,1)}, bf16[272,256]{1,0:T(8,128)(2,1)S(1)}, u32[]{:S(2)}, u32[]{:S(2)}) collective-permute-start(bf16[272,256]{1,0:T(8,128)(2,1)} %get-tuple-element.119), channel_id=1, source_target_pairs={{0,6},{1,7},{2,4},{3,5},{4,2},{5,3},{6,0},{7,1},{8,14},{9,15},{10,... | collective-permute-start | bytes 417800 | tf_op jit(solution)/shard_map/ppermute | solution.py:371
  61.7 5.5 %own_terms.3 = (f32[4,2,256,512]{3,2,1,0:T(8,128)}, f32[4,2,256,128]{3,2,1,0:T(8,128)}) custom-call(s32[2]{0:T(128)} %pad_add_fusion.scalars, bf16[4,256,256]{2,1,0:T(8,128)(2,1)} %get-tuple-element.100.refs_0_.q_own, bf16[4,256,256]{2,1,0:T(8,128)(2,1)} %get-tuple-element.76.refs_0_.refs_1_, ...), custom_call_target="tpu_custom_call", output_to_operand_aliasing={{0}: (10, {}), {1}: (11, {})} | custom-call | tf_op jit(solution)/shard_map/own_terms/pallas_call | solution.py:447
  67.3 0.0 copy-start.15
  67.3 0.6 copy-done.15
  67.9 0.7 copy-done.16
  68.6 7.5 %outputs.3 = (bf16[4,256,256]{2,1,0:T(8,128)(2,1)}, bf16[4,256,256]{2,1,0:T(8,128)(2,1)}) custom-call(s32[2]{0:T(128)} %pad_add_fusion.scalars, bf16[4,256,256]{2,1,0:T(8,128)(2,1)} %get-tuple-element.100.refs_0_.q_own, bf16[4,256,256]{2,1,0:T(8,128)(2,1)} %copy-done.1, f32[4,2,256,512]{3,2,1,0:T(8,128)} %get-tuple-element.114.numerators, ...), custom_call_target="tpu_custom_call" | custom-call | tf_op jit(solution)/shard_map/outputs/pallas_call | solution.py:489
  76.0 7.8 %collective-permute-start.21 = (bf16[4,256,256]{2,1,0:T(8,128)(2,1)}, bf16[4,256,256]{2,1,0:T(8,128)(2,1)S(1)}, u32[]{:S(2)}, u32[]{:S(2)}) collective-permute-start(bf16[4,256,256]{2,1,0:T(8,128)(2,1)} %get-tuple-element.126), channel_id=1, source_target_pairs={{0,1},{1,0},{2,3},{3,2},{4,5},{5,4},{6,7},{7,6},{8,9},{9,8},{10,11... | collective-permute-start | bytes 1572872 | tf_op jit(solution)/shard_map/ppermute | solution.py:367
  83.8 0.6 copy-done.11
  84.4 0.1 copy-done.12
  84.5 0.7 copy-done.13
  85.2 7.5 %outputs.2 = (bf16[4,256,256]{2,1,0:T(8,128)(2,1)}, bf16[4,256,256]{2,1,0:T(8,128)(2,1)}) custom-call(s32[2]{0:T(128)} %pad_add_fusion.scalars, bf16[4,256,256]{2,1,0:T(8,128)(2,1)} %get-tuple-element.100.refs_0_.q_own, bf16[4,256,256]{2,1,0:T(8,128)(2,1)} %copy-done.1, f32[4,2,256,512]{3,2,1,0:T(8,128)} %get-tuple-element.114.numerators, ...), custom_call_target="tpu_custom_call" | custom-call | tf_op jit(solution)/shard_map/outputs/pallas_call | solution.py:489
  92.6 0.0 collective-permute-start.20
  92.7 2.1 %collective-permute-done.20.refs_2_ = bf16[4,256,256]{2,1,0:T(8,128)(2,1)S(1)} collective-permute-done((bf16[4,256,256]{2,1,0:T(8,128)(2,1)}, bf16[4,256,256]{2,1,0:T(8,128)(2,1)S(1)}, u32[]{:S(2)}, u32[]{:S(2)}) %collective-permute-start.20) | collective-permute-done | bytes 524320 | tf_op jit(solution)/shard_map/ppermute | solution.py:367
  94.8 0.8 copy-done.10
  95.6 3.6 %merge.1 = bf16[256,8,512]{2,1,0:T(8,128)(2,1)} custom-call(s32[2]{0:T(128)} %pad_add_fusion.scalars, bf16[4,256,256]{2,1,0:T(8,128)(2,1)} %get-tuple-element.120.refs_0_, bf16[4,256,256]{2,1,0:T(8,128)(2,1)} %get-tuple-element.124.refs_1_, bf16[4,256,256]{2,1,0:T(8,128)(2,1)} %copy-done.10, bf16[4,256,256]{2,1,0:T(8,128)(2,1)} %copy-done.9), custom_call_target="tpu_custom_call" | custom-call | tf_op jit(solution)/shard_map/merge/pallas_call | solution.py:526
  (44 shorter events, 0.1 us)
Async XLA Ops:
  0.0 10.3 %copy-start.23 = (s32[1024]{0:T(1024)S(1)}, s32[1024]{0:T(1024)}, u32[]{:S(2)}) copy-start(s32[1024]{0:T(1024)} %param.11) | copy-start | bytes 12292
  0.7 10.2 %copy-start.21 = (bf16[16,256]{1,0:T(8,128)(2,1)}, bf16[16,256]{1,0:T(8,128)(2,1)S(1)}, u32[]{:S(2)}) copy-start(bf16[16,256]{1,0:T(8,128)(2,1)S(1)} %pad_maximum_fusion.g_own) | copy-start | bytes 24580
  0.7 5.7 %collective-permute-start = (bf16[16,256]{1,0:T(8,128)(2,1)S(1)}, bf16[16,256]{1,0:T(8,128)(2,1)S(1)}, u32[]{:S(2)}, u32[]{:S(2)}) collective-permute-start(bf16[16,256]{1,0:T(8,128)(2,1)S(1)} %pad_maximum_fusion.g_own), channel_id=1, source_target_pairs={{0,1},{1,0},{2,3},{3,2},{4,5},{5,4},{6,7},{7,6},{8,9},{9,8},{10,11... | collective-permute-start | bytes 24584 | tf_op jit(solution)/shard_map/ppermute | solution.py:367
  6.4 4.5 %copy-start.22 = (bf16[16,256]{1,0:T(8,128)(2,1)}, bf16[16,256]{1,0:T(8,128)(2,1)S(1)}, u32[]{:S(2)}) copy-start(bf16[16,256]{1,0:T(8,128)(2,1)S(1)} %collective-permute-done.g_oth) | copy-start | bytes 24580
  6.5 6.4 %collective-permute-start.3 = (bf16[4,256,512]{2,1,0:T(8,128)(2,1)}, bf16[4,256,512]{2,1,0:T(8,128)(2,1)S(1)}, u32[]{:S(2)}, u32[]{:S(2)}) collective-permute-start(bf16[4,256,512]{2,1,0:T(8,128)(2,1)} %get-tuple-element.70), channel_id=1, source_target_pairs={{0,1},{1,0},{2,3},{3,2},{4,5},{5,4},{6,7},{7,6},{8,9},{9,8},{10,11... | collective-permute-start | bytes 3145736 | tf_op jit(solution)/shard_map/ppermute | solution.py:367
  6.5 3.6 %collective-permute-start.1 = (bf16[4,256,256]{2,1,0:T(8,128)(2,1)}, bf16[4,256,256]{2,1,0:T(8,128)(2,1)S(1)}, u32[]{:S(2)}, u32[]{:S(2)}) collective-permute-start(bf16[4,256,256]{2,1,0:T(8,128)(2,1)} %get-tuple-element.73), channel_id=1, source_target_pairs={{0,1},{1,0},{2,3},{3,2},{4,5},{5,4},{6,7},{7,6},{8,9},{9,8},{10,11... | collective-permute-start | bytes 1572872 | tf_op jit(solution)/shard_map/ppermute | solution.py:367
  10.1 2.7 %copy-start.2 = (bf16[4,256,256]{2,1,0:T(8,128)(2,1)}, bf16[4,256,256]{2,1,0:T(8,128)(2,1)S(1)}, u32[]{:S(2)}) copy-start(bf16[4,256,256]{2,1,0:T(8,128)(2,1)S(1)} %collective-permute-done.1.refs_2_.refs_4_) | copy-start | bytes 1572868
  10.1 22.6 %collective-permute-start.2 = (bf16[4,256,256]{2,1,0:T(8,128)(2,1)}, bf16[4,256,256]{2,1,0:T(8,128)(2,1)S(1)}, u32[]{:S(2)}, u32[]{:S(2)}) collective-permute-start(bf16[4,256,256]{2,1,0:T(8,128)(2,1)} %get-tuple-element.75), channel_id=1, source_target_pairs={{0,1},{1,0},{2,3},{3,2},{4,5},{5,4},{6,7},{7,6},{8,9},{9,8},{10,11... | collective-permute-start | bytes 1572872 | tf_op jit(solution)/shard_map/ppermute | solution.py:367
  12.9 1.0 copy-start
  19.7 5.1 %collective-permute-start.7 = (bf16[272,256]{1,0:T(8,128)(2,1)}, bf16[272,256]{1,0:T(8,128)(2,1)S(1)}, u32[]{:S(2)}, u32[]{:S(2)}) collective-permute-start(bf16[272,256]{1,0:T(8,128)(2,1)} %get-tuple-element.88), channel_id=1, source_target_pairs={{0,2},{1,3},{2,0},{3,1},{4,6},{5,7},{6,4},{7,5},{8,10},{9,11},{10,... | collective-permute-start | bytes 417800 | tf_op jit(solution)/shard_map/ppermute | solution.py:371
  21.0 5.1 %collective-permute-start.8 = (bf16[272,256]{1,0:T(8,128)(2,1)}, bf16[272,256]{1,0:T(8,128)(2,1)S(1)}, u32[]{:S(2)}, u32[]{:S(2)}) collective-permute-start(bf16[272,256]{1,0:T(8,128)(2,1)} %get-tuple-element.89), channel_id=1, source_target_pairs={{0,4},{1,5},{2,6},{3,7},{4,0},{5,1},{6,2},{7,3},{8,12},{9,13},{10,... | collective-permute-start | bytes 417800 | tf_op jit(solution)/shard_map/ppermute | solution.py:371
  22.2 6.7 %collective-permute-start.9 = (bf16[272,256]{1,0:T(8,128)(2,1)}, bf16[272,256]{1,0:T(8,128)(2,1)S(1)}, u32[]{:S(2)}, u32[]{:S(2)}) collective-permute-start(bf16[272,256]{1,0:T(8,128)(2,1)} %get-tuple-element.90), channel_id=1, source_target_pairs={{0,6},{1,7},{2,4},{3,5},{4,2},{5,3},{6,0},{7,1},{8,14},{9,15},{10,... | collective-permute-start | bytes 417800 | tf_op jit(solution)/shard_map/ppermute | solution.py:371
  22.4 17.2 %collective-permute-start.4 = (bf16[272,256]{1,0:T(8,128)(2,1)}, bf16[272,256]{1,0:T(8,128)(2,1)S(1)}, u32[]{:S(2)}, u32[]{:S(2)}) collective-permute-start(bf16[272,256]{1,0:T(8,128)(2,1)} %get-tuple-element.84), channel_id=1, source_target_pairs={{0,2},{1,3},{2,0},{3,1},{4,6},{5,7},{6,4},{7,5},{8,10},{9,11},{10,... | collective-permute-start | bytes 417800 | tf_op jit(solution)/shard_map/ppermute | solution.py:371
  24.8 4.0 %copy-start.4 = (bf16[272,256]{1,0:T(8,128)(2,1)}, bf16[272,256]{1,0:T(8,128)(2,1)S(1)}, u32[]{:S(2)}) copy-start(bf16[272,256]{1,0:T(8,128)(2,1)S(1)} %collective-permute-done.7.refs_1_) | copy-start | bytes 417796
  24.8 14.8 %collective-permute-start.5 = (bf16[272,256]{1,0:T(8,128)(2,1)}, bf16[272,256]{1,0:T(8,128)(2,1)S(1)}, u32[]{:S(2)}, u32[]{:S(2)}) collective-permute-start(bf16[272,256]{1,0:T(8,128)(2,1)} %get-tuple-element.85), channel_id=1, source_target_pairs={{0,4},{1,5},{2,6},{3,7},{4,0},{5,1},{6,2},{7,3},{8,12},{9,13},{10,... | collective-permute-start | bytes 417800 | tf_op jit(solution)/shard_map/ppermute | solution.py:371
  26.1 2.8 %copy-start.6 = (bf16[272,256]{1,0:T(8,128)(2,1)}, bf16[272,256]{1,0:T(8,128)(2,1)S(1)}, u32[]{:S(2)}) copy-start(bf16[272,256]{1,0:T(8,128)(2,1)S(1)} %collective-permute-done.8.refs_2_) | copy-start | bytes 417796
  26.1 13.5 %collective-permute-start.6 = (bf16[272,256]{1,0:T(8,128)(2,1)}, bf16[272,256]{1,0:T(8,128)(2,1)S(1)}, u32[]{:S(2)}, u32[]{:S(2)}) collective-permute-start(bf16[272,256]{1,0:T(8,128)(2,1)} %get-tuple-element.86), channel_id=1, source_target_pairs={{0,6},{1,7},{2,4},{3,5},{4,2},{5,3},{6,0},{7,1},{8,14},{9,15},{10,... | collective-permute-start | bytes 417800 | tf_op jit(solution)/shard_map/ppermute | solution.py:371
  28.9 0.7 copy-start.7
  31.4 13.4 %collective-permute-start.10 = (bf16[272,256]{1,0:T(8,128)(2,1)}, bf16[272,256]{1,0:T(8,128)(2,1)S(1)}, u32[]{:S(2)}, u32[]{:S(2)}) collective-permute-start(bf16[272,256]{1,0:T(8,128)(2,1)} %group_total.2), channel_id=1, source_target_pairs={{0,8},{1,9},{2,10},{3,11},{4,12},{5,13},{6,14},{7,15},{8,16},{9,17... | collective-permute-start | bytes 417800 | tf_op jit(solution)/shard_map/ppermute | solution.py:375
  32.7 1.3 %copy-start.1 = (bf16[4,256,256]{2,1,0:T(8,128)(2,1)}, bf16[4,256,256]{2,1,0:T(8,128)(2,1)S(1)}, u32[]{:S(2)}) copy-start(bf16[4,256,256]{2,1,0:T(8,128)(2,1)S(1)} %collective-permute-done.2.refs_3_.q_oth) | copy-start | bytes 1572868
  32.7 12.1 %collective-permute-start.11 = (bf16[272,256]{1,0:T(8,128)(2,1)}, bf16[272,256]{1,0:T(8,128)(2,1)S(1)}, u32[]{:S(2)}, u32[]{:S(2)}) collective-permute-start(bf16[272,256]{1,0:T(8,128)(2,1)} %group_total.2), channel_id=1, source_target_pairs={{0,16},{1,17},{2,18},{3,19},{4,20},{5,21},{6,22},{7,23},{8,24},{9,... | collective-permute-start | bytes 417800 | tf_op jit(solution)/shard_map/ppermute | solution.py:375
  39.6 0.7 copy-start.3
  39.6 0.7 copy-start.5
  39.6 0.7 copy-start.8
  42.2 6.6 %collective-permute-start.12 = (bf16[272,256]{1,0:T(8,128)(2,1)}, bf16[272,256]{1,0:T(8,128)(2,1)S(1)}, u32[]{:S(2)}, u32[]{:S(2)}) collective-permute-start(bf16[272,256]{1,0:T(8,128)(2,1)} %group_total.3), channel_id=1, source_target_pairs={{0,8},{1,9},{2,10},{3,11},{4,12},{5,13},{6,14},{7,15},{8,16},{9,17... | collective-permute-start | bytes 417800 | tf_op jit(solution)/shard_map/ppermute | solution.py:375
  43.5 9.6 %collective-permute-start.13 = (bf16[272,256]{1,0:T(8,128)(2,1)}, bf16[272,256]{1,0:T(8,128)(2,1)S(1)}, u32[]{:S(2)}, u32[]{:S(2)}) collective-permute-start(bf16[272,256]{1,0:T(8,128)(2,1)} %group_total.3), channel_id=1, source_target_pairs={{0,16},{1,17},{2,18},{3,19},{4,20},{5,21},{6,22},{7,23},{8,24},{9,... | collective-permute-start | bytes 417800 | tf_op jit(solution)/shard_map/ppermute | solution.py:375
  44.8 0.7 copy-start.17
  45.5 0.6 copy-start.18
  48.9 4.2 %copy-start.19 = (bf16[272,256]{1,0:T(8,128)(2,1)}, bf16[272,256]{1,0:T(8,128)(2,1)S(1)}, u32[]{:S(2)}) copy-start(bf16[272,256]{1,0:T(8,128)(2,1)S(1)} %collective-permute-done.12.refs_4_) | copy-start | bytes 417796
  53.1 0.6 copy-start.20
  56.3 4.2 %collective-permute-start.17 = (bf16[272,256]{1,0:T(8,128)(2,1)}, bf16[272,256]{1,0:T(8,128)(2,1)S(1)}, u32[]{:S(2)}, u32[]{:S(2)}) collective-permute-start(bf16[272,256]{1,0:T(8,128)(2,1)} %get-tuple-element.121), channel_id=1, source_target_pairs={{0,2},{1,3},{2,0},{3,1},{4,6},{5,7},{6,4},{7,5},{8,10},{9,11},{10,... | collective-permute-start | bytes 417800 | tf_op jit(solution)/shard_map/ppermute | solution.py:371
  57.9 9.4 %collective-permute-start.18 = (bf16[272,256]{1,0:T(8,128)(2,1)}, bf16[272,256]{1,0:T(8,128)(2,1)S(1)}, u32[]{:S(2)}, u32[]{:S(2)}) collective-permute-start(bf16[272,256]{1,0:T(8,128)(2,1)} %get-tuple-element.122), channel_id=1, source_target_pairs={{0,4},{1,5},{2,6},{3,7},{4,0},{5,1},{6,2},{7,3},{8,12},{9,13},{10,... | collective-permute-start | bytes 417800 | tf_op jit(solution)/shard_map/ppermute | solution.py:371
  57.9 9.4 %collective-permute-start.19 = (bf16[272,256]{1,0:T(8,128)(2,1)}, bf16[272,256]{1,0:T(8,128)(2,1)S(1)}, u32[]{:S(2)}, u32[]{:S(2)}) collective-permute-start(bf16[272,256]{1,0:T(8,128)(2,1)} %get-tuple-element.123), channel_id=1, source_target_pairs={{0,6},{1,7},{2,4},{3,5},{4,2},{5,3},{6,0},{7,1},{8,14},{9,15},{10,... | collective-permute-start | bytes 417800 | tf_op jit(solution)/shard_map/ppermute | solution.py:371
  59.1 24.7 %collective-permute-start.14 = (bf16[272,256]{1,0:T(8,128)(2,1)}, bf16[272,256]{1,0:T(8,128)(2,1)S(1)}, u32[]{:S(2)}, u32[]{:S(2)}) collective-permute-start(bf16[272,256]{1,0:T(8,128)(2,1)} %get-tuple-element.117), channel_id=1, source_target_pairs={{0,2},{1,3},{2,0},{3,1},{4,6},{5,7},{6,4},{7,5},{8,10},{9,11},{10,... | collective-permute-start | bytes 417800 | tf_op jit(solution)/shard_map/ppermute | solution.py:371
  60.5 23.3 %collective-permute-start.15 = (bf16[272,256]{1,0:T(8,128)(2,1)}, bf16[272,256]{1,0:T(8,128)(2,1)S(1)}, u32[]{:S(2)}, u32[]{:S(2)}) collective-permute-start(bf16[272,256]{1,0:T(8,128)(2,1)} %get-tuple-element.118), channel_id=1, source_target_pairs={{0,4},{1,5},{2,6},{3,7},{4,0},{5,1},{6,2},{7,3},{8,12},{9,13},{10,... | collective-permute-start | bytes 417800 | tf_op jit(solution)/shard_map/ppermute | solution.py:371
  60.5 6.7 %copy-start.14 = (bf16[272,256]{1,0:T(8,128)(2,1)}, bf16[272,256]{1,0:T(8,128)(2,1)S(1)}, u32[]{:S(2)}) copy-start(bf16[272,256]{1,0:T(8,128)(2,1)S(1)} %collective-permute-done.17.refs_1_) | copy-start | bytes 417796
  60.5 23.3 %collective-permute-start.16 = (bf16[272,256]{1,0:T(8,128)(2,1)}, bf16[272,256]{1,0:T(8,128)(2,1)S(1)}, u32[]{:S(2)}, u32[]{:S(2)}) collective-permute-start(bf16[272,256]{1,0:T(8,128)(2,1)} %get-tuple-element.119), channel_id=1, source_target_pairs={{0,6},{1,7},{2,4},{3,5},{4,2},{5,3},{6,0},{7,1},{8,14},{9,15},{10,... | collective-permute-start | bytes 417800 | tf_op jit(solution)/shard_map/ppermute | solution.py:371
  67.3 0.7 copy-start.15
  67.9 0.7 copy-start.16
  76.0 16.6 %collective-permute-start.21 = (bf16[4,256,256]{2,1,0:T(8,128)(2,1)}, bf16[4,256,256]{2,1,0:T(8,128)(2,1)S(1)}, u32[]{:S(2)}, u32[]{:S(2)}) collective-permute-start(bf16[4,256,256]{2,1,0:T(8,128)(2,1)} %get-tuple-element.126), channel_id=1, source_target_pairs={{0,1},{1,0},{2,3},{3,2},{4,5},{5,4},{6,7},{7,6},{8,9},{9,8},{10,11... | collective-permute-start | bytes 1572872 | tf_op jit(solution)/shard_map/ppermute | solution.py:367
  83.8 0.7 copy-start.11
  83.8 0.7 copy-start.12
  84.5 0.7 copy-start.13
  92.6 2.1 %collective-permute-start.20 = (bf16[4,256,256]{2,1,0:T(8,128)(2,1)}, bf16[4,256,256]{2,1,0:T(8,128)(2,1)S(1)}, u32[]{:S(2)}, u32[]{:S(2)}) collective-permute-start(bf16[4,256,256]{2,1,0:T(8,128)(2,1)} %get-tuple-element.125), channel_id=1, source_target_pairs={{0,1},{1,0},{2,3},{3,2},{4,5},{5,4},{6,7},{7,6},{8,9},{9,8},{10,11... | collective-permute-start | bytes 1572872 | tf_op jit(solution)/shard_map/ppermute | solution.py:367
  92.7 2.1 %copy-start.9 = (bf16[4,256,256]{2,1,0:T(8,128)(2,1)}, bf16[4,256,256]{2,1,0:T(8,128)(2,1)S(1)}, u32[]{:S(2)}) copy-start(bf16[4,256,256]{2,1,0:T(8,128)(2,1)S(1)} %collective-permute-done.21.refs_3_) | copy-start | bytes 1572868
  94.8 0.8 copy-start.10

commit v5 on v4

--- a/solution.py
+++ b/solution.py
@@ -32,19 +32,20 @@
     return lax.broadcasted_iota(jnp.int32, shape, dim)
 
 
-def meta_rows(normalizer, top, decay, doc):
-    width = normalizer.shape[1]
-    row = iota((META, width), 0)
-    rows = jnp.where(row == 6, jnp.concatenate([doc] * (width // LANES), axis=1), 0.0)
+def meta_rows(normalizer, top, decay, doc, width):
+    used = normalizer.shape[1]
+    row = iota((META, used), 0)
+    rows = jnp.where(row == 6, wide(doc, used), 0.0)
     lines = split3(normalizer) + split3(jnp.concatenate([top, decay], axis=1))
     for index, line in enumerate(lines):
         rows = jnp.where(row == index, line, rows)
-    return rows.astype(BF16)
+    spare = jnp.zeros((META, width - used), F32)
+    return jnp.concatenate([rows, spare], axis=1).astype(BF16)
 
 
 def read_meta(refs):
     key_width = refs[0].shape[0] - META
-    rows = [ref[key_width:, :].astype(F32) for ref in refs]
+    rows = [ref[key_width:, : 2 * LANES].astype(F32) for ref in refs]
     normals = jnp.concatenate([(x[2:3] + x[1:2]) + x[0:1] for x in rows], axis=0)
     line = jnp.concatenate([(x[5:6] + x[4:5]) + x[3:4] for x in rows], axis=0)
     docs = jnp.concatenate([x[6:7, :LANES] for x in rows], axis=0)
@@ -102,7 +103,7 @@
 
 
 def gates_kernel(heads, scalars, g_own, g_oth, ids_ref, *outs):
-    factors, tops, decays, source_rows, columns = outs
+    factors, tops, decays, source_rows, decay_rows, columns = outs
     core = scalars[1]
     length = ids_ref.shape[1]
     gate_in, decay = gate_rows(core, g_own, g_oth, heads)
@@ -114,6 +115,7 @@
     tops[...] = jnp.broadcast_to(top, tops.shape)
     decays[...] = jnp.broadcast_to(decay[:, length - 1 :], decays.shape)
     source_rows[...] = gate_in - decay
+    decay_rows[...] = decay
     docs = ids.astype(F32) + 1.0
     filler = jnp.zeros((LANES - heads - 1, length), F32)
     columns[...] = jnp.concatenate([decay, docs, filler], axis=0).T
@@ -121,11 +123,10 @@
 
 def state_kernel(heads, scalars, *refs):
     k_own, v_own, k_oth, v_oth, factors, tops, decays, ids_ref = refs[:8]
-    outs, halves = refs[8:-1], refs[-1]
+    outs, payload = refs[8:-1], refs[-1]
     step = pl.program_id(0)
     mine, core = scalars[0], scalars[1]
     tokens, key_width = k_own.shape[1:]
-    part = v_own.shape[2] // 2
     length = 2 * tokens
     head = (heads // 2) * core + jnp.bitwise_xor(mine, step)
     row = factors[pl.ds(head, 1), :]
@@ -146,15 +147,15 @@
         total = piece if total is None else total + piece
         normal = line if normal is None else normal + line
     doc = jnp.broadcast_to(ids_ref[:, length - 1 :].astype(F32) + 1.0, (1, LANES))
-    rows = meta_rows(normal, tops[pl.ds(head, 1), :], decays[pl.ds(head, 1), :], doc)
-    for half in range(2):
-        halves[half, :key_width, :] = total[:, half * part : (half + 1) * part].astype(BF16)
-        halves[half, key_width:, :] = rows
+    payload[:key_width, :] = total.astype(BF16)
+    payload[key_width:, :] = meta_rows(
+        normal, tops[pl.ds(head, 1), :], decays[pl.ds(head, 1), :], doc, payload.shape[1]
+    )
     for i, out in enumerate(outs):
 
-        @pl.when(step == i // 2)
-        def _(out=out, i=i):
-            out[...] = halves[i % 2]
+        @pl.when(step == i)
+        def _(out=out):
+            out[...] = payload[...]
 
 
 def decay_before(mine, place, decays):
@@ -181,8 +182,8 @@
     out[:key_width, :] = weighted(
         states, [coefs[i : i + 1] for i in range(group)]
     ).astype(BF16)
-    normal = jnp.sum(wide(coefs, width) * normals, axis=0, keepdims=True)
-    out[key_width:, :] = meta_rows(normal, top, whole_decay, doc)
+    normal = jnp.sum(wide(coefs, key_width) * normals, axis=0, keepdims=True)
+    out[key_width:, :] = meta_rows(normal, top, whole_decay, doc, width)
 
 
 def entering_kernel(group, reach, scalars, *refs):
@@ -219,20 +220,20 @@
             [coefs[i : i + 1] for i in others]
             + [far_coefs[d : d + 1] for d in range(reach)],
         ).astype(BF16)
-        normal = jnp.sum(wide(coefs, width) * normals, axis=0, keepdims=True)
-        normal = normal + jnp.sum(wide(far_coefs, width) * far_normals, axis=0, keepdims=True)
-        outs[r][key_width:, :] = meta_rows(normal, top, zero, doc)
-
-
-def local_kernel(first_slot, heads, scalars, *refs):
-    q_own, k_own, v_own, q_oth, k_oth, v_oth, source_rows, columns, ids_ref = refs[:9]
-    numerators, stats = refs[-2:]
+        normal = jnp.sum(wide(coefs, key_width) * normals, axis=0, keepdims=True)
+        normal = normal + jnp.sum(wide(far_coefs, key_width) * far_normals, axis=0, keepdims=True)
+        outs[r][key_width:, :] = meta_rows(normal, top, zero, doc, width)
+
+
+def local_kernel(heads, scalars, *refs):
+    q_own, k_own, v_own, q_oth, k_oth, v_oth, source_rows, decay_rows, columns, ids_ref = refs[:10]
+    numerators, stats = refs[10:]
     step = pl.program_id(0)
     mine, core = scalars[0], scalars[1]
     tokens, key_width = q_own.shape[1:]
     length = 2 * tokens
     scaling = key_width**-0.5
-    head = (heads // 2) * core + jnp.bitwise_xor(mine, first_slot + step)
+    head = (heads // 2) * core + jnp.bitwise_xor(mine, step)
     is_first = core == 0
     source = source_rows[pl.ds(head, 1), :]
     lane = iota((length, LANES), 1)
@@ -273,10 +274,9 @@
         side = core if block == 0 else 1 - core
         numerators[0, side] = numerator
         lane = iota((tokens, LANES), 1)
-        stats[0, side] = jnp.where(
-            lane == 0,
-            stabilizer,
-            jnp.where(lane == 1, denominator, jnp.where(lane == 2, decay[rows], docs[rows])),
+        pair = jnp.where(lane == 0, stabilizer, denominator).T
+        stats[0, side] = jnp.concatenate(
+            [pair[:2], decay_rows[pl.ds(head, 1), rows], source_docs[:, rows], pair[4:8]], axis=0
         )
 
 
@@ -295,25 +295,29 @@
     pieces = jnp.concatenate(split3(normal) + (jnp.zeros((META - 3, key_width), F32),), axis=0)
     pieces = pieces.astype(BF16)
     memory = payload[:key_width, :]
+    width = memory.shape[1]
     for side, (q_ref, out) in enumerate(((q_own, keep), (q_oth, send))):
         query = q_ref[0]
+        tokens = query.shape[0]
         stat = stats[0, side]
-        local, docs = stat[:, 0:1], stat[:, 3:4]
-        carried = jnp.where(docs == doc[:, :1], stat[:, 2:3] + top[:, :1], FLOOR_NEG)
+        local = stat[0:1]
+        alive = stat[3:4] == wide(doc, tokens)
+        carried = jnp.where(alive, stat[2:3] + wide(top, tokens), FLOOR_NEG)
         stabilizer = jnp.maximum(local, carried)
         shrink = jnp.exp(local - stabilizer)
         retained = jnp.exp(carried - stabilizer) * scaling
-        seen = dot(query, pieces, NT)
-        seen = (seen[:, 2:3] + seen[:, 1:2]) + seen[:, 0:1]
-        denominator = shrink * stat[:, 1:2] + retained * seen
+        seen = dot(pieces, query, NT)
+        seen = (seen[2:3] + seen[1:2]) + seen[0:1]
+        denominator = shrink * stat[1:2] + retained * seen
         inverse = 1.0 / jnp.maximum(jnp.abs(denominator), 1.0)
-        result = (shrink * inverse) * numerators[0, side]
-        result = result + (retained * inverse) * dot(query, memory)
-        out[0] = result.astype(BF16)
+        near = jnp.broadcast_to(shrink * inverse, (LANES, tokens)).T
+        far = jnp.broadcast_to(retained * inverse, (LANES, tokens)).T
+        result = wide(near, width) * numerators[0, side]
+        out[0] = (result + wide(far, width) * dot(query, memory)).astype(BF16)
 
 
 def merge_kernel(heads, scalars, *refs):
-    kept, received, out = refs[:2], refs[2:4], refs[4]
+    stacks, out = refs[:-1], refs[-1]
     half = heads // 2
     n = LAY // heads
     mine, core = scalars[0], scalars[1]
@@ -323,15 +327,12 @@
     side = jnp.where(index < half, core, 1 - core)
     head = side * half + jnp.bitwise_xor(slot, mine)
     order = ((into % heads == head) & (into // heads == given % n)).astype(BF16)
-    _, tokens, width = kept[0].shape
+    _, tokens, width = stacks[0].shape
     for g in range(tokens // n):
         span = slice(g * n, (g + 1) * n)
-        for p in range(2):
-            rows = jnp.concatenate([kept[p][:, span, :], received[p][:, span, :]], axis=0)
-            turned = dot(order, rows.reshape(LAY, width))
-            out[span, :, p * width : (p + 1) * width] = turned.reshape(n, heads, width).astype(
-                BF16
-            )
+        rows = jnp.concatenate([stack[:, span, :] for stack in stacks], axis=0)
+        turned = dot(order, rows.reshape(LAY, width))
+        out[span] = turned.reshape(n, heads, width).astype(BF16)
 
 
 def whole(shape):
@@ -354,7 +355,6 @@
     value_width = value_vectors.shape[2]
     half = heads // 2
     group = half
-    part = value_width // 2
     chips = devices // 2
     levels = chips // group
     reach = max(1, levels // 2)
@@ -375,7 +375,7 @@
         return lax.ppermute(x, AXES, [(d, d + jump) for d in range(devices - jump)])
 
     rows = key_width + META
-    state = (rows, part)
+    state = (rows, value_width)
     sizes = {key_width: (half, tokens, key_width), value_width: (half, tokens, value_width)}
 
     def relayout(*sources):
@@ -396,18 +396,15 @@
     gates_oth, k_send, v_send = lax.optimization_barrier((gates_oth, k_send, v_send))
     k_oth = swap_cores(k_send)
     v_oth = swap_cores(v_send)
-    queries, _ = lax.optimization_barrier((queries, v_send))
-    q_keep, q_send = relayout(queries)
-    k_oth, q_send = lax.optimization_barrier((k_oth, q_send))
-    q_oth = swap_cores(q_send)
     gate_shapes = [
         (heads, 2 * tokens),
         (heads, LANES),
         (heads, LANES),
         (heads, 2 * tokens),
+        (heads, 2 * tokens),
         (2 * tokens, LANES),
     ]
-    factors, tops, decays, source_rows, columns = pl.pallas_call(
+    factors, tops, decays, source_rows, decay_rows, columns = pl.pallas_call(
         functools.partial(gates_kernel, heads),
         in_specs=[SMEM] + [whole(gates.shape)] * 2 + [whole(ids.shape)],
         out_specs=[whole(s) for s in gate_shapes],
@@ -428,101 +425,81 @@
             grid=(group,),
             in_specs=[by_slot(x) for x in (k_keep, v_keep, k_oth, v_oth)]
             + [whole(x.shape) for x in (factors, tops, decays, ids)],
-            out_specs=[whole(state)] * (2 * group),
-            scratch_shapes=[pltpu.VMEM((2,) + state, BF16)],
+            out_specs=[whole(state)] * group,
+            scratch_shapes=[pltpu.VMEM(state, BF16)],
         ),
-        out_shape=[shape_of(*state)] * (2 * group),
+        out_shape=[shape_of(*state)] * group,
         compiler_params=params(),
         name="states",
     )(scalars, k_keep, v_keep, k_oth, v_oth, factors, tops, decays, ids)
-    made = [made[p::2] for p in range(2)]
-    gathered = [
-        [made[p][0]] + [in_group(made[p][r], r) for r in range(1, group)] for p in range(2)
-    ]
-    local_shapes = [(half, 2, tokens, value_width), (half, 2, tokens, LANES)]
-
-    def own_terms(first_slot, count, q_own, into):
-        by_head = (q_own, k_keep, v_keep, q_oth, k_oth, v_oth)
-        small = (source_rows, columns, ids)
-        return pl.pallas_call(
-            functools.partial(local_kernel, first_slot, heads),
+    gathered = [made[0]] + [in_group(made[r], r) for r in range(1, group)]
+    total = pl.pallas_call(
+        functools.partial(total_kernel, group),
+        in_specs=[SMEM] + [whole(state)] * group,
+        out_specs=whole(state),
+        out_shape=shape_of(*state),
+        compiler_params=params(),
+        name="group_total",
+    )(scalars, *gathered)
+    totals = [to_later(total, d) for d in range(1, reach + 1)]
+
+    queries, gathered[0] = lax.optimization_barrier((queries, gathered[0]))
+    q_keep, q_send = relayout(queries)
+    q_oth = swap_cores(q_send)
+    by_head = (q_keep, k_keep, v_keep, q_oth, k_oth, v_oth)
+    small = (source_rows, decay_rows, columns, ids)
+    local_shapes = [(half, 2, tokens, value_width), (half, 2, 8, tokens)]
+    numerators, stats = pl.pallas_call(
+        functools.partial(local_kernel, heads),
+        grid_spec=pltpu.PrefetchScalarGridSpec(
+            num_scalar_prefetch=1,
+            grid=(group,),
+            in_specs=[by_slot(x) for x in by_head] + [whole(x.shape) for x in small],
+            out_specs=[
+                pl.BlockSpec((1,) + s[1:], lambda i, _: (i, 0, 0, 0)) for s in local_shapes
+            ],
+        ),
+        out_shape=[shape_of(*s, dtype=F32) for s in local_shapes],
+        compiler_params=params(),
+        name="own_terms",
+    )(scalars, *by_head, *small)
+    gathered[0], numerators = lax.optimization_barrier((gathered[0], numerators))
+
+    leaving = pl.pallas_call(
+        functools.partial(entering_kernel, group, reach),
+        in_specs=[SMEM] + [whole(state)] * (group + reach),
+        out_specs=[whole(state)] * group,
+        out_shape=[shape_of(*state)] * group,
+        compiler_params=params(),
+        name="entering",
+    )(scalars, *gathered, *totals)
+    entering = [leaving[0]] + [in_group(leaving[r], r) for r in range(1, group)]
+
+    kept, received = [], []
+    for first, count in ((0, 1), (1, group - 1)):
+        spec = pl.BlockSpec((1, tokens, value_width), lambda i, s: (i, 0, 0))
+        keep, send = pl.pallas_call(
+            output_kernel,
             grid_spec=pltpu.PrefetchScalarGridSpec(
                 num_scalar_prefetch=1,
                 grid=(count,),
-                in_specs=[by_slot(x, first_slot) for x in by_head]
-                + [whole(x.shape) for x in small]
-                + [pl.BlockSpec(memory_space=pl.ANY)] * len(into),
-                out_specs=[
-                    pl.BlockSpec((1,) + s[1:], lambda i, _: (first_slot + i, 0, 0, 0))
+                in_specs=[by_slot(q_keep, first), by_slot(q_oth, first)]
+                + [
+                    pl.BlockSpec((1,) + s[1:], lambda i, _, first=first: (first + i, 0, 0, 0))
                     for s in local_shapes
-                ],
-            ),
-            out_shape=[shape_of(*s, dtype=F32) for s in local_shapes],
-            input_output_aliases={10 + i: i for i in range(len(into))},
-            compiler_params=params(),
-            name="own_terms",
-        )(scalars, *by_head, *small, *into)
-
-    def group_total(states):
-        return pl.pallas_call(
-            functools.partial(total_kernel, group),
-            in_specs=[SMEM] + [whole(state)] * group,
-            out_specs=whole(state),
-            out_shape=shape_of(*state),
-            compiler_params=params(),
-            name="group_total",
-        )(scalars, *states)
-
-    def entering_states(states, total):
-        totals = [to_later(total, d) for d in range(1, reach + 1)]
-        return pl.pallas_call(
-            functools.partial(entering_kernel, group, reach),
-            in_specs=[SMEM] + [whole(state)] * (group + reach),
-            out_specs=[whole(state)] * group,
-            out_shape=[shape_of(*state)] * group,
-            compiler_params=params(),
-            name="entering",
-        )(scalars, *states, *totals)
-
-    def outputs(p, numerators, stats, entering):
-        spec = pl.BlockSpec((1, tokens, part), lambda i, s: (i, 0, 0))
-        return pl.pallas_call(
-            output_kernel,
-            grid_spec=pltpu.PrefetchScalarGridSpec(
-                num_scalar_prefetch=1,
-                grid=(group,),
-                in_specs=[by_slot(q_keep), by_slot(q_oth)]
-                + [
-                    pl.BlockSpec((1, 2, tokens, part), lambda i, s: (i, 0, 0, p)),
-                    pl.BlockSpec((1, 2, tokens, LANES), lambda i, s: (i, 0, 0, 0)),
                 ]
-                + [whole(state)] * group,
+                + [whole(state)] * count,
                 out_specs=[spec] * 2,
                 scratch_shapes=[pltpu.VMEM(state, BF16)],
             ),
-            out_shape=[shape_of(half, tokens, part)] * 2,
+            out_shape=[shape_of(count, tokens, value_width)] * 2,
             compiler_params=params(),
             name="outputs",
-        )(scalars, q_keep, q_oth, numerators, stats, *entering)
-
-    early = half // 2
-    first_total = group_total(gathered[0])
-    q_later, _ = lax.optimization_barrier((q_keep, first_total))
-    terms = own_terms(0, early, q_later, ())
-    gathered[1], terms = lax.optimization_barrier((gathered[1], terms))
-    second_total = group_total(gathered[1])
-    q_last, _ = lax.optimization_barrier((q_keep, second_total))
-    terms = own_terms(early, half - early, q_last, terms)
-    leaving = [entering_states(gathered[0], first_total)]
-    gathered[1], leaving[0] = lax.optimization_barrier((gathered[1], leaving[0]))
-    leaving.append(entering_states(gathered[1], second_total))
-    (numerators, stats), _ = lax.optimization_barrier((terms, leaving[1][0]))
-    kept, received = [], []
-    for p in range(2):
-        entering = [leaving[p][0]] + [in_group(leaving[p][r], r) for r in range(1, group)]
-        keep, send = outputs(p, numerators, stats, entering)
+        )(scalars, q_keep, q_oth, numerators, stats, *entering[first : first + count])
         kept.append(keep)
-        received.append(swap_cores(send))
+        swapped = swap_cores(send)
+        numerators, swapped = lax.optimization_barrier((numerators, swapped))
+        received.append(swapped)
     return pl.pallas_call(
         functools.partial(merge_kernel, heads),
         in_specs=[SMEM] + [whole(x.shape) for x in kept + received],

time: 101 us -> 90.4 us (0.90); the launches traced: 99.1 us -> 89.8 us
  waiting for transfers between devices: 9.84 us -> 24.9 us
  Pallas kernels: 53.3 us -> 41 us
  starting transfers between devices: 26 us -> 16.9 us
  local copies, waits for them, and re-layouts: 8.43 us -> 5.74 us
    pallas_call x8 -> x5, Pallas kernels: 34.9 us -> 22.6 us  [the longest x2 8.88 us: local(): pl.pallas_call(output_kernel, grid_spec=pltpu.PrefetchScalarGridSpec(num_...]
    ppermute x12 -> x6, waiting for transfers between devices: 2.89 us -> 12.4 us  [in_group(): return lax.ppermute(x, AXES, pairs)]
    ppermute x12 -> x6, starting transfers between devices: 11.7 us -> 6.36 us  [in_group(): return lax.ppermute(x, AXES, pairs)]
    ppermute x4 -> x2, waiting for transfers between devices: 4.4 us -> 8.43 us  [to_later(): return lax.ppermute(x, AXES, [(d, d + jump) for d in range(devices - jump)])]
    unnamed x48 -> x32, local copies, waits for them, and re-layouts: 7.78 us -> 5.07 us
    ppermute x4 -> x2, starting transfers between devices: 5.14 us -> 2.57 us  [to_later(): return lax.ppermute(x, AXES, [(d, d + jump) for d in range(devices - jump)])]
    ppermute x6, waiting for transfers between devices: 2.55 us -> 4.03 us  [swap_cores(): return lax.ppermute(x, AXES, [(d, d ^ 1) for d in range(devices)])]
    ppermute x6, starting transfers between devices: 9.15 us -> 7.93 us  [swap_cores(): return lax.ppermute(x, AXES, [(d, d ^ 1) for d in range(devices)])]
  transfers between devices with their start and end apart: 22 -> 14, of which waited for: 6 -> 8; matrix products, arithmetic and copies ran while one was open for 1% -> 1% of each run, Pallas kernels for 48% -> 25%
where the time goes in v5:
time: 90.4 us; the launch traced here: 89.8 us
  Pallas kernels  41 us (45%)
  waiting for transfers between devices  24.9 us (28%)
  starting transfers between devices  16.9 us (19%)
  local copies, waits for them, and re-layouts  5.74 us (6%)
  other arithmetic  1.27 us (1%)
    ppermute x6, waiting for transfers between devices, in_group(): return lax.ppermute(x, AXES, pairs)  12.4 us
    pallas_call x2, Pallas kernels, local(): pl.pallas_call(output_kernel, grid_spec=pltpu.PrefetchScalarGridSpec(num_...  8.88 us
    ppermute x2, waiting for transfers between devices, to_later(): return lax.ppermute(x, AXES, [(d, d + jump) for d in range(devices - jump)])  8.43 us
    pallas_call x1, Pallas kernels, local(): pl.pallas_call(functools.partial(local_kernel, heads), grid_spec=pltpu.Pr...  8.34 us
    ppermute x6, starting transfers between devices, swap_cores(): return lax.ppermute(x, AXES, [(d, d ^ 1) for d in range(devices)])  7.93 us
    pallas_call x2, Pallas kernels, relayout(): pl.pallas_call(functools.partial(relayout_kernel, half, len(sources)), in...  7.08 us
    ppermute x6, starting transfers between devices, in_group(): return lax.ppermute(x, AXES, pairs)  6.36 us
    pallas_call x1, Pallas kernels, local(): pl.pallas_call(functools.partial(state_kernel, heads), grid_spec=pltpu.Pr...  5.78 us
  transfers between devices with their start and end apart: 14, of which 8 were waited for; matrix products, arithmetic and copies ran while one was open for 1% of the time, Pallas kernels for 25%

profile of v5, /device:TPU:25, one launch (start us, length us, event | category | flops | bytes accessed | tf_op | source)
XLA Modules:
  0.0 89.8 jit_solution(1221828166356010901)
XLA Ops:
  0.0 0.0 copy-start.15
  0.0 0.7 pad_maximum_fusion.g_own
  0.7 0.0 copy-start.13
  0.7 0.7 collective-permute-start
  1.4 0.6 pad_add_fusion.scalars
  1.9 4.4 %relayout.2 = (bf16[4,256,256]{2,1,0:T(8,128)(2,1)}, bf16[4,256,512]{2,1,0:T(8,128)(2,1)}, bf16[4,256,256]{2,1,0:T(8,128)(2,1)}, bf16[4,256,512]{2,1,0:T(8,128)(2,1)}) custom-call(s32[2]{0:T(128)} %pad_add_fusion.scalars, bf16[256,8,256]{2,1,0:T(8,128)(2,1)} %refs_0_, bf16[256,8,512]{2,1,0:T(8,128)(2,1)} %refs_1_.1), custom_call_target="tpu_custom_call" | custom-call | tf_op jit(solution)/shard_map/relayout/pallas_call | solution.py:383
  6.4 0.0 collective-permute-done.g_oth
  6.4 0.0 copy-start.14
  6.4 0.1 collective-permute-start.2
  6.4 0.5 collective-permute-start.1
  6.9 0.0 copy-done.15
  6.9 0.7 dynamic_slice.3
  7.6 0.0 copy-done.13
  7.6 0.0 copy-done.14
  7.6 1.9 %gates.1 = (f32[8,512]{1,0:T(8,128)}, f32[8,128]{1,0:T(8,128)}, f32[8,128]{1,0:T(8,128)}, f32[8,512]{1,0:T(8,128)}, f32[8,512]{1,0:T(8,128)}, /*index=5*/f32[512,128]{1,0:T(8,128)}) custom-call(s32[2]{0:T(128)} %pad_add_fusion.scalars, bf16[16,256]{1,0:T(8,128)(2,1)} %copy-done.13, bf16[16,256]{1,0:T(8,128)(2,1)} %copy-done.14, s32[1,512]{1,0:T(1,128)} %bitcast.5), custom_call_target="tpu_custom_call" | custom-call | tf_op jit(solution)/shard_map/gates/pallas_call | solution.py:407
  9.5 0.5 collective-permute-done.1.refs_2_.refs_4_
  10.1 0.0 copy-start.2
  10.1 0.0 collective-permute-done.2.refs_3_.refs_5_
  10.1 0.8 copy-done.2
  10.8 0.4 copy-done.1
  11.3 5.8 %states.1 = (bf16[272,512]{1,0:T(8,128)(2,1)}, bf16[272,512]{1,0:T(8,128)(2,1)}, bf16[272,512]{1,0:T(8,128)(2,1)}, bf16[272,512]{1,0:T(8,128)(2,1)}) custom-call(s32[2]{0:T(128)} %pad_add_fusion.scalars, bf16[4,256,256]{2,1,0:T(8,128)(2,1)} %get-tuple-element.44.refs_0_.refs_1_, bf16[4,256,512]{2,1,0:T(8,128)(2,1)} %get-tuple-element.45.refs_1_.refs_2_, ...), custom_call_target="tpu_custom_call" | custom-call | tf_op jit(solution)/shard_map/states/pallas_call | solution.py:421
  17.0 1.2 %collective-permute-start.4 = (bf16[272,512]{1,0:T(8,128)(2,1)}, bf16[272,512]{1,0:T(8,128)(2,1)S(1)}, u32[]{:S(2)}, u32[]{:S(2)}) collective-permute-start(bf16[272,512]{1,0:T(8,128)(2,1)} %get-tuple-element.67), channel_id=1, source_target_pairs={{0,2},{1,3},{2,0},{3,1},{4,6},{5,7},{6,4},{7,5},{8,10},{9,11},{10,... | collective-permute-start | bytes 835592 | tf_op jit(solution)/shard_map/ppermute | solution.py:371
  18.3 1.3 %collective-permute-start.5 = (bf16[272,512]{1,0:T(8,128)(2,1)}, bf16[272,512]{1,0:T(8,128)(2,1)S(1)}, u32[]{:S(2)}, u32[]{:S(2)}) collective-permute-start(bf16[272,512]{1,0:T(8,128)(2,1)} %get-tuple-element.68), channel_id=1, source_target_pairs={{0,4},{1,5},{2,6},{3,7},{4,0},{5,1},{6,2},{7,3},{8,12},{9,13},{10,... | collective-permute-start | bytes 835592 | tf_op jit(solution)/shard_map/ppermute | solution.py:371
  19.5 0.2 collective-permute-start.6
  19.7 2.7 %relayout.3 = (bf16[4,256,256]{2,1,0:T(8,128)(2,1)}, bf16[4,256,256]{2,1,0:T(8,128)(2,1)}) custom-call(s32[2]{0:T(128)} %pad_add_fusion.scalars, bf16[256,8,256]{2,1,0:T(8,128)(2,1)} %refs_0_.1), custom_call_target="tpu_custom_call" | custom-call | tf_op jit(solution)/shard_map/relayout/pallas_call | solution.py:383
  22.4 1.0 %collective-permute-start.3 = (bf16[4,256,256]{2,1,0:T(8,128)(2,1)}, bf16[4,256,256]{2,1,0:T(8,128)(2,1)S(1)}, u32[]{:S(2)}, u32[]{:S(2)}) collective-permute-start(bf16[4,256,256]{2,1,0:T(8,128)(2,1)} %get-tuple-element.58), channel_id=1, source_target_pairs={{0,1},{1,0},{2,3},{3,2},{4,5},{5,4},{6,7},{7,6},{8,9},{9,8},{10,11... | collective-permute-start | bytes 1572872 | tf_op jit(solution)/shard_map/ppermute | solution.py:367
  23.3 2.0 %collective-permute-done.4.refs_1_ = bf16[272,512]{1,0:T(8,128)(2,1)S(1)} collective-permute-done((bf16[272,512]{1,0:T(8,128)(2,1)}, bf16[272,512]{1,0:T(8,128)(2,1)S(1)}, u32[]{:S(2)}, u32[]{:S(2)}) %collective-permute-start.4) | collective-permute-done | bytes 278560 | tf_op jit(solution)/shard_map/ppermute | solution.py:371
  25.3 0.9 %collective-permute-done.5.refs_2_ = bf16[272,512]{1,0:T(8,128)(2,1)S(1)} collective-permute-done((bf16[272,512]{1,0:T(8,128)(2,1)}, bf16[272,512]{1,0:T(8,128)(2,1)S(1)}, u32[]{:S(2)}, u32[]{:S(2)}) %collective-permute-start.5) | collective-permute-done | bytes 278560 | tf_op jit(solution)/shard_map/ppermute | solution.py:371
  26.3 6.0 %collective-permute-done.6.refs_3_ = bf16[272,512]{1,0:T(8,128)(2,1)S(1)} collective-permute-done((bf16[272,512]{1,0:T(8,128)(2,1)}, bf16[272,512]{1,0:T(8,128)(2,1)S(1)}, u32[]{:S(2)}, u32[]{:S(2)}) %collective-permute-start.6) | collective-permute-done | bytes 278560 | tf_op jit(solution)/shard_map/ppermute | solution.py:371
  32.3 0.0 copy-done.3
  32.3 0.0 copy-done.4
  32.3 0.7 copy-done.5
  33.0 2.2 %group_total.1 = bf16[272,512]{1,0:T(8,128)(2,1)} custom-call(s32[2]{0:T(128)} %pad_add_fusion.scalars, bf16[272,512]{1,0:T(8,128)(2,1)} %get-tuple-element.66.refs_0_, bf16[272,512]{1,0:T(8,128)(2,1)} %copy-done.3, bf16[272,512]{1,0:T(8,128)(2,1)} %copy-done.4, bf16[272,512]{1,0:T(8,128)(2,1)} %copy-done.5), custom_call_target="tpu_custom_call" | custom-call | tf_op jit(solution)/shard_map/group_total/pallas_call | solution.py:436
  35.2 1.3 %collective-permute-start.7 = (bf16[272,512]{1,0:T(8,128)(2,1)}, bf16[272,512]{1,0:T(8,128)(2,1)S(1)}, u32[]{:S(2)}, u32[]{:S(2)}) collective-permute-start(bf16[272,512]{1,0:T(8,128)(2,1)} %group_total.1), channel_id=1, source_target_pairs={{0,8},{1,9},{2,10},{3,11},{4,12},{5,13},{6,14},{7,15},{8,16},{9,17... | collective-permute-start | bytes 835592 | tf_op jit(solution)/shard_map/ppermute | solution.py:375
  36.5 1.3 %collective-permute-start.8 = (bf16[272,512]{1,0:T(8,128)(2,1)}, bf16[272,512]{1,0:T(8,128)(2,1)S(1)}, u32[]{:S(2)}, u32[]{:S(2)}) collective-permute-start(bf16[272,512]{1,0:T(8,128)(2,1)} %group_total.1), channel_id=1, source_target_pairs={{0,16},{1,17},{2,18},{3,19},{4,20},{5,21},{6,22},{7,23},{8,24},{9,... | collective-permute-start | bytes 835592 | tf_op jit(solution)/shard_map/ppermute | solution.py:375
  37.8 0.0 collective-permute-done.3.refs_3_.q_oth
  37.8 0.0 copy-start
  37.8 0.8 copy-done
  38.6 8.3 %own_terms.1 = (f32[4,2,256,512]{3,2,1,0:T(8,128)}, f32[4,2,8,256]{3,2,1,0:T(8,128)}) custom-call(s32[2]{0:T(128)} %pad_add_fusion.scalars, bf16[4,256,256]{2,1,0:T(8,128)(2,1)} %get-tuple-element.57.refs_0_.q_own, bf16[4,256,256]{2,1,0:T(8,128)(2,1)} %get-tuple-element.44.refs_0_.refs_1_, bf16[4,256,512]{2,1,0:T(8,128)(2,1)} %get-tuple-element.45.refs_1_.refs_2_, ...), custom_call_target="tpu_custom_call" | custom-call | tf_op jit(solution)/shard_map/own_terms/pallas_call | solution.py:452
  47.0 0.0 collective-permute-done.7.refs_4_
  47.0 0.0 copy-start.10
  47.0 8.4 %collective-permute-done.8.refs_5_ = bf16[272,512]{1,0:T(8,128)(2,1)S(1)} collective-permute-done((bf16[272,512]{1,0:T(8,128)(2,1)}, bf16[272,512]{1,0:T(8,128)(2,1)S(1)}, u32[]{:S(2)}, u32[]{:S(2)}) %collective-permute-start.8) | collective-permute-done | bytes 278560 | tf_op jit(solution)/shard_map/ppermute | solution.py:375
  55.4 0.0 copy-done.10
  55.4 0.7 copy-done.11
  56.2 3.2 %entering.1 = (bf16[272,512]{1,0:T(8,128)(2,1)}, bf16[272,512]{1,0:T(8,128)(2,1)}, bf16[272,512]{1,0:T(8,128)(2,1)}, bf16[272,512]{1,0:T(8,128)(2,1)}) custom-call(s32[2]{0:T(128)} %pad_add_fusion.scalars, bf16[272,512]{1,0:T(8,128)(2,1)} %get-tuple-element.66.refs_0_, bf16[272,512]{1,0:T(8,128)(2,1)} %copy-done.3, bf16[272,512]{1,0:T(8,128)(2,1)} %copy-done.4, ...), custom_call_target="tpu_custom_call" | custom-call | tf_op jit(solution)/shard_map/entering/pallas_call | solution.py:468
  59.4 2.1 %collective-permute-start.10 = (bf16[272,512]{1,0:T(8,128)(2,1)}, bf16[272,512]{1,0:T(8,128)(2,1)S(1)}, u32[]{:S(2)}, u32[]{:S(2)}) collective-permute-start(bf16[272,512]{1,0:T(8,128)(2,1)} %get-tuple-element.74), channel_id=1, source_target_pairs={{0,2},{1,3},{2,0},{3,1},{4,6},{5,7},{6,4},{7,5},{8,10},{9,11},{10,... | collective-permute-start | bytes 835592 | tf_op jit(solution)/shard_map/ppermute | solution.py:371
  61.5 0.4 collective-permute-start.11
  61.9 1.2 %collective-permute-start.12 = (bf16[272,512]{1,0:T(8,128)(2,1)}, bf16[272,512]{1,0:T(8,128)(2,1)S(1)}, u32[]{:S(2)}, u32[]{:S(2)}) collective-permute-start(bf16[272,512]{1,0:T(8,128)(2,1)} %get-tuple-element.76), channel_id=1, source_target_pairs={{0,6},{1,7},{2,4},{3,5},{4,2},{5,3},{6,0},{7,1},{8,14},{9,15},{10,... | collective-permute-start | bytes 835592 | tf_op jit(solution)/shard_map/ppermute | solution.py:371
  63.1 3.2 %outputs.2 = (bf16[1,256,512]{2,1,0:T(8,128)(2,1)}, bf16[1,256,512]{2,1,0:T(8,128)(2,1)}) custom-call(s32[2]{0:T(128)} %pad_add_fusion.scalars, bf16[4,256,256]{2,1,0:T(8,128)(2,1)} %get-tuple-element.57.refs_0_.q_own, bf16[4,256,256]{2,1,0:T(8,128)(2,1)} %copy-done, f32[4,2,256,512]{3,2,1,0:T(8,128)} %get-tuple-element.73.numerators, ...), custom_call_target="tpu_custom_call" | custom-call | tf_op jit(solution)/shard_map/outputs/pallas_call | solution.py:481
  66.3 2.7 %collective-permute-start.9 = (bf16[1,256,512]{2,1,0:T(8,128)(2,1)}, bf16[1,256,512]{2,1,0:T(8,128)(2,1)S(1)}, u32[]{:S(2)}, u32[]{:S(2)}) collective-permute-start(bf16[1,256,512]{2,1,0:T(8,128)(2,1)} %get-tuple-element.72), channel_id=1, source_target_pairs={{0,1},{1,0},{2,3},{3,2},{4,5},{5,4},{6,7},{7,6},{8,9},{9,8},{10,11... | collective-permute-start | bytes 786440 | tf_op jit(solution)/shard_map/ppermute | solution.py:367
  69.0 1.4 %collective-permute-done.9.refs_2_ = bf16[1,256,512]{2,1,0:T(8,128)(2,1)S(1)} collective-permute-done((bf16[1,256,512]{2,1,0:T(8,128)(2,1)}, bf16[1,256,512]{2,1,0:T(8,128)(2,1)S(1)}, u32[]{:S(2)}, u32[]{:S(2)}) %collective-permute-start.9) | collective-permute-done | bytes 262176 | tf_op jit(solution)/shard_map/ppermute | solution.py:367
  70.4 0.0 collective-permute-done.10.refs_0_
  70.4 0.0 collective-permute-done.11.refs_1_
  70.4 0.0 copy-start.8
  70.4 3.4 %collective-permute-done.12.refs_2_ = bf16[272,512]{1,0:T(8,128)(2,1)S(1)} collective-permute-done((bf16[272,512]{1,0:T(8,128)(2,1)}, bf16[272,512]{1,0:T(8,128)(2,1)S(1)}, u32[]{:S(2)}, u32[]{:S(2)}) %collective-permute-start.12) | collective-permute-done | bytes 278560 | tf_op jit(solution)/shard_map/ppermute | solution.py:371
  73.9 0.0 copy-done.7
  73.9 0.0 copy-done.8
  73.9 0.7 copy-done.9
  74.6 5.6 %outputs.3 = (bf16[3,256,512]{2,1,0:T(8,128)(2,1)}, bf16[3,256,512]{2,1,0:T(8,128)(2,1)}) custom-call(s32[2]{0:T(128)} %pad_add_fusion.scalars, bf16[4,256,256]{2,1,0:T(8,128)(2,1)} %get-tuple-element.57.refs_0_.q_own, bf16[4,256,256]{2,1,0:T(8,128)(2,1)} %copy-done, f32[4,2,256,512]{3,2,1,0:T(8,128)} %get-tuple-element.73.numerators, ...), custom_call_target="tpu_custom_call" | custom-call | tf_op jit(solution)/shard_map/outputs/pallas_call | solution.py:481
  80.2 3.0 %collective-permute-start.13 = (bf16[3,256,512]{2,1,0:T(8,128)(2,1)}, bf16[3,256,512]{2,1,0:T(8,128)(2,1)S(1)}, u32[]{:S(2)}, u32[]{:S(2)}) collective-permute-start(bf16[3,256,512]{2,1,0:T(8,128)(2,1)} %get-tuple-element.79), channel_id=1, source_target_pairs={{0,1},{1,0},{2,3},{3,2},{4,5},{5,4},{6,7},{7,6},{8,9},{9,8},{10,11... | collective-permute-start | bytes 2359304 | tf_op jit(solution)/shard_map/ppermute | solution.py:367
  83.2 2.1 %collective-permute-done.13.refs_3_ = bf16[3,256,512]{2,1,0:T(8,128)(2,1)S(1)} collective-permute-done((bf16[3,256,512]{2,1,0:T(8,128)(2,1)}, bf16[3,256,512]{2,1,0:T(8,128)(2,1)S(1)}, u32[]{:S(2)}, u32[]{:S(2)}) %collective-permute-start.13) | collective-permute-done | bytes 786464 | tf_op jit(solution)/shard_map/ppermute | solution.py:367
  85.4 0.0 copy-done.12
  85.4 0.9 copy-done.6
  86.2 3.6 %merge.1 = bf16[256,8,512]{2,1,0:T(8,128)(2,1)} custom-call(s32[2]{0:T(128)} %pad_add_fusion.scalars, bf16[1,256,512]{2,1,0:T(8,128)(2,1)} %get-tuple-element.71.refs_0_, bf16[3,256,512]{2,1,0:T(8,128)(2,1)} %get-tuple-element.77.refs_1_, bf16[1,256,512]{2,1,0:T(8,128)(2,1)} %copy-done.12, bf16[3,256,512]{2,1,0:T(8,128)(2,1)} %copy-done.6), custom_call_target="tpu_custom_call" | custom-call | tf_op jit(solution)/shard_map/merge/pallas_call | solution.py:503
  (9 shorter events, 0.0 us)
Async XLA Ops:
  0.0 6.9 %copy-start.15 = (s32[1024]{0:T(1024)S(1)}, s32[1024]{0:T(1024)}, u32[]{:S(2)}) copy-start(s32[1024]{0:T(1024)} %param.11) | copy-start | bytes 12292
  0.7 6.9 %copy-start.13 = (bf16[16,256]{1,0:T(8,128)(2,1)}, bf16[16,256]{1,0:T(8,128)(2,1)S(1)}, u32[]{:S(2)}) copy-start(bf16[16,256]{1,0:T(8,128)(2,1)S(1)} %pad_maximum_fusion.g_own) | copy-start | bytes 24580
  0.7 5.6 %collective-permute-start = (bf16[16,256]{1,0:T(8,128)(2,1)S(1)}, bf16[16,256]{1,0:T(8,128)(2,1)S(1)}, u32[]{:S(2)}, u32[]{:S(2)}) collective-permute-start(bf16[16,256]{1,0:T(8,128)(2,1)S(1)} %pad_maximum_fusion.g_own), channel_id=1, source_target_pairs={{0,1},{1,0},{2,3},{3,2},{4,5},{5,4},{6,7},{7,6},{8,9},{9,8},{10,11... | collective-permute-start | bytes 24584 | tf_op jit(solution)/shard_map/ppermute | solution.py:367
  6.4 1.2 %copy-start.14 = (bf16[16,256]{1,0:T(8,128)(2,1)}, bf16[16,256]{1,0:T(8,128)(2,1)S(1)}, u32[]{:S(2)}) copy-start(bf16[16,256]{1,0:T(8,128)(2,1)S(1)} %collective-permute-done.g_oth) | copy-start | bytes 24580
  6.4 3.7 %collective-permute-start.2 = (bf16[4,256,512]{2,1,0:T(8,128)(2,1)}, bf16[4,256,512]{2,1,0:T(8,128)(2,1)S(1)}, u32[]{:S(2)}, u32[]{:S(2)}) collective-permute-start(bf16[4,256,512]{2,1,0:T(8,128)(2,1)} %get-tuple-element.50), channel_id=1, source_target_pairs={{0,1},{1,0},{2,3},{3,2},{4,5},{5,4},{6,7},{7,6},{8,9},{9,8},{10,11... | collective-permute-start | bytes 3145736 | tf_op jit(solution)/shard_map/ppermute | solution.py:367
  6.4 3.6 %collective-permute-start.1 = (bf16[4,256,256]{2,1,0:T(8,128)(2,1)}, bf16[4,256,256]{2,1,0:T(8,128)(2,1)S(1)}, u32[]{:S(2)}, u32[]{:S(2)}) collective-permute-start(bf16[4,256,256]{2,1,0:T(8,128)(2,1)} %get-tuple-element.49), channel_id=1, source_target_pairs={{0,1},{1,0},{2,3},{3,2},{4,5},{5,4},{6,7},{7,6},{8,9},{9,8},{10,11... | collective-permute-start | bytes 1572872 | tf_op jit(solution)/shard_map/ppermute | solution.py:367
  10.1 0.8 copy-start.2
  10.1 1.2 %copy-start.1 = (bf16[4,256,512]{2,1,0:T(8,128)(2,1)}, bf16[4,256,512]{2,1,0:T(8,128)(2,1)S(1)}, u32[]{:S(2)}) copy-start(bf16[4,256,512]{2,1,0:T(8,128)(2,1)S(1)} %collective-permute-done.2.refs_3_.refs_5_) | copy-start | bytes 3145732
  17.0 8.3 %collective-permute-start.4 = (bf16[272,512]{1,0:T(8,128)(2,1)}, bf16[272,512]{1,0:T(8,128)(2,1)S(1)}, u32[]{:S(2)}, u32[]{:S(2)}) collective-permute-start(bf16[272,512]{1,0:T(8,128)(2,1)} %get-tuple-element.67), channel_id=1, source_target_pairs={{0,2},{1,3},{2,0},{3,1},{4,6},{5,7},{6,4},{7,5},{8,10},{9,11},{10,... | collective-permute-start | bytes 835592 | tf_op jit(solution)/shard_map/ppermute | solution.py:371
  18.3 8.0 %collective-permute-start.5 = (bf16[272,512]{1,0:T(8,128)(2,1)}, bf16[272,512]{1,0:T(8,128)(2,1)S(1)}, u32[]{:S(2)}, u32[]{:S(2)}) collective-permute-start(bf16[272,512]{1,0:T(8,128)(2,1)} %get-tuple-element.68), channel_id=1, source_target_pairs={{0,4},{1,5},{2,6},{3,7},{4,0},{5,1},{6,2},{7,3},{8,12},{9,13},{10,... | collective-permute-start | bytes 835592 | tf_op jit(solution)/shard_map/ppermute | solution.py:371
  19.5 12.8 %collective-permute-start.6 = (bf16[272,512]{1,0:T(8,128)(2,1)}, bf16[272,512]{1,0:T(8,128)(2,1)S(1)}, u32[]{:S(2)}, u32[]{:S(2)}) collective-permute-start(bf16[272,512]{1,0:T(8,128)(2,1)} %get-tuple-element.69), channel_id=1, source_target_pairs={{0,6},{1,7},{2,4},{3,5},{4,2},{5,3},{6,0},{7,1},{8,14},{9,15},{10,... | collective-permute-start | bytes 835592 | tf_op jit(solution)/shard_map/ppermute | solution.py:371
  22.4 15.5 %collective-permute-start.3 = (bf16[4,256,256]{2,1,0:T(8,128)(2,1)}, bf16[4,256,256]{2,1,0:T(8,128)(2,1)S(1)}, u32[]{:S(2)}, u32[]{:S(2)}) collective-permute-start(bf16[4,256,256]{2,1,0:T(8,128)(2,1)} %get-tuple-element.58), channel_id=1, source_target_pairs={{0,1},{1,0},{2,3},{3,2},{4,5},{5,4},{6,7},{7,6},{8,9},{9,8},{10,11... | collective-permute-start | bytes 1572872 | tf_op jit(solution)/shard_map/ppermute | solution.py:367
  25.3 7.0 %copy-start.3 = (bf16[272,512]{1,0:T(8,128)(2,1)}, bf16[272,512]{1,0:T(8,128)(2,1)S(1)}, u32[]{:S(2)}) copy-start(bf16[272,512]{1,0:T(8,128)(2,1)S(1)} %collective-permute-done.4.refs_1_) | copy-start | bytes 835588
  26.3 6.0 %copy-start.4 = (bf16[272,512]{1,0:T(8,128)(2,1)}, bf16[272,512]{1,0:T(8,128)(2,1)S(1)}, u32[]{:S(2)}) copy-start(bf16[272,512]{1,0:T(8,128)(2,1)S(1)} %collective-permute-done.5.refs_2_) | copy-start | bytes 835588
  32.3 0.7 copy-start.5
  35.2 11.7 %collective-permute-start.7 = (bf16[272,512]{1,0:T(8,128)(2,1)}, bf16[272,512]{1,0:T(8,128)(2,1)S(1)}, u32[]{:S(2)}, u32[]{:S(2)}) collective-permute-start(bf16[272,512]{1,0:T(8,128)(2,1)} %group_total.1), channel_id=1, source_target_pairs={{0,8},{1,9},{2,10},{3,11},{4,12},{5,13},{6,14},{7,15},{8,16},{9,17... | collective-permute-start | bytes 835592 | tf_op jit(solution)/shard_map/ppermute | solution.py:375
  36.5 18.9 %collective-permute-start.8 = (bf16[272,512]{1,0:T(8,128)(2,1)}, bf16[272,512]{1,0:T(8,128)(2,1)S(1)}, u32[]{:S(2)}, u32[]{:S(2)}) collective-permute-start(bf16[272,512]{1,0:T(8,128)(2,1)} %group_total.1), channel_id=1, source_target_pairs={{0,16},{1,17},{2,18},{3,19},{4,20},{5,21},{6,22},{7,23},{8,24},{9,... | collective-permute-start | bytes 835592 | tf_op jit(solution)/shard_map/ppermute | solution.py:375
  37.8 0.8 copy-start
  47.0 8.4 %copy-start.10 = (bf16[272,512]{1,0:T(8,128)(2,1)}, bf16[272,512]{1,0:T(8,128)(2,1)S(1)}, u32[]{:S(2)}) copy-start(bf16[272,512]{1,0:T(8,128)(2,1)S(1)} %collective-permute-done.7.refs_4_) | copy-start | bytes 835588
  55.4 0.7 copy-start.11
  59.4 11.0 %collective-permute-start.10 = (bf16[272,512]{1,0:T(8,128)(2,1)}, bf16[272,512]{1,0:T(8,128)(2,1)S(1)}, u32[]{:S(2)}, u32[]{:S(2)}) collective-permute-start(bf16[272,512]{1,0:T(8,128)(2,1)} %get-tuple-element.74), channel_id=1, source_target_pairs={{0,2},{1,3},{2,0},{3,1},{4,6},{5,7},{6,4},{7,5},{8,10},{9,11},{10,... | collective-permute-start | bytes 835592 | tf_op jit(solution)/shard_map/ppermute | solution.py:371
  61.5 9.0 %collective-permute-start.11 = (bf16[272,512]{1,0:T(8,128)(2,1)}, bf16[272,512]{1,0:T(8,128)(2,1)S(1)}, u32[]{:S(2)}, u32[]{:S(2)}) collective-permute-start(bf16[272,512]{1,0:T(8,128)(2,1)} %get-tuple-element.75), channel_id=1, source_target_pairs={{0,4},{1,5},{2,6},{3,7},{4,0},{5,1},{6,2},{7,3},{8,12},{9,13},{10,... | collective-permute-start | bytes 835592 | tf_op jit(solution)/shard_map/ppermute | solution.py:371
  61.9 12.0 %collective-permute-start.12 = (bf16[272,512]{1,0:T(8,128)(2,1)}, bf16[272,512]{1,0:T(8,128)(2,1)S(1)}, u32[]{:S(2)}, u32[]{:S(2)}) collective-permute-start(bf16[272,512]{1,0:T(8,128)(2,1)} %get-tuple-element.76), channel_id=1, source_target_pairs={{0,6},{1,7},{2,4},{3,5},{4,2},{5,3},{6,0},{7,1},{8,14},{9,15},{10,... | collective-permute-start | bytes 835592 | tf_op jit(solution)/shard_map/ppermute | solution.py:371
  66.3 4.1 %collective-permute-start.9 = (bf16[1,256,512]{2,1,0:T(8,128)(2,1)}, bf16[1,256,512]{2,1,0:T(8,128)(2,1)S(1)}, u32[]{:S(2)}, u32[]{:S(2)}) collective-permute-start(bf16[1,256,512]{2,1,0:T(8,128)(2,1)} %get-tuple-element.72), channel_id=1, source_target_pairs={{0,1},{1,0},{2,3},{3,2},{4,5},{5,4},{6,7},{7,6},{8,9},{9,8},{10,11... | collective-permute-start | bytes 786440 | tf_op jit(solution)/shard_map/ppermute | solution.py:367
  70.4 14.9 %copy-start.12 = (bf16[1,256,512]{2,1,0:T(8,128)(2,1)}, bf16[1,256,512]{2,1,0:T(8,128)(2,1)S(1)}, u32[]{:S(2)}) copy-start(bf16[1,256,512]{2,1,0:T(8,128)(2,1)S(1)} %collective-permute-done.9.refs_2_) | copy-start | bytes 786436
  70.4 3.5 %copy-start.7 = (bf16[272,512]{1,0:T(8,128)(2,1)}, bf16[272,512]{1,0:T(8,128)(2,1)S(1)}, u32[]{:S(2)}) copy-start(bf16[272,512]{1,0:T(8,128)(2,1)S(1)} %collective-permute-done.10.refs_0_) | copy-start | bytes 835588
  70.4 3.5 %copy-start.8 = (bf16[272,512]{1,0:T(8,128)(2,1)}, bf16[272,512]{1,0:T(8,128)(2,1)S(1)}, u32[]{:S(2)}) copy-start(bf16[272,512]{1,0:T(8,128)(2,1)S(1)} %collective-permute-done.11.refs_1_) | copy-start | bytes 835588
  73.9 0.7 copy-start.9
  80.2 5.1 %collective-permute-start.13 = (bf16[3,256,512]{2,1,0:T(8,128)(2,1)}, bf16[3,256,512]{2,1,0:T(8,128)(2,1)S(1)}, u32[]{:S(2)}, u32[]{:S(2)}) collective-permute-start(bf16[3,256,512]{2,1,0:T(8,128)(2,1)} %get-tuple-element.79), channel_id=1, source_target_pairs={{0,1},{1,0},{2,3},{3,2},{4,5},{5,4},{6,7},{7,6},{8,9},{9,8},{10,11... | collective-permute-start | bytes 2359304 | tf_op jit(solution)/shard_map/ppermute | solution.py:367
  85.4 0.9 copy-start.6

commit v6 on v5

--- a/solution.py
+++ b/solution.py
@@ -121,31 +121,31 @@
     columns[...] = jnp.concatenate([decay, docs, filler], axis=0).T
 
 
-def state_kernel(heads, scalars, *refs):
+def state_kernel(slot_of, heads, scalars, *refs):
     k_own, v_own, k_oth, v_oth, factors, tops, decays, ids_ref = refs[:8]
     outs, payload = refs[8:-1], refs[-1]
     step = pl.program_id(0)
     mine, core = scalars[0], scalars[1]
     tokens, key_width = k_own.shape[1:]
     length = 2 * tokens
-    head = (heads // 2) * core + jnp.bitwise_xor(mine, step)
+    head = (heads // 2) * core + jnp.bitwise_xor(mine, slot_of(step))
     row = factors[pl.ds(head, 1), :]
     first, last = row[:, :tokens], row[:, tokens:]
-    total, normal = None, None
+    high, low, values, normal = [], [], [], None
     for k_ref, v_ref, f in (
         (k_own, v_own, jnp.where(core == 0, first, last)),
         (k_oth, v_oth, jnp.where(core == 0, last, first)),
     ):
-        keys, values = k_ref[0], v_ref[0]
+        keys = k_ref[0]
         scaled = keys.astype(F32).T * f
-        high = scaled.astype(BF16)
-        low = (scaled - high.astype(F32)).astype(BF16)
-        piece = dot(low, values) + dot(high, values)
+        high.append(scaled.astype(BF16))
+        low.append((scaled - high[-1].astype(F32)).astype(BF16))
+        values.append(v_ref[0])
         pieces = jnp.concatenate(split3(f) + (jnp.zeros((META - 3, tokens), F32),), axis=0)
         sums = dot(pieces.astype(BF16), keys)
         line = (sums[2:3] + sums[1:2]) + sums[0:1]
-        total = piece if total is None else total + piece
         normal = line if normal is None else normal + line
+    total = dot(jnp.concatenate(low + high, axis=1), jnp.concatenate(values * 2, axis=0))
     doc = jnp.broadcast_to(ids_ref[:, length - 1 :].astype(F32) + 1.0, (1, LANES))
     payload[:key_width, :] = total.astype(BF16)
     payload[key_width:, :] = meta_rows(
@@ -260,17 +260,19 @@
         stabilizer = functools.reduce(
             jnp.maximum, [jnp.max(x, axis=1, keepdims=True) for x in exponents]
         )
-        numerator, denominator = None, None
+        factors, sources, denominator = [], [], None
         for s in range(block + 1):
             weights = dot(queries[block], keys[s], NT) * scaling
             weights = weights * jnp.exp(exponents[s] - stabilizer)
             high = weights.astype(BF16)
-            part = dot(high, values[s])
+            factors.append(high)
+            sources.append(values[s])
             if s < block:
-                part = part + dot((weights - high.astype(F32)).astype(BF16), values[s])
-            numerator = part if s == 0 else numerator + part
+                factors.append((weights - high.astype(F32)).astype(BF16))
+                sources.append(values[s])
             part = jnp.sum(weights, axis=1, keepdims=True)
             denominator = part if s == 0 else denominator + part
+        numerator = dot(jnp.concatenate(factors, axis=1), jnp.concatenate(sources, axis=0))
         side = core if block == 0 else 1 - core
         numerators[0, side] = numerator
         lane = iota((tokens, LANES), 1)
@@ -280,10 +282,13 @@
         )
 
 
-def output_kernel(scalars, q_own, q_oth, numerators, stats, *refs):
-    entering, (keep, send, payload) = refs[:-3], refs[-3:]
+def output_kernel(sides, scalars, *refs):
+    count = len(sides)
+    query_refs, numerators, stats = refs[:count], refs[count], refs[count + 1]
+    outs, payload = refs[-1 - count : -1], refs[-1]
+    entering = refs[count + 2 : -1 - count]
     step = pl.program_id(0)
-    key_width = q_own.shape[2]
+    key_width = query_refs[0].shape[2]
     scaling = key_width**-0.5
     for i, ref in enumerate(entering):
 
@@ -296,7 +301,7 @@
     pieces = pieces.astype(BF16)
     memory = payload[:key_width, :]
     width = memory.shape[1]
-    for side, (q_ref, out) in enumerate(((q_own, keep), (q_oth, send))):
+    for side, (q_ref, out) in enumerate(zip(query_refs, outs, strict=True)):
         query = q_ref[0]
         tokens = query.shape[0]
         stat = stats[0, side]
@@ -413,25 +418,31 @@
         name="gates",
     )(scalars, gates, gates_oth, ids)
 
-    def by_slot(x, first_slot=0):
+    def by_slot(x, slot_of=lambda i: i):
         return pl.BlockSpec(
-            (1,) + x.shape[1:], lambda i, s: (jnp.bitwise_xor(s[0], first_slot + i), 0, 0)
+            (1,) + x.shape[1:], lambda i, s: (jnp.bitwise_xor(s[0], slot_of(i)), 0, 0)
         )
 
-    made = pl.pallas_call(
-        functools.partial(state_kernel, heads),
-        grid_spec=pltpu.PrefetchScalarGridSpec(
-            num_scalar_prefetch=1,
-            grid=(group,),
-            in_specs=[by_slot(x) for x in (k_keep, v_keep, k_oth, v_oth)]
-            + [whole(x.shape) for x in (factors, tops, decays, ids)],
-            out_specs=[whole(state)] * group,
-            scratch_shapes=[pltpu.VMEM(state, BF16)],
-        ),
-        out_shape=[shape_of(*state)] * group,
-        compiler_params=params(),
-        name="states",
-    )(scalars, k_keep, v_keep, k_oth, v_oth, factors, tops, decays, ids)
+    made = [None] * group
+    for first in (1, 0):
+        slot_of = lambda i, first=first: group - 2 + first - 2 * i
+        slots = [slot_of(i) for i in range(half // 2)]
+        outs = pl.pallas_call(
+            functools.partial(state_kernel, slot_of, heads),
+            grid_spec=pltpu.PrefetchScalarGridSpec(
+                num_scalar_prefetch=1,
+                grid=(len(slots),),
+                in_specs=[by_slot(x, slot_of) for x in (k_keep, v_keep, k_oth, v_oth)]
+                + [whole(x.shape) for x in (factors, tops, decays, ids)],
+                out_specs=[whole(state)] * len(slots),
+                scratch_shapes=[pltpu.VMEM(state, BF16)],
+            ),
+            out_shape=[shape_of(*state)] * len(slots),
+            compiler_params=params(),
+            name="states",
+        )(scalars, k_keep, v_keep, k_oth, v_oth, factors, tops, decays, ids)
+        for slot, out in zip(slots, outs, strict=True):
+            made[slot] = out
     gathered = [made[0]] + [in_group(made[r], r) for r in range(1, group)]
     total = pl.pallas_call(
         functools.partial(total_kernel, group),
@@ -475,31 +486,37 @@
     )(scalars, *gathered, *totals)
     entering = [leaving[0]] + [in_group(leaving[r], r) for r in range(1, group)]
 
-    kept, received = [], []
-    for first, count in ((0, 1), (1, group - 1)):
+    def outputs(first, count, first_side, sides):
         spec = pl.BlockSpec((1, tokens, value_width), lambda i, s: (i, 0, 0))
-        keep, send = pl.pallas_call(
-            output_kernel,
+        relaid = (q_keep, q_oth)[first_side : first_side + sides]
+        return pl.pallas_call(
+            functools.partial(output_kernel, range(sides)),
             grid_spec=pltpu.PrefetchScalarGridSpec(
                 num_scalar_prefetch=1,
                 grid=(count,),
-                in_specs=[by_slot(q_keep, first), by_slot(q_oth, first)]
+                in_specs=[by_slot(x, lambda i: first + i) for x in relaid]
                 + [
-                    pl.BlockSpec((1,) + s[1:], lambda i, _, first=first: (first + i, 0, 0, 0))
+                    pl.BlockSpec(
+                        (1, sides) + s[2:], lambda i, _: (first + i, first_side // sides, 0, 0)
+                    )
                     for s in local_shapes
                 ]
                 + [whole(state)] * count,
-                out_specs=[spec] * 2,
+                out_specs=[spec] * sides,
                 scratch_shapes=[pltpu.VMEM(state, BF16)],
             ),
-            out_shape=[shape_of(count, tokens, value_width)] * 2,
+            out_shape=[shape_of(count, tokens, value_width)] * sides,
             compiler_params=params(),
             name="outputs",
-        )(scalars, q_keep, q_oth, numerators, stats, *entering[first : first + count])
-        kept.append(keep)
-        swapped = swap_cores(send)
-        numerators, swapped = lax.optimization_barrier((numerators, swapped))
-        received.append(swapped)
+        )(scalars, *relaid, numerators, stats, *entering[first : first + count])
+
+    keep, send = outputs(0, 1, 0, 2)
+    swapped = swap_cores(send)
+    numerators, swapped = lax.optimization_barrier((numerators, swapped))
+    [send] = outputs(1, group - 1, 1, 1)
+    numerators, _ = lax.optimization_barrier((numerators, send))
+    [keep_far] = outputs(1, group - 1, 0, 1)
+    kept, received = [keep, keep_far], [swapped, swap_cores(send)]
     return pl.pallas_call(
         functools.partial(merge_kernel, heads),
         in_specs=[SMEM] + [whole(x.shape) for x in kept + received],

time: 90.4 us -> 94.2 us (1.042)
  Pallas kernels: 41 us -> 46.3 us
  waiting for transfers between devices: 24.9 us -> 23.3 us
    pallas_call x3 -> x5, Pallas kernels: 14.7 us -> 20.4 us  [the longest x3 12.9 us: outputs(): pl.pallas_call(functools.partial(output_kernel, range(sides)), grid_spec=...]
    ppermute x6, waiting for transfers between devices: 4.03 us -> 1.93 us  [swap_cores(): return lax.ppermute(x, AXES, [(d, d ^ 1) for d in range(devices)])]
    ppermute x6, starting transfers between devices: 6.36 us -> 5.33 us  [in_group(): return lax.ppermute(x, AXES, pairs)]
    ppermute x2, waiting for transfers between devices: 8.43 us -> 9.44 us  [to_later(): return lax.ppermute(x, AXES, [(d, d + jump) for d in range(devices - jump)])]
    unnamed x32 -> x34, local copies, waits for them, and re-layouts: 5.07 us -> 5.79 us
  transfers between devices with their start and end apart: 14 -> 14, of which waited for: 8 -> 5; matrix products, arithmetic and copies ran while one was open for 1% -> 1% of each run, Pallas kernels for 25% -> 33%
where the time goes in v6:
time: 94.2 us; the launch traced here: 93.5 us
  Pallas kernels  46.3 us (49%)
  waiting for transfers between devices  23.3 us (25%)
  starting transfers between devices  16.1 us (17%)
  local copies, waits for them, and re-layouts  6.44 us (7%)
  other arithmetic  1.31 us (1%)
    pallas_call x3, Pallas kernels, outputs(): pl.pallas_call(functools.partial(output_kernel, range(sides)), grid_spec=...  12.9 us
    ppermute x6, waiting for transfers between devices, in_group(): return lax.ppermute(x, AXES, pairs)  11.9 us
    ppermute x2, waiting for transfers between devices, to_later(): return lax.ppermute(x, AXES, [(d, d + jump) for d in range(devices - jump)])  9.44 us
    ppermute x6, starting transfers between devices, swap_cores(): return lax.ppermute(x, AXES, [(d, d ^ 1) for d in range(devices)])  8.16 us
    pallas_call x1, Pallas kernels, local(): pl.pallas_call(functools.partial(local_kernel, heads), grid_spec=pltpu.Pr...  7.98 us
    pallas_call x2, Pallas kernels, local(): pl.pallas_call(functools.partial(state_kernel, slot_of, heads), grid_spec...  7.5 us
    pallas_call x2, Pallas kernels, relayout(): pl.pallas_call(functools.partial(relayout_kernel, half, len(sources)), in...  7.07 us
    unnamed x34, local copies, waits for them, and re-layouts  5.79 us
  transfers between devices with their start and end apart: 14, of which 5 were waited for; matrix products, arithmetic and copies ran while one was open for 1% of the time, Pallas kernels for 33%

profile of v6, /device:TPU:25, one launch (start us, length us, event | category | flops | bytes accessed | tf_op | source)
XLA Modules:
  0.0 93.5 jit_solution(16675406310763468985)
XLA Ops:
  0.0 0.7 pad_maximum_fusion.g_own
  0.7 0.7 collective-permute-start
  1.4 0.6 pad_add_fusion.scalars
  2.0 4.4 %relayout.2 = (bf16[4,256,256]{2,1,0:T(8,128)(2,1)}, bf16[4,256,512]{2,1,0:T(8,128)(2,1)}, bf16[4,256,256]{2,1,0:T(8,128)(2,1)}, bf16[4,256,512]{2,1,0:T(8,128)(2,1)}) custom-call(s32[2]{0:T(128)} %pad_add_fusion.scalars, bf16[256,8,256]{2,1,0:T(8,128)(2,1)} %refs_0_, bf16[256,8,512]{2,1,0:T(8,128)(2,1)} %refs_1_.1), custom_call_target="tpu_custom_call" | custom-call | tf_op jit(solution)/shard_map/relayout/pallas_call | solution.py:388
  6.4 0.0 collective-permute-done.g_oth
  6.4 0.1 collective-permute-start.2
  6.5 0.5 collective-permute-start.1
  7.0 0.0 copy-done.15
  7.0 0.6 dynamic_slice.3
  7.6 0.0 copy-done.13
  7.6 0.0 copy-done.14
  7.6 1.9 %gates.1 = (f32[8,512]{1,0:T(8,128)}, f32[8,128]{1,0:T(8,128)}, f32[8,128]{1,0:T(8,128)}, f32[8,512]{1,0:T(8,128)}, f32[8,512]{1,0:T(8,128)}, /*index=5*/f32[512,128]{1,0:T(8,128)}) custom-call(s32[2]{0:T(128)} %pad_add_fusion.scalars, bf16[16,256]{1,0:T(8,128)(2,1)} %copy-done.13, bf16[16,256]{1,0:T(8,128)(2,1)} %copy-done.14, s32[1,512]{1,0:T(1,128)} %bitcast.5), custom_call_target="tpu_custom_call" | custom-call | tf_op jit(solution)/shard_map/gates/pallas_call | solution.py:412
  9.5 0.5 collective-permute-done.1.refs_2_.refs_4_
  10.1 0.0 collective-permute-done.2.refs_3_.refs_5_
  10.1 0.8 copy-done.2
  10.9 0.4 copy-done
  11.3 3.7 %states.3 = (bf16[272,512]{1,0:T(8,128)(2,1)}, bf16[272,512]{1,0:T(8,128)(2,1)}) custom-call(s32[2]{0:T(128)} %pad_add_fusion.scalars, bf16[4,256,256]{2,1,0:T(8,128)(2,1)} %get-tuple-element.42.refs_0_.refs_1_, bf16[4,256,512]{2,1,0:T(8,128)(2,1)} %get-tuple-element.43.refs_1_.refs_2_, bf16[4,256,256]{2,1,0:T(8,128)(2,1)} %copy-done.2, ...), custom_call_target="tpu_custom_call" | custom-call | tf_op jit(solution)/shard_map/states/pallas_call | solution.py:430
  15.0 1.3 %collective-permute-start.4 = (bf16[272,512]{1,0:T(8,128)(2,1)}, bf16[272,512]{1,0:T(8,128)(2,1)S(1)}, u32[]{:S(2)}, u32[]{:S(2)}) collective-permute-start(bf16[272,512]{1,0:T(8,128)(2,1)} %get-tuple-element.65), channel_id=1, source_target_pairs={{0,2},{1,3},{2,0},{3,1},{4,6},{5,7},{6,4},{7,5},{8,10},{9,11},{10,... | collective-permute-start | bytes 835592 | tf_op jit(solution)/shard_map/ppermute | solution.py:376
  16.3 3.7 %states.2 = (bf16[272,512]{1,0:T(8,128)(2,1)}, bf16[272,512]{1,0:T(8,128)(2,1)}) custom-call(s32[2]{0:T(128)} %pad_add_fusion.scalars, bf16[4,256,256]{2,1,0:T(8,128)(2,1)} %get-tuple-element.42.refs_0_.refs_1_, bf16[4,256,512]{2,1,0:T(8,128)(2,1)} %get-tuple-element.43.refs_1_.refs_2_, bf16[4,256,256]{2,1,0:T(8,128)(2,1)} %copy-done.2, ...), custom_call_target="tpu_custom_call" | custom-call | tf_op jit(solution)/shard_map/states/pallas_call | solution.py:430
  20.0 1.2 %collective-permute-start.5 = (bf16[272,512]{1,0:T(8,128)(2,1)}, bf16[272,512]{1,0:T(8,128)(2,1)S(1)}, u32[]{:S(2)}, u32[]{:S(2)}) collective-permute-start(bf16[272,512]{1,0:T(8,128)(2,1)} %get-tuple-element.66), channel_id=1, source_target_pairs={{0,4},{1,5},{2,6},{3,7},{4,0},{5,1},{6,2},{7,3},{8,12},{9,13},{10,... | collective-permute-start | bytes 835592 | tf_op jit(solution)/shard_map/ppermute | solution.py:376
  21.3 0.0 copy-done.16
  21.3 0.2 collective-permute-start.6
  21.5 2.7 %relayout.3 = (bf16[4,256,256]{2,1,0:T(8,128)(2,1)}, bf16[4,256,256]{2,1,0:T(8,128)(2,1)}) custom-call(s32[2]{0:T(128)} %pad_add_fusion.scalars, bf16[256,8,256]{2,1,0:T(8,128)(2,1)} %refs_0_.1), custom_call_target="tpu_custom_call" | custom-call | tf_op jit(solution)/shard_map/relayout/pallas_call | solution.py:388
  24.1 1.0 %collective-permute-start.3 = (bf16[4,256,256]{2,1,0:T(8,128)(2,1)}, bf16[4,256,256]{2,1,0:T(8,128)(2,1)S(1)}, u32[]{:S(2)}, u32[]{:S(2)}) collective-permute-start(bf16[4,256,256]{2,1,0:T(8,128)(2,1)} %get-tuple-element.56), channel_id=1, source_target_pairs={{0,1},{1,0},{2,3},{3,2},{4,5},{5,4},{6,7},{7,6},{8,9},{9,8},{10,11... | collective-permute-start | bytes 1572872 | tf_op jit(solution)/shard_map/ppermute | solution.py:372
  25.1 0.0 collective-permute-done.4.refs_1_
  25.1 8.9 %collective-permute-done.5.refs_2_ = bf16[272,512]{1,0:T(8,128)(2,1)S(1)} collective-permute-done((bf16[272,512]{1,0:T(8,128)(2,1)}, bf16[272,512]{1,0:T(8,128)(2,1)S(1)}, u32[]{:S(2)}, u32[]{:S(2)}) %collective-permute-start.5) | collective-permute-done | bytes 278560 | tf_op jit(solution)/shard_map/ppermute | solution.py:376
  34.0 0.0 collective-permute-done.6.refs_3_
  34.0 0.0 copy-done.6
  34.0 0.7 copy-done.7
  34.8 0.7 copy-done.8
  35.5 2.2 %group_total.1 = bf16[272,512]{1,0:T(8,128)(2,1)} custom-call(s32[2]{0:T(128)} %pad_add_fusion.scalars, bf16[272,512]{1,0:T(8,128)(2,1)} %get-tuple-element.64.refs_0_, bf16[272,512]{1,0:T(8,128)(2,1)} %copy-done.6, bf16[272,512]{1,0:T(8,128)(2,1)} %copy-done.7, bf16[272,512]{1,0:T(8,128)(2,1)} %copy-done.8), custom_call_target="tpu_custom_call" | custom-call | tf_op jit(solution)/shard_map/group_total/pallas_call | solution.py:447
  37.7 1.3 %collective-permute-start.7 = (bf16[272,512]{1,0:T(8,128)(2,1)}, bf16[272,512]{1,0:T(8,128)(2,1)S(1)}, u32[]{:S(2)}, u32[]{:S(2)}) collective-permute-start(bf16[272,512]{1,0:T(8,128)(2,1)} %group_total.1), channel_id=1, source_target_pairs={{0,8},{1,9},{2,10},{3,11},{4,12},{5,13},{6,14},{7,15},{8,16},{9,17... | collective-permute-start | bytes 835592 | tf_op jit(solution)/shard_map/ppermute | solution.py:380
  39.0 1.3 %collective-permute-start.8 = (bf16[272,512]{1,0:T(8,128)(2,1)}, bf16[272,512]{1,0:T(8,128)(2,1)S(1)}, u32[]{:S(2)}, u32[]{:S(2)}) collective-permute-start(bf16[272,512]{1,0:T(8,128)(2,1)} %group_total.1), channel_id=1, source_target_pairs={{0,16},{1,17},{2,18},{3,19},{4,20},{5,21},{6,22},{7,23},{8,24},{9,... | collective-permute-start | bytes 835592 | tf_op jit(solution)/shard_map/ppermute | solution.py:380
  40.3 0.0 collective-permute-done.3.refs_3_.refs_1_.refs_0_
  40.3 0.0 copy-start.1
  40.3 0.8 copy-done.1
  41.1 8.0 %own_terms.1 = (f32[4,2,256,512]{3,2,1,0:T(8,128)}, f32[4,2,8,256]{3,2,1,0:T(8,128)}) custom-call(s32[2]{0:T(128)} %pad_add_fusion.scalars, bf16[4,256,256]{2,1,0:T(8,128)(2,1)} %get-tuple-element.55.refs_0_, bf16[4,256,256]{2,1,0:T(8,128)(2,1)} %get-tuple-element.42.refs_0_.refs_1_, bf16[4,256,512]{2,1,0:T(8,128)(2,1)} %get-tuple-element.43.refs_1_.refs_2_, ...), custom_call_target="tpu_custom_call" | custom-call | tf_op jit(solution)/shard_map/own_terms/pallas_call | solution.py:463
  49.1 0.0 collective-permute-done.7.refs_4_
  49.1 0.0 copy-start.10
  49.1 9.4 %collective-permute-done.8.refs_5_ = bf16[272,512]{1,0:T(8,128)(2,1)S(1)} collective-permute-done((bf16[272,512]{1,0:T(8,128)(2,1)}, bf16[272,512]{1,0:T(8,128)(2,1)S(1)}, u32[]{:S(2)}, u32[]{:S(2)}) %collective-permute-start.8) | collective-permute-done | bytes 278560 | tf_op jit(solution)/shard_map/ppermute | solution.py:380
  58.5 0.0 copy-done.10
  58.5 0.7 copy-done.11
  59.3 3.2 %entering.1 = (bf16[272,512]{1,0:T(8,128)(2,1)}, bf16[272,512]{1,0:T(8,128)(2,1)}, bf16[272,512]{1,0:T(8,128)(2,1)}, bf16[272,512]{1,0:T(8,128)(2,1)}) custom-call(s32[2]{0:T(128)} %pad_add_fusion.scalars, bf16[272,512]{1,0:T(8,128)(2,1)} %get-tuple-element.64.refs_0_, bf16[272,512]{1,0:T(8,128)(2,1)} %copy-done.6, bf16[272,512]{1,0:T(8,128)(2,1)} %copy-done.7, ...), custom_call_target="tpu_custom_call" | custom-call | tf_op jit(solution)/shard_map/entering/pallas_call | solution.py:479
  62.5 0.2 collective-permute-start.10
  62.7 1.2 %collective-permute-start.11 = (bf16[272,512]{1,0:T(8,128)(2,1)}, bf16[272,512]{1,0:T(8,128)(2,1)S(1)}, u32[]{:S(2)}, u32[]{:S(2)}) collective-permute-start(bf16[272,512]{1,0:T(8,128)(2,1)} %get-tuple-element.73), channel_id=1, source_target_pairs={{0,4},{1,5},{2,6},{3,7},{4,0},{5,1},{6,2},{7,3},{8,12},{9,13},{10,... | collective-permute-start | bytes 835592 | tf_op jit(solution)/shard_map/ppermute | solution.py:376
  64.0 1.2 %collective-permute-start.12 = (bf16[272,512]{1,0:T(8,128)(2,1)}, bf16[272,512]{1,0:T(8,128)(2,1)S(1)}, u32[]{:S(2)}, u32[]{:S(2)}) collective-permute-start(bf16[272,512]{1,0:T(8,128)(2,1)} %get-tuple-element.74), channel_id=1, source_target_pairs={{0,6},{1,7},{2,4},{3,5},{4,2},{5,3},{6,0},{7,1},{8,14},{9,15},{10,... | collective-permute-start | bytes 835592 | tf_op jit(solution)/shard_map/ppermute | solution.py:376
  65.1 3.2 %outputs.3 = (bf16[1,256,512]{2,1,0:T(8,128)(2,1)}, bf16[1,256,512]{2,1,0:T(8,128)(2,1)}) custom-call(s32[2]{0:T(128)} %pad_add_fusion.scalars, bf16[4,256,256]{2,1,0:T(8,128)(2,1)} %get-tuple-element.55.refs_0_, bf16[4,256,256]{2,1,0:T(8,128)(2,1)} %copy-done.1, f32[4,2,256,512]{3,2,1,0:T(8,128)} %get-tuple-element.75.refs_2_.refs_1_, ...), custom_call_target="tpu_custom_call" | custom-call | tf_op jit(solution)/shard_map/outputs/pallas_call | solution.py:492
  68.4 3.0 %collective-permute-start.9 = (bf16[1,256,512]{2,1,0:T(8,128)(2,1)}, bf16[1,256,512]{2,1,0:T(8,128)(2,1)S(1)}, u32[]{:S(2)}, u32[]{:S(2)}) collective-permute-start(bf16[1,256,512]{2,1,0:T(8,128)(2,1)} %get-tuple-element.70), channel_id=1, source_target_pairs={{0,1},{1,0},{2,3},{3,2},{4,5},{5,4},{6,7},{7,6},{8,9},{9,8},{10,11... | collective-permute-start | bytes 786440 | tf_op jit(solution)/shard_map/ppermute | solution.py:372
  71.4 1.4 %collective-permute-done.9.refs_2_ = bf16[1,256,512]{2,1,0:T(8,128)(2,1)S(1)} collective-permute-done((bf16[1,256,512]{2,1,0:T(8,128)(2,1)}, bf16[1,256,512]{2,1,0:T(8,128)(2,1)S(1)}, u32[]{:S(2)}, u32[]{:S(2)}) %collective-permute-start.9) | collective-permute-done | bytes 262176 | tf_op jit(solution)/shard_map/ppermute | solution.py:372
  72.7 0.0 collective-permute-done.10.refs_3_
  72.7 0.0 collective-permute-done.11.refs_4_
  72.7 0.0 copy-start.4
  72.8 3.0 %collective-permute-done.12.refs_5_ = bf16[272,512]{1,0:T(8,128)(2,1)S(1)} collective-permute-done((bf16[272,512]{1,0:T(8,128)(2,1)}, bf16[272,512]{1,0:T(8,128)(2,1)S(1)}, u32[]{:S(2)}, u32[]{:S(2)}) %collective-permute-start.12) | collective-permute-done | bytes 278560 | tf_op jit(solution)/shard_map/ppermute | solution.py:376
  75.7 0.0 copy-done.3
  75.8 0.0 copy-done.4
  75.8 0.7 copy-done.5
  76.5 4.8 %outputs.4 = bf16[3,256,512]{2,1,0:T(8,128)(2,1)} custom-call(s32[2]{0:T(128)} %pad_add_fusion.scalars, bf16[4,256,256]{2,1,0:T(8,128)(2,1)} %copy-done.1, f32[4,2,256,512]{3,2,1,0:T(8,128)} %get-tuple-element.75.refs_2_.refs_1_, f32[4,2,8,256]{3,2,1,0:T(8,128)} %get-tuple-element.63.refs_3_.refs_2_, bf16[272,512]{1,0:T(8,128)(2,1)} %copy-done.3, ...), custom_call_target="tpu_custom_call" | custom-call | tf_op jit(solution)/shard_map/outputs/pallas_call | solution.py:492
  81.3 3.0 %collective-permute-start.13 = (bf16[3,256,512]{2,1,0:T(8,128)(2,1)}, bf16[3,256,512]{2,1,0:T(8,128)(2,1)S(1)}, u32[]{:S(2)}, u32[]{:S(2)}) collective-permute-start(bf16[3,256,512]{2,1,0:T(8,128)(2,1)} %outputs.4), channel_id=1, source_target_pairs={{0,1},{1,0},{2,3},{3,2},{4,5},{5,4},{6,7},{7,6},{8,9},{9,8},{10,11... | collective-permute-start | bytes 2359304 | tf_op jit(solution)/shard_map/ppermute | solution.py:372
  84.2 4.8 %outputs.5.refs_1_ = bf16[3,256,512]{2,1,0:T(8,128)(2,1)} custom-call(s32[2]{0:T(128)} %pad_add_fusion.scalars, bf16[4,256,256]{2,1,0:T(8,128)(2,1)} %get-tuple-element.55.refs_0_, f32[4,2,256,512]{3,2,1,0:T(8,128)} %get-tuple-element.75.refs_2_.refs_1_, f32[4,2,8,256]{3,2,1,0:T(8,128)} %get-tuple-element.63.refs_3_.refs_2_, bf16[272,512]{1,0:T(8,128)(2,1)} %copy-done.3, ...), custom_call_target="tpu_custom_call" | custom-call | tf_op jit(solution)/shard_map/outputs/pallas_call | solution.py:492
  89.1 0.0 copy-done.12
  89.1 0.0 collective-permute-done.13.refs_3_
  89.1 0.0 copy-start.9
  89.1 0.9 copy-done.9
  90.0 3.6 %merge.1 = bf16[256,8,512]{2,1,0:T(8,128)(2,1)} custom-call(s32[2]{0:T(128)} %pad_add_fusion.scalars, bf16[1,256,512]{2,1,0:T(8,128)(2,1)} %get-tuple-element.69.refs_0_, bf16[3,256,512]{2,1,0:T(8,128)(2,1)} %outputs.5.refs_1_, bf16[1,256,512]{2,1,0:T(8,128)(2,1)} %copy-done.12, bf16[3,256,512]{2,1,0:T(8,128)(2,1)} %copy-done.9), custom_call_target="tpu_custom_call" | custom-call | tf_op jit(solution)/shard_map/merge/pallas_call | solution.py:520
  (13 shorter events, 0.0 us)
Async XLA Ops:
  0.0 7.0 %copy-start.15 = (s32[1024]{0:T(1024)S(1)}, s32[1024]{0:T(1024)}, u32[]{:S(2)}) copy-start(s32[1024]{0:T(1024)} %param.11) | copy-start | bytes 12292
  0.7 6.9 %copy-start.13 = (bf16[16,256]{1,0:T(8,128)(2,1)}, bf16[16,256]{1,0:T(8,128)(2,1)S(1)}, u32[]{:S(2)}) copy-start(bf16[16,256]{1,0:T(8,128)(2,1)S(1)} %pad_maximum_fusion.g_own) | copy-start | bytes 24580
  0.7 5.7 %collective-permute-start = (bf16[16,256]{1,0:T(8,128)(2,1)S(1)}, bf16[16,256]{1,0:T(8,128)(2,1)S(1)}, u32[]{:S(2)}, u32[]{:S(2)}) collective-permute-start(bf16[16,256]{1,0:T(8,128)(2,1)S(1)} %pad_maximum_fusion.g_own), channel_id=1, source_target_pairs={{0,1},{1,0},{2,3},{3,2},{4,5},{5,4},{6,7},{7,6},{8,9},{9,8},{10,11... | collective-permute-start | bytes 24584 | tf_op jit(solution)/shard_map/ppermute | solution.py:372
  6.4 1.2 %copy-start.14 = (bf16[16,256]{1,0:T(8,128)(2,1)}, bf16[16,256]{1,0:T(8,128)(2,1)S(1)}, u32[]{:S(2)}) copy-start(bf16[16,256]{1,0:T(8,128)(2,1)S(1)} %collective-permute-done.g_oth) | copy-start | bytes 24580
  6.4 3.7 %collective-permute-start.2 = (bf16[4,256,512]{2,1,0:T(8,128)(2,1)}, bf16[4,256,512]{2,1,0:T(8,128)(2,1)S(1)}, u32[]{:S(2)}, u32[]{:S(2)}) collective-permute-start(bf16[4,256,512]{2,1,0:T(8,128)(2,1)} %get-tuple-element.48), channel_id=1, source_target_pairs={{0,1},{1,0},{2,3},{3,2},{4,5},{5,4},{6,7},{7,6},{8,9},{9,8},{10,11... | collective-permute-start | bytes 3145736 | tf_op jit(solution)/shard_map/ppermute | solution.py:372
  6.5 3.6 %collective-permute-start.1 = (bf16[4,256,256]{2,1,0:T(8,128)(2,1)}, bf16[4,256,256]{2,1,0:T(8,128)(2,1)S(1)}, u32[]{:S(2)}, u32[]{:S(2)}) collective-permute-start(bf16[4,256,256]{2,1,0:T(8,128)(2,1)} %get-tuple-element.47), channel_id=1, source_target_pairs={{0,1},{1,0},{2,3},{3,2},{4,5},{5,4},{6,7},{7,6},{8,9},{9,8},{10,11... | collective-permute-start | bytes 1572872 | tf_op jit(solution)/shard_map/ppermute | solution.py:372
  10.1 0.8 copy-start.2
  10.1 1.2 %copy-start = (bf16[4,256,512]{2,1,0:T(8,128)(2,1)}, bf16[4,256,512]{2,1,0:T(8,128)(2,1)S(1)}, u32[]{:S(2)}) copy-start(bf16[4,256,512]{2,1,0:T(8,128)(2,1)S(1)} %collective-permute-done.2.refs_3_.refs_5_) | copy-start | bytes 3145732
  15.0 6.2 %copy-start.16 = (bf16[272,512]{1,0:T(8,128)(2,1)S(1)}, bf16[272,512]{1,0:T(8,128)(2,1)}, u32[]{:S(2)}) copy-start(bf16[272,512]{1,0:T(8,128)(2,1)} %get-tuple-element.67) | copy-start | bytes 835588
  15.0 10.1 %collective-permute-start.4 = (bf16[272,512]{1,0:T(8,128)(2,1)}, bf16[272,512]{1,0:T(8,128)(2,1)S(1)}, u32[]{:S(2)}, u32[]{:S(2)}) collective-permute-start(bf16[272,512]{1,0:T(8,128)(2,1)} %get-tuple-element.65), channel_id=1, source_target_pairs={{0,2},{1,3},{2,0},{3,1},{4,6},{5,7},{6,4},{7,5},{8,10},{9,11},{10,... | collective-permute-start | bytes 835592 | tf_op jit(solution)/shard_map/ppermute | solution.py:376
  20.0 14.0 %collective-permute-start.5 = (bf16[272,512]{1,0:T(8,128)(2,1)}, bf16[272,512]{1,0:T(8,128)(2,1)S(1)}, u32[]{:S(2)}, u32[]{:S(2)}) collective-permute-start(bf16[272,512]{1,0:T(8,128)(2,1)} %get-tuple-element.66), channel_id=1, source_target_pairs={{0,4},{1,5},{2,6},{3,7},{4,0},{5,1},{6,2},{7,3},{8,12},{9,13},{10,... | collective-permute-start | bytes 835592 | tf_op jit(solution)/shard_map/ppermute | solution.py:376
  21.3 12.7 %collective-permute-start.6 = (bf16[272,512]{1,0:T(8,128)(2,1)S(1)}, bf16[272,512]{1,0:T(8,128)(2,1)S(1)}, u32[]{:S(2)}, u32[]{:S(2)}) collective-permute-start(bf16[272,512]{1,0:T(8,128)(2,1)S(1)} %copy-done.16), channel_id=1, source_target_pairs={{0,6},{1,7},{2,4},{3,5},{4,2},{5,3},{6,0},{7,1},{8,14},{9,15},{10,... | collective-permute-start | bytes 835592 | tf_op jit(solution)/shard_map/ppermute | solution.py:376
  24.1 16.1 %collective-permute-start.3 = (bf16[4,256,256]{2,1,0:T(8,128)(2,1)}, bf16[4,256,256]{2,1,0:T(8,128)(2,1)S(1)}, u32[]{:S(2)}, u32[]{:S(2)}) collective-permute-start(bf16[4,256,256]{2,1,0:T(8,128)(2,1)} %get-tuple-element.56), channel_id=1, source_target_pairs={{0,1},{1,0},{2,3},{3,2},{4,5},{5,4},{6,7},{7,6},{8,9},{9,8},{10,11... | collective-permute-start | bytes 1572872 | tf_op jit(solution)/shard_map/ppermute | solution.py:372
  25.1 8.9 %copy-start.6 = (bf16[272,512]{1,0:T(8,128)(2,1)}, bf16[272,512]{1,0:T(8,128)(2,1)S(1)}, u32[]{:S(2)}) copy-start(bf16[272,512]{1,0:T(8,128)(2,1)S(1)} %collective-permute-done.4.refs_1_) | copy-start | bytes 835588
  34.0 0.7 copy-start.7
  34.8 0.7 copy-start.8
  37.7 11.4 %collective-permute-start.7 = (bf16[272,512]{1,0:T(8,128)(2,1)}, bf16[272,512]{1,0:T(8,128)(2,1)S(1)}, u32[]{:S(2)}, u32[]{:S(2)}) collective-permute-start(bf16[272,512]{1,0:T(8,128)(2,1)} %group_total.1), channel_id=1, source_target_pairs={{0,8},{1,9},{2,10},{3,11},{4,12},{5,13},{6,14},{7,15},{8,16},{9,17... | collective-permute-start | bytes 835592 | tf_op jit(solution)/shard_map/ppermute | solution.py:380
  39.0 19.6 %collective-permute-start.8 = (bf16[272,512]{1,0:T(8,128)(2,1)}, bf16[272,512]{1,0:T(8,128)(2,1)S(1)}, u32[]{:S(2)}, u32[]{:S(2)}) collective-permute-start(bf16[272,512]{1,0:T(8,128)(2,1)} %group_total.1), channel_id=1, source_target_pairs={{0,16},{1,17},{2,18},{3,19},{4,20},{5,21},{6,22},{7,23},{8,24},{9,... | collective-permute-start | bytes 835592 | tf_op jit(solution)/shard_map/ppermute | solution.py:380
  40.3 0.8 copy-start.1
  49.1 9.5 %copy-start.10 = (bf16[272,512]{1,0:T(8,128)(2,1)}, bf16[272,512]{1,0:T(8,128)(2,1)S(1)}, u32[]{:S(2)}) copy-start(bf16[272,512]{1,0:T(8,128)(2,1)S(1)} %collective-permute-done.7.refs_4_) | copy-start | bytes 835588
  58.5 0.7 copy-start.11
  62.5 10.2 %collective-permute-start.10 = (bf16[272,512]{1,0:T(8,128)(2,1)}, bf16[272,512]{1,0:T(8,128)(2,1)S(1)}, u32[]{:S(2)}, u32[]{:S(2)}) collective-permute-start(bf16[272,512]{1,0:T(8,128)(2,1)} %get-tuple-element.72), channel_id=1, source_target_pairs={{0,2},{1,3},{2,0},{3,1},{4,6},{5,7},{6,4},{7,5},{8,10},{9,11},{10,... | collective-permute-start | bytes 835592 | tf_op jit(solution)/shard_map/ppermute | solution.py:376
  62.7 10.0 %collective-permute-start.11 = (bf16[272,512]{1,0:T(8,128)(2,1)}, bf16[272,512]{1,0:T(8,128)(2,1)S(1)}, u32[]{:S(2)}, u32[]{:S(2)}) collective-permute-start(bf16[272,512]{1,0:T(8,128)(2,1)} %get-tuple-element.73), channel_id=1, source_target_pairs={{0,4},{1,5},{2,6},{3,7},{4,0},{5,1},{6,2},{7,3},{8,12},{9,13},{10,... | collective-permute-start | bytes 835592 | tf_op jit(solution)/shard_map/ppermute | solution.py:376
  64.0 11.8 %collective-permute-start.12 = (bf16[272,512]{1,0:T(8,128)(2,1)}, bf16[272,512]{1,0:T(8,128)(2,1)S(1)}, u32[]{:S(2)}, u32[]{:S(2)}) collective-permute-start(bf16[272,512]{1,0:T(8,128)(2,1)} %get-tuple-element.74), channel_id=1, source_target_pairs={{0,6},{1,7},{2,4},{3,5},{4,2},{5,3},{6,0},{7,1},{8,14},{9,15},{10,... | collective-permute-start | bytes 835592 | tf_op jit(solution)/shard_map/ppermute | solution.py:376
  68.4 4.3 %collective-permute-start.9 = (bf16[1,256,512]{2,1,0:T(8,128)(2,1)}, bf16[1,256,512]{2,1,0:T(8,128)(2,1)S(1)}, u32[]{:S(2)}, u32[]{:S(2)}) collective-permute-start(bf16[1,256,512]{2,1,0:T(8,128)(2,1)} %get-tuple-element.70), channel_id=1, source_target_pairs={{0,1},{1,0},{2,3},{3,2},{4,5},{5,4},{6,7},{7,6},{8,9},{9,8},{10,11... | collective-permute-start | bytes 786440 | tf_op jit(solution)/shard_map/ppermute | solution.py:372
  72.7 16.3 %copy-start.12 = (bf16[1,256,512]{2,1,0:T(8,128)(2,1)}, bf16[1,256,512]{2,1,0:T(8,128)(2,1)S(1)}, u32[]{:S(2)}) copy-start(bf16[1,256,512]{2,1,0:T(8,128)(2,1)S(1)} %collective-permute-done.9.refs_2_) | copy-start | bytes 786436
  72.7 3.0 %copy-start.3 = (bf16[272,512]{1,0:T(8,128)(2,1)}, bf16[272,512]{1,0:T(8,128)(2,1)S(1)}, u32[]{:S(2)}) copy-start(bf16[272,512]{1,0:T(8,128)(2,1)S(1)} %collective-permute-done.10.refs_3_) | copy-start | bytes 835588
  72.7 3.0 %copy-start.4 = (bf16[272,512]{1,0:T(8,128)(2,1)}, bf16[272,512]{1,0:T(8,128)(2,1)S(1)}, u32[]{:S(2)}) copy-start(bf16[272,512]{1,0:T(8,128)(2,1)S(1)} %collective-permute-done.11.refs_4_) | copy-start | bytes 835588
  75.8 0.7 copy-start.5
  81.3 7.8 %collective-permute-start.13 = (bf16[3,256,512]{2,1,0:T(8,128)(2,1)}, bf16[3,256,512]{2,1,0:T(8,128)(2,1)S(1)}, u32[]{:S(2)}, u32[]{:S(2)}) collective-permute-start(bf16[3,256,512]{2,1,0:T(8,128)(2,1)} %outputs.4), channel_id=1, source_target_pairs={{0,1},{1,0},{2,3},{3,2},{4,5},{5,4},{6,7},{7,6},{8,9},{9,8},{10,11... | collective-permute-start | bytes 2359304 | tf_op jit(solution)/shard_map/ppermute | solution.py:372
  89.1 0.9 copy-start.9

commit v7 on v5

--- a/solution.py
+++ b/solution.py
@@ -56,13 +56,18 @@
     return jnp.concatenate([x] * (width // LANES), axis=1)
 
 
-def weighted(refs, coefs):
+CHUNK = 32
+
+
+def weighted(refs, outs, coefs):
     key_width, width = refs[0].shape[0] - META, refs[0].shape[1]
-    total = None
-    for ref, coef in zip(refs, coefs, strict=True):
-        term = wide(coef, width) * ref[:key_width, :].astype(F32)
-        total = term if total is None else total + term
-    return total
+    coefs = [[None if c is None else wide(c, width) for c in line] for line in coefs]
+    for start in range(0, key_width, CHUNK):
+        rows = slice(start, start + CHUNK)
+        parts = [ref[rows, :].astype(F32) for ref in refs]
+        for out, line in zip(outs, coefs, strict=True):
+            terms = [c * part for c, part in zip(line, parts, strict=True) if c is not None]
+            out[rows, :] = functools.reduce(jnp.add, terms).astype(BF16)
 
 
 def gate_rows(core, own_ref, other_ref, heads):
@@ -123,39 +128,36 @@
 
 def state_kernel(heads, scalars, *refs):
     k_own, v_own, k_oth, v_oth, factors, tops, decays, ids_ref = refs[:8]
-    outs, payload = refs[8:-1], refs[-1]
-    step = pl.program_id(0)
+    outs = refs[8:]
     mine, core = scalars[0], scalars[1]
     tokens, key_width = k_own.shape[1:]
     length = 2 * tokens
-    head = (heads // 2) * core + jnp.bitwise_xor(mine, step)
-    row = factors[pl.ds(head, 1), :]
-    first, last = row[:, :tokens], row[:, tokens:]
-    total, normal = None, None
-    for k_ref, v_ref, f in (
-        (k_own, v_own, jnp.where(core == 0, first, last)),
-        (k_oth, v_oth, jnp.where(core == 0, last, first)),
-    ):
-        keys, values = k_ref[0], v_ref[0]
-        scaled = keys.astype(F32).T * f
-        high = scaled.astype(BF16)
-        low = (scaled - high.astype(F32)).astype(BF16)
-        piece = dot(low, values) + dot(high, values)
-        pieces = jnp.concatenate(split3(f) + (jnp.zeros((META - 3, tokens), F32),), axis=0)
-        sums = dot(pieces.astype(BF16), keys)
-        line = (sums[2:3] + sums[1:2]) + sums[0:1]
-        total = piece if total is None else total + piece
-        normal = line if normal is None else normal + line
     doc = jnp.broadcast_to(ids_ref[:, length - 1 :].astype(F32) + 1.0, (1, LANES))
-    payload[:key_width, :] = total.astype(BF16)
-    payload[key_width:, :] = meta_rows(
-        normal, tops[pl.ds(head, 1), :], decays[pl.ds(head, 1), :], doc, payload.shape[1]
-    )
-    for i, out in enumerate(outs):
-
-        @pl.when(step == i)
-        def _(out=out):
-            out[...] = payload[...]
+    for slot in range(len(outs) - 1, -1, -1):
+        out = outs[slot]
+        local_head = jnp.bitwise_xor(mine, slot)
+        head = (heads // 2) * core + local_head
+        row = factors[pl.ds(head, 1), :]
+        first, last = row[:, :tokens], row[:, tokens:]
+        high, low, values, normal = [], [], [], None
+        for k_ref, v_ref, f in (
+            (k_own, v_own, jnp.where(core == 0, first, last)),
+            (k_oth, v_oth, jnp.where(core == 0, last, first)),
+        ):
+            keys = k_ref[local_head]
+            scaled = keys.astype(F32).T * f
+            high.append(scaled.astype(BF16))
+            low.append((scaled - high[-1].astype(F32)).astype(BF16))
+            values.append(v_ref[local_head])
+            pieces = jnp.concatenate(split3(f) + (jnp.zeros((META - 3, tokens), F32),), axis=0)
+            sums = dot(pieces.astype(BF16), keys)
+            line = (sums[2:3] + sums[1:2]) + sums[0:1]
+            normal = line if normal is None else normal + line
+        total = dot(jnp.concatenate(low + high, axis=1), jnp.concatenate(values * 2, axis=0))
+        out[:key_width, :] = total.astype(BF16)
+        out[key_width:, :] = meta_rows(
+            normal, tops[pl.ds(head, 1), :], decays[pl.ds(head, 1), :], doc, out.shape[1]
+        )
 
 
 def decay_before(mine, place, decays):
@@ -179,9 +181,7 @@
     reached = jnp.where(alive, tops + after, FLOOR_NEG)
     top = jnp.max(reached, axis=0, keepdims=True)
     coefs = jnp.where(alive, jnp.exp(reached - top), 0.0)
-    out[:key_width, :] = weighted(
-        states, [coefs[i : i + 1] for i in range(group)]
-    ).astype(BF16)
+    weighted(states, [out], [[coefs[i : i + 1] for i in range(group)]])
     normal = jnp.sum(wide(coefs, key_width) * normals, axis=0, keepdims=True)
     out[key_width:, :] = meta_rows(normal, top, whole_decay, doc, width)
 
@@ -195,7 +195,7 @@
     place = jnp.bitwise_xor(iota((group, LANES), 0), mine)
     before = decay_before(mine, place, decays)
     zero = jnp.zeros((1, LANES), F32)
-    far_reached, passed = [], zero
+    far_reached, passed, lines = [], zero, []
     for d in range(reach):
         far_reached.append(far_tops[d : d + 1] + passed)
         passed = passed + far_decays[d : d + 1]
@@ -214,15 +214,14 @@
         )
         coefs = jnp.where(alive, jnp.exp(reached - top), 0.0)
         far_coefs = jnp.where(far_alive, jnp.exp(far - top), 0.0)
-        others = [i for i in range(group) if i != r]
-        outs[r][:key_width, :] = weighted(
-            [states[i] for i in others] + list(totals),
-            [coefs[i : i + 1] for i in others]
-            + [far_coefs[d : d + 1] for d in range(reach)],
-        ).astype(BF16)
+        lines.append(
+            [None if i == r else coefs[i : i + 1] for i in range(group)]
+            + [far_coefs[d : d + 1] for d in range(reach)]
+        )
         normal = jnp.sum(wide(coefs, key_width) * normals, axis=0, keepdims=True)
         normal = normal + jnp.sum(wide(far_coefs, key_width) * far_normals, axis=0, keepdims=True)
         outs[r][key_width:, :] = meta_rows(normal, top, zero, doc, width)
+    weighted(list(states) + list(totals), outs, lines)
 
 
 def local_kernel(heads, scalars, *refs):
@@ -260,17 +259,19 @@
         stabilizer = functools.reduce(
             jnp.maximum, [jnp.max(x, axis=1, keepdims=True) for x in exponents]
         )
-        numerator, denominator = None, None
+        factors, sources, denominator = [], [], None
         for s in range(block + 1):
             weights = dot(queries[block], keys[s], NT) * scaling
             weights = weights * jnp.exp(exponents[s] - stabilizer)
             high = weights.astype(BF16)
-            part = dot(high, values[s])
+            factors.append(high)
+            sources.append(values[s])
             if s < block:
-                part = part + dot((weights - high.astype(F32)).astype(BF16), values[s])
-            numerator = part if s == 0 else numerator + part
+                factors.append((weights - high.astype(F32)).astype(BF16))
+                sources.append(values[s])
             part = jnp.sum(weights, axis=1, keepdims=True)
             denominator = part if s == 0 else denominator + part
+        numerator = dot(jnp.concatenate(factors, axis=1), jnp.concatenate(sources, axis=0))
         side = core if block == 0 else 1 - core
         numerators[0, side] = numerator
         lane = iota((tokens, LANES), 1)
@@ -280,40 +281,36 @@
         )
 
 
-def output_kernel(scalars, q_own, q_oth, numerators, stats, *refs):
-    entering, (keep, send, payload) = refs[:-3], refs[-3:]
-    step = pl.program_id(0)
+def output_kernel(first, count, scalars, q_own, q_oth, numerators, stats, *refs):
+    entering, (keep, send) = refs[:count], refs[count:]
     key_width = q_own.shape[2]
     scaling = key_width**-0.5
-    for i, ref in enumerate(entering):
-
-        @pl.when(step == i)
-        def _(ref=ref):
-            payload[...] = ref[...]
-
-    normal, top, _, doc = read_meta([payload])
-    pieces = jnp.concatenate(split3(normal) + (jnp.zeros((META - 3, key_width), F32),), axis=0)
-    pieces = pieces.astype(BF16)
-    memory = payload[:key_width, :]
-    width = memory.shape[1]
-    for side, (q_ref, out) in enumerate(((q_own, keep), (q_oth, send))):
-        query = q_ref[0]
-        tokens = query.shape[0]
-        stat = stats[0, side]
-        local = stat[0:1]
-        alive = stat[3:4] == wide(doc, tokens)
-        carried = jnp.where(alive, stat[2:3] + wide(top, tokens), FLOOR_NEG)
-        stabilizer = jnp.maximum(local, carried)
-        shrink = jnp.exp(local - stabilizer)
-        retained = jnp.exp(carried - stabilizer) * scaling
-        seen = dot(pieces, query, NT)
-        seen = (seen[2:3] + seen[1:2]) + seen[0:1]
-        denominator = shrink * stat[1:2] + retained * seen
-        inverse = 1.0 / jnp.maximum(jnp.abs(denominator), 1.0)
-        near = jnp.broadcast_to(shrink * inverse, (LANES, tokens)).T
-        far = jnp.broadcast_to(retained * inverse, (LANES, tokens)).T
-        result = wide(near, width) * numerators[0, side]
-        out[0] = (result + wide(far, width) * dot(query, memory)).astype(BF16)
+    for i, payload in enumerate(entering):
+        at = first + i
+        local_head = jnp.bitwise_xor(scalars[0], first + i)
+        normal, top, _, doc = read_meta([payload])
+        pieces = split3(normal) + (jnp.zeros((META - 3, key_width), F32),)
+        pieces = jnp.concatenate(pieces, axis=0).astype(BF16)
+        memory = payload[:key_width, :]
+        width = memory.shape[1]
+        for side, (q_ref, out) in enumerate(((q_own, keep), (q_oth, send))):
+            query = q_ref[local_head]
+            tokens = query.shape[0]
+            stat = stats[at, side]
+            local = stat[0:1]
+            alive = stat[3:4] == wide(doc, tokens)
+            carried = jnp.where(alive, stat[2:3] + wide(top, tokens), FLOOR_NEG)
+            stabilizer = jnp.maximum(local, carried)
+            shrink = jnp.exp(local - stabilizer)
+            retained = jnp.exp(carried - stabilizer) * scaling
+            seen = dot(pieces, query, NT)
+            seen = (seen[2:3] + seen[1:2]) + seen[0:1]
+            denominator = shrink * stat[1:2] + retained * seen
+            inverse = 1.0 / jnp.maximum(jnp.abs(denominator), 1.0)
+            near = jnp.broadcast_to(shrink * inverse, (LANES, tokens)).T
+            far = jnp.broadcast_to(retained * inverse, (LANES, tokens)).T
+            result = wide(near, width) * numerators[at, side]
+            out[i] = (result + wide(far, width) * dot(query, memory)).astype(BF16)
 
 
 def merge_kernel(heads, scalars, *refs):
@@ -370,8 +367,8 @@
         pairs = [(d, d ^ (2 * r)) for d in range(devices)]
         return lax.ppermute(x, AXES, pairs)
 
-    def to_later(x, levels_on):
-        jump = 2 * group * levels_on
+    def to_next(x):
+        jump = 2 * group
         return lax.ppermute(x, AXES, [(d, d + jump) for d in range(devices - jump)])
 
     rows = key_width + META
@@ -413,25 +410,18 @@
         name="gates",
     )(scalars, gates, gates_oth, ids)
 
-    def by_slot(x, first_slot=0):
-        return pl.BlockSpec(
-            (1,) + x.shape[1:], lambda i, s: (jnp.bitwise_xor(s[0], first_slot + i), 0, 0)
-        )
-
+    def by_slot(x):
+        return pl.BlockSpec((1,) + x.shape[1:], lambda i, s: (jnp.bitwise_xor(s[0], i), 0, 0))
+
+    by_core = (k_keep, v_keep, k_oth, v_oth, factors, tops, decays, ids)
     made = pl.pallas_call(
         functools.partial(state_kernel, heads),
-        grid_spec=pltpu.PrefetchScalarGridSpec(
-            num_scalar_prefetch=1,
-            grid=(group,),
-            in_specs=[by_slot(x) for x in (k_keep, v_keep, k_oth, v_oth)]
-            + [whole(x.shape) for x in (factors, tops, decays, ids)],
-            out_specs=[whole(state)] * group,
-            scratch_shapes=[pltpu.VMEM(state, BF16)],
-        ),
+        in_specs=[SMEM] + [whole(x.shape) for x in by_core],
+        out_specs=[whole(state)] * group,
         out_shape=[shape_of(*state)] * group,
         compiler_params=params(),
         name="states",
-    )(scalars, k_keep, v_keep, k_oth, v_oth, factors, tops, decays, ids)
+    )(scalars, *by_core)
     gathered = [made[0]] + [in_group(made[r], r) for r in range(1, group)]
     total = pl.pallas_call(
         functools.partial(total_kernel, group),
@@ -441,7 +431,9 @@
         compiler_params=params(),
         name="group_total",
     )(scalars, *gathered)
-    totals = [to_later(total, d) for d in range(1, reach + 1)]
+    totals = [to_next(total)]
+    while len(totals) < reach:
+        totals.append(to_next(totals[-1]))
 
     queries, gathered[0] = lax.optimization_barrier((queries, gathered[0]))
     q_keep, q_send = relayout(queries)
@@ -475,31 +467,23 @@
     )(scalars, *gathered, *totals)
     entering = [leaving[0]] + [in_group(leaving[r], r) for r in range(1, group)]
 
-    kept, received = [], []
-    for first, count in ((0, 1), (1, group - 1)):
-        spec = pl.BlockSpec((1, tokens, value_width), lambda i, s: (i, 0, 0))
-        keep, send = pl.pallas_call(
-            output_kernel,
-            grid_spec=pltpu.PrefetchScalarGridSpec(
-                num_scalar_prefetch=1,
-                grid=(count,),
-                in_specs=[by_slot(q_keep, first), by_slot(q_oth, first)]
-                + [
-                    pl.BlockSpec((1,) + s[1:], lambda i, _, first=first: (first + i, 0, 0, 0))
-                    for s in local_shapes
-                ]
-                + [whole(state)] * count,
-                out_specs=[spec] * 2,
-                scratch_shapes=[pltpu.VMEM(state, BF16)],
-            ),
+    def outputs(first, count):
+        return pl.pallas_call(
+            functools.partial(output_kernel, first, count),
+            in_specs=[SMEM, whole(q_keep.shape), whole(q_oth.shape)]
+            + [whole(x) for x in local_shapes]
+            + [whole(state)] * count,
+            out_specs=[whole((count, tokens, value_width))] * 2,
             out_shape=[shape_of(count, tokens, value_width)] * 2,
             compiler_params=params(),
             name="outputs",
         )(scalars, q_keep, q_oth, numerators, stats, *entering[first : first + count])
-        kept.append(keep)
-        swapped = swap_cores(send)
-        numerators, swapped = lax.optimization_barrier((numerators, swapped))
-        received.append(swapped)
+
+    keep, send = outputs(0, 1)
+    swapped = swap_cores(send)
+    numerators, swapped = lax.optimization_barrier((numerators, swapped))
+    keep_far, send = outputs(1, group - 1)
+    kept, received = [keep, keep_far], [swapped, swap_cores(send)]
     return pl.pallas_call(
         functools.partial(merge_kernel, heads),
         in_specs=[SMEM] + [whole(x.shape) for x in kept + received],

time: 90.4 us -> 89.5 us (0.990)
  the two profiles are of different devices: /device:TPU:25 before, /device:TPU:0 now
where the time goes in v7:
time: 89.5 us; the launch traced here: 89 us
  Pallas kernels  38.4 us (43%)
  waiting for transfers between devices  26.3 us (29%)
  starting transfers between devices  16.5 us (18%)
  local copies, waits for them, and re-layouts  6.5 us (7%)
  other arithmetic  1.27 us (1%)
    ppermute x6, waiting for transfers between devices, in_group(): return lax.ppermute(x, AXES, pairs)  18.6 us
    pallas_call x2, Pallas kernels, outputs(): pl.pallas_call(functools.partial(output_kernel, first, count), in_specs=[...  8.36 us
    pallas_call x1, Pallas kernels, local(): pl.pallas_call(functools.partial(local_kernel, heads), grid_spec=pltpu.Pr...  7.98 us
    ppermute x2, starting transfers between devices, to_next(): return lax.ppermute(x, AXES, [(d, d + jump) for d in range(devices - jump)])  7.77 us
    ppermute x6, starting transfers between devices, in_group(): return lax.ppermute(x, AXES, pairs)  7.63 us
    pallas_call x2, Pallas kernels, relayout(): pl.pallas_call(functools.partial(relayout_kernel, half, len(sources)), in...  7.08 us
    unnamed x32, local copies, waits for them, and re-layouts  5.84 us
    ppermute x6, waiting for transfers between devices, swap_cores(): return lax.ppermute(x, AXES, [(d, d ^ 1) for d in range(devices)])  4.77 us
  transfers between devices with their start and end apart: 14, of which 8 were waited for; matrix products, arithmetic and copies ran while one was open for 1% of the time, Pallas kernels for 23%

profile of v7, /device:TPU:0, one launch (start us, length us, event | category | flops | bytes accessed | tf_op | source)
XLA Modules:
  0.0 89.0 jit_solution(4691854039391072230)
XLA Ops:
  0.0 0.7 pad_maximum_fusion.g_own
  0.7 0.5 collective-permute-start
  1.2 0.6 pad_add_fusion.scalars
  1.8 4.4 %relayout.2 = (bf16[4,256,256]{2,1,0:T(8,128)(2,1)}, bf16[4,256,512]{2,1,0:T(8,128)(2,1)}, bf16[4,256,256]{2,1,0:T(8,128)(2,1)}, bf16[4,256,512]{2,1,0:T(8,128)(2,1)}) custom-call(s32[2]{0:T(128)} %pad_add_fusion.scalars, bf16[256,8,256]{2,1,0:T(8,128)(2,1)} %refs_0_, bf16[256,8,512]{2,1,0:T(8,128)(2,1)} %refs_1_.1), custom_call_target="tpu_custom_call" | custom-call | tf_op jit(solution)/shard_map/relayout/pallas_call | solution.py:380
  6.2 0.0 collective-permute-done.g_oth
  6.2 0.0 copy-start.14
  6.2 0.1 collective-permute-start.2
  6.3 0.5 collective-permute-start.1
  6.8 0.0 copy-done.15
  6.8 0.7 dynamic_slice.3
  7.4 0.0 copy-done.13
  7.4 0.0 copy-done.14
  7.4 1.9 %gates.1 = (f32[8,512]{1,0:T(8,128)}, f32[8,128]{1,0:T(8,128)}, f32[8,128]{1,0:T(8,128)}, f32[8,512]{1,0:T(8,128)}, f32[8,512]{1,0:T(8,128)}, /*index=5*/f32[512,128]{1,0:T(8,128)}) custom-call(s32[2]{0:T(128)} %pad_add_fusion.scalars, bf16[16,256]{1,0:T(8,128)(2,1)} %copy-done.13, bf16[16,256]{1,0:T(8,128)(2,1)} %copy-done.14, s32[1,512]{1,0:T(1,128)} %bitcast.5), custom_call_target="tpu_custom_call" | custom-call | tf_op jit(solution)/shard_map/gates/pallas_call | solution.py:404
  9.3 0.5 collective-permute-done.1.refs_2_.refs_4_
  9.9 0.0 copy-start.2
  9.9 0.0 collective-permute-done.2.refs_3_.refs_5_
  9.9 0.0 copy-start.1
  9.9 0.8 copy-done.2
  10.6 0.4 copy-done.1
  11.1 4.2 %states.1 = (bf16[272,512]{1,0:T(8,128)(2,1)}, bf16[272,512]{1,0:T(8,128)(2,1)}, bf16[272,512]{1,0:T(8,128)(2,1)}, bf16[272,512]{1,0:T(8,128)(2,1)}) custom-call(s32[2]{0:T(128)} %pad_add_fusion.scalars, bf16[4,256,256]{2,1,0:T(8,128)(2,1)} %get-tuple-element.43.refs_0_.refs_1_, bf16[4,256,512]{2,1,0:T(8,128)(2,1)} %get-tuple-element.44.refs_1_.refs_2_, ...), custom_call_target="tpu_custom_call" | custom-call | tf_op jit(solution)/shard_map/states/pallas_call | solution.py:417
  15.2 2.6 %collective-permute-start.4 = (bf16[272,512]{1,0:T(8,128)(2,1)}, bf16[272,512]{1,0:T(8,128)(2,1)S(1)}, u32[]{:S(2)}, u32[]{:S(2)}) collective-permute-start(bf16[272,512]{1,0:T(8,128)(2,1)} %get-tuple-element.66), channel_id=1, source_target_pairs={{0,2},{1,3},{2,0},{3,1},{4,6},{5,7},{6,4},{7,5},{8,10},{9,11},{10,... | collective-permute-start | bytes 835592 | tf_op jit(solution)/shard_map/ppermute | solution.py:368
  17.8 1.5 %collective-permute-start.5 = (bf16[272,512]{1,0:T(8,128)(2,1)}, bf16[272,512]{1,0:T(8,128)(2,1)S(1)}, u32[]{:S(2)}, u32[]{:S(2)}) collective-permute-start(bf16[272,512]{1,0:T(8,128)(2,1)} %get-tuple-element.67), channel_id=1, source_target_pairs={{0,4},{1,5},{2,6},{3,7},{4,0},{5,1},{6,2},{7,3},{8,12},{9,13},{10,... | collective-permute-start | bytes 835592 | tf_op jit(solution)/shard_map/ppermute | solution.py:368
  19.4 0.0 collective-permute-start.6
  19.4 6.2 %collective-permute-done.4.refs_1_ = bf16[272,512]{1,0:T(8,128)(2,1)S(1)} collective-permute-done((bf16[272,512]{1,0:T(8,128)(2,1)}, bf16[272,512]{1,0:T(8,128)(2,1)S(1)}, u32[]{:S(2)}, u32[]{:S(2)}) %collective-permute-start.4) | collective-permute-done | bytes 278560 | tf_op jit(solution)/shard_map/ppermute | solution.py:368
  25.6 0.0 copy-start.3
  25.6 7.1 %collective-permute-done.5.refs_2_ = bf16[272,512]{1,0:T(8,128)(2,1)S(1)} collective-permute-done((bf16[272,512]{1,0:T(8,128)(2,1)}, bf16[272,512]{1,0:T(8,128)(2,1)S(1)}, u32[]{:S(2)}, u32[]{:S(2)}) %collective-permute-start.5) | collective-permute-done | bytes 278560 | tf_op jit(solution)/shard_map/ppermute | solution.py:368
  32.7 0.0 copy-start.4
  32.7 0.0 collective-permute-done.6.refs_3_
  32.7 0.0 copy-done.3
  32.7 0.7 copy-done.4
  33.4 0.1 copy-done.5
  33.5 2.2 %group_total.1 = bf16[272,512]{1,0:T(8,128)(2,1)} custom-call(s32[2]{0:T(128)} %pad_add_fusion.scalars, bf16[272,512]{1,0:T(8,128)(2,1)} %get-tuple-element.65.refs_0_, bf16[272,512]{1,0:T(8,128)(2,1)} %copy-done.3, bf16[272,512]{1,0:T(8,128)(2,1)} %copy-done.4, bf16[272,512]{1,0:T(8,128)(2,1)} %copy-done.5), custom_call_target="tpu_custom_call" | custom-call | tf_op jit(solution)/shard_map/group_total/pallas_call | solution.py:426
  35.7 3.5 %collective-permute-start.7 = (bf16[272,512]{1,0:T(8,128)(2,1)}, bf16[272,512]{1,0:T(8,128)(2,1)S(1)}, u32[]{:S(2)}, u32[]{:S(2)}) collective-permute-start(bf16[272,512]{1,0:T(8,128)(2,1)} %group_total.1), channel_id=1, source_target_pairs={{0,8},{1,9},{2,10},{3,11},{4,12},{5,13},{6,14},{7,15},{8,16},{9,17... | collective-permute-start | bytes 835592 | tf_op jit(solution)/shard_map/ppermute | solution.py:372
  39.2 2.7 %relayout.3 = (bf16[4,256,256]{2,1,0:T(8,128)(2,1)}, bf16[4,256,256]{2,1,0:T(8,128)(2,1)}) custom-call(s32[2]{0:T(128)} %pad_add_fusion.scalars, bf16[256,8,256]{2,1,0:T(8,128)(2,1)} %refs_0_.1), custom_call_target="tpu_custom_call" | custom-call | tf_op jit(solution)/shard_map/relayout/pallas_call | solution.py:380
  41.9 0.0 collective-permute-start.3
  41.9 2.9 %collective-permute-done.7.refs_4_ = bf16[272,512]{1,0:T(8,128)(2,1)S(1)} collective-permute-done((bf16[272,512]{1,0:T(8,128)(2,1)}, bf16[272,512]{1,0:T(8,128)(2,1)S(1)}, u32[]{:S(2)}, u32[]{:S(2)}) %collective-permute-start.7) | collective-permute-done | bytes 278560 | tf_op jit(solution)/shard_map/ppermute | solution.py:372
  44.8 4.3 %collective-permute-start.8 = (bf16[272,512]{1,0:T(8,128)(2,1)S(1)}, bf16[272,512]{1,0:T(8,128)(2,1)S(1)}, u32[]{:S(2)}, u32[]{:S(2)}) collective-permute-start(bf16[272,512]{1,0:T(8,128)(2,1)S(1)} %collective-permute-done.7.refs_4_), channel_id=1, source_target_pairs={{0,8},{1,9},{2,10},{3,11},{4,12},{5,13},{6,14},{7,15},{8,16},{9,17... | collective-permute-start | bytes 835592 | tf_op jit(solution)/shard_map/ppermute | solution.py:372
  49.1 0.0 collective-permute-done.3.refs_3_.q_oth
  49.1 0.0 copy-start
  49.1 0.8 copy-done
  49.9 8.0 %own_terms.1 = (f32[4,2,256,512]{3,2,1,0:T(8,128)}, f32[4,2,8,256]{3,2,1,0:T(8,128)}) custom-call(s32[2]{0:T(128)} %pad_add_fusion.scalars, bf16[4,256,256]{2,1,0:T(8,128)(2,1)} %get-tuple-element.56.refs_0_.q_own, bf16[4,256,256]{2,1,0:T(8,128)(2,1)} %get-tuple-element.43.refs_0_.refs_1_, bf16[4,256,512]{2,1,0:T(8,128)(2,1)} %get-tuple-element.44.refs_1_.refs_2_, ...), custom_call_target="tpu_custom_call" | custom-call | tf_op jit(solution)/shard_map/own_terms/pallas_call | solution.py:444
  57.9 0.0 collective-permute-done.8.refs_5_
  57.9 0.0 copy-done.10
  57.9 0.0 copy-start.11
  57.9 0.7 copy-done.11
  58.6 3.1 %entering.1 = (bf16[272,512]{1,0:T(8,128)(2,1)}, bf16[272,512]{1,0:T(8,128)(2,1)}, bf16[272,512]{1,0:T(8,128)(2,1)}, bf16[272,512]{1,0:T(8,128)(2,1)}) custom-call(s32[2]{0:T(128)} %pad_add_fusion.scalars, bf16[272,512]{1,0:T(8,128)(2,1)} %get-tuple-element.65.refs_0_, bf16[272,512]{1,0:T(8,128)(2,1)} %copy-done.3, bf16[272,512]{1,0:T(8,128)(2,1)} %copy-done.4, ...), custom_call_target="tpu_custom_call" | custom-call | tf_op jit(solution)/shard_map/entering/pallas_call | solution.py:460
  61.7 1.4 %collective-permute-start.10 = (bf16[272,512]{1,0:T(8,128)(2,1)}, bf16[272,512]{1,0:T(8,128)(2,1)S(1)}, u32[]{:S(2)}, u32[]{:S(2)}) collective-permute-start(bf16[272,512]{1,0:T(8,128)(2,1)} %get-tuple-element.73), channel_id=1, source_target_pairs={{0,2},{1,3},{2,0},{3,1},{4,6},{5,7},{6,4},{7,5},{8,10},{9,11},{10,... | collective-permute-start | bytes 835592 | tf_op jit(solution)/shard_map/ppermute | solution.py:368
  63.2 0.5 collective-permute-start.11
  63.7 1.5 %collective-permute-start.12 = (bf16[272,512]{1,0:T(8,128)(2,1)}, bf16[272,512]{1,0:T(8,128)(2,1)S(1)}, u32[]{:S(2)}, u32[]{:S(2)}) collective-permute-start(bf16[272,512]{1,0:T(8,128)(2,1)} %get-tuple-element.75), channel_id=1, source_target_pairs={{0,6},{1,7},{2,4},{3,5},{4,2},{5,3},{6,0},{7,1},{8,14},{9,15},{10,... | collective-permute-start | bytes 835592 | tf_op jit(solution)/shard_map/ppermute | solution.py:368
  65.2 3.7 %outputs.2 = (bf16[1,256,512]{2,1,0:T(8,128)(2,1)}, bf16[1,256,512]{2,1,0:T(8,128)(2,1)}) custom-call(s32[2]{0:T(128)} %pad_add_fusion.scalars, bf16[4,256,256]{2,1,0:T(8,128)(2,1)} %get-tuple-element.56.refs_0_.q_own, bf16[4,256,256]{2,1,0:T(8,128)(2,1)} %copy-done, f32[4,2,256,512]{3,2,1,0:T(8,128)} %get-tuple-element.72.numerators, ...), custom_call_target="tpu_custom_call" | custom-call | tf_op jit(solution)/shard_map/outputs/pallas_call | solution.py:471
  68.9 0.0 collective-permute-start.9
  68.9 1.7 %collective-permute-done.9.refs_2_ = bf16[1,256,512]{2,1,0:T(8,128)(2,1)S(1)} collective-permute-done((bf16[1,256,512]{2,1,0:T(8,128)(2,1)}, bf16[1,256,512]{2,1,0:T(8,128)(2,1)S(1)}, u32[]{:S(2)}, u32[]{:S(2)}) %collective-permute-start.9) | collective-permute-done | bytes 262176 | tf_op jit(solution)/shard_map/ppermute | solution.py:364
  70.7 0.8 collective-permute-done.10.refs_0_
  71.5 4.5 %collective-permute-done.11.refs_1_ = bf16[272,512]{1,0:T(8,128)(2,1)S(1)} collective-permute-done((bf16[272,512]{1,0:T(8,128)(2,1)}, bf16[272,512]{1,0:T(8,128)(2,1)S(1)}, u32[]{:S(2)}, u32[]{:S(2)}) %collective-permute-start.11) | collective-permute-done | bytes 278560 | tf_op jit(solution)/shard_map/ppermute | solution.py:368
  76.0 0.0 collective-permute-done.12.refs_2_
  76.0 0.0 copy-done.7
  76.0 0.7 copy-done.8
  76.7 0.7 copy-done.9
  77.4 4.6 %outputs.3 = (bf16[3,256,512]{2,1,0:T(8,128)(2,1)}, bf16[3,256,512]{2,1,0:T(8,128)(2,1)}) custom-call(s32[2]{0:T(128)} %pad_add_fusion.scalars, bf16[4,256,256]{2,1,0:T(8,128)(2,1)} %get-tuple-element.56.refs_0_.q_own, bf16[4,256,256]{2,1,0:T(8,128)(2,1)} %copy-done, f32[4,2,256,512]{3,2,1,0:T(8,128)} %get-tuple-element.72.numerators, ...), custom_call_target="tpu_custom_call" | custom-call | tf_op jit(solution)/shard_map/outputs/pallas_call | solution.py:471
  82.1 0.0 collective-permute-start.13
  82.1 2.5 %collective-permute-done.13.refs_3_ = bf16[3,256,512]{2,1,0:T(8,128)(2,1)S(1)} collective-permute-done((bf16[3,256,512]{2,1,0:T(8,128)(2,1)}, bf16[3,256,512]{2,1,0:T(8,128)(2,1)S(1)}, u32[]{:S(2)}, u32[]{:S(2)}) %collective-permute-start.13) | collective-permute-done | bytes 786464 | tf_op jit(solution)/shard_map/ppermute | solution.py:364
  84.6 0.0 copy-done.12
  84.6 0.9 copy-done.6
  85.4 3.6 %merge.1 = bf16[256,8,512]{2,1,0:T(8,128)(2,1)} custom-call(s32[2]{0:T(128)} %pad_add_fusion.scalars, bf16[1,256,512]{2,1,0:T(8,128)(2,1)} %get-tuple-element.70.refs_0_, bf16[3,256,512]{2,1,0:T(8,128)(2,1)} %get-tuple-element.76.refs_1_, bf16[1,256,512]{2,1,0:T(8,128)(2,1)} %copy-done.12, bf16[3,256,512]{2,1,0:T(8,128)(2,1)} %copy-done.6), custom_call_target="tpu_custom_call" | custom-call | tf_op jit(solution)/shard_map/merge/pallas_call | solution.py:487
  (9 shorter events, 0.0 us)
Async XLA Ops:
  0.0 6.8 %copy-start.15 = (s32[1024]{0:T(1024)S(1)}, s32[1024]{0:T(1024)}, u32[]{:S(2)}) copy-start(s32[1024]{0:T(1024)} %param.11) | copy-start | bytes 12292
  0.7 6.7 %copy-start.13 = (bf16[16,256]{1,0:T(8,128)(2,1)}, bf16[16,256]{1,0:T(8,128)(2,1)S(1)}, u32[]{:S(2)}) copy-start(bf16[16,256]{1,0:T(8,128)(2,1)S(1)} %pad_maximum_fusion.g_own) | copy-start | bytes 24580
  0.7 5.5 %collective-permute-start = (bf16[16,256]{1,0:T(8,128)(2,1)S(1)}, bf16[16,256]{1,0:T(8,128)(2,1)S(1)}, u32[]{:S(2)}, u32[]{:S(2)}) collective-permute-start(bf16[16,256]{1,0:T(8,128)(2,1)S(1)} %pad_maximum_fusion.g_own), channel_id=1, source_target_pairs={{0,1},{1,0},{2,3},{3,2},{4,5},{5,4},{6,7},{7,6},{8,9},{9,8},{10,11... | collective-permute-start | bytes 24584 | tf_op jit(solution)/shard_map/ppermute | solution.py:364
  6.2 1.2 %copy-start.14 = (bf16[16,256]{1,0:T(8,128)(2,1)}, bf16[16,256]{1,0:T(8,128)(2,1)S(1)}, u32[]{:S(2)}) copy-start(bf16[16,256]{1,0:T(8,128)(2,1)S(1)} %collective-permute-done.g_oth) | copy-start | bytes 24580
  6.2 3.7 %collective-permute-start.2 = (bf16[4,256,512]{2,1,0:T(8,128)(2,1)}, bf16[4,256,512]{2,1,0:T(8,128)(2,1)S(1)}, u32[]{:S(2)}, u32[]{:S(2)}) collective-permute-start(bf16[4,256,512]{2,1,0:T(8,128)(2,1)} %get-tuple-element.49), channel_id=1, source_target_pairs={{0,1},{1,0},{2,3},{3,2},{4,5},{5,4},{6,7},{7,6},{8,9},{9,8},{10,11... | collective-permute-start | bytes 3145736 | tf_op jit(solution)/shard_map/ppermute | solution.py:364
  6.3 3.6 %collective-permute-start.1 = (bf16[4,256,256]{2,1,0:T(8,128)(2,1)}, bf16[4,256,256]{2,1,0:T(8,128)(2,1)S(1)}, u32[]{:S(2)}, u32[]{:S(2)}) collective-permute-start(bf16[4,256,256]{2,1,0:T(8,128)(2,1)} %get-tuple-element.48), channel_id=1, source_target_pairs={{0,1},{1,0},{2,3},{3,2},{4,5},{5,4},{6,7},{7,6},{8,9},{9,8},{10,11... | collective-permute-start | bytes 1572872 | tf_op jit(solution)/shard_map/ppermute | solution.py:364
  9.9 0.8 copy-start.2
  9.9 1.2 %copy-start.1 = (bf16[4,256,512]{2,1,0:T(8,128)(2,1)}, bf16[4,256,512]{2,1,0:T(8,128)(2,1)S(1)}, u32[]{:S(2)}) copy-start(bf16[4,256,512]{2,1,0:T(8,128)(2,1)S(1)} %collective-permute-done.2.refs_3_.refs_5_) | copy-start | bytes 3145732
  15.2 10.3 %collective-permute-start.4 = (bf16[272,512]{1,0:T(8,128)(2,1)}, bf16[272,512]{1,0:T(8,128)(2,1)S(1)}, u32[]{:S(2)}, u32[]{:S(2)}) collective-permute-start(bf16[272,512]{1,0:T(8,128)(2,1)} %get-tuple-element.66), channel_id=1, source_target_pairs={{0,2},{1,3},{2,0},{3,1},{4,6},{5,7},{6,4},{7,5},{8,10},{9,11},{10,... | collective-permute-start | bytes 835592 | tf_op jit(solution)/shard_map/ppermute | solution.py:368
  17.8 14.8 %collective-permute-start.5 = (bf16[272,512]{1,0:T(8,128)(2,1)}, bf16[272,512]{1,0:T(8,128)(2,1)S(1)}, u32[]{:S(2)}, u32[]{:S(2)}) collective-permute-start(bf16[272,512]{1,0:T(8,128)(2,1)} %get-tuple-element.67), channel_id=1, source_target_pairs={{0,4},{1,5},{2,6},{3,7},{4,0},{5,1},{6,2},{7,3},{8,12},{9,13},{10,... | collective-permute-start | bytes 835592 | tf_op jit(solution)/shard_map/ppermute | solution.py:368
  19.4 13.3 %collective-permute-start.6 = (bf16[272,512]{1,0:T(8,128)(2,1)}, bf16[272,512]{1,0:T(8,128)(2,1)S(1)}, u32[]{:S(2)}, u32[]{:S(2)}) collective-permute-start(bf16[272,512]{1,0:T(8,128)(2,1)} %get-tuple-element.68), channel_id=1, source_target_pairs={{0,6},{1,7},{2,4},{3,5},{4,2},{5,3},{6,0},{7,1},{8,14},{9,15},{10,... | collective-permute-start | bytes 835592 | tf_op jit(solution)/shard_map/ppermute | solution.py:368
  25.6 7.1 %copy-start.3 = (bf16[272,512]{1,0:T(8,128)(2,1)}, bf16[272,512]{1,0:T(8,128)(2,1)S(1)}, u32[]{:S(2)}) copy-start(bf16[272,512]{1,0:T(8,128)(2,1)S(1)} %collective-permute-done.4.refs_1_) | copy-start | bytes 835588
  32.7 0.7 copy-start.4
  32.7 0.8 copy-start.5
  35.7 9.0 %collective-permute-start.7 = (bf16[272,512]{1,0:T(8,128)(2,1)}, bf16[272,512]{1,0:T(8,128)(2,1)S(1)}, u32[]{:S(2)}, u32[]{:S(2)}) collective-permute-start(bf16[272,512]{1,0:T(8,128)(2,1)} %group_total.1), channel_id=1, source_target_pairs={{0,8},{1,9},{2,10},{3,11},{4,12},{5,13},{6,14},{7,15},{8,16},{9,17... | collective-permute-start | bytes 835592 | tf_op jit(solution)/shard_map/ppermute | solution.py:372
  41.9 7.2 %collective-permute-start.3 = (bf16[4,256,256]{2,1,0:T(8,128)(2,1)}, bf16[4,256,256]{2,1,0:T(8,128)(2,1)S(1)}, u32[]{:S(2)}, u32[]{:S(2)}) collective-permute-start(bf16[4,256,256]{2,1,0:T(8,128)(2,1)} %get-tuple-element.57), channel_id=1, source_target_pairs={{0,1},{1,0},{2,3},{3,2},{4,5},{5,4},{6,7},{7,6},{8,9},{9,8},{10,11... | collective-permute-start | bytes 1572872 | tf_op jit(solution)/shard_map/ppermute | solution.py:364
  44.8 13.1 %copy-start.10 = (bf16[272,512]{1,0:T(8,128)(2,1)}, bf16[272,512]{1,0:T(8,128)(2,1)S(1)}, u32[]{:S(2)}) copy-start(bf16[272,512]{1,0:T(8,128)(2,1)S(1)} %collective-permute-done.7.refs_4_) | copy-start | bytes 835588
  44.8 13.1 %collective-permute-start.8 = (bf16[272,512]{1,0:T(8,128)(2,1)S(1)}, bf16[272,512]{1,0:T(8,128)(2,1)S(1)}, u32[]{:S(2)}, u32[]{:S(2)}) collective-permute-start(bf16[272,512]{1,0:T(8,128)(2,1)S(1)} %collective-permute-done.7.refs_4_), channel_id=1, source_target_pairs={{0,8},{1,9},{2,10},{3,11},{4,12},{5,13},{6,14},{7,15},{8,16},{9,17... | collective-permute-start | bytes 835592 | tf_op jit(solution)/shard_map/ppermute | solution.py:372
  49.1 0.8 copy-start
  57.9 0.7 copy-start.11
  61.7 9.7 %collective-permute-start.10 = (bf16[272,512]{1,0:T(8,128)(2,1)}, bf16[272,512]{1,0:T(8,128)(2,1)S(1)}, u32[]{:S(2)}, u32[]{:S(2)}) collective-permute-start(bf16[272,512]{1,0:T(8,128)(2,1)} %get-tuple-element.73), channel_id=1, source_target_pairs={{0,2},{1,3},{2,0},{3,1},{4,6},{5,7},{6,4},{7,5},{8,10},{9,11},{10,... | collective-permute-start | bytes 835592 | tf_op jit(solution)/shard_map/ppermute | solution.py:368
  63.2 12.8 %collective-permute-start.11 = (bf16[272,512]{1,0:T(8,128)(2,1)}, bf16[272,512]{1,0:T(8,128)(2,1)S(1)}, u32[]{:S(2)}, u32[]{:S(2)}) collective-permute-start(bf16[272,512]{1,0:T(8,128)(2,1)} %get-tuple-element.74), channel_id=1, source_target_pairs={{0,4},{1,5},{2,6},{3,7},{4,0},{5,1},{6,2},{7,3},{8,12},{9,13},{10,... | collective-permute-start | bytes 835592 | tf_op jit(solution)/shard_map/ppermute | solution.py:368
  63.7 12.3 %collective-permute-start.12 = (bf16[272,512]{1,0:T(8,128)(2,1)}, bf16[272,512]{1,0:T(8,128)(2,1)S(1)}, u32[]{:S(2)}, u32[]{:S(2)}) collective-permute-start(bf16[272,512]{1,0:T(8,128)(2,1)} %get-tuple-element.75), channel_id=1, source_target_pairs={{0,6},{1,7},{2,4},{3,5},{4,2},{5,3},{6,0},{7,1},{8,14},{9,15},{10,... | collective-permute-start | bytes 835592 | tf_op jit(solution)/shard_map/ppermute | solution.py:368
  68.9 1.7 %collective-permute-start.9 = (bf16[1,256,512]{2,1,0:T(8,128)(2,1)}, bf16[1,256,512]{2,1,0:T(8,128)(2,1)S(1)}, u32[]{:S(2)}, u32[]{:S(2)}) collective-permute-start(bf16[1,256,512]{2,1,0:T(8,128)(2,1)} %get-tuple-element.71), channel_id=1, source_target_pairs={{0,1},{1,0},{2,3},{3,2},{4,5},{5,4},{6,7},{7,6},{8,9},{9,8},{10,11... | collective-permute-start | bytes 786440 | tf_op jit(solution)/shard_map/ppermute | solution.py:364
  70.7 13.9 %copy-start.12 = (bf16[1,256,512]{2,1,0:T(8,128)(2,1)}, bf16[1,256,512]{2,1,0:T(8,128)(2,1)S(1)}, u32[]{:S(2)}) copy-start(bf16[1,256,512]{2,1,0:T(8,128)(2,1)S(1)} %collective-permute-done.9.refs_2_) | copy-start | bytes 786436
  71.5 4.6 %copy-start.7 = (bf16[272,512]{1,0:T(8,128)(2,1)}, bf16[272,512]{1,0:T(8,128)(2,1)S(1)}, u32[]{:S(2)}) copy-start(bf16[272,512]{1,0:T(8,128)(2,1)S(1)} %collective-permute-done.10.refs_0_) | copy-start | bytes 835588
  76.0 0.7 copy-start.8
  76.7 0.7 copy-start.9
  82.1 2.5 %collective-permute-start.13 = (bf16[3,256,512]{2,1,0:T(8,128)(2,1)}, bf16[3,256,512]{2,1,0:T(8,128)(2,1)S(1)}, u32[]{:S(2)}, u32[]{:S(2)}) collective-permute-start(bf16[3,256,512]{2,1,0:T(8,128)(2,1)} %get-tuple-element.78), channel_id=1, source_target_pairs={{0,1},{1,0},{2,3},{3,2},{4,5},{5,4},{6,7},{7,6},{8,9},{9,8},{10,11... | collective-permute-start | bytes 2359304 | tf_op jit(solution)/shard_map/ppermute | solution.py:364
  84.6 0.9 copy-start.6

commit v8 on v7

--- a/solution.py
+++ b/solution.py
@@ -90,11 +90,11 @@
     return ((inside % heads == out // n) & (inside // heads == out % n)).astype(BF16)
 
 
-def relayout_kernel(half, count, scalars, *refs):
+def relayout_kernel(half, count, *refs):
     sources, outs = refs[:count], refs[count:]
     heads = 2 * half
     n = LAY // heads
-    core = scalars[1]
+    core = lax.axis_index("hv") % 2
     order = by_head_order(heads)
     for index, source in enumerate(sources):
         keep, send = outs[index], outs[count + index]
@@ -224,15 +224,15 @@
     weighted(list(states) + list(totals), outs, lines)
 
 
-def local_kernel(heads, scalars, *refs):
+def local_kernel(first_slot, heads, scalars, *refs):
     q_own, k_own, v_own, q_oth, k_oth, v_oth, source_rows, decay_rows, columns, ids_ref = refs[:10]
-    numerators, stats = refs[10:]
+    numerators, stats = refs[-2:]
     step = pl.program_id(0)
     mine, core = scalars[0], scalars[1]
     tokens, key_width = q_own.shape[1:]
     length = 2 * tokens
     scaling = key_width**-0.5
-    head = (heads // 2) * core + jnp.bitwise_xor(mine, step)
+    head = (heads // 2) * core + jnp.bitwise_xor(mine, first_slot + step)
     is_first = core == 0
     source = source_rows[pl.ds(head, 1), :]
     lane = iota((length, LANES), 1)
@@ -282,19 +282,33 @@
 
 
 def output_kernel(first, count, scalars, q_own, q_oth, numerators, stats, *refs):
-    entering, (keep, send) = refs[:count], refs[count:]
+    entering, (keep, send, near_terms, queries, landed) = refs[:count], refs[count:]
     key_width = q_own.shape[2]
     scaling = key_width**-0.5
+    copies = []
+    for i in range(count):
+        local_head = jnp.bitwise_xor(scalars[0], first + i)
+        moves = [
+            (q_own.at[local_head], queries.at[i, 0]),
+            (q_oth.at[local_head], queries.at[i, 1]),
+            (numerators.at[first + i], near_terms.at[i]),
+        ]
+        copies.append(
+            [pltpu.make_async_copy(x, y, landed.at[i, n]) for n, (x, y) in enumerate(moves)]
+        )
+        for copy in copies[-1]:
+            copy.start()
     for i, payload in enumerate(entering):
         at = first + i
-        local_head = jnp.bitwise_xor(scalars[0], first + i)
+        for copy in copies[i]:
+            copy.wait()
         normal, top, _, doc = read_meta([payload])
         pieces = split3(normal) + (jnp.zeros((META - 3, key_width), F32),)
         pieces = jnp.concatenate(pieces, axis=0).astype(BF16)
         memory = payload[:key_width, :]
         width = memory.shape[1]
-        for side, (q_ref, out) in enumerate(((q_own, keep), (q_oth, send))):
-            query = q_ref[local_head]
+        for side, out in enumerate((keep, send)):
+            query = queries[i, side]
             tokens = query.shape[0]
             stat = stats[at, side]
             local = stat[0:1]
@@ -309,7 +323,7 @@
             inverse = 1.0 / jnp.maximum(jnp.abs(denominator), 1.0)
             near = jnp.broadcast_to(shrink * inverse, (LANES, tokens)).T
             far = jnp.broadcast_to(retained * inverse, (LANES, tokens)).T
-            result = wide(near, width) * numerators[at, side]
+            result = wide(near, width) * near_terms[i, side]
             out[i] = (result + wide(far, width) * dot(query, memory)).astype(BF16)
 
 
@@ -341,6 +355,7 @@
 
 
 SMEM = pl.BlockSpec(memory_space=pltpu.SMEM)
+HERE = pl.BlockSpec(memory_space=pl.ANY)
 
 
 def shape_of(*dims, dtype=BF16):
@@ -379,12 +394,12 @@
         outs = [sizes[x.shape[2]] for x in sources] * 2
         return pl.pallas_call(
             functools.partial(relayout_kernel, half, len(sources)),
-            in_specs=[SMEM] + [whole(x.shape) for x in sources],
+            in_specs=[whole(x.shape) for x in sources],
             out_specs=[whole(s) for s in outs],
             out_shape=[shape_of(*s) for s in outs],
             compiler_params=params(),
-            name="relayout",
-        )(scalars, *sources)
+                name="relayout",
+        )(*sources)
 
     gates = jnp.concatenate([input_gate.T, forget_gate.T], axis=0)
     gates, key_vectors = lax.optimization_barrier((gates, key_vectors))
@@ -410,8 +425,10 @@
         name="gates",
     )(scalars, gates, gates_oth, ids)
 
-    def by_slot(x):
-        return pl.BlockSpec((1,) + x.shape[1:], lambda i, s: (jnp.bitwise_xor(s[0], i), 0, 0))
+    def by_slot(x, first_slot):
+        return pl.BlockSpec(
+            (1,) + x.shape[1:], lambda i, s: (jnp.bitwise_xor(s[0], first_slot + i), 0, 0)
+        )
 
     by_core = (k_keep, v_keep, k_oth, v_oth, factors, tops, decays, ids)
     made = pl.pallas_call(
@@ -431,31 +448,42 @@
         compiler_params=params(),
         name="group_total",
     )(scalars, *gathered)
-    totals = [to_next(total)]
-    while len(totals) < reach:
-        totals.append(to_next(totals[-1]))
-
     queries, gathered[0] = lax.optimization_barrier((queries, gathered[0]))
     q_keep, q_send = relayout(queries)
     q_oth = swap_cores(q_send)
-    by_head = (q_keep, k_keep, v_keep, q_oth, k_oth, v_oth)
     small = (source_rows, decay_rows, columns, ids)
     local_shapes = [(half, 2, tokens, value_width), (half, 2, 8, tokens)]
-    numerators, stats = pl.pallas_call(
-        functools.partial(local_kernel, heads),
-        grid_spec=pltpu.PrefetchScalarGridSpec(
-            num_scalar_prefetch=1,
-            grid=(group,),
-            in_specs=[by_slot(x) for x in by_head] + [whole(x.shape) for x in small],
-            out_specs=[
-                pl.BlockSpec((1,) + s[1:], lambda i, _: (i, 0, 0, 0)) for s in local_shapes
-            ],
-        ),
-        out_shape=[shape_of(*s, dtype=F32) for s in local_shapes],
-        compiler_params=params(),
-        name="own_terms",
-    )(scalars, *by_head, *small)
-    gathered[0], numerators = lax.optimization_barrier((gathered[0], numerators))
+
+    def own_terms(first_slot, count, q_own, into):
+        by_head = (q_own, k_keep, v_keep, q_oth, k_oth, v_oth)
+        return pl.pallas_call(
+            functools.partial(local_kernel, first_slot, heads),
+            grid_spec=pltpu.PrefetchScalarGridSpec(
+                num_scalar_prefetch=1,
+                grid=(count,),
+                in_specs=[by_slot(x, first_slot) for x in by_head]
+                + [whole(x.shape) for x in small]
+                + [HERE] * len(into),
+                out_specs=[
+                    pl.BlockSpec((1,) + s[1:], lambda i, _: (first_slot + i, 0, 0, 0))
+                    for s in local_shapes
+                ],
+            ),
+            out_shape=[shape_of(*s, dtype=F32) for s in local_shapes],
+            input_output_aliases={11 + i: i for i in range(len(into))},
+            compiler_params=params(),
+            name="own_terms",
+        )(scalars, *by_head, *small, *into)
+
+    early = half // 2
+    q_first, _ = lax.optimization_barrier((q_keep, total))
+    terms = own_terms(0, early, q_first, ())
+    totals = [to_next(total)]
+    totals[0], terms = lax.optimization_barrier((totals[0], terms))
+    while len(totals) < reach:
+        totals.append(to_next(totals[-1]))
+    terms = own_terms(early, half - early, q_keep, terms)
+    gathered[0], (numerators, stats) = lax.optimization_barrier((gathered[0], terms))
 
     leaving = pl.pallas_call(
         functools.partial(entering_kernel, group, reach),
@@ -470,10 +498,13 @@
     def outputs(first, count):
         return pl.pallas_call(
             functools.partial(output_kernel, first, count),
-            in_specs=[SMEM, whole(q_keep.shape), whole(q_oth.shape)]
-            + [whole(x) for x in local_shapes]
-            + [whole(state)] * count,
+            in_specs=[SMEM, HERE, HERE, HERE, whole(local_shapes[1])] + [whole(state)] * count,
             out_specs=[whole((count, tokens, value_width))] * 2,
+            scratch_shapes=[
+                pltpu.VMEM((count, 2, tokens, value_width), F32),
+                pltpu.VMEM((count, 2, tokens, key_width), BF16),
+                pltpu.SemaphoreType.DMA((count, 3)),
+            ],
             out_shape=[shape_of(count, tokens, value_width)] * 2,
             compiler_params=params(),
             name="outputs",

time: 89.5 us -> 86.4 us (0.965)
  the two profiles are of different devices: /device:TPU:0 before, /device:TPU:25 now
where the time goes in v8:
time: 86.4 us; the launch traced here: 84.7 us
  Pallas kernels  41.1 us (48%)
  starting transfers between devices  20.3 us (23%)
  waiting for transfers between devices  15.6 us (18%)
  local copies, waits for them, and re-layouts  6.37 us (7%)
  other arithmetic  1.26 us (1%)
    pallas_call x2, Pallas kernels, own_terms(): pl.pallas_call(functools.partial(local_kernel, first_slot, heads), grid_s...  10.6 us
    ppermute x6, starting transfers between devices, swap_cores(): return lax.ppermute(x, AXES, [(d, d ^ 1) for d in range(devices)])  10.6 us
    ppermute x6, waiting for transfers between devices, in_group(): return lax.ppermute(x, AXES, pairs)  10.3 us
    pallas_call x2, Pallas kernels, outputs(): pl.pallas_call(functools.partial(output_kernel, first, count), in_specs=[...  8.57 us
    ppermute x6, starting transfers between devices, in_group(): return lax.ppermute(x, AXES, pairs)  7.14 us
    pallas_call x2, Pallas kernels, relayout(): pl.pallas_call(functools.partial(relayout_kernel, half, len(sources)), in...  7.05 us
    unnamed x30, local copies, waits for them, and re-layouts  5.02 us
    pallas_call x1, Pallas kernels, local(): pl.pallas_call(functools.partial(state_kernel, heads), in_specs=[SMEM] +...  4.15 us
  transfers between devices with their start and end apart: 14, of which 8 were waited for; matrix products, arithmetic and copies ran while one was open for 2% of the time, Pallas kernels for 30%

profile of v8, /device:TPU:25, one launch (start us, length us, event | category | flops | bytes accessed | tf_op | source)
XLA Modules:
  0.0 84.7 jit_solution(17167089496525514185)
XLA Ops:
  0.0 0.7 pad_maximum_fusion.g_own
  0.7 0.0 copy-start.13
  0.7 0.7 collective-permute-start
  1.4 4.4 %relayout.2 = (bf16[4,256,256]{2,1,0:T(8,128)(2,1)}, bf16[4,256,512]{2,1,0:T(8,128)(2,1)}, bf16[4,256,256]{2,1,0:T(8,128)(2,1)}, bf16[4,256,512]{2,1,0:T(8,128)(2,1)}) custom-call(bf16[256,8,256]{2,1,0:T(8,128)(2,1)} %refs_0_, bf16[256,8,512]{2,1,0:T(8,128)(2,1)} %refs_1_.1), custom_call_target="tpu_custom_call" | custom-call | tf_op jit(solution)/shard_map/relayout/pallas_call | solution.py:395
  5.8 0.0 collective-permute-done.g_oth
  5.8 0.0 copy-start.14
  5.8 0.0 collective-permute-start.2
  5.8 0.5 collective-permute-start.1
  6.3 1.4 %dynamic_slice.3 = s32[512]{0:T(512)} dynamic-slice(s32[1024]{0:T(1024)} %param.11, s32[]{:T(128)S(6)} %select_n.22), dynamic_slice_sizes={512} | dynamic-slice | bytes 4100 | tf_op jit(solution)/shard_map/dynamic_slice | solution.py:376
  7.7 0.6 pad_add_fusion.scalars
  8.2 0.0 copy-done.13
  8.2 0.0 copy-done.14
  8.2 1.9 %gates.1 = (f32[8,512]{1,0:T(8,128)}, f32[8,128]{1,0:T(8,128)}, f32[8,128]{1,0:T(8,128)}, f32[8,512]{1,0:T(8,128)}, f32[8,512]{1,0:T(8,128)}, /*index=5*/f32[512,128]{1,0:T(8,128)}) custom-call(s32[2]{0:T(128)} %pad_add_fusion.scalars, bf16[16,256]{1,0:T(8,128)(2,1)} %copy-done.13, bf16[16,256]{1,0:T(8,128)(2,1)} %copy-done.14, s32[1,512]{1,0:T(1,128)} %bitcast.5), custom_call_target="tpu_custom_call" | custom-call | tf_op jit(solution)/shard_map/gates/pallas_call | solution.py:419
  10.1 0.0 collective-permute-done.1.refs_2_.refs_4_
  10.1 0.0 copy-start.2
  10.1 0.0 collective-permute-done.2.refs_3_.refs_5_
  10.1 0.0 copy-start
  10.1 0.7 copy-done.2
  10.9 0.4 copy-done
  11.3 4.2 %states.1 = (bf16[272,512]{1,0:T(8,128)(2,1)}, bf16[272,512]{1,0:T(8,128)(2,1)}, bf16[272,512]{1,0:T(8,128)(2,1)}, bf16[272,512]{1,0:T(8,128)(2,1)}) custom-call(s32[2]{0:T(128)} %pad_add_fusion.scalars, bf16[4,256,256]{2,1,0:T(8,128)(2,1)} %get-tuple-element.50.refs_0_.refs_1_, bf16[4,256,512]{2,1,0:T(8,128)(2,1)} %get-tuple-element.51.refs_1_.refs_2_, ...), custom_call_target="tpu_custom_call" | custom-call | tf_op jit(solution)/shard_map/states/pallas_call | solution.py:434
  15.5 1.2 %collective-permute-start.4 = (bf16[272,512]{1,0:T(8,128)(2,1)}, bf16[272,512]{1,0:T(8,128)(2,1)S(1)}, u32[]{:S(2)}, u32[]{:S(2)}) collective-permute-start(bf16[272,512]{1,0:T(8,128)(2,1)} %get-tuple-element.69), channel_id=1, source_target_pairs={{0,2},{1,3},{2,0},{3,1},{4,6},{5,7},{6,4},{7,5},{8,10},{9,11},{10,... | collective-permute-start | bytes 835592 | tf_op jit(solution)/shard_map/ppermute | solution.py:383
  16.7 1.2 %collective-permute-start.5 = (bf16[272,512]{1,0:T(8,128)(2,1)}, bf16[272,512]{1,0:T(8,128)(2,1)S(1)}, u32[]{:S(2)}, u32[]{:S(2)}) collective-permute-start(bf16[272,512]{1,0:T(8,128)(2,1)} %get-tuple-element.70), channel_id=1, source_target_pairs={{0,4},{1,5},{2,6},{3,7},{4,0},{5,1},{6,2},{7,3},{8,12},{9,13},{10,... | collective-permute-start | bytes 835592 | tf_op jit(solution)/shard_map/ppermute | solution.py:383
  17.9 0.2 collective-permute-start.6
  18.1 2.7 %relayout.3 = (bf16[4,256,256]{2,1,0:T(8,128)(2,1)}, bf16[4,256,256]{2,1,0:T(8,128)(2,1)}) custom-call(bf16[256,8,256]{2,1,0:T(8,128)(2,1)} %refs_0_.1), custom_call_target="tpu_custom_call" | custom-call | tf_op jit(solution)/shard_map/relayout/pallas_call | solution.py:395
  20.8 0.9 %collective-permute-start.3 = (bf16[4,256,256]{2,1,0:T(8,128)(2,1)}, bf16[4,256,256]{2,1,0:T(8,128)(2,1)S(1)}, u32[]{:S(2)}, u32[]{:S(2)}) collective-permute-start(bf16[4,256,256]{2,1,0:T(8,128)(2,1)} %get-tuple-element.64), channel_id=1, source_target_pairs={{0,1},{1,0},{2,3},{3,2},{4,5},{5,4},{6,7},{7,6},{8,9},{9,8},{10,11... | collective-permute-start | bytes 1572872 | tf_op jit(solution)/shard_map/ppermute | solution.py:379
  21.7 2.1 %collective-permute-done.4.refs_1_ = bf16[272,512]{1,0:T(8,128)(2,1)S(1)} collective-permute-done((bf16[272,512]{1,0:T(8,128)(2,1)}, bf16[272,512]{1,0:T(8,128)(2,1)S(1)}, u32[]{:S(2)}, u32[]{:S(2)}) %collective-permute-start.4) | collective-permute-done | bytes 278560 | tf_op jit(solution)/shard_map/ppermute | solution.py:383
  23.8 0.0 copy-start.3
  23.8 5.9 %collective-permute-done.5.refs_2_ = bf16[272,512]{1,0:T(8,128)(2,1)S(1)} collective-permute-done((bf16[272,512]{1,0:T(8,128)(2,1)}, bf16[272,512]{1,0:T(8,128)(2,1)S(1)}, u32[]{:S(2)}, u32[]{:S(2)}) %collective-permute-start.5) | collective-permute-done | bytes 278560 | tf_op jit(solution)/shard_map/ppermute | solution.py:383
  29.7 1.1 %collective-permute-done.6.refs_3_ = bf16[272,512]{1,0:T(8,128)(2,1)S(1)} collective-permute-done((bf16[272,512]{1,0:T(8,128)(2,1)}, bf16[272,512]{1,0:T(8,128)(2,1)S(1)}, u32[]{:S(2)}, u32[]{:S(2)}) %collective-permute-start.6) | collective-permute-done | bytes 278560 | tf_op jit(solution)/shard_map/ppermute | solution.py:383
  30.8 0.0 copy-done.3
  30.8 0.0 copy-done.4
  30.8 0.7 copy-done.5
  31.5 2.2 %group_total.1 = bf16[272,512]{1,0:T(8,128)(2,1)} custom-call(s32[2]{0:T(128)} %pad_add_fusion.scalars, bf16[272,512]{1,0:T(8,128)(2,1)} %get-tuple-element.81.refs_0_, bf16[272,512]{1,0:T(8,128)(2,1)} %copy-done.3, bf16[272,512]{1,0:T(8,128)(2,1)} %copy-done.4, bf16[272,512]{1,0:T(8,128)(2,1)} %copy-done.5), custom_call_target="tpu_custom_call" | custom-call | tf_op jit(solution)/shard_map/group_total/pallas_call | solution.py:443
  33.7 1.3 %collective-permute-start.7 = (bf16[272,512]{1,0:T(8,128)(2,1)}, bf16[272,512]{1,0:T(8,128)(2,1)S(1)}, u32[]{:S(2)}, u32[]{:S(2)}) collective-permute-start(bf16[272,512]{1,0:T(8,128)(2,1)} %group_total.1), channel_id=1, source_target_pairs={{0,8},{1,9},{2,10},{3,11},{4,12},{5,13},{6,14},{7,15},{8,16},{9,17... | collective-permute-start | bytes 835592 | tf_op jit(solution)/shard_map/ppermute | solution.py:387
  35.0 0.0 collective-permute-done.3.refs_3_.q_oth
  35.0 0.0 copy-start.1
  35.0 0.8 copy-done.1
  35.8 5.3 %own_terms.2 = (f32[4,2,256,512]{3,2,1,0:T(8,128)}, f32[4,2,8,256]{3,2,1,0:T(8,128)}) custom-call(s32[2]{0:T(128)} %pad_add_fusion.scalars, bf16[4,256,256]{2,1,0:T(8,128)(2,1)} %get-tuple-element.72.refs_0_.q_own, bf16[4,256,256]{2,1,0:T(8,128)(2,1)} %get-tuple-element.50.refs_0_.refs_1_, bf16[4,256,512]{2,1,0:T(8,128)(2,1)} %get-tuple-element.51.refs_1_.refs_2_, ...), custom_call_target="tpu_custom_call" | custom-call | tf_op jit(solution)/shard_map/own_terms/pallas_call | solution.py:459
  41.1 1.1 %collective-permute-done.7.refs_4_ = bf16[272,512]{1,0:T(8,128)(2,1)S(1)} collective-permute-done((bf16[272,512]{1,0:T(8,128)(2,1)}, bf16[272,512]{1,0:T(8,128)(2,1)S(1)}, u32[]{:S(2)}, u32[]{:S(2)}) %collective-permute-start.7) | collective-permute-done | bytes 278560 | tf_op jit(solution)/shard_map/ppermute | solution.py:387
  42.2 1.3 %collective-permute-start.8 = (bf16[272,512]{1,0:T(8,128)(2,1)S(1)}, bf16[272,512]{1,0:T(8,128)(2,1)S(1)}, u32[]{:S(2)}, u32[]{:S(2)}) collective-permute-start(bf16[272,512]{1,0:T(8,128)(2,1)S(1)} %collective-permute-done.7.refs_4_), channel_id=1, source_target_pairs={{0,8},{1,9},{2,10},{3,11},{4,12},{5,13},{6,14},{7,15},{8,16},{9,17... | collective-permute-start | bytes 835592 | tf_op jit(solution)/shard_map/ppermute | solution.py:387
  43.5 5.3 %own_terms.3 = (f32[4,2,256,512]{3,2,1,0:T(8,128)}, f32[4,2,8,256]{3,2,1,0:T(8,128)}) custom-call(s32[2]{0:T(128)} %pad_add_fusion.scalars, bf16[4,256,256]{2,1,0:T(8,128)(2,1)} %get-tuple-element.72.refs_0_.q_own, bf16[4,256,256]{2,1,0:T(8,128)(2,1)} %get-tuple-element.50.refs_0_.refs_1_, ...), custom_call_target="tpu_custom_call", output_to_operand_aliasing={{0}: (11, {}), {1}: (12, {})} | custom-call | tf_op jit(solution)/shard_map/own_terms/pallas_call | solution.py:459
  48.8 0.0 copy-done.10
  48.8 0.7 collective-permute-done.8.refs_5_
  49.5 0.7 copy-done.11
  50.2 3.1 %entering.1 = (bf16[272,512]{1,0:T(8,128)(2,1)}, bf16[272,512]{1,0:T(8,128)(2,1)}, bf16[272,512]{1,0:T(8,128)(2,1)}, bf16[272,512]{1,0:T(8,128)(2,1)}) custom-call(s32[2]{0:T(128)} %pad_add_fusion.scalars, bf16[272,512]{1,0:T(8,128)(2,1)} %get-tuple-element.81.refs_0_, bf16[272,512]{1,0:T(8,128)(2,1)} %copy-done.3, bf16[272,512]{1,0:T(8,128)(2,1)} %copy-done.4, ...), custom_call_target="tpu_custom_call" | custom-call | tf_op jit(solution)/shard_map/entering/pallas_call | solution.py:488
  53.3 3.1 %collective-permute-start.10 = (bf16[272,512]{1,0:T(8,128)(2,1)}, bf16[272,512]{1,0:T(8,128)(2,1)S(1)}, u32[]{:S(2)}, u32[]{:S(2)}) collective-permute-start(bf16[272,512]{1,0:T(8,128)(2,1)} %get-tuple-element.87), channel_id=1, source_target_pairs={{0,2},{1,3},{2,0},{3,1},{4,6},{5,7},{6,4},{7,5},{8,10},{9,11},{10,... | collective-permute-start | bytes 835592 | tf_op jit(solution)/shard_map/ppermute | solution.py:383
  56.4 0.2 collective-permute-start.11
  56.6 1.2 %collective-permute-start.12 = (bf16[272,512]{1,0:T(8,128)(2,1)}, bf16[272,512]{1,0:T(8,128)(2,1)S(1)}, u32[]{:S(2)}, u32[]{:S(2)}) collective-permute-start(bf16[272,512]{1,0:T(8,128)(2,1)} %get-tuple-element.89), channel_id=1, source_target_pairs={{0,6},{1,7},{2,4},{3,5},{4,2},{5,3},{6,0},{7,1},{8,14},{9,15},{10,... | collective-permute-start | bytes 835592 | tf_op jit(solution)/shard_map/ppermute | solution.py:383
  57.8 3.6 %outputs.2 = (bf16[1,256,512]{2,1,0:T(8,128)(2,1)}, bf16[1,256,512]{2,1,0:T(8,128)(2,1)}) custom-call(s32[2]{0:T(128)} %pad_add_fusion.scalars, bf16[4,256,256]{2,1,0:T(8,128)(2,1)} %get-tuple-element.72.refs_0_.q_own, bf16[4,256,256]{2,1,0:T(8,128)(2,1)} %copy-done.1, f32[4,2,256,512]{3,2,1,0:T(8,128)} %get-tuple-element.86.numerators, ...), custom_call_target="tpu_custom_call" | custom-call | tf_op jit(solution)/shard_map/outputs/pallas_call | solution.py:499
  61.3 3.5 %collective-permute-start.9 = (bf16[1,256,512]{2,1,0:T(8,128)(2,1)}, bf16[1,256,512]{2,1,0:T(8,128)(2,1)S(1)}, u32[]{:S(2)}, u32[]{:S(2)}) collective-permute-start(bf16[1,256,512]{2,1,0:T(8,128)(2,1)} %get-tuple-element.85), channel_id=1, source_target_pairs={{0,1},{1,0},{2,3},{3,2},{4,5},{5,4},{6,7},{7,6},{8,9},{9,8},{10,11... | collective-permute-start | bytes 786440 | tf_op jit(solution)/shard_map/ppermute | solution.py:379
  64.9 1.4 %collective-permute-done.9.refs_2_ = bf16[1,256,512]{2,1,0:T(8,128)(2,1)S(1)} collective-permute-done((bf16[1,256,512]{2,1,0:T(8,128)(2,1)}, bf16[1,256,512]{2,1,0:T(8,128)(2,1)S(1)}, u32[]{:S(2)}, u32[]{:S(2)}) %collective-permute-start.9) | collective-permute-done | bytes 262176 | tf_op jit(solution)/shard_map/ppermute | solution.py:379
  66.2 0.0 collective-permute-done.10.refs_0_
  66.3 0.0 collective-permute-done.11.refs_1_
  66.3 0.0 copy-start.8
  66.3 1.2 %collective-permute-done.12.refs_2_ = bf16[272,512]{1,0:T(8,128)(2,1)S(1)} collective-permute-done((bf16[272,512]{1,0:T(8,128)(2,1)}, bf16[272,512]{1,0:T(8,128)(2,1)S(1)}, u32[]{:S(2)}, u32[]{:S(2)}) %collective-permute-start.12) | collective-permute-done | bytes 278560 | tf_op jit(solution)/shard_map/ppermute | solution.py:383
  67.5 0.0 copy-done.7
  67.5 0.0 copy-done.8
  67.5 0.7 copy-done.9
  68.2 5.0 %outputs.3 = (bf16[3,256,512]{2,1,0:T(8,128)(2,1)}, bf16[3,256,512]{2,1,0:T(8,128)(2,1)}) custom-call(s32[2]{0:T(128)} %pad_add_fusion.scalars, bf16[4,256,256]{2,1,0:T(8,128)(2,1)} %get-tuple-element.72.refs_0_.q_own, bf16[4,256,256]{2,1,0:T(8,128)(2,1)} %copy-done.1, f32[4,2,256,512]{3,2,1,0:T(8,128)} %get-tuple-element.86.numerators, ...), custom_call_target="tpu_custom_call" | custom-call | tf_op jit(solution)/shard_map/outputs/pallas_call | solution.py:499
  73.2 4.9 %collective-permute-start.13 = (bf16[3,256,512]{2,1,0:T(8,128)(2,1)}, bf16[3,256,512]{2,1,0:T(8,128)(2,1)S(1)}, u32[]{:S(2)}, u32[]{:S(2)}) collective-permute-start(bf16[3,256,512]{2,1,0:T(8,128)(2,1)} %get-tuple-element.92), channel_id=1, source_target_pairs={{0,1},{1,0},{2,3},{3,2},{4,5},{5,4},{6,7},{7,6},{8,9},{9,8},{10,11... | collective-permute-start | bytes 2359304 | tf_op jit(solution)/shard_map/ppermute | solution.py:379
  78.2 2.1 %collective-permute-done.13.refs_3_ = bf16[3,256,512]{2,1,0:T(8,128)(2,1)S(1)} collective-permute-done((bf16[3,256,512]{2,1,0:T(8,128)(2,1)}, bf16[3,256,512]{2,1,0:T(8,128)(2,1)S(1)}, u32[]{:S(2)}, u32[]{:S(2)}) %collective-permute-start.13) | collective-permute-done | bytes 786464 | tf_op jit(solution)/shard_map/ppermute | solution.py:379
  80.3 0.0 copy-done.12
  80.3 0.9 %copy-done.6 = bf16[3,256,512]{2,1,0:T(8,128)(2,1)} copy-done((bf16[3,256,512]{2,1,0:T(8,128)(2,1)}, bf16[3,256,512]{2,1,0:T(8,128)(2,1)S(1)}, u32[]{:S(2)}) %copy-start.6) | copy-done | bytes 786456
  81.2 3.6 %merge.1 = bf16[256,8,512]{2,1,0:T(8,128)(2,1)} custom-call(s32[2]{0:T(128)} %pad_add_fusion.scalars, bf16[1,256,512]{2,1,0:T(8,128)(2,1)} %get-tuple-element.84.refs_0_, bf16[3,256,512]{2,1,0:T(8,128)(2,1)} %get-tuple-element.90.refs_1_, bf16[1,256,512]{2,1,0:T(8,128)(2,1)} %copy-done.12, bf16[3,256,512]{2,1,0:T(8,128)(2,1)} %copy-done.6), custom_call_target="tpu_custom_call" | custom-call | tf_op jit(solution)/shard_map/merge/pallas_call | solution.py:518
  (8 shorter events, 0.0 us)
Async XLA Ops:
  0.7 7.5 %copy-start.13 = (bf16[16,256]{1,0:T(8,128)(2,1)}, bf16[16,256]{1,0:T(8,128)(2,1)S(1)}, u32[]{:S(2)}) copy-start(bf16[16,256]{1,0:T(8,128)(2,1)S(1)} %pad_maximum_fusion.g_own) | copy-start | bytes 24580
  0.7 5.1 %collective-permute-start = (bf16[16,256]{1,0:T(8,128)(2,1)S(1)}, bf16[16,256]{1,0:T(8,128)(2,1)S(1)}, u32[]{:S(2)}, u32[]{:S(2)}) collective-permute-start(bf16[16,256]{1,0:T(8,128)(2,1)S(1)} %pad_maximum_fusion.g_own), channel_id=1, source_target_pairs={{0,1},{1,0},{2,3},{3,2},{4,5},{5,4},{6,7},{7,6},{8,9},{9,8},{10,11... | collective-permute-start | bytes 24584 | tf_op jit(solution)/shard_map/ppermute | solution.py:379
  5.8 2.4 %copy-start.14 = (bf16[16,256]{1,0:T(8,128)(2,1)}, bf16[16,256]{1,0:T(8,128)(2,1)S(1)}, u32[]{:S(2)}) copy-start(bf16[16,256]{1,0:T(8,128)(2,1)S(1)} %collective-permute-done.g_oth) | copy-start | bytes 24580
  5.8 4.3 %collective-permute-start.2 = (bf16[4,256,512]{2,1,0:T(8,128)(2,1)}, bf16[4,256,512]{2,1,0:T(8,128)(2,1)S(1)}, u32[]{:S(2)}, u32[]{:S(2)}) collective-permute-start(bf16[4,256,512]{2,1,0:T(8,128)(2,1)} %get-tuple-element.56), channel_id=1, source_target_pairs={{0,1},{1,0},{2,3},{3,2},{4,5},{5,4},{6,7},{7,6},{8,9},{9,8},{10,11... | collective-permute-start | bytes 3145736 | tf_op jit(solution)/shard_map/ppermute | solution.py:379
  5.8 4.3 %collective-permute-start.1 = (bf16[4,256,256]{2,1,0:T(8,128)(2,1)}, bf16[4,256,256]{2,1,0:T(8,128)(2,1)S(1)}, u32[]{:S(2)}, u32[]{:S(2)}) collective-permute-start(bf16[4,256,256]{2,1,0:T(8,128)(2,1)} %get-tuple-element.55), channel_id=1, source_target_pairs={{0,1},{1,0},{2,3},{3,2},{4,5},{5,4},{6,7},{7,6},{8,9},{9,8},{10,11... | collective-permute-start | bytes 1572872 | tf_op jit(solution)/shard_map/ppermute | solution.py:379
  10.1 0.8 copy-start.2
  10.1 1.2 %copy-start = (bf16[4,256,512]{2,1,0:T(8,128)(2,1)}, bf16[4,256,512]{2,1,0:T(8,128)(2,1)S(1)}, u32[]{:S(2)}) copy-start(bf16[4,256,512]{2,1,0:T(8,128)(2,1)S(1)} %collective-permute-done.2.refs_3_.refs_5_) | copy-start | bytes 3145732
  15.5 8.4 %collective-permute-start.4 = (bf16[272,512]{1,0:T(8,128)(2,1)}, bf16[272,512]{1,0:T(8,128)(2,1)S(1)}, u32[]{:S(2)}, u32[]{:S(2)}) collective-permute-start(bf16[272,512]{1,0:T(8,128)(2,1)} %get-tuple-element.69), channel_id=1, source_target_pairs={{0,2},{1,3},{2,0},{3,1},{4,6},{5,7},{6,4},{7,5},{8,10},{9,11},{10,... | collective-permute-start | bytes 835592 | tf_op jit(solution)/shard_map/ppermute | solution.py:383
  16.7 13.1 %collective-permute-start.5 = (bf16[272,512]{1,0:T(8,128)(2,1)}, bf16[272,512]{1,0:T(8,128)(2,1)S(1)}, u32[]{:S(2)}, u32[]{:S(2)}) collective-permute-start(bf16[272,512]{1,0:T(8,128)(2,1)} %get-tuple-element.70), channel_id=1, source_target_pairs={{0,4},{1,5},{2,6},{3,7},{4,0},{5,1},{6,2},{7,3},{8,12},{9,13},{10,... | collective-permute-start | bytes 835592 | tf_op jit(solution)/shard_map/ppermute | solution.py:383
  17.9 12.9 %collective-permute-start.6 = (bf16[272,512]{1,0:T(8,128)(2,1)}, bf16[272,512]{1,0:T(8,128)(2,1)S(1)}, u32[]{:S(2)}, u32[]{:S(2)}) collective-permute-start(bf16[272,512]{1,0:T(8,128)(2,1)} %get-tuple-element.71), channel_id=1, source_target_pairs={{0,6},{1,7},{2,4},{3,5},{4,2},{5,3},{6,0},{7,1},{8,14},{9,15},{10,... | collective-permute-start | bytes 835592 | tf_op jit(solution)/shard_map/ppermute | solution.py:383
  20.8 14.2 %collective-permute-start.3 = (bf16[4,256,256]{2,1,0:T(8,128)(2,1)}, bf16[4,256,256]{2,1,0:T(8,128)(2,1)S(1)}, u32[]{:S(2)}, u32[]{:S(2)}) collective-permute-start(bf16[4,256,256]{2,1,0:T(8,128)(2,1)} %get-tuple-element.64), channel_id=1, source_target_pairs={{0,1},{1,0},{2,3},{3,2},{4,5},{5,4},{6,7},{7,6},{8,9},{9,8},{10,11... | collective-permute-start | bytes 1572872 | tf_op jit(solution)/shard_map/ppermute | solution.py:379
  23.8 7.0 %copy-start.3 = (bf16[272,512]{1,0:T(8,128)(2,1)}, bf16[272,512]{1,0:T(8,128)(2,1)S(1)}, u32[]{:S(2)}) copy-start(bf16[272,512]{1,0:T(8,128)(2,1)S(1)} %collective-permute-done.4.refs_1_) | copy-start | bytes 835588
  29.7 1.1 %copy-start.4 = (bf16[272,512]{1,0:T(8,128)(2,1)}, bf16[272,512]{1,0:T(8,128)(2,1)S(1)}, u32[]{:S(2)}) copy-start(bf16[272,512]{1,0:T(8,128)(2,1)S(1)} %collective-permute-done.5.refs_2_) | copy-start | bytes 835588
  30.8 0.7 copy-start.5
  33.7 8.4 %collective-permute-start.7 = (bf16[272,512]{1,0:T(8,128)(2,1)}, bf16[272,512]{1,0:T(8,128)(2,1)S(1)}, u32[]{:S(2)}, u32[]{:S(2)}) collective-permute-start(bf16[272,512]{1,0:T(8,128)(2,1)} %group_total.1), channel_id=1, source_target_pairs={{0,8},{1,9},{2,10},{3,11},{4,12},{5,13},{6,14},{7,15},{8,16},{9,17... | collective-permute-start | bytes 835592 | tf_op jit(solution)/shard_map/ppermute | solution.py:387
  35.0 0.8 copy-start.1
  42.2 6.6 %copy-start.10 = (bf16[272,512]{1,0:T(8,128)(2,1)}, bf16[272,512]{1,0:T(8,128)(2,1)S(1)}, u32[]{:S(2)}) copy-start(bf16[272,512]{1,0:T(8,128)(2,1)S(1)} %collective-permute-done.7.refs_4_) | copy-start | bytes 835588
  42.2 7.3 %collective-permute-start.8 = (bf16[272,512]{1,0:T(8,128)(2,1)S(1)}, bf16[272,512]{1,0:T(8,128)(2,1)S(1)}, u32[]{:S(2)}, u32[]{:S(2)}) collective-permute-start(bf16[272,512]{1,0:T(8,128)(2,1)S(1)} %collective-permute-done.7.refs_4_), channel_id=1, source_target_pairs={{0,8},{1,9},{2,10},{3,11},{4,12},{5,13},{6,14},{7,15},{8,16},{9,17... | collective-permute-start | bytes 835592 | tf_op jit(solution)/shard_map/ppermute | solution.py:387
  49.5 0.7 copy-start.11
  53.3 13.0 %collective-permute-start.10 = (bf16[272,512]{1,0:T(8,128)(2,1)}, bf16[272,512]{1,0:T(8,128)(2,1)S(1)}, u32[]{:S(2)}, u32[]{:S(2)}) collective-permute-start(bf16[272,512]{1,0:T(8,128)(2,1)} %get-tuple-element.87), channel_id=1, source_target_pairs={{0,2},{1,3},{2,0},{3,1},{4,6},{5,7},{6,4},{7,5},{8,10},{9,11},{10,... | collective-permute-start | bytes 835592 | tf_op jit(solution)/shard_map/ppermute | solution.py:383
  56.4 9.8 %collective-permute-start.11 = (bf16[272,512]{1,0:T(8,128)(2,1)}, bf16[272,512]{1,0:T(8,128)(2,1)S(1)}, u32[]{:S(2)}, u32[]{:S(2)}) collective-permute-start(bf16[272,512]{1,0:T(8,128)(2,1)} %get-tuple-element.88), channel_id=1, source_target_pairs={{0,4},{1,5},{2,6},{3,7},{4,0},{5,1},{6,2},{7,3},{8,12},{9,13},{10,... | collective-permute-start | bytes 835592 | tf_op jit(solution)/shard_map/ppermute | solution.py:383
  56.6 10.9 %collective-permute-start.12 = (bf16[272,512]{1,0:T(8,128)(2,1)}, bf16[272,512]{1,0:T(8,128)(2,1)S(1)}, u32[]{:S(2)}, u32[]{:S(2)}) collective-permute-start(bf16[272,512]{1,0:T(8,128)(2,1)} %get-tuple-element.89), channel_id=1, source_target_pairs={{0,6},{1,7},{2,4},{3,5},{4,2},{5,3},{6,0},{7,1},{8,14},{9,15},{10,... | collective-permute-start | bytes 835592 | tf_op jit(solution)/shard_map/ppermute | solution.py:383
  61.3 4.9 %collective-permute-start.9 = (bf16[1,256,512]{2,1,0:T(8,128)(2,1)}, bf16[1,256,512]{2,1,0:T(8,128)(2,1)S(1)}, u32[]{:S(2)}, u32[]{:S(2)}) collective-permute-start(bf16[1,256,512]{2,1,0:T(8,128)(2,1)} %get-tuple-element.85), channel_id=1, source_target_pairs={{0,1},{1,0},{2,3},{3,2},{4,5},{5,4},{6,7},{7,6},{8,9},{9,8},{10,11... | collective-permute-start | bytes 786440 | tf_op jit(solution)/shard_map/ppermute | solution.py:379
  66.2 14.0 %copy-start.12 = (bf16[1,256,512]{2,1,0:T(8,128)(2,1)}, bf16[1,256,512]{2,1,0:T(8,128)(2,1)S(1)}, u32[]{:S(2)}) copy-start(bf16[1,256,512]{2,1,0:T(8,128)(2,1)S(1)} %collective-permute-done.9.refs_2_) | copy-start | bytes 786436
  66.2 1.2 %copy-start.7 = (bf16[272,512]{1,0:T(8,128)(2,1)}, bf16[272,512]{1,0:T(8,128)(2,1)S(1)}, u32[]{:S(2)}) copy-start(bf16[272,512]{1,0:T(8,128)(2,1)S(1)} %collective-permute-done.10.refs_0_) | copy-start | bytes 835588
  66.3 1.2 %copy-start.8 = (bf16[272,512]{1,0:T(8,128)(2,1)}, bf16[272,512]{1,0:T(8,128)(2,1)S(1)}, u32[]{:S(2)}) copy-start(bf16[272,512]{1,0:T(8,128)(2,1)S(1)} %collective-permute-done.11.refs_1_) | copy-start | bytes 835588
  67.5 0.7 copy-start.9
  73.2 7.1 %collective-permute-start.13 = (bf16[3,256,512]{2,1,0:T(8,128)(2,1)}, bf16[3,256,512]{2,1,0:T(8,128)(2,1)S(1)}, u32[]{:S(2)}, u32[]{:S(2)}) collective-permute-start(bf16[3,256,512]{2,1,0:T(8,128)(2,1)} %get-tuple-element.92), channel_id=1, source_target_pairs={{0,1},{1,0},{2,3},{3,2},{4,5},{5,4},{6,7},{7,6},{8,9},{9,8},{10,11... | collective-permute-start | bytes 2359304 | tf_op jit(solution)/shard_map/ppermute | solution.py:379
  80.3 0.9 %copy-start.6 = (bf16[3,256,512]{2,1,0:T(8,128)(2,1)}, bf16[3,256,512]{2,1,0:T(8,128)(2,1)S(1)}, u32[]{:S(2)}) copy-start(bf16[3,256,512]{2,1,0:T(8,128)(2,1)S(1)} %collective-permute-done.13.refs_3_) | copy-start | bytes 2359300

commit v9 on v7

--- a/solution.py
+++ b/solution.py
@@ -90,11 +90,11 @@
     return ((inside % heads == out // n) & (inside // heads == out % n)).astype(BF16)
 
 
-def relayout_kernel(half, count, scalars, *refs):
+def relayout_kernel(half, count, *refs):
     sources, outs = refs[:count], refs[count:]
     heads = 2 * half
     n = LAY // heads
-    core = scalars[1]
+    core = lax.axis_index("hv") % 2
     order = by_head_order(heads)
     for index, source in enumerate(sources):
         keep, send = outs[index], outs[count + index]
@@ -108,11 +108,12 @@
 
 
 def gates_kernel(heads, scalars, g_own, g_oth, ids_ref, *outs):
-    factors, tops, decays, source_rows, decay_rows, columns = outs
+    factors, tops, decays, source_rows, decay_rows, columns, docs_row = outs
     core = scalars[1]
-    length = ids_ref.shape[1]
+    length = factors.shape[1]
     gate_in, decay = gate_rows(core, g_own, g_oth, heads)
-    ids = ids_ref[...]
+    chip = lax.axis_index("hv") // 2
+    ids = ids_ref[:, pl.ds(pl.multiple_of(chip * length, length), length)]
     exponent = decay[:, length - 1 :] - decay + gate_in
     exponent = jnp.where(ids == ids[:, length - 1 :], exponent, FLOOR_NEG)
     top = jnp.max(exponent, axis=1, keepdims=True)
@@ -122,17 +123,18 @@
     source_rows[...] = gate_in - decay
     decay_rows[...] = decay
     docs = ids.astype(F32) + 1.0
+    docs_row[...] = docs
     filler = jnp.zeros((LANES - heads - 1, length), F32)
     columns[...] = jnp.concatenate([decay, docs, filler], axis=0).T
 
 
 def state_kernel(heads, scalars, *refs):
-    k_own, v_own, k_oth, v_oth, factors, tops, decays, ids_ref = refs[:8]
+    k_own, v_own, k_oth, v_oth, factors, tops, decays, docs_ref = refs[:8]
     outs = refs[8:]
     mine, core = scalars[0], scalars[1]
     tokens, key_width = k_own.shape[1:]
     length = 2 * tokens
-    doc = jnp.broadcast_to(ids_ref[:, length - 1 :].astype(F32) + 1.0, (1, LANES))
+    doc = jnp.broadcast_to(docs_ref[:, length - 1 :], (1, LANES))
     for slot in range(len(outs) - 1, -1, -1):
         out = outs[slot]
         local_head = jnp.bitwise_xor(mine, slot)
@@ -224,70 +226,74 @@
     weighted(list(states) + list(totals), outs, lines)
 
 
-def local_kernel(heads, scalars, *refs):
-    q_own, k_own, v_own, q_oth, k_oth, v_oth, source_rows, decay_rows, columns, ids_ref = refs[:10]
-    numerators, stats = refs[10:]
-    step = pl.program_id(0)
+def local_kernel(first_slot, heads, scalars, *refs):
+    q_own, k_own, v_own, q_oth, k_oth, v_oth, source_rows, decay_rows, columns, docs_ref = refs[:10]
+    numerators, stats = refs[-2:]
     mine, core = scalars[0], scalars[1]
     tokens, key_width = q_own.shape[1:]
     length = 2 * tokens
     scaling = key_width**-0.5
-    head = (heads // 2) * core + jnp.bitwise_xor(mine, step)
     is_first = core == 0
-    source = source_rows[pl.ds(head, 1), :]
     lane = iota((length, LANES), 1)
     turned = columns[...]
-    decay = jnp.sum(jnp.where(lane == head, turned, 0.0), axis=1, keepdims=True)
     docs = turned[:, heads : heads + 1]
-    source_docs = ids_ref[...].astype(F32) + 1.0
+    source_docs = docs_ref[...]
     causal = iota((tokens, tokens), 0) >= iota((tokens, tokens), 1)
-
-    def ordered(own, other):
-        own, other = own[0], other[0]
-        return jnp.where(is_first, own, other), jnp.where(is_first, other, own)
-
-    queries, keys, values = ordered(q_own, q_oth), ordered(k_own, k_oth), ordered(v_own, v_oth)
-    for block in range(2):
-        rows = slice(block * tokens, (block + 1) * tokens)
-        exponents = []
-        for s in range(block + 1):
-            cols = slice(s * tokens, (s + 1) * tokens)
-            allowed = docs[rows] == source_docs[:, cols]
-            if s == block:
-                allowed = allowed & causal
-            exponents.append(jnp.where(allowed, decay[rows] + source[:, cols], FLOOR_NEG))
-        stabilizer = functools.reduce(
-            jnp.maximum, [jnp.max(x, axis=1, keepdims=True) for x in exponents]
-        )
-        factors, sources, denominator = [], [], None
-        for s in range(block + 1):
-            weights = dot(queries[block], keys[s], NT) * scaling
-            weights = weights * jnp.exp(exponents[s] - stabilizer)
-            high = weights.astype(BF16)
-            factors.append(high)
-            sources.append(values[s])
-            if s < block:
-                factors.append((weights - high.astype(F32)).astype(BF16))
+    for step in range(numerators.shape[0]):
+        local_head = jnp.bitwise_xor(mine, first_slot + step)
+        head = (heads // 2) * core + local_head
+        source = source_rows[pl.ds(head, 1), :]
+        decay = jnp.sum(jnp.where(lane == head, turned, 0.0), axis=1, keepdims=True)
+
+        def ordered(own, other):
+            own, other = own[local_head], other[local_head]
+            return jnp.where(is_first, own, other), jnp.where(is_first, other, own)
+
+        queries, keys, values = ordered(q_own, q_oth), ordered(k_own, k_oth), ordered(v_own, v_oth)
+        for block in range(2):
+            rows = slice(block * tokens, (block + 1) * tokens)
+            exponents = []
+            for s in range(block + 1):
+                cols = slice(s * tokens, (s + 1) * tokens)
+                allowed = docs[rows] == source_docs[:, cols]
+                if s == block:
+                    allowed = allowed & causal
+                exponents.append(jnp.where(allowed, decay[rows] + source[:, cols], FLOOR_NEG))
+            stabilizer = functools.reduce(
+                jnp.maximum, [jnp.max(x, axis=1, keepdims=True) for x in exponents]
+            )
+            factors, sources, denominator = [], [], None
+            for s in range(block + 1):
+                weights = dot(queries[block], keys[s], NT) * scaling
+                weights = weights * jnp.exp(exponents[s] - stabilizer)
+                high = weights.astype(BF16)
+                factors.append(high)
                 sources.append(values[s])
-            part = jnp.sum(weights, axis=1, keepdims=True)
-            denominator = part if s == 0 else denominator + part
-        numerator = dot(jnp.concatenate(factors, axis=1), jnp.concatenate(sources, axis=0))
-        side = core if block == 0 else 1 - core
-        numerators[0, side] = numerator
-        lane = iota((tokens, LANES), 1)
-        pair = jnp.where(lane == 0, stabilizer, denominator).T
-        stats[0, side] = jnp.concatenate(
-            [pair[:2], decay_rows[pl.ds(head, 1), rows], source_docs[:, rows], pair[4:8]], axis=0
-        )
-
-
-def output_kernel(first, count, scalars, q_own, q_oth, numerators, stats, *refs):
-    entering, (keep, send) = refs[:count], refs[count:]
+                if s < block:
+                    factors.append((weights - high.astype(F32)).astype(BF16))
+                    sources.append(values[s])
+                part = jnp.sum(weights, axis=1, keepdims=True)
+                denominator = part if s == 0 else denominator + part
+            numerator = dot(jnp.concatenate(factors, axis=1), jnp.concatenate(sources, axis=0))
+            side = core if block == 0 else 1 - core
+            numerators[step, side] = numerator
+            first_lane = iota((tokens, LANES), 1) == 0
+            pair = jnp.where(first_lane, stabilizer, denominator).T
+            stats[step, side] = jnp.concatenate(
+                [pair[:2], decay_rows[pl.ds(head, 1), rows], source_docs[:, rows], pair[4:8]], axis=0
+            )
+
+
+def output_kernel(first, count, scalars, q_own, q_oth, *refs):
+    terms, entering, (keep, send) = refs[:4], refs[4 : 4 + count], refs[4 + count :]
     key_width = q_own.shape[2]
     scaling = key_width**-0.5
+    early = terms[0].shape[0]
     for i, payload in enumerate(entering):
-        at = first + i
-        local_head = jnp.bitwise_xor(scalars[0], first + i)
+        slot = first + i
+        numerators, stats = terms[:2] if slot < early else terms[2:]
+        at = slot % early
+        local_head = jnp.bitwise_xor(scalars[0], slot)
         normal, top, _, doc = read_meta([payload])
         pieces = split3(normal) + (jnp.zeros((META - 3, key_width), F32),)
         pieces = jnp.concatenate(pieces, axis=0).astype(BF16)
@@ -337,10 +343,11 @@
 
 
 def params():
-    return pltpu.CompilerParams(vmem_limit_bytes=56 * 2**20)
+    return pltpu.CompilerParams(vmem_limit_bytes=16 * 2**20)
 
 
 SMEM = pl.BlockSpec(memory_space=pltpu.SMEM)
+VMEM = pl.BlockSpec(memory_space=pltpu.VMEM)
 
 
 def shape_of(*dims, dtype=BF16):
@@ -358,7 +365,7 @@
     ctx, hv = lax.axis_index("ctx"), lax.axis_index("hv")
     chip = ctx * (lax.axis_size("hv") // 2) + hv // 2
     scalars = jnp.stack([chip % group, hv % 2]).astype(jnp.int32)
-    ids = lax.dynamic_slice(doc_ids, ((hv // 2) * 2 * tokens,), (2 * tokens,))[None, :]
+    ids = doc_ids[None, :]
 
     def swap_cores(x):
         return lax.ppermute(x, AXES, [(d, d ^ 1) for d in range(devices)])
@@ -379,12 +386,12 @@
         outs = [sizes[x.shape[2]] for x in sources] * 2
         return pl.pallas_call(
             functools.partial(relayout_kernel, half, len(sources)),
-            in_specs=[SMEM] + [whole(x.shape) for x in sources],
-            out_specs=[whole(s) for s in outs],
+            in_specs=[whole(x.shape) for x in sources],
+            out_specs=[VMEM] * len(outs),
             out_shape=[shape_of(*s) for s in outs],
             compiler_params=params(),
-            name="relayout",
-        )(scalars, *sources)
+                name="relayout",
+        )(*sources)
 
     gates = jnp.concatenate([input_gate.T, forget_gate.T], axis=0)
     gates, key_vectors = lax.optimization_barrier((gates, key_vectors))
@@ -400,24 +407,22 @@
         (heads, 2 * tokens),
         (heads, 2 * tokens),
         (2 * tokens, LANES),
+        (1, 2 * tokens),
     ]
-    factors, tops, decays, source_rows, decay_rows, columns = pl.pallas_call(
+    factors, tops, decays, source_rows, decay_rows, columns, docs = pl.pallas_call(
         functools.partial(gates_kernel, heads),
-        in_specs=[SMEM] + [whole(gates.shape)] * 2 + [whole(ids.shape)],
-        out_specs=[whole(s) for s in gate_shapes],
+        in_specs=[SMEM, VMEM, VMEM, VMEM],
+        out_specs=[VMEM] * len(gate_shapes),
         out_shape=[shape_of(*s, dtype=F32) for s in gate_shapes],
         compiler_params=params(),
         name="gates",
     )(scalars, gates, gates_oth, ids)
 
-    def by_slot(x):
-        return pl.BlockSpec((1,) + x.shape[1:], lambda i, s: (jnp.bitwise_xor(s[0], i), 0, 0))
-
-    by_core = (k_keep, v_keep, k_oth, v_oth, factors, tops, decays, ids)
+    by_core = (k_keep, v_keep, k_oth, v_oth, factors, tops, decays, docs)
     made = pl.pallas_call(
         functools.partial(state_kernel, heads),
-        in_specs=[SMEM] + [whole(x.shape) for x in by_core],
-        out_specs=[whole(state)] * group,
+        in_specs=[SMEM] + [VMEM] * len(by_core),
+        out_specs=[VMEM] * group,
         out_shape=[shape_of(*state)] * group,
         compiler_params=params(),
         name="states",
@@ -425,42 +430,47 @@
     gathered = [made[0]] + [in_group(made[r], r) for r in range(1, group)]
     total = pl.pallas_call(
         functools.partial(total_kernel, group),
-        in_specs=[SMEM] + [whole(state)] * group,
-        out_specs=whole(state),
+        in_specs=[SMEM] + [VMEM] * group,
+        out_specs=VMEM,
         out_shape=shape_of(*state),
         compiler_params=params(),
         name="group_total",
     )(scalars, *gathered)
-    totals = [to_next(total)]
-    while len(totals) < reach:
-        totals.append(to_next(totals[-1]))
-
     queries, gathered[0] = lax.optimization_barrier((queries, gathered[0]))
     q_keep, q_send = relayout(queries)
     q_oth = swap_cores(q_send)
-    by_head = (q_keep, k_keep, v_keep, q_oth, k_oth, v_oth)
-    small = (source_rows, decay_rows, columns, ids)
-    local_shapes = [(half, 2, tokens, value_width), (half, 2, 8, tokens)]
-    numerators, stats = pl.pallas_call(
-        functools.partial(local_kernel, heads),
-        grid_spec=pltpu.PrefetchScalarGridSpec(
-            num_scalar_prefetch=1,
-            grid=(group,),
-            in_specs=[by_slot(x) for x in by_head] + [whole(x.shape) for x in small],
-            out_specs=[
-                pl.BlockSpec((1,) + s[1:], lambda i, _: (i, 0, 0, 0)) for s in local_shapes
+    small = (source_rows, decay_rows, columns, docs)
+    early = half // 2
+
+    def own_terms(first_slot, q_own):
+        operands = (q_own, k_keep, v_keep, q_oth, k_oth, v_oth, *small)
+        return pl.pallas_call(
+            functools.partial(local_kernel, first_slot, heads),
+            in_specs=[SMEM] + [VMEM] * len(operands),
+            out_specs=[VMEM] * 2,
+            out_shape=[
+                shape_of(early, 2, tokens, value_width, dtype=F32),
+                shape_of(early, 2, 8, tokens, dtype=F32),
             ],
-        ),
-        out_shape=[shape_of(*s, dtype=F32) for s in local_shapes],
-        compiler_params=params(),
-        name="own_terms",
-    )(scalars, *by_head, *small)
-    gathered[0], numerators = lax.optimization_barrier((gathered[0], numerators))
+            compiler_params=params(),
+            name="own_terms",
+        )(scalars, *operands)
+
+    q_first, _ = lax.optimization_barrier((q_keep, total))
+    first_terms = own_terms(0, q_first)
+    totals = [to_next(total)]
+    totals[0], first_terms = lax.optimization_barrier((totals[0], first_terms))
+    while len(totals) < reach:
+        totals.append(to_next(totals[-1]))
+    q_last, _ = lax.optimization_barrier((q_keep, totals[0]))
+    last_terms = own_terms(early, q_last)
+    gathered[0], last_terms = lax.optimization_barrier((gathered[0], last_terms))
+    terms = [*first_terms, *last_terms]
 
     leaving = pl.pallas_call(
         functools.partial(entering_kernel, group, reach),
-        in_specs=[SMEM] + [whole(state)] * (group + reach),
-        out_specs=[whole(state)] * group,
+        in_specs=[SMEM] + [VMEM] * (group + reach),
+        out_specs=[VMEM] * group,
         out_shape=[shape_of(*state)] * group,
         compiler_params=params(),
         name="entering",
@@ -470,23 +480,21 @@
     def outputs(first, count):
         return pl.pallas_call(
             functools.partial(output_kernel, first, count),
-            in_specs=[SMEM, whole(q_keep.shape), whole(q_oth.shape)]
-            + [whole(x) for x in local_shapes]
-            + [whole(state)] * count,
-            out_specs=[whole((count, tokens, value_width))] * 2,
+            in_specs=[SMEM] + [VMEM] * (6 + count),
+            out_specs=[VMEM] * 2,
             out_shape=[shape_of(count, tokens, value_width)] * 2,
             compiler_params=params(),
             name="outputs",
-        )(scalars, q_keep, q_oth, numerators, stats, *entering[first : first + count])
+        )(scalars, q_keep, q_oth, *terms, *entering[first : first + count])
 
     keep, send = outputs(0, 1)
     swapped = swap_cores(send)
-    numerators, swapped = lax.optimization_barrier((numerators, swapped))
+    terms, swapped = lax.optimization_barrier((terms, swapped))
     keep_far, send = outputs(1, group - 1)
     kept, received = [keep, keep_far], [swapped, swap_cores(send)]
     return pl.pallas_call(
         functools.partial(merge_kernel, heads),
-        in_specs=[SMEM] + [whole(x.shape) for x in kept + received],
+        in_specs=[SMEM] + [VMEM] * 4,
         out_specs=whole(value_vectors.shape),
         out_shape=shape_of(*value_vectors.shape),
         compiler_params=params(),

time: 89.5 us -> 69.4 us (0.78)
  the two profiles are of different devices: /device:TPU:0 before, /device:TPU:25 now
where the time goes in v9:
time: 69.4 us; the launch traced here: 68.9 us
  waiting for transfers between devices  29.1 us (42%)
  starting transfers between devices  19.1 us (28%)
  Pallas kernels  17.1 us (25%)
  local copies, waits for them, and re-layouts  2.82 us (4%)
  other arithmetic  0.79 us (1%)
    ppermute x6, waiting for transfers between devices, in_group(): return lax.ppermute(x, AXES, pairs)  14 us
    ppermute x6, starting transfers between devices, swap_cores(): return lax.ppermute(x, AXES, [(d, d ^ 1) for d in range(devices)])  10.9 us
    ppermute x2, waiting for transfers between devices, to_next(): return lax.ppermute(x, AXES, [(d, d + jump) for d in range(devices - jump)])  9.91 us
    ppermute x6, starting transfers between devices, in_group(): return lax.ppermute(x, AXES, pairs)  5.63 us
    ppermute x6, waiting for transfers between devices, swap_cores(): return lax.ppermute(x, AXES, [(d, d ^ 1) for d in range(devices)])  5.18 us
    pallas_call x2, Pallas kernels, own_terms(): pl.pallas_call(functools.partial(local_kernel, first_slot, heads), in_spe...  4.44 us
    unnamed x8, local copies, waits for them, and re-layouts  2.82 us
    pallas_call x1, Pallas kernels, local(): pl.pallas_call(functools.partial(merge_kernel, heads), in_specs=[SMEM] +...  2.58 us
  transfers between devices with their start and end apart: 14, of which 10 were waited for; matrix products, arithmetic and copies ran while one was open for 0% of the time, Pallas kernels for 14%

profile of v9, /device:TPU:25, one launch (start us, length us, event | category | flops | bytes accessed | tf_op | source)
XLA Modules:
  0.0 68.9 jit_solution(9317501548305870171)
XLA Ops:
  0.0 0.0 copy-start.3
  0.0 0.7 %pad_maximum_fusion.g_own = bf16[16,256]{1,0:T(8,128)(2,1)S(1)} fusion(bf16[8,256]{1,0:T(8,128)(2,1)} %bitcast.6, bf16[8,256]{1,0:T(8,128)(2,1)} %bitcast.7), kind=kLoop, calls=%fused_computation | loop fusion | flops 16384 | bytes 16384 | tf_op jit(solution)/shard_map/concatenate | solution.py:396
  0.7 0.7 collective-permute-start
  1.4 0.0 copy-start
  1.4 1.6 %copy-done = bf16[256,8,512]{2,1,0:T(8,128)(2,1)S(1)} copy-done((bf16[256,8,512]{2,1,0:T(8,128)(2,1)S(1)}, bf16[256,8,512]{2,1,0:T(8,128)(2,1)}, u32[]{:S(2)}) %copy-start) | copy-done | bytes 2097176
  3.0 0.0 copy-start.1
  3.0 1.2 %copy-done.1 = bf16[256,8,256]{2,1,0:T(8,128)(2,1)S(1)} copy-done((bf16[256,8,256]{2,1,0:T(8,128)(2,1)S(1)}, bf16[256,8,256]{2,1,0:T(8,128)(2,1)}, u32[]{:S(2)}) %copy-start.1) | copy-done | bytes 1048600
  4.2 2.0 %relayout.2 = (bf16[4,256,256]{2,1,0:T(8,128)(2,1)S(1)}, bf16[4,256,512]{2,1,0:T(8,128)(2,1)S(1)}, bf16[4,256,256]{2,1,0:T(8,128)(2,1)}, bf16[4,256,512]{2,1,0:T(8,128)(2,1)}) custom-call(bf16[256,8,256]{2,1,0:T(8,128)(2,1)S(1)} %copy-done.1, bf16[256,8,512]{2,1,0:T(8,128)(2,1)S(1)} %copy-done), custom_call_target="tpu_custom_call" | custom-call | tf_op jit(solution)/shard_map/relayout/pallas_call | solution.py:387
  6.2 0.0 collective-permute-done.g_oth
  6.2 0.0 collective-permute-start.2
  6.2 0.5 collective-permute-start.1
  6.7 0.0 copy-start.2
  6.7 0.1 pad_add_fusion.scalars
  6.8 0.0 copy-done.3
  6.8 0.9 %gates.1 = (f32[8,512]{1,0:T(8,128)S(1)}, f32[8,128]{1,0:T(8,128)S(1)}, f32[8,128]{1,0:T(8,128)S(1)}, f32[8,512]{1,0:T(8,128)S(1)}, f32[8,512]{1,0:T(8,128)S(1)}...) custom-call(s32[2]{0:T(128)S(1)} %pad_add_fusion.scalars, bf16[16,256]{1,0:T(8,128)(2,1)S(1)} %pad_maximum_fusion.g_own, ...), custom_call_target="tpu_custom_call" | custom-call | tf_op jit(solution)/shard_map/gates/pallas_call | solution.py:412
  7.7 2.1 %collective-permute-done.1.refs_2_.refs_4_ = bf16[4,256,256]{2,1,0:T(8,128)(2,1)S(1)} collective-permute-done((bf16[4,256,256]{2,1,0:T(8,128)(2,1)}, bf16[4,256,256]{2,1,0:T(8,128)(2,1)S(1)}, u32[]{:S(2)}, u32[]{:S(2)}) %collective-permute-start.1) | collective-permute-done | bytes 524320 | tf_op jit(solution)/shard_map/ppermute | solution.py:371
  9.8 0.0 collective-permute-done.2.refs_3_.refs_5_
  9.8 2.1 %states.1 = (bf16[272,512]{1,0:T(8,128)(2,1)S(1)}, bf16[272,512]{1,0:T(8,128)(2,1)S(1)}, bf16[272,512]{1,0:T(8,128)(2,1)S(1)}, bf16[272,512]{1,0:T(8,128)(2,1)S(1)}) custom-call(s32[2]{0:T(128)S(1)} %pad_add_fusion.scalars, bf16[4,256,256]{2,1,0:T(8,128)(2,1)S(1)} %get-tuple-element.55.refs_0_.refs_1_, ...), custom_call_target="tpu_custom_call" | custom-call | tf_op jit(solution)/shard_map/states/pallas_call | solution.py:422
  11.9 1.3 %collective-permute-start.4 = (bf16[272,512]{1,0:T(8,128)(2,1)S(1)}, bf16[272,512]{1,0:T(8,128)(2,1)S(1)}, u32[]{:S(2)}, u32[]{:S(2)}) collective-permute-start(bf16[272,512]{1,0:T(8,128)(2,1)S(1)} %get-tuple-element.71), channel_id=1, source_target_pairs={{0,2},{1,3},{2,0},{3,1},{4,6},{5,7},{6,4},{7,5},{8,10},{9,11},{10,... | collective-permute-start | bytes 835592 | tf_op jit(solution)/shard_map/ppermute | solution.py:375
  13.1 1.2 %collective-permute-start.5 = (bf16[272,512]{1,0:T(8,128)(2,1)S(1)}, bf16[272,512]{1,0:T(8,128)(2,1)S(1)}, u32[]{:S(2)}, u32[]{:S(2)}) collective-permute-start(bf16[272,512]{1,0:T(8,128)(2,1)S(1)} %get-tuple-element.72), channel_id=1, source_target_pairs={{0,4},{1,5},{2,6},{3,7},{4,0},{5,1},{6,2},{7,3},{8,12},{9,13},{10,... | collective-permute-start | bytes 835592 | tf_op jit(solution)/shard_map/ppermute | solution.py:375
  14.4 0.2 collective-permute-start.6
  14.6 0.0 copy-done.2
  14.6 0.4 relayout.3
  15.0 1.0 %collective-permute-start.3 = (bf16[4,256,256]{2,1,0:T(8,128)(2,1)S(1)}, bf16[4,256,256]{2,1,0:T(8,128)(2,1)S(1)}, u32[]{:S(2)}, u32[]{:S(2)}) collective-permute-start(bf16[4,256,256]{2,1,0:T(8,128)(2,1)S(1)} %get-tuple-element.70), channel_id=1, source_target_pairs={{0,1},{1,0},{2,3},{3,2},{4,5},{5,4},{6,7},{7,6},{8,9},{9,8},{10,11... | collective-permute-start | bytes 1572872 | tf_op jit(solution)/shard_map/ppermute | solution.py:371
  16.1 3.9 %collective-permute-done.4.refs_1_ = bf16[272,512]{1,0:T(8,128)(2,1)S(1)} collective-permute-done((bf16[272,512]{1,0:T(8,128)(2,1)S(1)}, bf16[272,512]{1,0:T(8,128)(2,1)S(1)}, u32[]{:S(2)}, u32[]{:S(2)}) %collective-permute-start.4) | collective-permute-done | bytes 278560 | tf_op jit(solution)/shard_map/ppermute | solution.py:375
  20.0 0.9 %collective-permute-done.5.refs_2_ = bf16[272,512]{1,0:T(8,128)(2,1)S(1)} collective-permute-done((bf16[272,512]{1,0:T(8,128)(2,1)S(1)}, bf16[272,512]{1,0:T(8,128)(2,1)S(1)}, u32[]{:S(2)}, u32[]{:S(2)}) %collective-permute-start.5) | collective-permute-done | bytes 278560 | tf_op jit(solution)/shard_map/ppermute | solution.py:375
  21.0 6.0 %collective-permute-done.6.refs_3_ = bf16[272,512]{1,0:T(8,128)(2,1)S(1)} collective-permute-done((bf16[272,512]{1,0:T(8,128)(2,1)S(1)}, bf16[272,512]{1,0:T(8,128)(2,1)S(1)}, u32[]{:S(2)}, u32[]{:S(2)}) %collective-permute-start.6) | collective-permute-done | bytes 278560 | tf_op jit(solution)/shard_map/ppermute | solution.py:375
  27.0 0.8 %group_total.1 = bf16[272,512]{1,0:T(8,128)(2,1)S(1)} custom-call(s32[2]{0:T(128)S(1)} %pad_add_fusion.scalars, bf16[272,512]{1,0:T(8,128)(2,1)S(1)} %get-tuple-element.89.refs_0_, bf16[272,512]{1,0:T(8,128)(2,1)S(1)} %collective-permute-done.4.refs_1_, bf16[272,512]{1,0:T(8,128)(2,1)S(1)} %collective-permute-done.5.refs_2_, ...), custom_call_target="tpu_custom_call" | custom-call | tf_op jit(solution)/shard_map/group_total/pallas_call | solution.py:431
  27.8 1.3 %collective-permute-start.7 = (bf16[272,512]{1,0:T(8,128)(2,1)S(1)}, bf16[272,512]{1,0:T(8,128)(2,1)S(1)}, u32[]{:S(2)}, u32[]{:S(2)}) collective-permute-start(bf16[272,512]{1,0:T(8,128)(2,1)S(1)} %group_total.1), channel_id=1, source_target_pairs={{0,8},{1,9},{2,10},{3,11},{4,12},{5,13},{6,14},{7,15},{8,16},{9,17... | collective-permute-start | bytes 835592 | tf_op jit(solution)/shard_map/ppermute | solution.py:379
  29.1 0.0 collective-permute-done.3.refs_3_.q_oth
  29.1 2.2 %own_terms.2 = (f32[2,2,256,512]{3,2,1,0:T(8,128)S(1)}, f32[2,2,8,256]{3,2,1,0:T(8,128)S(1)}) custom-call(s32[2]{0:T(128)S(1)} %pad_add_fusion.scalars, bf16[4,256,256]{2,1,0:T(8,128)(2,1)S(1)} %get-tuple-element.84.refs_0_.q_own, bf16[4,256,256]{2,1,0:T(8,128)(2,1)S(1)} %get-tuple-element.55.refs_0_.refs_1_, ...), custom_call_target="tpu_custom_call" | custom-call | tf_op jit(solution)/shard_map/own_terms/pallas_call | solution.py:447
  31.3 5.4 %collective-permute-done.7.refs_4_ = bf16[272,512]{1,0:T(8,128)(2,1)S(1)} collective-permute-done((bf16[272,512]{1,0:T(8,128)(2,1)S(1)}, bf16[272,512]{1,0:T(8,128)(2,1)S(1)}, u32[]{:S(2)}, u32[]{:S(2)}) %collective-permute-start.7) | collective-permute-done | bytes 278560 | tf_op jit(solution)/shard_map/ppermute | solution.py:379
  36.7 1.3 %collective-permute-start.8 = (bf16[272,512]{1,0:T(8,128)(2,1)S(1)}, bf16[272,512]{1,0:T(8,128)(2,1)S(1)}, u32[]{:S(2)}, u32[]{:S(2)}) collective-permute-start(bf16[272,512]{1,0:T(8,128)(2,1)S(1)} %collective-permute-done.7.refs_4_), channel_id=1, source_target_pairs={{0,8},{1,9},{2,10},{3,11},{4,12},{5,13},{6,14},{7,15},{8,16},{9,17... | collective-permute-start | bytes 835592 | tf_op jit(solution)/shard_map/ppermute | solution.py:379
  38.0 2.2 %own_terms.3 = (f32[2,2,256,512]{3,2,1,0:T(8,128)S(1)}, f32[2,2,8,256]{3,2,1,0:T(8,128)S(1)}) custom-call(s32[2]{0:T(128)S(1)} %pad_add_fusion.scalars, bf16[4,256,256]{2,1,0:T(8,128)(2,1)S(1)} %get-tuple-element.84.refs_0_.q_own, bf16[4,256,256]{2,1,0:T(8,128)(2,1)S(1)} %get-tuple-element.55.refs_0_.refs_1_, ...), custom_call_target="tpu_custom_call" | custom-call | tf_op jit(solution)/shard_map/own_terms/pallas_call | solution.py:447
  40.2 4.5 %collective-permute-done.8.refs_5_ = bf16[272,512]{1,0:T(8,128)(2,1)S(1)} collective-permute-done((bf16[272,512]{1,0:T(8,128)(2,1)S(1)}, bf16[272,512]{1,0:T(8,128)(2,1)S(1)}, u32[]{:S(2)}, u32[]{:S(2)}) %collective-permute-start.8) | collective-permute-done | bytes 278560 | tf_op jit(solution)/shard_map/ppermute | solution.py:379
  44.7 1.4 %entering.1 = (bf16[272,512]{1,0:T(8,128)(2,1)S(1)}, bf16[272,512]{1,0:T(8,128)(2,1)S(1)}, bf16[272,512]{1,0:T(8,128)(2,1)S(1)}, bf16[272,512]{1,0:T(8,128)(2,1)S(1)}) custom-call(s32[2]{0:T(128)S(1)} %pad_add_fusion.scalars, bf16[272,512]{1,0:T(8,128)(2,1)S(1)} %get-tuple-element.89.refs_0_, bf16[272,512]{1,0:T(8,128)(2,1)S(1)} %collective-permute-done.4.refs_1_, ...), custom_call_target="tpu_custom_call" | custom-call | tf_op jit(solution)/shard_map/entering/pallas_call | solution.py:470
  46.1 1.7 %collective-permute-start.10 = (bf16[272,512]{1,0:T(8,128)(2,1)S(1)}, bf16[272,512]{1,0:T(8,128)(2,1)S(1)}, u32[]{:S(2)}, u32[]{:S(2)}) collective-permute-start(bf16[272,512]{1,0:T(8,128)(2,1)S(1)} %get-tuple-element.97), channel_id=1, source_target_pairs={{0,2},{1,3},{2,0},{3,1},{4,6},{5,7},{6,4},{7,5},{8,10},{9,11},{10,... | collective-permute-start | bytes 835592 | tf_op jit(solution)/shard_map/ppermute | solution.py:375
  47.8 0.0 collective-permute-start.11
  47.8 1.3 %collective-permute-start.12 = (bf16[272,512]{1,0:T(8,128)(2,1)S(1)}, bf16[272,512]{1,0:T(8,128)(2,1)S(1)}, u32[]{:S(2)}, u32[]{:S(2)}) collective-permute-start(bf16[272,512]{1,0:T(8,128)(2,1)S(1)} %get-tuple-element.99), channel_id=1, source_target_pairs={{0,6},{1,7},{2,4},{3,5},{4,2},{5,3},{6,0},{7,1},{8,14},{9,15},{10,... | collective-permute-start | bytes 835592 | tf_op jit(solution)/shard_map/ppermute | solution.py:375
  49.0 1.0 %outputs.2 = (bf16[1,256,512]{2,1,0:T(8,128)(2,1)S(1)}, bf16[1,256,512]{2,1,0:T(8,128)(2,1)S(1)}) custom-call(s32[2]{0:T(128)S(1)} %pad_add_fusion.scalars, bf16[4,256,256]{2,1,0:T(8,128)(2,1)S(1)} %get-tuple-element.84.refs_0_.q_own, bf16[4,256,256]{2,1,0:T(8,128)(2,1)S(1)} %collective-permute-done.3.refs_3_.q_oth, ...), custom_call_target="tpu_custom_call" | custom-call | tf_op jit(solution)/shard_map/outputs/pallas_call | solution.py:481
  50.0 3.6 %collective-permute-start.9 = (bf16[1,256,512]{2,1,0:T(8,128)(2,1)S(1)}, bf16[1,256,512]{2,1,0:T(8,128)(2,1)S(1)}, u32[]{:S(2)}, u32[]{:S(2)}) collective-permute-start(bf16[1,256,512]{2,1,0:T(8,128)(2,1)S(1)} %get-tuple-element.92), channel_id=1, source_target_pairs={{0,1},{1,0},{2,3},{3,2},{4,5},{5,4},{6,7},{7,6},{8,9},{9,8},{10,11... | collective-permute-start | bytes 786440 | tf_op jit(solution)/shard_map/ppermute | solution.py:371
  53.7 1.2 %collective-permute-done.9.refs_2_ = bf16[1,256,512]{2,1,0:T(8,128)(2,1)S(1)} collective-permute-done((bf16[1,256,512]{2,1,0:T(8,128)(2,1)S(1)}, bf16[1,256,512]{2,1,0:T(8,128)(2,1)S(1)}, u32[]{:S(2)}, u32[]{:S(2)}) %collective-permute-start.9) | collective-permute-done | bytes 262176 | tf_op jit(solution)/shard_map/ppermute | solution.py:371
  54.8 0.0 collective-permute-done.10.refs_4_
  54.8 0.8 %collective-permute-done.11.refs_5_ = bf16[272,512]{1,0:T(8,128)(2,1)S(1)} collective-permute-done((bf16[272,512]{1,0:T(8,128)(2,1)S(1)}, bf16[272,512]{1,0:T(8,128)(2,1)S(1)}, u32[]{:S(2)}, u32[]{:S(2)}) %collective-permute-start.11) | collective-permute-done | bytes 278560 | tf_op jit(solution)/shard_map/ppermute | solution.py:375
  55.6 2.3 %collective-permute-done.12.refs_6_ = bf16[272,512]{1,0:T(8,128)(2,1)S(1)} collective-permute-done((bf16[272,512]{1,0:T(8,128)(2,1)S(1)}, bf16[272,512]{1,0:T(8,128)(2,1)S(1)}, u32[]{:S(2)}, u32[]{:S(2)}) %collective-permute-start.12) | collective-permute-done | bytes 278560 | tf_op jit(solution)/shard_map/ppermute | solution.py:375
  57.9 1.5 %outputs.3 = (bf16[3,256,512]{2,1,0:T(8,128)(2,1)S(1)}, bf16[3,256,512]{2,1,0:T(8,128)(2,1)S(1)}) custom-call(s32[2]{0:T(128)S(1)} %pad_add_fusion.scalars, bf16[4,256,256]{2,1,0:T(8,128)(2,1)S(1)} %get-tuple-element.84.refs_0_.q_own, bf16[4,256,256]{2,1,0:T(8,128)(2,1)S(1)} %collective-permute-done.3.refs_3_.q_oth, ...), custom_call_target="tpu_custom_call" | custom-call | tf_op jit(solution)/shard_map/outputs/pallas_call | solution.py:481
  59.4 5.0 %collective-permute-start.13 = (bf16[3,256,512]{2,1,0:T(8,128)(2,1)S(1)}, bf16[3,256,512]{2,1,0:T(8,128)(2,1)S(1)}, u32[]{:S(2)}, u32[]{:S(2)}) collective-permute-start(bf16[3,256,512]{2,1,0:T(8,128)(2,1)S(1)} %get-tuple-element.102), channel_id=1, source_target_pairs={{0,1},{1,0},{2,3},{3,2},{4,5},{5,4},{6,7},{7,6},{8,9},{9,8},{10,11... | collective-permute-start | bytes 2359304 | tf_op jit(solution)/shard_map/ppermute | solution.py:371
  64.4 1.9 %collective-permute-done.13.refs_3_ = bf16[3,256,512]{2,1,0:T(8,128)(2,1)S(1)} collective-permute-done((bf16[3,256,512]{2,1,0:T(8,128)(2,1)S(1)}, bf16[3,256,512]{2,1,0:T(8,128)(2,1)S(1)}, u32[]{:S(2)}, u32[]{:S(2)}) %collective-permute-start.13) | collective-permute-done | bytes 786464 | tf_op jit(solution)/shard_map/ppermute | solution.py:371
  66.3 2.6 %merge.1 = bf16[256,8,512]{2,1,0:T(8,128)(2,1)} custom-call(s32[2]{0:T(128)S(1)} %pad_add_fusion.scalars, bf16[1,256,512]{2,1,0:T(8,128)(2,1)S(1)} %get-tuple-element.91.refs_0_, bf16[3,256,512]{2,1,0:T(8,128)(2,1)S(1)} %get-tuple-element.100.refs_1_, bf16[1,256,512]{2,1,0:T(8,128)(2,1)S(1)} %collective-permute-done.9.refs_2_, ...), custom_call_target="tpu_custom_call" | custom-call | tf_op jit(solution)/shard_map/merge/pallas_call | solution.py:495
Async XLA Ops:
  0.0 6.8 %copy-start.3 = (s32[1024]{0:T(1024)S(1)}, s32[1024]{0:T(1024)}, u32[]{:S(2)}) copy-start(s32[1024]{0:T(1024)} %param.11) | copy-start | bytes 12292
  0.7 5.5 %collective-permute-start = (bf16[16,256]{1,0:T(8,128)(2,1)S(1)}, bf16[16,256]{1,0:T(8,128)(2,1)S(1)}, u32[]{:S(2)}, u32[]{:S(2)}) collective-permute-start(bf16[16,256]{1,0:T(8,128)(2,1)S(1)} %pad_maximum_fusion.g_own), channel_id=1, source_target_pairs={{0,1},{1,0},{2,3},{3,2},{4,5},{5,4},{6,7},{7,6},{8,9},{9,8},{10,11... | collective-permute-start | bytes 24584 | tf_op jit(solution)/shard_map/ppermute | solution.py:371
  1.4 1.6 %copy-start = (bf16[256,8,512]{2,1,0:T(8,128)(2,1)S(1)}, bf16[256,8,512]{2,1,0:T(8,128)(2,1)}, u32[]{:S(2)}) copy-start(bf16[256,8,512]{2,1,0:T(8,128)(2,1)} %refs_1_.1) | copy-start | bytes 6291460
  3.0 1.2 %copy-start.1 = (bf16[256,8,256]{2,1,0:T(8,128)(2,1)S(1)}, bf16[256,8,256]{2,1,0:T(8,128)(2,1)}, u32[]{:S(2)}) copy-start(bf16[256,8,256]{2,1,0:T(8,128)(2,1)} %refs_0_) | copy-start | bytes 3145732
  6.2 3.6 %collective-permute-start.2 = (bf16[4,256,512]{2,1,0:T(8,128)(2,1)}, bf16[4,256,512]{2,1,0:T(8,128)(2,1)S(1)}, u32[]{:S(2)}, u32[]{:S(2)}) collective-permute-start(bf16[4,256,512]{2,1,0:T(8,128)(2,1)} %get-tuple-element.61), channel_id=1, source_target_pairs={{0,1},{1,0},{2,3},{3,2},{4,5},{5,4},{6,7},{7,6},{8,9},{9,8},{10,11... | collective-permute-start | bytes 3145736 | tf_op jit(solution)/shard_map/ppermute | solution.py:371
  6.2 3.6 %collective-permute-start.1 = (bf16[4,256,256]{2,1,0:T(8,128)(2,1)}, bf16[4,256,256]{2,1,0:T(8,128)(2,1)S(1)}, u32[]{:S(2)}, u32[]{:S(2)}) collective-permute-start(bf16[4,256,256]{2,1,0:T(8,128)(2,1)} %get-tuple-element.60), channel_id=1, source_target_pairs={{0,1},{1,0},{2,3},{3,2},{4,5},{5,4},{6,7},{7,6},{8,9},{9,8},{10,11... | collective-permute-start | bytes 1572872 | tf_op jit(solution)/shard_map/ppermute | solution.py:371
  6.7 7.9 %copy-start.2 = (bf16[256,8,256]{2,1,0:T(8,128)(2,1)S(1)}, bf16[256,8,256]{2,1,0:T(8,128)(2,1)}, u32[]{:S(2)}) copy-start(bf16[256,8,256]{2,1,0:T(8,128)(2,1)} %refs_0_.1) | copy-start | bytes 3145732
  11.9 8.1 %collective-permute-start.4 = (bf16[272,512]{1,0:T(8,128)(2,1)S(1)}, bf16[272,512]{1,0:T(8,128)(2,1)S(1)}, u32[]{:S(2)}, u32[]{:S(2)}) collective-permute-start(bf16[272,512]{1,0:T(8,128)(2,1)S(1)} %get-tuple-element.71), channel_id=1, source_target_pairs={{0,2},{1,3},{2,0},{3,1},{4,6},{5,7},{6,4},{7,5},{8,10},{9,11},{10,... | collective-permute-start | bytes 835592 | tf_op jit(solution)/shard_map/ppermute | solution.py:375
  13.1 7.8 %collective-permute-start.5 = (bf16[272,512]{1,0:T(8,128)(2,1)S(1)}, bf16[272,512]{1,0:T(8,128)(2,1)S(1)}, u32[]{:S(2)}, u32[]{:S(2)}) collective-permute-start(bf16[272,512]{1,0:T(8,128)(2,1)S(1)} %get-tuple-element.72), channel_id=1, source_target_pairs={{0,4},{1,5},{2,6},{3,7},{4,0},{5,1},{6,2},{7,3},{8,12},{9,13},{10,... | collective-permute-start | bytes 835592 | tf_op jit(solution)/shard_map/ppermute | solution.py:375
  14.4 12.6 %collective-permute-start.6 = (bf16[272,512]{1,0:T(8,128)(2,1)S(1)}, bf16[272,512]{1,0:T(8,128)(2,1)S(1)}, u32[]{:S(2)}, u32[]{:S(2)}) collective-permute-start(bf16[272,512]{1,0:T(8,128)(2,1)S(1)} %get-tuple-element.73), channel_id=1, source_target_pairs={{0,6},{1,7},{2,4},{3,5},{4,2},{5,3},{6,0},{7,1},{8,14},{9,15},{10,... | collective-permute-start | bytes 835592 | tf_op jit(solution)/shard_map/ppermute | solution.py:375
  15.0 14.1 %collective-permute-start.3 = (bf16[4,256,256]{2,1,0:T(8,128)(2,1)S(1)}, bf16[4,256,256]{2,1,0:T(8,128)(2,1)S(1)}, u32[]{:S(2)}, u32[]{:S(2)}) collective-permute-start(bf16[4,256,256]{2,1,0:T(8,128)(2,1)S(1)} %get-tuple-element.70), channel_id=1, source_target_pairs={{0,1},{1,0},{2,3},{3,2},{4,5},{5,4},{6,7},{7,6},{8,9},{9,8},{10,11... | collective-permute-start | bytes 1572872 | tf_op jit(solution)/shard_map/ppermute | solution.py:371
  27.8 8.9 %collective-permute-start.7 = (bf16[272,512]{1,0:T(8,128)(2,1)S(1)}, bf16[272,512]{1,0:T(8,128)(2,1)S(1)}, u32[]{:S(2)}, u32[]{:S(2)}) collective-permute-start(bf16[272,512]{1,0:T(8,128)(2,1)S(1)} %group_total.1), channel_id=1, source_target_pairs={{0,8},{1,9},{2,10},{3,11},{4,12},{5,13},{6,14},{7,15},{8,16},{9,17... | collective-permute-start | bytes 835592 | tf_op jit(solution)/shard_map/ppermute | solution.py:379
  36.7 8.0 %collective-permute-start.8 = (bf16[272,512]{1,0:T(8,128)(2,1)S(1)}, bf16[272,512]{1,0:T(8,128)(2,1)S(1)}, u32[]{:S(2)}, u32[]{:S(2)}) collective-permute-start(bf16[272,512]{1,0:T(8,128)(2,1)S(1)} %collective-permute-done.7.refs_4_), channel_id=1, source_target_pairs={{0,8},{1,9},{2,10},{3,11},{4,12},{5,13},{6,14},{7,15},{8,16},{9,17... | collective-permute-start | bytes 835592 | tf_op jit(solution)/shard_map/ppermute | solution.py:379
  46.1 8.7 %collective-permute-start.10 = (bf16[272,512]{1,0:T(8,128)(2,1)S(1)}, bf16[272,512]{1,0:T(8,128)(2,1)S(1)}, u32[]{:S(2)}, u32[]{:S(2)}) collective-permute-start(bf16[272,512]{1,0:T(8,128)(2,1)S(1)} %get-tuple-element.97), channel_id=1, source_target_pairs={{0,2},{1,3},{2,0},{3,1},{4,6},{5,7},{6,4},{7,5},{8,10},{9,11},{10,... | collective-permute-start | bytes 835592 | tf_op jit(solution)/shard_map/ppermute | solution.py:375
  47.8 7.8 %collective-permute-start.11 = (bf16[272,512]{1,0:T(8,128)(2,1)S(1)}, bf16[272,512]{1,0:T(8,128)(2,1)S(1)}, u32[]{:S(2)}, u32[]{:S(2)}) collective-permute-start(bf16[272,512]{1,0:T(8,128)(2,1)S(1)} %get-tuple-element.98), channel_id=1, source_target_pairs={{0,4},{1,5},{2,6},{3,7},{4,0},{5,1},{6,2},{7,3},{8,12},{9,13},{10,... | collective-permute-start | bytes 835592 | tf_op jit(solution)/shard_map/ppermute | solution.py:375
  47.8 10.1 %collective-permute-start.12 = (bf16[272,512]{1,0:T(8,128)(2,1)S(1)}, bf16[272,512]{1,0:T(8,128)(2,1)S(1)}, u32[]{:S(2)}, u32[]{:S(2)}) collective-permute-start(bf16[272,512]{1,0:T(8,128)(2,1)S(1)} %get-tuple-element.99), channel_id=1, source_target_pairs={{0,6},{1,7},{2,4},{3,5},{4,2},{5,3},{6,0},{7,1},{8,14},{9,15},{10,... | collective-permute-start | bytes 835592 | tf_op jit(solution)/shard_map/ppermute | solution.py:375
  50.0 4.8 %collective-permute-start.9 = (bf16[1,256,512]{2,1,0:T(8,128)(2,1)S(1)}, bf16[1,256,512]{2,1,0:T(8,128)(2,1)S(1)}, u32[]{:S(2)}, u32[]{:S(2)}) collective-permute-start(bf16[1,256,512]{2,1,0:T(8,128)(2,1)S(1)} %get-tuple-element.92), channel_id=1, source_target_pairs={{0,1},{1,0},{2,3},{3,2},{4,5},{5,4},{6,7},{7,6},{8,9},{9,8},{10,11... | collective-permute-start | bytes 786440 | tf_op jit(solution)/shard_map/ppermute | solution.py:371
  59.4 6.9 %collective-permute-start.13 = (bf16[3,256,512]{2,1,0:T(8,128)(2,1)S(1)}, bf16[3,256,512]{2,1,0:T(8,128)(2,1)S(1)}, u32[]{:S(2)}, u32[]{:S(2)}) collective-permute-start(bf16[3,256,512]{2,1,0:T(8,128)(2,1)S(1)} %get-tuple-element.102), channel_id=1, source_target_pairs={{0,1},{1,0},{2,3},{3,2},{4,5},{5,4},{6,7},{7,6},{8,9},{9,8},{10,11... | collective-permute-start | bytes 2359304 | tf_op jit(solution)/shard_map/ppermute | solution.py:371

commit v10 on v9

--- a/solution.py
+++ b/solution.py
@@ -320,7 +320,7 @@
 
 
 def merge_kernel(heads, scalars, *refs):
-    stacks, out = refs[:-1], refs[-1]
+    stacks, (out, result, written) = refs[:-3], refs[-3:]
     half = heads // 2
     n = LAY // heads
     mine, core = scalars[0], scalars[1]
@@ -331,11 +331,16 @@
     head = side * half + jnp.bitwise_xor(slot, mine)
     order = ((into % heads == head) & (into // heads == given % n)).astype(BF16)
     _, tokens, width = stacks[0].shape
+    copies = []
     for g in range(tokens // n):
         span = slice(g * n, (g + 1) * n)
         rows = jnp.concatenate([stack[:, span, :] for stack in stacks], axis=0)
         turned = dot(order, rows.reshape(LAY, width))
-        out[span] = turned.reshape(n, heads, width).astype(BF16)
+        result[span] = turned.reshape(n, heads, width).astype(BF16)
+        copies.append(pltpu.make_async_copy(result.at[span], out.at[span], written.at[g]))
+        copies[-1].start()
+    for copy in copies:
+        copy.wait()
 
 
 def whole(shape):
@@ -394,12 +399,13 @@
         )(*sources)
 
     gates = jnp.concatenate([input_gate.T, forget_gate.T], axis=0)
-    gates, key_vectors = lax.optimization_barrier((gates, key_vectors))
+    gates, value_vectors = lax.optimization_barrier((gates, value_vectors))
     gates_oth = swap_cores(gates)
-    k_keep, v_keep, k_send, v_send = relayout(key_vectors, value_vectors)
-    gates_oth, k_send, v_send = lax.optimization_barrier((gates_oth, k_send, v_send))
+    v_keep, v_send = relayout(value_vectors)
+    gates_oth, v_send = lax.optimization_barrier((gates_oth, v_send))
+    v_oth = swap_cores(v_send)
+    k_keep, k_send = relayout(key_vectors)
     k_oth = swap_cores(k_send)
-    v_oth = swap_cores(v_send)
     gate_shapes = [
         (heads, 2 * tokens),
         (heads, LANES),
@@ -487,16 +493,24 @@
             name="outputs",
         )(scalars, q_keep, q_oth, *terms, *entering[first : first + count])
 
-    keep, send = outputs(0, 1)
-    swapped = swap_cores(send)
-    terms, swapped = lax.optimization_barrier((terms, swapped))
-    keep_far, send = outputs(1, group - 1)
-    kept, received = [keep, keep_far], [swapped, swap_cores(send)]
+    kept, received = [], []
+    for r in range(group):
+        keep, send = outputs(r, 1)
+        kept.append(keep)
+        received.append(swap_cores(send))
+        if r == 0:
+            terms, received[0] = lax.optimization_barrier((terms, received[0]))
+        else:
+            terms, _ = lax.optimization_barrier((terms, send))
     return pl.pallas_call(
         functools.partial(merge_kernel, heads),
-        in_specs=[SMEM] + [VMEM] * 4,
-        out_specs=whole(value_vectors.shape),
+        in_specs=[SMEM] + [VMEM] * heads,
+        out_specs=pl.BlockSpec(memory_space=pl.ANY),
         out_shape=shape_of(*value_vectors.shape),
+        scratch_shapes=[
+            pltpu.VMEM(value_vectors.shape, BF16),
+            pltpu.SemaphoreType.DMA((tokens // (LAY // heads),)),
+        ],
         compiler_params=params(),
         name="merge",
     )(scalars, *kept, *received)

time: 69.4 us -> 67 us (0.965)
  waiting for transfers between devices: 29.1 us -> 23.9 us
  starting transfers between devices: 19.1 us -> 21.3 us
  Pallas kernels: 17.1 us -> 19 us
  local copies, waits for them, and re-layouts: 2.82 us -> 1.6 us
    ppermute x6, waiting for transfers between devices: 14 us -> 10.7 us  [in_group(): return lax.ppermute(x, AXES, pairs)]
    ppermute x6 -> x8, starting transfers between devices: 10.9 us -> 13.1 us  [swap_cores(): return lax.ppermute(x, AXES, [(d, d ^ 1) for d in range(devices)])]
    ppermute x6 -> x8, waiting for transfers between devices: 5.18 us -> 3.52 us  [swap_cores(): return lax.ppermute(x, AXES, [(d, d ^ 1) for d in range(devices)])]
    pallas_call x2 -> x4, Pallas kernels: 2.49 us -> 3.94 us  [outputs(): pl.pallas_call(functools.partial(output_kernel, first, count), in_specs=[...]
    unnamed x8, local copies, waits for them, and re-layouts: 2.82 us -> 1.6 us
    pallas_call x2 -> x3, Pallas kernels: 2.4 us -> 3.38 us  [relayout(): pl.pallas_call(functools.partial(relayout_kernel, half, len(sources)), in...]
  transfers between devices with their start and end apart: 14 -> 16, of which waited for: 10 -> 9; matrix products, arithmetic and copies ran while one was open for 0% -> 0% of each run, Pallas kernels for 14% -> 20%
where the time goes in v10:
time: 67 us; the launch traced here: 66.7 us
  waiting for transfers between devices  23.9 us (36%)
  starting transfers between devices  21.3 us (32%)
  Pallas kernels  19 us (28%)
  local copies, waits for them, and re-layouts  1.6 us (2%)
  other arithmetic  0.79 us (1%)
    ppermute x8, starting transfers between devices, swap_cores(): return lax.ppermute(x, AXES, [(d, d ^ 1) for d in range(devices)])  13.1 us
    ppermute x6, waiting for transfers between devices, in_group(): return lax.ppermute(x, AXES, pairs)  10.7 us
    ppermute x2, waiting for transfers between devices, to_next(): return lax.ppermute(x, AXES, [(d, d + jump) for d in range(devices - jump)])  9.69 us
    ppermute x6, starting transfers between devices, in_group(): return lax.ppermute(x, AXES, pairs)  5.59 us
    pallas_call x2, Pallas kernels, own_terms(): pl.pallas_call(functools.partial(local_kernel, first_slot, heads), in_spe...  4.41 us
    pallas_call x4, Pallas kernels, outputs(): pl.pallas_call(functools.partial(output_kernel, first, count), in_specs=[...  3.94 us
    ppermute x8, waiting for transfers between devices, swap_cores(): return lax.ppermute(x, AXES, [(d, d ^ 1) for d in range(devices)])  3.52 us
    pallas_call x3, Pallas kernels, relayout(): pl.pallas_call(functools.partial(relayout_kernel, half, len(sources)), in...  3.38 us
  transfers between devices with their start and end apart: 16, of which 9 were waited for; matrix products, arithmetic and copies ran while one was open for 0% of the time, Pallas kernels for 20%

profile of v10, /device:TPU:25, one launch (start us, length us, event | category | flops | bytes accessed | tf_op | source)
XLA Modules:
  0.0 66.7 jit_solution(5070841877233590357)
XLA Ops:
  0.0 0.0 copy-start.3
  0.0 0.7 %pad_maximum_fusion.g_own = bf16[16,256]{1,0:T(8,128)(2,1)S(1)} fusion(bf16[8,256]{1,0:T(8,128)(2,1)} %bitcast.6, bf16[8,256]{1,0:T(8,128)(2,1)} %bitcast.7), kind=kLoop, calls=%fused_computation | loop fusion | flops 16384 | bytes 16384 | tf_op jit(solution)/shard_map/concatenate | solution.py:401
  0.7 0.7 %collective-permute-start.1 = (bf16[16,256]{1,0:T(8,128)(2,1)S(1)}, bf16[16,256]{1,0:T(8,128)(2,1)S(1)}, u32[]{:S(2)}, u32[]{:S(2)}) collective-permute-start(bf16[16,256]{1,0:T(8,128)(2,1)S(1)} %pad_maximum_fusion.g_own), channel_id=1, source_target_pairs={{0,1},{1,0},{2,3},{3,2},{4,5},{5,4},{6,7},{7,6},{8,9},{9,8},{10,11... | collective-permute-start | bytes 24584 | tf_op jit(solution)/shard_map/ppermute | solution.py:376
  1.4 0.0 copy-start
  1.4 1.6 %copy-done = bf16[256,8,512]{2,1,0:T(8,128)(2,1)S(1)} copy-done((bf16[256,8,512]{2,1,0:T(8,128)(2,1)S(1)}, bf16[256,8,512]{2,1,0:T(8,128)(2,1)}, u32[]{:S(2)}) %copy-start) | copy-done | bytes 2097176
  3.0 0.0 copy-start.1
  3.0 1.7 %relayout.4 = (bf16[4,256,512]{2,1,0:T(8,128)(2,1)S(1)}, bf16[4,256,512]{2,1,0:T(8,128)(2,1)}) custom-call(bf16[256,8,512]{2,1,0:T(8,128)(2,1)S(1)} %copy-done), custom_call_target="tpu_custom_call" | custom-call | tf_op jit(solution)/shard_map/relayout/pallas_call | solution.py:392
  4.7 0.0 collective-permute-done.1.g_oth
  4.7 0.0 collective-permute-start.2
  4.7 0.0 copy-done.1
  4.7 1.3 %relayout.3 = (bf16[4,256,256]{2,1,0:T(8,128)(2,1)S(1)}, bf16[4,256,256]{2,1,0:T(8,128)(2,1)}) custom-call(bf16[256,8,256]{2,1,0:T(8,128)(2,1)S(1)} %copy-done.1), custom_call_target="tpu_custom_call" | custom-call | tf_op jit(solution)/shard_map/relayout/pallas_call | solution.py:392
  6.0 0.5 collective-permute-start
  6.5 0.0 copy-start.2
  6.5 0.1 pad_add_fusion.scalars
  6.5 0.0 copy-done.3
  6.5 0.9 %gates.1 = (f32[8,512]{1,0:T(8,128)S(1)}, f32[8,128]{1,0:T(8,128)S(1)}, f32[8,128]{1,0:T(8,128)S(1)}, f32[8,512]{1,0:T(8,128)S(1)}, f32[8,512]{1,0:T(8,128)S(1)}...) custom-call(s32[2]{0:T(128)S(1)} %pad_add_fusion.scalars, bf16[16,256]{1,0:T(8,128)(2,1)S(1)} %pad_maximum_fusion.g_own, ...), custom_call_target="tpu_custom_call" | custom-call | tf_op jit(solution)/shard_map/gates/pallas_call | solution.py:418
  7.5 0.8 %collective-permute-done.refs_2_.refs_4_ = bf16[4,256,256]{2,1,0:T(8,128)(2,1)S(1)} collective-permute-done((bf16[4,256,256]{2,1,0:T(8,128)(2,1)}, bf16[4,256,256]{2,1,0:T(8,128)(2,1)S(1)}, u32[]{:S(2)}, u32[]{:S(2)}) %collective-permute-start) | collective-permute-done | bytes 524320 | tf_op jit(solution)/shard_map/ppermute | solution.py:376
  8.3 0.0 collective-permute-done.2.refs_3_.refs_5_
  8.3 2.1 %states.1 = (bf16[272,512]{1,0:T(8,128)(2,1)S(1)}, bf16[272,512]{1,0:T(8,128)(2,1)S(1)}, bf16[272,512]{1,0:T(8,128)(2,1)S(1)}, bf16[272,512]{1,0:T(8,128)(2,1)S(1)}) custom-call(s32[2]{0:T(128)S(1)} %pad_add_fusion.scalars, bf16[4,256,256]{2,1,0:T(8,128)(2,1)S(1)} %get-tuple-element.65.refs_0_.refs_1_, ...), custom_call_target="tpu_custom_call" | custom-call | tf_op jit(solution)/shard_map/states/pallas_call | solution.py:428
  10.4 1.3 %collective-permute-start.4 = (bf16[272,512]{1,0:T(8,128)(2,1)S(1)}, bf16[272,512]{1,0:T(8,128)(2,1)S(1)}, u32[]{:S(2)}, u32[]{:S(2)}) collective-permute-start(bf16[272,512]{1,0:T(8,128)(2,1)S(1)} %get-tuple-element.81), channel_id=1, source_target_pairs={{0,2},{1,3},{2,0},{3,1},{4,6},{5,7},{6,4},{7,5},{8,10},{9,11},{10,... | collective-permute-start | bytes 835592 | tf_op jit(solution)/shard_map/ppermute | solution.py:380
  11.6 1.2 %collective-permute-start.5 = (bf16[272,512]{1,0:T(8,128)(2,1)S(1)}, bf16[272,512]{1,0:T(8,128)(2,1)S(1)}, u32[]{:S(2)}, u32[]{:S(2)}) collective-permute-start(bf16[272,512]{1,0:T(8,128)(2,1)S(1)} %get-tuple-element.82), channel_id=1, source_target_pairs={{0,4},{1,5},{2,6},{3,7},{4,0},{5,1},{6,2},{7,3},{8,12},{9,13},{10,... | collective-permute-start | bytes 835592 | tf_op jit(solution)/shard_map/ppermute | solution.py:380
  12.9 0.2 collective-permute-start.6
  13.1 0.0 copy-done.2
  13.1 0.4 relayout.5
  13.5 1.2 %collective-permute-start.3 = (bf16[4,256,256]{2,1,0:T(8,128)(2,1)S(1)}, bf16[4,256,256]{2,1,0:T(8,128)(2,1)S(1)}, u32[]{:S(2)}, u32[]{:S(2)}) collective-permute-start(bf16[4,256,256]{2,1,0:T(8,128)(2,1)S(1)} %get-tuple-element.80), channel_id=1, source_target_pairs={{0,1},{1,0},{2,3},{3,2},{4,5},{5,4},{6,7},{7,6},{8,9},{9,8},{10,11... | collective-permute-start | bytes 1572872 | tf_op jit(solution)/shard_map/ppermute | solution.py:376
  14.7 3.7 %collective-permute-done.4.refs_1_ = bf16[272,512]{1,0:T(8,128)(2,1)S(1)} collective-permute-done((bf16[272,512]{1,0:T(8,128)(2,1)S(1)}, bf16[272,512]{1,0:T(8,128)(2,1)S(1)}, u32[]{:S(2)}, u32[]{:S(2)}) %collective-permute-start.4) | collective-permute-done | bytes 278560 | tf_op jit(solution)/shard_map/ppermute | solution.py:380
  18.4 0.9 %collective-permute-done.5.refs_2_ = bf16[272,512]{1,0:T(8,128)(2,1)S(1)} collective-permute-done((bf16[272,512]{1,0:T(8,128)(2,1)S(1)}, bf16[272,512]{1,0:T(8,128)(2,1)S(1)}, u32[]{:S(2)}, u32[]{:S(2)}) %collective-permute-start.5) | collective-permute-done | bytes 278560 | tf_op jit(solution)/shard_map/ppermute | solution.py:380
  19.3 6.1 %collective-permute-done.6.refs_3_ = bf16[272,512]{1,0:T(8,128)(2,1)S(1)} collective-permute-done((bf16[272,512]{1,0:T(8,128)(2,1)S(1)}, bf16[272,512]{1,0:T(8,128)(2,1)S(1)}, u32[]{:S(2)}, u32[]{:S(2)}) %collective-permute-start.6) | collective-permute-done | bytes 278560 | tf_op jit(solution)/shard_map/ppermute | solution.py:380
  25.4 0.8 %group_total.1 = bf16[272,512]{1,0:T(8,128)(2,1)S(1)} custom-call(s32[2]{0:T(128)S(1)} %pad_add_fusion.scalars, bf16[272,512]{1,0:T(8,128)(2,1)S(1)} %get-tuple-element.99.refs_0_, bf16[272,512]{1,0:T(8,128)(2,1)S(1)} %collective-permute-done.4.refs_1_, bf16[272,512]{1,0:T(8,128)(2,1)S(1)} %collective-permute-done.5.refs_2_, ...), custom_call_target="tpu_custom_call" | custom-call | tf_op jit(solution)/shard_map/group_total/pallas_call | solution.py:437
  26.2 1.3 %collective-permute-start.7 = (bf16[272,512]{1,0:T(8,128)(2,1)S(1)}, bf16[272,512]{1,0:T(8,128)(2,1)S(1)}, u32[]{:S(2)}, u32[]{:S(2)}) collective-permute-start(bf16[272,512]{1,0:T(8,128)(2,1)S(1)} %group_total.1), channel_id=1, source_target_pairs={{0,8},{1,9},{2,10},{3,11},{4,12},{5,13},{6,14},{7,15},{8,16},{9,17... | collective-permute-start | bytes 835592 | tf_op jit(solution)/shard_map/ppermute | solution.py:384
  27.5 0.0 collective-permute-done.3.refs_3_.q_oth
  27.5 2.2 %own_terms.2 = (f32[2,2,256,512]{3,2,1,0:T(8,128)S(1)}, f32[2,2,8,256]{3,2,1,0:T(8,128)S(1)}) custom-call(s32[2]{0:T(128)S(1)} %pad_add_fusion.scalars, bf16[4,256,256]{2,1,0:T(8,128)(2,1)S(1)} %get-tuple-element.94.refs_0_.q_own, bf16[4,256,256]{2,1,0:T(8,128)(2,1)S(1)} %get-tuple-element.65.refs_0_.refs_1_, ...), custom_call_target="tpu_custom_call" | custom-call | tf_op jit(solution)/shard_map/own_terms/pallas_call | solution.py:453
  29.7 5.3 %collective-permute-done.7.refs_4_ = bf16[272,512]{1,0:T(8,128)(2,1)S(1)} collective-permute-done((bf16[272,512]{1,0:T(8,128)(2,1)S(1)}, bf16[272,512]{1,0:T(8,128)(2,1)S(1)}, u32[]{:S(2)}, u32[]{:S(2)}) %collective-permute-start.7) | collective-permute-done | bytes 278560 | tf_op jit(solution)/shard_map/ppermute | solution.py:384
  34.9 1.3 %collective-permute-start.8 = (bf16[272,512]{1,0:T(8,128)(2,1)S(1)}, bf16[272,512]{1,0:T(8,128)(2,1)S(1)}, u32[]{:S(2)}, u32[]{:S(2)}) collective-permute-start(bf16[272,512]{1,0:T(8,128)(2,1)S(1)} %collective-permute-done.7.refs_4_), channel_id=1, source_target_pairs={{0,8},{1,9},{2,10},{3,11},{4,12},{5,13},{6,14},{7,15},{8,16},{9,17... | collective-permute-start | bytes 835592 | tf_op jit(solution)/shard_map/ppermute | solution.py:384
  36.2 2.2 %own_terms.3 = (f32[2,2,256,512]{3,2,1,0:T(8,128)S(1)}, f32[2,2,8,256]{3,2,1,0:T(8,128)S(1)}) custom-call(s32[2]{0:T(128)S(1)} %pad_add_fusion.scalars, bf16[4,256,256]{2,1,0:T(8,128)(2,1)S(1)} %get-tuple-element.94.refs_0_.q_own, bf16[4,256,256]{2,1,0:T(8,128)(2,1)S(1)} %get-tuple-element.65.refs_0_.refs_1_, ...), custom_call_target="tpu_custom_call" | custom-call | tf_op jit(solution)/shard_map/own_terms/pallas_call | solution.py:453
  38.4 4.4 %collective-permute-done.8.refs_5_ = bf16[272,512]{1,0:T(8,128)(2,1)S(1)} collective-permute-done((bf16[272,512]{1,0:T(8,128)(2,1)S(1)}, bf16[272,512]{1,0:T(8,128)(2,1)S(1)}, u32[]{:S(2)}, u32[]{:S(2)}) %collective-permute-start.8) | collective-permute-done | bytes 278560 | tf_op jit(solution)/shard_map/ppermute | solution.py:384
  42.9 1.4 %entering.1 = (bf16[272,512]{1,0:T(8,128)(2,1)S(1)}, bf16[272,512]{1,0:T(8,128)(2,1)S(1)}, bf16[272,512]{1,0:T(8,128)(2,1)S(1)}, bf16[272,512]{1,0:T(8,128)(2,1)S(1)}) custom-call(s32[2]{0:T(128)S(1)} %pad_add_fusion.scalars, bf16[272,512]{1,0:T(8,128)(2,1)S(1)} %get-tuple-element.99.refs_0_, bf16[272,512]{1,0:T(8,128)(2,1)S(1)} %collective-permute-done.4.refs_1_, ...), custom_call_target="tpu_custom_call" | custom-call | tf_op jit(solution)/shard_map/entering/pallas_call | solution.py:476
  44.2 1.6 %collective-permute-start.10 = (bf16[272,512]{1,0:T(8,128)(2,1)S(1)}, bf16[272,512]{1,0:T(8,128)(2,1)S(1)}, u32[]{:S(2)}, u32[]{:S(2)}) collective-permute-start(bf16[272,512]{1,0:T(8,128)(2,1)S(1)} %get-tuple-element.107), channel_id=1, source_target_pairs={{0,2},{1,3},{2,0},{3,1},{4,6},{5,7},{6,4},{7,5},{8,10},{9,11},{10,... | collective-permute-start | bytes 835592 | tf_op jit(solution)/shard_map/ppermute | solution.py:380
  45.9 0.0 collective-permute-start.11
  45.9 1.3 %collective-permute-start.12 = (bf16[272,512]{1,0:T(8,128)(2,1)S(1)}, bf16[272,512]{1,0:T(8,128)(2,1)S(1)}, u32[]{:S(2)}, u32[]{:S(2)}) collective-permute-start(bf16[272,512]{1,0:T(8,128)(2,1)S(1)} %get-tuple-element.121), channel_id=1, source_target_pairs={{0,6},{1,7},{2,4},{3,5},{4,2},{5,3},{6,0},{7,1},{8,14},{9,15},{10,... | collective-permute-start | bytes 835592 | tf_op jit(solution)/shard_map/ppermute | solution.py:380
  47.1 1.0 %outputs.4 = (bf16[1,256,512]{2,1,0:T(8,128)(2,1)S(1)}, bf16[1,256,512]{2,1,0:T(8,128)(2,1)S(1)}) custom-call(s32[2]{0:T(128)S(1)} %pad_add_fusion.scalars, bf16[4,256,256]{2,1,0:T(8,128)(2,1)S(1)} %get-tuple-element.94.refs_0_.q_own, bf16[4,256,256]{2,1,0:T(8,128)(2,1)S(1)} %collective-permute-done.3.refs_3_.q_oth, ...), custom_call_target="tpu_custom_call" | custom-call | tf_op jit(solution)/shard_map/outputs/pallas_call | solution.py:487
  48.1 3.8 %collective-permute-start.9 = (bf16[1,256,512]{2,1,0:T(8,128)(2,1)S(1)}, bf16[1,256,512]{2,1,0:T(8,128)(2,1)S(1)}, u32[]{:S(2)}, u32[]{:S(2)}) collective-permute-start(bf16[1,256,512]{2,1,0:T(8,128)(2,1)S(1)} %get-tuple-element.102), channel_id=1, source_target_pairs={{0,1},{1,0},{2,3},{3,2},{4,5},{5,4},{6,7},{7,6},{8,9},{9,8},{10,11... | collective-permute-start | bytes 786440 | tf_op jit(solution)/shard_map/ppermute | solution.py:376
  51.9 1.2 %collective-permute-done.9.refs_4_ = bf16[1,256,512]{2,1,0:T(8,128)(2,1)S(1)} collective-permute-done((bf16[1,256,512]{2,1,0:T(8,128)(2,1)S(1)}, bf16[1,256,512]{2,1,0:T(8,128)(2,1)S(1)}, u32[]{:S(2)}, u32[]{:S(2)}) %collective-permute-start.9) | collective-permute-done | bytes 262176 | tf_op jit(solution)/shard_map/ppermute | solution.py:376
  53.1 0.0 collective-permute-done.10.refs_4_
  53.1 1.0 %outputs.5 = (bf16[1,256,512]{2,1,0:T(8,128)(2,1)S(1)}, bf16[1,256,512]{2,1,0:T(8,128)(2,1)S(1)}) custom-call(s32[2]{0:T(128)S(1)} %pad_add_fusion.scalars, bf16[4,256,256]{2,1,0:T(8,128)(2,1)S(1)} %get-tuple-element.94.refs_0_.q_own, bf16[4,256,256]{2,1,0:T(8,128)(2,1)S(1)} %collective-permute-done.3.refs_3_.q_oth, ...), custom_call_target="tpu_custom_call" | custom-call | tf_op jit(solution)/shard_map/outputs/pallas_call | solution.py:487
  54.1 3.5 %collective-permute-start.13 = (bf16[1,256,512]{2,1,0:T(8,128)(2,1)S(1)}, bf16[1,256,512]{2,1,0:T(8,128)(2,1)S(1)}, u32[]{:S(2)}, u32[]{:S(2)}) collective-permute-start(bf16[1,256,512]{2,1,0:T(8,128)(2,1)S(1)} %get-tuple-element.109), channel_id=1, source_target_pairs={{0,1},{1,0},{2,3},{3,2},{4,5},{5,4},{6,7},{7,6},{8,9},{9,8},{10,11... | collective-permute-start | bytes 786440 | tf_op jit(solution)/shard_map/ppermute | solution.py:376
  57.5 0.0 collective-permute-done.11.refs_4_
  57.5 1.0 %outputs.6 = (bf16[1,256,512]{2,1,0:T(8,128)(2,1)S(1)}, bf16[1,256,512]{2,1,0:T(8,128)(2,1)S(1)}) custom-call(s32[2]{0:T(128)S(1)} %pad_add_fusion.scalars, bf16[4,256,256]{2,1,0:T(8,128)(2,1)S(1)} %get-tuple-element.94.refs_0_.q_own, bf16[4,256,256]{2,1,0:T(8,128)(2,1)S(1)} %collective-permute-done.3.refs_3_.q_oth, ...), custom_call_target="tpu_custom_call" | custom-call | tf_op jit(solution)/shard_map/outputs/pallas_call | solution.py:487
  58.5 3.4 %collective-permute-start.14 = (bf16[1,256,512]{2,1,0:T(8,128)(2,1)S(1)}, bf16[1,256,512]{2,1,0:T(8,128)(2,1)S(1)}, u32[]{:S(2)}, u32[]{:S(2)}) collective-permute-start(bf16[1,256,512]{2,1,0:T(8,128)(2,1)S(1)} %get-tuple-element.116), channel_id=1, source_target_pairs={{0,1},{1,0},{2,3},{3,2},{4,5},{5,4},{6,7},{7,6},{8,9},{9,8},{10,11... | collective-permute-start | bytes 786440 | tf_op jit(solution)/shard_map/ppermute | solution.py:376
  62.0 0.0 collective-permute-done.12.refs_4_
  62.0 1.0 %outputs.7 = (bf16[1,256,512]{2,1,0:T(8,128)(2,1)S(1)}, bf16[1,256,512]{2,1,0:T(8,128)(2,1)S(1)}) custom-call(s32[2]{0:T(128)S(1)} %pad_add_fusion.scalars, bf16[4,256,256]{2,1,0:T(8,128)(2,1)S(1)} %get-tuple-element.94.refs_0_.q_own, bf16[4,256,256]{2,1,0:T(8,128)(2,1)S(1)} %collective-permute-done.3.refs_3_.q_oth, ...), custom_call_target="tpu_custom_call" | custom-call | tf_op jit(solution)/shard_map/outputs/pallas_call | solution.py:487
  63.0 0.1 collective-permute-start.15
  63.0 0.0 collective-permute-done.13.refs_5_
  63.0 0.1 collective-permute-done.14.refs_6_
  63.1 1.4 %collective-permute-done.15.refs_7_ = bf16[1,256,512]{2,1,0:T(8,128)(2,1)S(1)} collective-permute-done((bf16[1,256,512]{2,1,0:T(8,128)(2,1)S(1)}, bf16[1,256,512]{2,1,0:T(8,128)(2,1)S(1)}, u32[]{:S(2)}, u32[]{:S(2)}) %collective-permute-start.15) | collective-permute-done | bytes 262176 | tf_op jit(solution)/shard_map/ppermute | solution.py:376
  64.6 2.2 %merge.1 = bf16[256,8,512]{2,1,0:T(8,128)(2,1)} custom-call(s32[2]{0:T(128)S(1)} %pad_add_fusion.scalars, bf16[1,256,512]{2,1,0:T(8,128)(2,1)S(1)} %get-tuple-element.101.refs_0_, bf16[1,256,512]{2,1,0:T(8,128)(2,1)S(1)} %get-tuple-element.108.refs_1_, bf16[1,256,512]{2,1,0:T(8,128)(2,1)S(1)} %get-tuple-element.115.refs_2_, ...), custom_call_target="tpu_custom_call" | custom-call | tf_op jit(solution)/shard_map/merge/pallas_call | solution.py:505
Async XLA Ops:
  0.0 6.5 %copy-start.3 = (s32[1024]{0:T(1024)S(1)}, s32[1024]{0:T(1024)}, u32[]{:S(2)}) copy-start(s32[1024]{0:T(1024)} %param.11) | copy-start | bytes 12292
  0.7 4.0 %collective-permute-start.1 = (bf16[16,256]{1,0:T(8,128)(2,1)S(1)}, bf16[16,256]{1,0:T(8,128)(2,1)S(1)}, u32[]{:S(2)}, u32[]{:S(2)}) collective-permute-start(bf16[16,256]{1,0:T(8,128)(2,1)S(1)} %pad_maximum_fusion.g_own), channel_id=1, source_target_pairs={{0,1},{1,0},{2,3},{3,2},{4,5},{5,4},{6,7},{7,6},{8,9},{9,8},{10,11... | collective-permute-start | bytes 24584 | tf_op jit(solution)/shard_map/ppermute | solution.py:376
  1.4 1.6 %copy-start = (bf16[256,8,512]{2,1,0:T(8,128)(2,1)S(1)}, bf16[256,8,512]{2,1,0:T(8,128)(2,1)}, u32[]{:S(2)}) copy-start(bf16[256,8,512]{2,1,0:T(8,128)(2,1)} %refs_0_.2) | copy-start | bytes 6291460
  3.0 1.7 %copy-start.1 = (bf16[256,8,256]{2,1,0:T(8,128)(2,1)S(1)}, bf16[256,8,256]{2,1,0:T(8,128)(2,1)}, u32[]{:S(2)}) copy-start(bf16[256,8,256]{2,1,0:T(8,128)(2,1)} %refs_0_.1) | copy-start | bytes 3145732
  4.7 3.6 %collective-permute-start.2 = (bf16[4,256,512]{2,1,0:T(8,128)(2,1)}, bf16[4,256,512]{2,1,0:T(8,128)(2,1)S(1)}, u32[]{:S(2)}, u32[]{:S(2)}) collective-permute-start(bf16[4,256,512]{2,1,0:T(8,128)(2,1)} %get-tuple-element.71), channel_id=1, source_target_pairs={{0,1},{1,0},{2,3},{3,2},{4,5},{5,4},{6,7},{7,6},{8,9},{9,8},{10,11... | collective-permute-start | bytes 3145736 | tf_op jit(solution)/shard_map/ppermute | solution.py:376
  6.0 2.4 %collective-permute-start = (bf16[4,256,256]{2,1,0:T(8,128)(2,1)}, bf16[4,256,256]{2,1,0:T(8,128)(2,1)S(1)}, u32[]{:S(2)}, u32[]{:S(2)}) collective-permute-start(bf16[4,256,256]{2,1,0:T(8,128)(2,1)} %get-tuple-element.68), channel_id=1, source_target_pairs={{0,1},{1,0},{2,3},{3,2},{4,5},{5,4},{6,7},{7,6},{8,9},{9,8},{10,11... | collective-permute-start | bytes 1572872 | tf_op jit(solution)/shard_map/ppermute | solution.py:376
  6.5 6.6 %copy-start.2 = (bf16[256,8,256]{2,1,0:T(8,128)(2,1)S(1)}, bf16[256,8,256]{2,1,0:T(8,128)(2,1)}, u32[]{:S(2)}) copy-start(bf16[256,8,256]{2,1,0:T(8,128)(2,1)} %refs_0_.3) | copy-start | bytes 3145732
  10.4 8.0 %collective-permute-start.4 = (bf16[272,512]{1,0:T(8,128)(2,1)S(1)}, bf16[272,512]{1,0:T(8,128)(2,1)S(1)}, u32[]{:S(2)}, u32[]{:S(2)}) collective-permute-start(bf16[272,512]{1,0:T(8,128)(2,1)S(1)} %get-tuple-element.81), channel_id=1, source_target_pairs={{0,2},{1,3},{2,0},{3,1},{4,6},{5,7},{6,4},{7,5},{8,10},{9,11},{10,... | collective-permute-start | bytes 835592 | tf_op jit(solution)/shard_map/ppermute | solution.py:380
  11.6 7.7 %collective-permute-start.5 = (bf16[272,512]{1,0:T(8,128)(2,1)S(1)}, bf16[272,512]{1,0:T(8,128)(2,1)S(1)}, u32[]{:S(2)}, u32[]{:S(2)}) collective-permute-start(bf16[272,512]{1,0:T(8,128)(2,1)S(1)} %get-tuple-element.82), channel_id=1, source_target_pairs={{0,4},{1,5},{2,6},{3,7},{4,0},{5,1},{6,2},{7,3},{8,12},{9,13},{10,... | collective-permute-start | bytes 835592 | tf_op jit(solution)/shard_map/ppermute | solution.py:380
  12.9 12.5 %collective-permute-start.6 = (bf16[272,512]{1,0:T(8,128)(2,1)S(1)}, bf16[272,512]{1,0:T(8,128)(2,1)S(1)}, u32[]{:S(2)}, u32[]{:S(2)}) collective-permute-start(bf16[272,512]{1,0:T(8,128)(2,1)S(1)} %get-tuple-element.83), channel_id=1, source_target_pairs={{0,6},{1,7},{2,4},{3,5},{4,2},{5,3},{6,0},{7,1},{8,14},{9,15},{10,... | collective-permute-start | bytes 835592 | tf_op jit(solution)/shard_map/ppermute | solution.py:380
  13.5 13.9 %collective-permute-start.3 = (bf16[4,256,256]{2,1,0:T(8,128)(2,1)S(1)}, bf16[4,256,256]{2,1,0:T(8,128)(2,1)S(1)}, u32[]{:S(2)}, u32[]{:S(2)}) collective-permute-start(bf16[4,256,256]{2,1,0:T(8,128)(2,1)S(1)} %get-tuple-element.80), channel_id=1, source_target_pairs={{0,1},{1,0},{2,3},{3,2},{4,5},{5,4},{6,7},{7,6},{8,9},{9,8},{10,11... | collective-permute-start | bytes 1572872 | tf_op jit(solution)/shard_map/ppermute | solution.py:376
  26.2 8.8 %collective-permute-start.7 = (bf16[272,512]{1,0:T(8,128)(2,1)S(1)}, bf16[272,512]{1,0:T(8,128)(2,1)S(1)}, u32[]{:S(2)}, u32[]{:S(2)}) collective-permute-start(bf16[272,512]{1,0:T(8,128)(2,1)S(1)} %group_total.1), channel_id=1, source_target_pairs={{0,8},{1,9},{2,10},{3,11},{4,12},{5,13},{6,14},{7,15},{8,16},{9,17... | collective-permute-start | bytes 835592 | tf_op jit(solution)/shard_map/ppermute | solution.py:384
  34.9 7.9 %collective-permute-start.8 = (bf16[272,512]{1,0:T(8,128)(2,1)S(1)}, bf16[272,512]{1,0:T(8,128)(2,1)S(1)}, u32[]{:S(2)}, u32[]{:S(2)}) collective-permute-start(bf16[272,512]{1,0:T(8,128)(2,1)S(1)} %collective-permute-done.7.refs_4_), channel_id=1, source_target_pairs={{0,8},{1,9},{2,10},{3,11},{4,12},{5,13},{6,14},{7,15},{8,16},{9,17... | collective-permute-start | bytes 835592 | tf_op jit(solution)/shard_map/ppermute | solution.py:384
  44.2 8.8 %collective-permute-start.10 = (bf16[272,512]{1,0:T(8,128)(2,1)S(1)}, bf16[272,512]{1,0:T(8,128)(2,1)S(1)}, u32[]{:S(2)}, u32[]{:S(2)}) collective-permute-start(bf16[272,512]{1,0:T(8,128)(2,1)S(1)} %get-tuple-element.107), channel_id=1, source_target_pairs={{0,2},{1,3},{2,0},{3,1},{4,6},{5,7},{6,4},{7,5},{8,10},{9,11},{10,... | collective-permute-start | bytes 835592 | tf_op jit(solution)/shard_map/ppermute | solution.py:380
  45.9 11.7 %collective-permute-start.11 = (bf16[272,512]{1,0:T(8,128)(2,1)S(1)}, bf16[272,512]{1,0:T(8,128)(2,1)S(1)}, u32[]{:S(2)}, u32[]{:S(2)}) collective-permute-start(bf16[272,512]{1,0:T(8,128)(2,1)S(1)} %get-tuple-element.114), channel_id=1, source_target_pairs={{0,4},{1,5},{2,6},{3,7},{4,0},{5,1},{6,2},{7,3},{8,12},{9,13},{10,... | collective-permute-start | bytes 835592 | tf_op jit(solution)/shard_map/ppermute | solution.py:380
  45.9 16.1 %collective-permute-start.12 = (bf16[272,512]{1,0:T(8,128)(2,1)S(1)}, bf16[272,512]{1,0:T(8,128)(2,1)S(1)}, u32[]{:S(2)}, u32[]{:S(2)}) collective-permute-start(bf16[272,512]{1,0:T(8,128)(2,1)S(1)} %get-tuple-element.121), channel_id=1, source_target_pairs={{0,6},{1,7},{2,4},{3,5},{4,2},{5,3},{6,0},{7,1},{8,14},{9,15},{10,... | collective-permute-start | bytes 835592 | tf_op jit(solution)/shard_map/ppermute | solution.py:380
  48.1 4.9 %collective-permute-start.9 = (bf16[1,256,512]{2,1,0:T(8,128)(2,1)S(1)}, bf16[1,256,512]{2,1,0:T(8,128)(2,1)S(1)}, u32[]{:S(2)}, u32[]{:S(2)}) collective-permute-start(bf16[1,256,512]{2,1,0:T(8,128)(2,1)S(1)} %get-tuple-element.102), channel_id=1, source_target_pairs={{0,1},{1,0},{2,3},{3,2},{4,5},{5,4},{6,7},{7,6},{8,9},{9,8},{10,11... | collective-permute-start | bytes 786440 | tf_op jit(solution)/shard_map/ppermute | solution.py:376
  54.1 9.0 %collective-permute-start.13 = (bf16[1,256,512]{2,1,0:T(8,128)(2,1)S(1)}, bf16[1,256,512]{2,1,0:T(8,128)(2,1)S(1)}, u32[]{:S(2)}, u32[]{:S(2)}) collective-permute-start(bf16[1,256,512]{2,1,0:T(8,128)(2,1)S(1)} %get-tuple-element.109), channel_id=1, source_target_pairs={{0,1},{1,0},{2,3},{3,2},{4,5},{5,4},{6,7},{7,6},{8,9},{9,8},{10,11... | collective-permute-start | bytes 786440 | tf_op jit(solution)/shard_map/ppermute | solution.py:376
  58.5 4.6 %collective-permute-start.14 = (bf16[1,256,512]{2,1,0:T(8,128)(2,1)S(1)}, bf16[1,256,512]{2,1,0:T(8,128)(2,1)S(1)}, u32[]{:S(2)}, u32[]{:S(2)}) collective-permute-start(bf16[1,256,512]{2,1,0:T(8,128)(2,1)S(1)} %get-tuple-element.116), channel_id=1, source_target_pairs={{0,1},{1,0},{2,3},{3,2},{4,5},{5,4},{6,7},{7,6},{8,9},{9,8},{10,11... | collective-permute-start | bytes 786440 | tf_op jit(solution)/shard_map/ppermute | solution.py:376
  63.0 1.6 %collective-permute-start.15 = (bf16[1,256,512]{2,1,0:T(8,128)(2,1)S(1)}, bf16[1,256,512]{2,1,0:T(8,128)(2,1)S(1)}, u32[]{:S(2)}, u32[]{:S(2)}) collective-permute-start(bf16[1,256,512]{2,1,0:T(8,128)(2,1)S(1)} %get-tuple-element.124), channel_id=1, source_target_pairs={{0,1},{1,0},{2,3},{3,2},{4,5},{5,4},{6,7},{7,6},{8,9},{9,8},{10,11... | collective-permute-start | bytes 786440 | tf_op jit(solution)/shard_map/ppermute | solution.py:376

commit v11 on v10

--- a/solution.py
+++ b/solution.py
@@ -9,7 +9,8 @@
 
 AXES = ("ctx", "hv")
 FLOOR_NEG = -1e30
-META = 16
+META = 8
+PAD = 16
 LANES = 128
 LAY = 256
 F32, BF16 = jnp.float32, jnp.bfloat16
@@ -90,21 +91,25 @@
     return ((inside % heads == out // n) & (inside // heads == out % n)).astype(BF16)
 
 
-def relayout_kernel(half, count, *refs):
-    sources, outs = refs[:count], refs[count:]
+def relayout_kernel(half, source, keep, send, held, landed):
     heads = 2 * half
     n = LAY // heads
     core = lax.axis_index("hv") % 2
+    tokens, _, width = source.shape
+    spans = [slice(g * n, (g + 1) * n) for g in range(tokens // n)]
+    copies = [
+        pltpu.make_async_copy(source.at[span], held.at[span], landed.at[g])
+        for g, span in enumerate(spans)
+    ]
+    for copy in copies:
+        copy.start()
     order = by_head_order(heads)
-    for index, source in enumerate(sources):
-        keep, send = outs[index], outs[count + index]
-        tokens, _, width = source.shape
-        for g in range(tokens // n):
-            span = slice(g * n, (g + 1) * n)
-            rows = dot(order, source[span].reshape(LAY, width)).astype(BF16)
-            rows = rows.reshape(heads, n, width)
-            keep[:, span, :] = jnp.where(core == 0, rows[:half], rows[half:])
-            send[:, span, :] = jnp.where(core == 0, rows[half:], rows[:half])
+    for span, copy in zip(spans, copies, strict=True):
+        copy.wait()
+        rows = dot(order, held[span].reshape(LAY, width)).astype(BF16)
+        rows = rows.reshape(heads, n, width)
+        keep[:, span, :] = jnp.where(core == 0, rows[:half], rows[half:])
+        send[:, span, :] = jnp.where(core == 0, rows[half:], rows[:half])
 
 
 def gates_kernel(heads, scalars, g_own, g_oth, ids_ref, *outs):
@@ -151,7 +156,7 @@
             high.append(scaled.astype(BF16))
             low.append((scaled - high[-1].astype(F32)).astype(BF16))
             values.append(v_ref[local_head])
-            pieces = jnp.concatenate(split3(f) + (jnp.zeros((META - 3, tokens), F32),), axis=0)
+            pieces = jnp.concatenate(split3(f) + (jnp.zeros((PAD - 3, tokens), F32),), axis=0)
             sums = dot(pieces.astype(BF16), keys)
             line = (sums[2:3] + sums[1:2]) + sums[0:1]
             normal = line if normal is None else normal + line
@@ -295,7 +300,7 @@
         at = slot % early
         local_head = jnp.bitwise_xor(scalars[0], slot)
         normal, top, _, doc = read_meta([payload])
-        pieces = split3(normal) + (jnp.zeros((META - 3, key_width), F32),)
+        pieces = split3(normal) + (jnp.zeros((PAD - 3, key_width), F32),)
         pieces = jnp.concatenate(pieces, axis=0).astype(BF16)
         memory = payload[:key_width, :]
         width = memory.shape[1]
@@ -387,19 +392,22 @@
     state = (rows, value_width)
     sizes = {key_width: (half, tokens, key_width), value_width: (half, tokens, value_width)}
 
-    def relayout(*sources):
-        outs = [sizes[x.shape[2]] for x in sources] * 2
+    def relayout(source):
+        size = sizes[source.shape[2]]
         return pl.pallas_call(
-            functools.partial(relayout_kernel, half, len(sources)),
-            in_specs=[whole(x.shape) for x in sources],
-            out_specs=[VMEM] * len(outs),
-            out_shape=[shape_of(*s) for s in outs],
+            functools.partial(relayout_kernel, half),
+            in_specs=[pl.BlockSpec(memory_space=pl.ANY)],
+            out_specs=[VMEM] * 2,
+            out_shape=[shape_of(*size)] * 2,
+            scratch_shapes=[
+                pltpu.VMEM(source.shape, BF16),
+                pltpu.SemaphoreType.DMA((tokens // (LAY // heads),)),
+            ],
             compiler_params=params(),
-                name="relayout",
-        )(*sources)
+            name="relayout",
+        )(source)
 
     gates = jnp.concatenate([input_gate.T, forget_gate.T], axis=0)
-    gates, value_vectors = lax.optimization_barrier((gates, value_vectors))
     gates_oth = swap_cores(gates)
     v_keep, v_send = relayout(value_vectors)
     gates_oth, v_send = lax.optimization_barrier((gates_oth, v_send))

time: 67 us -> 69.9 us (1.043)
  Pallas kernels: 19 us -> 25.9 us
  waiting for transfers between devices: 23.9 us -> 19.7 us
    pallas_call x3, Pallas kernels: 3.38 us -> 10.3 us  [relayout(): pl.pallas_call(functools.partial(relayout_kernel, half), in_specs=[pl.Blo...]
    ppermute x6, waiting for transfers between devices: 10.7 us -> 7.34 us  [in_group(): return lax.ppermute(x, AXES, pairs)]
    ppermute x2, waiting for transfers between devices: 9.69 us -> 8.96 us  [to_next(): return lax.ppermute(x, AXES, [(d, d + jump) for d in range(devices - jump)])]
  transfers between devices with their start and end apart: 16 -> 16, of which waited for: 9 -> 9; matrix products, arithmetic and copies ran while one was open for 0% -> 0% of each run, Pallas kernels for 20% -> 29%
where the time goes in v11:
time: 69.9 us; the launch traced here: 69.7 us
  Pallas kernels  25.9 us (37%)
  starting transfers between devices  21.3 us (30%)
  waiting for transfers between devices  19.7 us (28%)
  local copies, waits for them, and re-layouts  1.6 us (2%)
  other arithmetic  0.79 us (1%)
    ppermute x8, starting transfers between devices, swap_cores(): return lax.ppermute(x, AXES, [(d, d ^ 1) for d in range(devices)])  13 us
    pallas_call x3, Pallas kernels, relayout(): pl.pallas_call(functools.partial(relayout_kernel, half), in_specs=[pl.Blo...  10.3 us
    ppermute x2, waiting for transfers between devices, to_next(): return lax.ppermute(x, AXES, [(d, d + jump) for d in range(devices - jump)])  8.96 us
    ppermute x6, waiting for transfers between devices, in_group(): return lax.ppermute(x, AXES, pairs)  7.34 us
    ppermute x6, starting transfers between devices, in_group(): return lax.ppermute(x, AXES, pairs)  5.58 us
    pallas_call x2, Pallas kernels, own_terms(): pl.pallas_call(functools.partial(local_kernel, first_slot, heads), in_spe...  4.4 us
    pallas_call x4, Pallas kernels, outputs(): pl.pallas_call(functools.partial(output_kernel, first, count), in_specs=[...  3.94 us
    ppermute x8, waiting for transfers between devices, swap_cores(): return lax.ppermute(x, AXES, [(d, d ^ 1) for d in range(devices)])  3.42 us
  transfers between devices with their start and end apart: 16, of which 9 were waited for; matrix products, arithmetic and copies ran while one was open for 0% of the time, Pallas kernels for 29%

profile of v11, /device:TPU:25, one launch (start us, length us, event | category | flops | bytes accessed | tf_op | source)
XLA Modules:
  0.0 69.7 jit_solution(4244859327323172718)
XLA Ops:
  0.0 0.0 copy-start.3
  0.0 0.7 %pad_maximum_fusion.g_own = bf16[16,256]{1,0:T(8,128)(2,1)S(1)} fusion(bf16[8,256]{1,0:T(8,128)(2,1)} %bitcast.6, bf16[8,256]{1,0:T(8,128)(2,1)} %bitcast.7), kind=kLoop, calls=%fused_computation | loop fusion | flops 16384 | bytes 16384 | tf_op jit(solution)/shard_map/concatenate | solution.py:410
  0.7 0.7 collective-permute-start.1
  1.4 0.0 copy-start
  1.4 1.6 %copy-done = bf16[256,8,512]{2,1,0:T(8,128)(2,1)S(1)} copy-done((bf16[256,8,512]{2,1,0:T(8,128)(2,1)S(1)}, bf16[256,8,512]{2,1,0:T(8,128)(2,1)}, u32[]{:S(2)}) %copy-start) | copy-done | bytes 2097176
  3.0 0.0 copy-start.1
  3.0 3.1 %relayout.4 = (bf16[4,256,512]{2,1,0:T(8,128)(2,1)S(1)}, bf16[4,256,512]{2,1,0:T(8,128)(2,1)}) custom-call(bf16[256,8,512]{2,1,0:T(8,128)(2,1)S(1)} %copy-done), custom_call_target="tpu_custom_call" | custom-call | tf_op jit(solution)/shard_map/relayout/pallas_call | solution.py:397
  6.1 0.0 collective-permute-done.1.g_oth
  6.1 0.1 collective-permute-start.2
  6.2 0.0 copy-done.1
  6.2 4.0 %relayout.3 = (bf16[4,256,256]{2,1,0:T(8,128)(2,1)S(1)}, bf16[4,256,256]{2,1,0:T(8,128)(2,1)}) custom-call(bf16[256,8,256]{2,1,0:T(8,128)(2,1)S(1)} %copy-done.1), custom_call_target="tpu_custom_call" | custom-call | tf_op jit(solution)/shard_map/relayout/pallas_call | solution.py:397
  10.2 0.5 collective-permute-start
  10.7 0.0 copy-start.2
  10.7 0.1 pad_add_fusion.scalars
  10.8 0.0 copy-done.3
  10.8 0.9 %gates.1 = (f32[8,512]{1,0:T(8,128)S(1)}, f32[8,128]{1,0:T(8,128)S(1)}, f32[8,128]{1,0:T(8,128)S(1)}, f32[8,512]{1,0:T(8,128)S(1)}, f32[8,512]{1,0:T(8,128)S(1)}...) custom-call(s32[2]{0:T(128)S(1)} %pad_add_fusion.scalars, bf16[16,256]{1,0:T(8,128)(2,1)S(1)} %pad_maximum_fusion.g_own, ...), custom_call_target="tpu_custom_call" | custom-call | tf_op jit(solution)/shard_map/gates/pallas_call | solution.py:426
  11.7 0.7 %collective-permute-done.refs_2_.refs_4_ = bf16[4,256,256]{2,1,0:T(8,128)(2,1)S(1)} collective-permute-done((bf16[4,256,256]{2,1,0:T(8,128)(2,1)}, bf16[4,256,256]{2,1,0:T(8,128)(2,1)S(1)}, u32[]{:S(2)}, u32[]{:S(2)}) %collective-permute-start) | collective-permute-done | bytes 524320 | tf_op jit(solution)/shard_map/ppermute | solution.py:381
  12.5 0.0 collective-permute-done.2.refs_3_.refs_5_
  12.5 2.1 %states.1 = (bf16[264,512]{1,0:T(8,128)(2,1)S(1)}, bf16[264,512]{1,0:T(8,128)(2,1)S(1)}, bf16[264,512]{1,0:T(8,128)(2,1)S(1)}, bf16[264,512]{1,0:T(8,128)(2,1)S(1)}) custom-call(s32[2]{0:T(128)S(1)} %pad_add_fusion.scalars, bf16[4,256,256]{2,1,0:T(8,128)(2,1)S(1)} %get-tuple-element.63.refs_0_.refs_1_, ...), custom_call_target="tpu_custom_call" | custom-call | tf_op jit(solution)/shard_map/states/pallas_call | solution.py:436
  14.5 1.3 %collective-permute-start.4 = (bf16[264,512]{1,0:T(8,128)(2,1)S(1)}, bf16[264,512]{1,0:T(8,128)(2,1)S(1)}, u32[]{:S(2)}, u32[]{:S(2)}) collective-permute-start(bf16[264,512]{1,0:T(8,128)(2,1)S(1)} %get-tuple-element.77), channel_id=1, source_target_pairs={{0,2},{1,3},{2,0},{3,1},{4,6},{5,7},{6,4},{7,5},{8,10},{9,11},{10,... | collective-permute-start | bytes 811016 | tf_op jit(solution)/shard_map/ppermute | solution.py:385
  15.8 1.2 %collective-permute-start.5 = (bf16[264,512]{1,0:T(8,128)(2,1)S(1)}, bf16[264,512]{1,0:T(8,128)(2,1)S(1)}, u32[]{:S(2)}, u32[]{:S(2)}) collective-permute-start(bf16[264,512]{1,0:T(8,128)(2,1)S(1)} %get-tuple-element.78), channel_id=1, source_target_pairs={{0,4},{1,5},{2,6},{3,7},{4,0},{5,1},{6,2},{7,3},{8,12},{9,13},{10,... | collective-permute-start | bytes 811016 | tf_op jit(solution)/shard_map/ppermute | solution.py:385
  17.0 0.2 collective-permute-start.6
  17.2 0.0 copy-done.2
  17.2 3.2 %relayout.5 = (bf16[4,256,256]{2,1,0:T(8,128)(2,1)S(1)}, bf16[4,256,256]{2,1,0:T(8,128)(2,1)S(1)}) custom-call(bf16[256,8,256]{2,1,0:T(8,128)(2,1)S(1)} %copy-done.2), custom_call_target="tpu_custom_call" | custom-call | tf_op jit(solution)/shard_map/relayout/pallas_call | solution.py:397
  20.4 1.3 %collective-permute-start.3 = (bf16[4,256,256]{2,1,0:T(8,128)(2,1)S(1)}, bf16[4,256,256]{2,1,0:T(8,128)(2,1)S(1)}, u32[]{:S(2)}, u32[]{:S(2)}) collective-permute-start(bf16[4,256,256]{2,1,0:T(8,128)(2,1)S(1)} %get-tuple-element.76), channel_id=1, source_target_pairs={{0,1},{1,0},{2,3},{3,2},{4,5},{5,4},{6,7},{7,6},{8,9},{9,8},{10,11... | collective-permute-start | bytes 1572872 | tf_op jit(solution)/shard_map/ppermute | solution.py:381
  21.7 0.5 collective-permute-done.4.refs_1_
  22.3 0.9 %collective-permute-done.5.refs_2_ = bf16[264,512]{1,0:T(8,128)(2,1)S(1)} collective-permute-done((bf16[264,512]{1,0:T(8,128)(2,1)S(1)}, bf16[264,512]{1,0:T(8,128)(2,1)S(1)}, u32[]{:S(2)}, u32[]{:S(2)}) %collective-permute-start.5) | collective-permute-done | bytes 270368 | tf_op jit(solution)/shard_map/ppermute | solution.py:385
  23.2 5.9 %collective-permute-done.6.refs_3_ = bf16[264,512]{1,0:T(8,128)(2,1)S(1)} collective-permute-done((bf16[264,512]{1,0:T(8,128)(2,1)S(1)}, bf16[264,512]{1,0:T(8,128)(2,1)S(1)}, u32[]{:S(2)}, u32[]{:S(2)}) %collective-permute-start.6) | collective-permute-done | bytes 270368 | tf_op jit(solution)/shard_map/ppermute | solution.py:385
  29.1 0.8 %group_total.1 = bf16[264,512]{1,0:T(8,128)(2,1)S(1)} custom-call(s32[2]{0:T(128)S(1)} %pad_add_fusion.scalars, bf16[264,512]{1,0:T(8,128)(2,1)S(1)} %get-tuple-element.95.refs_0_, bf16[264,512]{1,0:T(8,128)(2,1)S(1)} %collective-permute-done.4.refs_1_, bf16[264,512]{1,0:T(8,128)(2,1)S(1)} %collective-permute-done.5.refs_2_, ...), custom_call_target="tpu_custom_call" | custom-call | tf_op jit(solution)/shard_map/group_total/pallas_call | solution.py:445
  29.9 1.3 %collective-permute-start.7 = (bf16[264,512]{1,0:T(8,128)(2,1)S(1)}, bf16[264,512]{1,0:T(8,128)(2,1)S(1)}, u32[]{:S(2)}, u32[]{:S(2)}) collective-permute-start(bf16[264,512]{1,0:T(8,128)(2,1)S(1)} %group_total.1), channel_id=1, source_target_pairs={{0,8},{1,9},{2,10},{3,11},{4,12},{5,13},{6,14},{7,15},{8,16},{9,17... | collective-permute-start | bytes 811016 | tf_op jit(solution)/shard_map/ppermute | solution.py:389
  31.2 0.0 collective-permute-done.3.refs_3_.q_oth
  31.2 2.2 %own_terms.2 = (f32[2,2,256,512]{3,2,1,0:T(8,128)S(1)}, f32[2,2,8,256]{3,2,1,0:T(8,128)S(1)}) custom-call(s32[2]{0:T(128)S(1)} %pad_add_fusion.scalars, bf16[4,256,256]{2,1,0:T(8,128)(2,1)S(1)} %get-tuple-element.90.refs_0_.q_own, bf16[4,256,256]{2,1,0:T(8,128)(2,1)S(1)} %get-tuple-element.63.refs_0_.refs_1_, ...), custom_call_target="tpu_custom_call" | custom-call | tf_op jit(solution)/shard_map/own_terms/pallas_call | solution.py:461
  33.4 5.0 %collective-permute-done.7.refs_4_ = bf16[264,512]{1,0:T(8,128)(2,1)S(1)} collective-permute-done((bf16[264,512]{1,0:T(8,128)(2,1)S(1)}, bf16[264,512]{1,0:T(8,128)(2,1)S(1)}, u32[]{:S(2)}, u32[]{:S(2)}) %collective-permute-start.7) | collective-permute-done | bytes 270368 | tf_op jit(solution)/shard_map/ppermute | solution.py:389
  38.4 1.5 %collective-permute-start.8 = (bf16[264,512]{1,0:T(8,128)(2,1)S(1)}, bf16[264,512]{1,0:T(8,128)(2,1)S(1)}, u32[]{:S(2)}, u32[]{:S(2)}) collective-permute-start(bf16[264,512]{1,0:T(8,128)(2,1)S(1)} %collective-permute-done.7.refs_4_), channel_id=1, source_target_pairs={{0,8},{1,9},{2,10},{3,11},{4,12},{5,13},{6,14},{7,15},{8,16},{9,17... | collective-permute-start | bytes 811016 | tf_op jit(solution)/shard_map/ppermute | solution.py:389
  39.8 2.2 %own_terms.3 = (f32[2,2,256,512]{3,2,1,0:T(8,128)S(1)}, f32[2,2,8,256]{3,2,1,0:T(8,128)S(1)}) custom-call(s32[2]{0:T(128)S(1)} %pad_add_fusion.scalars, bf16[4,256,256]{2,1,0:T(8,128)(2,1)S(1)} %get-tuple-element.90.refs_0_.q_own, bf16[4,256,256]{2,1,0:T(8,128)(2,1)S(1)} %get-tuple-element.63.refs_0_.refs_1_, ...), custom_call_target="tpu_custom_call" | custom-call | tf_op jit(solution)/shard_map/own_terms/pallas_call | solution.py:461
  42.0 4.0 %collective-permute-done.8.refs_5_ = bf16[264,512]{1,0:T(8,128)(2,1)S(1)} collective-permute-done((bf16[264,512]{1,0:T(8,128)(2,1)S(1)}, bf16[264,512]{1,0:T(8,128)(2,1)S(1)}, u32[]{:S(2)}, u32[]{:S(2)}) %collective-permute-start.8) | collective-permute-done | bytes 270368 | tf_op jit(solution)/shard_map/ppermute | solution.py:389
  46.0 1.4 %entering.1 = (bf16[264,512]{1,0:T(8,128)(2,1)S(1)}, bf16[264,512]{1,0:T(8,128)(2,1)S(1)}, bf16[264,512]{1,0:T(8,128)(2,1)S(1)}, bf16[264,512]{1,0:T(8,128)(2,1)S(1)}) custom-call(s32[2]{0:T(128)S(1)} %pad_add_fusion.scalars, bf16[264,512]{1,0:T(8,128)(2,1)S(1)} %get-tuple-element.95.refs_0_, bf16[264,512]{1,0:T(8,128)(2,1)S(1)} %collective-permute-done.4.refs_1_, ...), custom_call_target="tpu_custom_call" | custom-call | tf_op jit(solution)/shard_map/entering/pallas_call | solution.py:484
  47.4 1.6 %collective-permute-start.10 = (bf16[264,512]{1,0:T(8,128)(2,1)S(1)}, bf16[264,512]{1,0:T(8,128)(2,1)S(1)}, u32[]{:S(2)}, u32[]{:S(2)}) collective-permute-start(bf16[264,512]{1,0:T(8,128)(2,1)S(1)} %get-tuple-element.103), channel_id=1, source_target_pairs={{0,2},{1,3},{2,0},{3,1},{4,6},{5,7},{6,4},{7,5},{8,10},{9,11},{10,... | collective-permute-start | bytes 811016 | tf_op jit(solution)/shard_map/ppermute | solution.py:385
  49.0 0.0 collective-permute-start.11
  49.0 1.3 %collective-permute-start.12 = (bf16[264,512]{1,0:T(8,128)(2,1)S(1)}, bf16[264,512]{1,0:T(8,128)(2,1)S(1)}, u32[]{:S(2)}, u32[]{:S(2)}) collective-permute-start(bf16[264,512]{1,0:T(8,128)(2,1)S(1)} %get-tuple-element.117), channel_id=1, source_target_pairs={{0,6},{1,7},{2,4},{3,5},{4,2},{5,3},{6,0},{7,1},{8,14},{9,15},{10,... | collective-permute-start | bytes 811016 | tf_op jit(solution)/shard_map/ppermute | solution.py:385
  50.3 1.0 %outputs.4 = (bf16[1,256,512]{2,1,0:T(8,128)(2,1)S(1)}, bf16[1,256,512]{2,1,0:T(8,128)(2,1)S(1)}) custom-call(s32[2]{0:T(128)S(1)} %pad_add_fusion.scalars, bf16[4,256,256]{2,1,0:T(8,128)(2,1)S(1)} %get-tuple-element.90.refs_0_.q_own, bf16[4,256,256]{2,1,0:T(8,128)(2,1)S(1)} %collective-permute-done.3.refs_3_.q_oth, ...), custom_call_target="tpu_custom_call" | custom-call | tf_op jit(solution)/shard_map/outputs/pallas_call | solution.py:495
  51.2 3.9 %collective-permute-start.9 = (bf16[1,256,512]{2,1,0:T(8,128)(2,1)S(1)}, bf16[1,256,512]{2,1,0:T(8,128)(2,1)S(1)}, u32[]{:S(2)}, u32[]{:S(2)}) collective-permute-start(bf16[1,256,512]{2,1,0:T(8,128)(2,1)S(1)} %get-tuple-element.98), channel_id=1, source_target_pairs={{0,1},{1,0},{2,3},{3,2},{4,5},{5,4},{6,7},{7,6},{8,9},{9,8},{10,11... | collective-permute-start | bytes 786440 | tf_op jit(solution)/shard_map/ppermute | solution.py:381
  55.1 1.2 %collective-permute-done.9.refs_4_ = bf16[1,256,512]{2,1,0:T(8,128)(2,1)S(1)} collective-permute-done((bf16[1,256,512]{2,1,0:T(8,128)(2,1)S(1)}, bf16[1,256,512]{2,1,0:T(8,128)(2,1)S(1)}, u32[]{:S(2)}, u32[]{:S(2)}) %collective-permute-start.9) | collective-permute-done | bytes 262176 | tf_op jit(solution)/shard_map/ppermute | solution.py:381
  56.3 0.0 collective-permute-done.10.refs_4_
  56.3 1.0 %outputs.5 = (bf16[1,256,512]{2,1,0:T(8,128)(2,1)S(1)}, bf16[1,256,512]{2,1,0:T(8,128)(2,1)S(1)}) custom-call(s32[2]{0:T(128)S(1)} %pad_add_fusion.scalars, bf16[4,256,256]{2,1,0:T(8,128)(2,1)S(1)} %get-tuple-element.90.refs_0_.q_own, bf16[4,256,256]{2,1,0:T(8,128)(2,1)S(1)} %collective-permute-done.3.refs_3_.q_oth, ...), custom_call_target="tpu_custom_call" | custom-call | tf_op jit(solution)/shard_map/outputs/pallas_call | solution.py:495
  57.3 3.1 %collective-permute-start.13 = (bf16[1,256,512]{2,1,0:T(8,128)(2,1)S(1)}, bf16[1,256,512]{2,1,0:T(8,128)(2,1)S(1)}, u32[]{:S(2)}, u32[]{:S(2)}) collective-permute-start(bf16[1,256,512]{2,1,0:T(8,128)(2,1)S(1)} %get-tuple-element.105), channel_id=1, source_target_pairs={{0,1},{1,0},{2,3},{3,2},{4,5},{5,4},{6,7},{7,6},{8,9},{9,8},{10,11... | collective-permute-start | bytes 786440 | tf_op jit(solution)/shard_map/ppermute | solution.py:381
  60.4 0.0 collective-permute-done.11.refs_4_
  60.4 1.0 %outputs.6 = (bf16[1,256,512]{2,1,0:T(8,128)(2,1)S(1)}, bf16[1,256,512]{2,1,0:T(8,128)(2,1)S(1)}) custom-call(s32[2]{0:T(128)S(1)} %pad_add_fusion.scalars, bf16[4,256,256]{2,1,0:T(8,128)(2,1)S(1)} %get-tuple-element.90.refs_0_.q_own, bf16[4,256,256]{2,1,0:T(8,128)(2,1)S(1)} %collective-permute-done.3.refs_3_.q_oth, ...), custom_call_target="tpu_custom_call" | custom-call | tf_op jit(solution)/shard_map/outputs/pallas_call | solution.py:495
  61.4 3.4 %collective-permute-start.14 = (bf16[1,256,512]{2,1,0:T(8,128)(2,1)S(1)}, bf16[1,256,512]{2,1,0:T(8,128)(2,1)S(1)}, u32[]{:S(2)}, u32[]{:S(2)}) collective-permute-start(bf16[1,256,512]{2,1,0:T(8,128)(2,1)S(1)} %get-tuple-element.112), channel_id=1, source_target_pairs={{0,1},{1,0},{2,3},{3,2},{4,5},{5,4},{6,7},{7,6},{8,9},{9,8},{10,11... | collective-permute-start | bytes 786440 | tf_op jit(solution)/shard_map/ppermute | solution.py:381
  64.7 0.0 collective-permute-done.12.refs_4_
  64.7 1.0 %outputs.7 = (bf16[1,256,512]{2,1,0:T(8,128)(2,1)S(1)}, bf16[1,256,512]{2,1,0:T(8,128)(2,1)S(1)}) custom-call(s32[2]{0:T(128)S(1)} %pad_add_fusion.scalars, bf16[4,256,256]{2,1,0:T(8,128)(2,1)S(1)} %get-tuple-element.90.refs_0_.q_own, bf16[4,256,256]{2,1,0:T(8,128)(2,1)S(1)} %collective-permute-done.3.refs_3_.q_oth, ...), custom_call_target="tpu_custom_call" | custom-call | tf_op jit(solution)/shard_map/outputs/pallas_call | solution.py:495
  65.7 0.1 collective-permute-start.15
  65.8 0.0 collective-permute-done.13.refs_5_
  65.8 0.1 collective-permute-done.14.refs_6_
  65.9 1.4 %collective-permute-done.15.refs_7_ = bf16[1,256,512]{2,1,0:T(8,128)(2,1)S(1)} collective-permute-done((bf16[1,256,512]{2,1,0:T(8,128)(2,1)S(1)}, bf16[1,256,512]{2,1,0:T(8,128)(2,1)S(1)}, u32[]{:S(2)}, u32[]{:S(2)}) %collective-permute-start.15) | collective-permute-done | bytes 262176 | tf_op jit(solution)/shard_map/ppermute | solution.py:381
  67.3 2.1 %merge.1 = bf16[256,8,512]{2,1,0:T(8,128)(2,1)} custom-call(s32[2]{0:T(128)S(1)} %pad_add_fusion.scalars, bf16[1,256,512]{2,1,0:T(8,128)(2,1)S(1)} %get-tuple-element.97.refs_0_, bf16[1,256,512]{2,1,0:T(8,128)(2,1)S(1)} %get-tuple-element.104.refs_1_, bf16[1,256,512]{2,1,0:T(8,128)(2,1)S(1)} %get-tuple-element.111.refs_2_, ...), custom_call_target="tpu_custom_call" | custom-call | tf_op jit(solution)/shard_map/merge/pallas_call | solution.py:513
Async XLA Ops:
  0.0 10.8 %copy-start.3 = (s32[1024]{0:T(1024)S(1)}, s32[1024]{0:T(1024)}, u32[]{:S(2)}) copy-start(s32[1024]{0:T(1024)} %param.11) | copy-start | bytes 12292
  0.7 5.3 %collective-permute-start.1 = (bf16[16,256]{1,0:T(8,128)(2,1)S(1)}, bf16[16,256]{1,0:T(8,128)(2,1)S(1)}, u32[]{:S(2)}, u32[]{:S(2)}) collective-permute-start(bf16[16,256]{1,0:T(8,128)(2,1)S(1)} %pad_maximum_fusion.g_own), channel_id=1, source_target_pairs={{0,1},{1,0},{2,3},{3,2},{4,5},{5,4},{6,7},{7,6},{8,9},{9,8},{10,11... | collective-permute-start | bytes 24584 | tf_op jit(solution)/shard_map/ppermute | solution.py:381
  1.4 1.6 %copy-start = (bf16[256,8,512]{2,1,0:T(8,128)(2,1)S(1)}, bf16[256,8,512]{2,1,0:T(8,128)(2,1)}, u32[]{:S(2)}) copy-start(bf16[256,8,512]{2,1,0:T(8,128)(2,1)} %source.3) | copy-start | bytes 6291460
  3.0 3.2 %copy-start.1 = (bf16[256,8,256]{2,1,0:T(8,128)(2,1)S(1)}, bf16[256,8,256]{2,1,0:T(8,128)(2,1)}, u32[]{:S(2)}) copy-start(bf16[256,8,256]{2,1,0:T(8,128)(2,1)} %source.2) | copy-start | bytes 3145732
  6.1 6.4 %collective-permute-start.2 = (bf16[4,256,512]{2,1,0:T(8,128)(2,1)}, bf16[4,256,512]{2,1,0:T(8,128)(2,1)S(1)}, u32[]{:S(2)}, u32[]{:S(2)}) collective-permute-start(bf16[4,256,512]{2,1,0:T(8,128)(2,1)} %get-tuple-element.67), channel_id=1, source_target_pairs={{0,1},{1,0},{2,3},{3,2},{4,5},{5,4},{6,7},{7,6},{8,9},{9,8},{10,11... | collective-permute-start | bytes 3145736 | tf_op jit(solution)/shard_map/ppermute | solution.py:381
  10.2 2.3 %collective-permute-start = (bf16[4,256,256]{2,1,0:T(8,128)(2,1)}, bf16[4,256,256]{2,1,0:T(8,128)(2,1)S(1)}, u32[]{:S(2)}, u32[]{:S(2)}) collective-permute-start(bf16[4,256,256]{2,1,0:T(8,128)(2,1)} %get-tuple-element.65), channel_id=1, source_target_pairs={{0,1},{1,0},{2,3},{3,2},{4,5},{5,4},{6,7},{7,6},{8,9},{9,8},{10,11... | collective-permute-start | bytes 1572872 | tf_op jit(solution)/shard_map/ppermute | solution.py:381
  10.7 6.5 %copy-start.2 = (bf16[256,8,256]{2,1,0:T(8,128)(2,1)S(1)}, bf16[256,8,256]{2,1,0:T(8,128)(2,1)}, u32[]{:S(2)}) copy-start(bf16[256,8,256]{2,1,0:T(8,128)(2,1)} %source.4) | copy-start | bytes 3145732
  14.5 7.7 %collective-permute-start.4 = (bf16[264,512]{1,0:T(8,128)(2,1)S(1)}, bf16[264,512]{1,0:T(8,128)(2,1)S(1)}, u32[]{:S(2)}, u32[]{:S(2)}) collective-permute-start(bf16[264,512]{1,0:T(8,128)(2,1)S(1)} %get-tuple-element.77), channel_id=1, source_target_pairs={{0,2},{1,3},{2,0},{3,1},{4,6},{5,7},{6,4},{7,5},{8,10},{9,11},{10,... | collective-permute-start | bytes 811016 | tf_op jit(solution)/shard_map/ppermute | solution.py:385
  15.8 7.4 %collective-permute-start.5 = (bf16[264,512]{1,0:T(8,128)(2,1)S(1)}, bf16[264,512]{1,0:T(8,128)(2,1)S(1)}, u32[]{:S(2)}, u32[]{:S(2)}) collective-permute-start(bf16[264,512]{1,0:T(8,128)(2,1)S(1)} %get-tuple-element.78), channel_id=1, source_target_pairs={{0,4},{1,5},{2,6},{3,7},{4,0},{5,1},{6,2},{7,3},{8,12},{9,13},{10,... | collective-permute-start | bytes 811016 | tf_op jit(solution)/shard_map/ppermute | solution.py:385
  17.0 12.0 %collective-permute-start.6 = (bf16[264,512]{1,0:T(8,128)(2,1)S(1)}, bf16[264,512]{1,0:T(8,128)(2,1)S(1)}, u32[]{:S(2)}, u32[]{:S(2)}) collective-permute-start(bf16[264,512]{1,0:T(8,128)(2,1)S(1)} %get-tuple-element.79), channel_id=1, source_target_pairs={{0,6},{1,7},{2,4},{3,5},{4,2},{5,3},{6,0},{7,1},{8,14},{9,15},{10,... | collective-permute-start | bytes 811016 | tf_op jit(solution)/shard_map/ppermute | solution.py:385
  20.4 10.7 %collective-permute-start.3 = (bf16[4,256,256]{2,1,0:T(8,128)(2,1)S(1)}, bf16[4,256,256]{2,1,0:T(8,128)(2,1)S(1)}, u32[]{:S(2)}, u32[]{:S(2)}) collective-permute-start(bf16[4,256,256]{2,1,0:T(8,128)(2,1)S(1)} %get-tuple-element.76), channel_id=1, source_target_pairs={{0,1},{1,0},{2,3},{3,2},{4,5},{5,4},{6,7},{7,6},{8,9},{9,8},{10,11... | collective-permute-start | bytes 1572872 | tf_op jit(solution)/shard_map/ppermute | solution.py:381
  29.9 8.5 %collective-permute-start.7 = (bf16[264,512]{1,0:T(8,128)(2,1)S(1)}, bf16[264,512]{1,0:T(8,128)(2,1)S(1)}, u32[]{:S(2)}, u32[]{:S(2)}) collective-permute-start(bf16[264,512]{1,0:T(8,128)(2,1)S(1)} %group_total.1), channel_id=1, source_target_pairs={{0,8},{1,9},{2,10},{3,11},{4,12},{5,13},{6,14},{7,15},{8,16},{9,17... | collective-permute-start | bytes 811016 | tf_op jit(solution)/shard_map/ppermute | solution.py:389
  38.4 7.6 %collective-permute-start.8 = (bf16[264,512]{1,0:T(8,128)(2,1)S(1)}, bf16[264,512]{1,0:T(8,128)(2,1)S(1)}, u32[]{:S(2)}, u32[]{:S(2)}) collective-permute-start(bf16[264,512]{1,0:T(8,128)(2,1)S(1)} %collective-permute-done.7.refs_4_), channel_id=1, source_target_pairs={{0,8},{1,9},{2,10},{3,11},{4,12},{5,13},{6,14},{7,15},{8,16},{9,17... | collective-permute-start | bytes 811016 | tf_op jit(solution)/shard_map/ppermute | solution.py:389
  47.4 8.9 %collective-permute-start.10 = (bf16[264,512]{1,0:T(8,128)(2,1)S(1)}, bf16[264,512]{1,0:T(8,128)(2,1)S(1)}, u32[]{:S(2)}, u32[]{:S(2)}) collective-permute-start(bf16[264,512]{1,0:T(8,128)(2,1)S(1)} %get-tuple-element.103), channel_id=1, source_target_pairs={{0,2},{1,3},{2,0},{3,1},{4,6},{5,7},{6,4},{7,5},{8,10},{9,11},{10,... | collective-permute-start | bytes 811016 | tf_op jit(solution)/shard_map/ppermute | solution.py:385
  49.0 11.4 %collective-permute-start.11 = (bf16[264,512]{1,0:T(8,128)(2,1)S(1)}, bf16[264,512]{1,0:T(8,128)(2,1)S(1)}, u32[]{:S(2)}, u32[]{:S(2)}) collective-permute-start(bf16[264,512]{1,0:T(8,128)(2,1)S(1)} %get-tuple-element.110), channel_id=1, source_target_pairs={{0,4},{1,5},{2,6},{3,7},{4,0},{5,1},{6,2},{7,3},{8,12},{9,13},{10,... | collective-permute-start | bytes 811016 | tf_op jit(solution)/shard_map/ppermute | solution.py:385
  49.0 15.7 %collective-permute-start.12 = (bf16[264,512]{1,0:T(8,128)(2,1)S(1)}, bf16[264,512]{1,0:T(8,128)(2,1)S(1)}, u32[]{:S(2)}, u32[]{:S(2)}) collective-permute-start(bf16[264,512]{1,0:T(8,128)(2,1)S(1)} %get-tuple-element.117), channel_id=1, source_target_pairs={{0,6},{1,7},{2,4},{3,5},{4,2},{5,3},{6,0},{7,1},{8,14},{9,15},{10,... | collective-permute-start | bytes 811016 | tf_op jit(solution)/shard_map/ppermute | solution.py:385
  51.2 5.1 %collective-permute-start.9 = (bf16[1,256,512]{2,1,0:T(8,128)(2,1)S(1)}, bf16[1,256,512]{2,1,0:T(8,128)(2,1)S(1)}, u32[]{:S(2)}, u32[]{:S(2)}) collective-permute-start(bf16[1,256,512]{2,1,0:T(8,128)(2,1)S(1)} %get-tuple-element.98), channel_id=1, source_target_pairs={{0,1},{1,0},{2,3},{3,2},{4,5},{5,4},{6,7},{7,6},{8,9},{9,8},{10,11... | collective-permute-start | bytes 786440 | tf_op jit(solution)/shard_map/ppermute | solution.py:381
  57.3 8.5 %collective-permute-start.13 = (bf16[1,256,512]{2,1,0:T(8,128)(2,1)S(1)}, bf16[1,256,512]{2,1,0:T(8,128)(2,1)S(1)}, u32[]{:S(2)}, u32[]{:S(2)}) collective-permute-start(bf16[1,256,512]{2,1,0:T(8,128)(2,1)S(1)} %get-tuple-element.105), channel_id=1, source_target_pairs={{0,1},{1,0},{2,3},{3,2},{4,5},{5,4},{6,7},{7,6},{8,9},{9,8},{10,11... | collective-permute-start | bytes 786440 | tf_op jit(solution)/shard_map/ppermute | solution.py:381
  61.4 4.5 %collective-permute-start.14 = (bf16[1,256,512]{2,1,0:T(8,128)(2,1)S(1)}, bf16[1,256,512]{2,1,0:T(8,128)(2,1)S(1)}, u32[]{:S(2)}, u32[]{:S(2)}) collective-permute-start(bf16[1,256,512]{2,1,0:T(8,128)(2,1)S(1)} %get-tuple-element.112), channel_id=1, source_target_pairs={{0,1},{1,0},{2,3},{3,2},{4,5},{5,4},{6,7},{7,6},{8,9},{9,8},{10,11... | collective-permute-start | bytes 786440 | tf_op jit(solution)/shard_map/ppermute | solution.py:381
  65.7 1.6 %collective-permute-start.15 = (bf16[1,256,512]{2,1,0:T(8,128)(2,1)S(1)}, bf16[1,256,512]{2,1,0:T(8,128)(2,1)S(1)}, u32[]{:S(2)}, u32[]{:S(2)}) collective-permute-start(bf16[1,256,512]{2,1,0:T(8,128)(2,1)S(1)} %get-tuple-element.120), channel_id=1, source_target_pairs={{0,1},{1,0},{2,3},{3,2},{4,5},{5,4},{6,7},{7,6},{8,9},{9,8},{10,11... | collective-permute-start | bytes 786440 | tf_op jit(solution)/shard_map/ppermute | solution.py:381

commit v12 on v10

--- a/solution.py
+++ b/solution.py
@@ -9,7 +9,8 @@
 
 AXES = ("ctx", "hv")
 FLOOR_NEG = -1e30
-META = 16
+META = 8
+PAD = 16
 LANES = 128
 LAY = 256
 F32, BF16 = jnp.float32, jnp.bfloat16
@@ -151,7 +152,7 @@
             high.append(scaled.astype(BF16))
             low.append((scaled - high[-1].astype(F32)).astype(BF16))
             values.append(v_ref[local_head])
-            pieces = jnp.concatenate(split3(f) + (jnp.zeros((META - 3, tokens), F32),), axis=0)
+            pieces = jnp.concatenate(split3(f) + (jnp.zeros((PAD - 3, tokens), F32),), axis=0)
             sums = dot(pieces.astype(BF16), keys)
             line = (sums[2:3] + sums[1:2]) + sums[0:1]
             normal = line if normal is None else normal + line
@@ -295,7 +296,7 @@
         at = slot % early
         local_head = jnp.bitwise_xor(scalars[0], slot)
         normal, top, _, doc = read_meta([payload])
-        pieces = split3(normal) + (jnp.zeros((META - 3, key_width), F32),)
+        pieces = split3(normal) + (jnp.zeros((PAD - 3, key_width), F32),)
         pieces = jnp.concatenate(pieces, axis=0).astype(BF16)
         memory = payload[:key_width, :]
         width = memory.shape[1]

time: 67 us -> 65.9 us (0.984)
  waiting for transfers between devices: 23.9 us -> 23.2 us
where the time goes in v12:
time: 65.9 us; the launch traced here: 65.7 us
  waiting for transfers between devices  23.2 us (35%)
  starting transfers between devices  21 us (32%)
  Pallas kernels  19 us (29%)
  local copies, waits for them, and re-layouts  1.6 us (2%)
  other arithmetic  0.79 us (1%)
    ppermute x8, starting transfers between devices, swap_cores(): return lax.ppermute(x, AXES, [(d, d ^ 1) for d in range(devices)])  12.8 us
    ppermute x6, waiting for transfers between devices, in_group(): return lax.ppermute(x, AXES, pairs)  10.3 us
    ppermute x2, waiting for transfers between devices, to_next(): return lax.ppermute(x, AXES, [(d, d + jump) for d in range(devices - jump)])  9.35 us
    ppermute x6, starting transfers between devices, in_group(): return lax.ppermute(x, AXES, pairs)  5.59 us
    pallas_call x2, Pallas kernels, own_terms(): pl.pallas_call(functools.partial(local_kernel, first_slot, heads), in_spe...  4.4 us
    pallas_call x4, Pallas kernels, outputs(): pl.pallas_call(functools.partial(output_kernel, first, count), in_specs=[...  3.94 us
    ppermute x8, waiting for transfers between devices, swap_cores(): return lax.ppermute(x, AXES, [(d, d ^ 1) for d in range(devices)])  3.52 us
    pallas_call x3, Pallas kernels, relayout(): pl.pallas_call(functools.partial(relayout_kernel, half, len(sources)), in...  3.38 us
  transfers between devices with their start and end apart: 16, of which 9 were waited for; matrix products, arithmetic and copies ran while one was open for 0% of the time, Pallas kernels for 20%

profile of v12, /device:TPU:25, one launch (start us, length us, event | category | flops | bytes accessed | tf_op | source)
XLA Modules:
  0.0 65.7 jit_solution(12987066337157606389)
XLA Ops:
  0.0 0.0 copy-start.3
  0.0 0.7 %pad_maximum_fusion.g_own = bf16[16,256]{1,0:T(8,128)(2,1)S(1)} fusion(bf16[8,256]{1,0:T(8,128)(2,1)} %bitcast.6, bf16[8,256]{1,0:T(8,128)(2,1)} %bitcast.7), kind=kLoop, calls=%fused_computation | loop fusion | flops 16384 | bytes 16384 | tf_op jit(solution)/shard_map/concatenate | solution.py:402
  0.7 0.7 %collective-permute-start.1 = (bf16[16,256]{1,0:T(8,128)(2,1)S(1)}, bf16[16,256]{1,0:T(8,128)(2,1)S(1)}, u32[]{:S(2)}, u32[]{:S(2)}) collective-permute-start(bf16[16,256]{1,0:T(8,128)(2,1)S(1)} %pad_maximum_fusion.g_own), channel_id=1, source_target_pairs={{0,1},{1,0},{2,3},{3,2},{4,5},{5,4},{6,7},{7,6},{8,9},{9,8},{10,11... | collective-permute-start | bytes 24584 | tf_op jit(solution)/shard_map/ppermute | solution.py:377
  1.4 0.0 copy-start
  1.4 1.6 %copy-done = bf16[256,8,512]{2,1,0:T(8,128)(2,1)S(1)} copy-done((bf16[256,8,512]{2,1,0:T(8,128)(2,1)S(1)}, bf16[256,8,512]{2,1,0:T(8,128)(2,1)}, u32[]{:S(2)}) %copy-start) | copy-done | bytes 2097176
  3.0 0.0 copy-start.1
  3.0 1.7 %relayout.4 = (bf16[4,256,512]{2,1,0:T(8,128)(2,1)S(1)}, bf16[4,256,512]{2,1,0:T(8,128)(2,1)}) custom-call(bf16[256,8,512]{2,1,0:T(8,128)(2,1)S(1)} %copy-done), custom_call_target="tpu_custom_call" | custom-call | tf_op jit(solution)/shard_map/relayout/pallas_call | solution.py:393
  4.7 0.0 collective-permute-done.1.g_oth
  4.7 0.0 collective-permute-start.2
  4.7 0.0 copy-done.1
  4.7 1.3 %relayout.3 = (bf16[4,256,256]{2,1,0:T(8,128)(2,1)S(1)}, bf16[4,256,256]{2,1,0:T(8,128)(2,1)}) custom-call(bf16[256,8,256]{2,1,0:T(8,128)(2,1)S(1)} %copy-done.1), custom_call_target="tpu_custom_call" | custom-call | tf_op jit(solution)/shard_map/relayout/pallas_call | solution.py:393
  6.0 0.5 collective-permute-start
  6.5 0.0 copy-start.2
  6.5 0.1 pad_add_fusion.scalars
  6.5 0.0 copy-done.3
  6.5 0.9 %gates.1 = (f32[8,512]{1,0:T(8,128)S(1)}, f32[8,128]{1,0:T(8,128)S(1)}, f32[8,128]{1,0:T(8,128)S(1)}, f32[8,512]{1,0:T(8,128)S(1)}, f32[8,512]{1,0:T(8,128)S(1)}...) custom-call(s32[2]{0:T(128)S(1)} %pad_add_fusion.scalars, bf16[16,256]{1,0:T(8,128)(2,1)S(1)} %pad_maximum_fusion.g_own, ...), custom_call_target="tpu_custom_call" | custom-call | tf_op jit(solution)/shard_map/gates/pallas_call | solution.py:419
  7.5 0.8 %collective-permute-done.refs_2_.refs_4_ = bf16[4,256,256]{2,1,0:T(8,128)(2,1)S(1)} collective-permute-done((bf16[4,256,256]{2,1,0:T(8,128)(2,1)}, bf16[4,256,256]{2,1,0:T(8,128)(2,1)S(1)}, u32[]{:S(2)}, u32[]{:S(2)}) %collective-permute-start) | collective-permute-done | bytes 524320 | tf_op jit(solution)/shard_map/ppermute | solution.py:377
  8.3 0.0 collective-permute-done.2.refs_3_.refs_5_
  8.3 2.1 %states.1 = (bf16[264,512]{1,0:T(8,128)(2,1)S(1)}, bf16[264,512]{1,0:T(8,128)(2,1)S(1)}, bf16[264,512]{1,0:T(8,128)(2,1)S(1)}, bf16[264,512]{1,0:T(8,128)(2,1)S(1)}) custom-call(s32[2]{0:T(128)S(1)} %pad_add_fusion.scalars, bf16[4,256,256]{2,1,0:T(8,128)(2,1)S(1)} %get-tuple-element.65.refs_0_.refs_1_, ...), custom_call_target="tpu_custom_call" | custom-call | tf_op jit(solution)/shard_map/states/pallas_call | solution.py:429
  10.4 1.3 %collective-permute-start.4 = (bf16[264,512]{1,0:T(8,128)(2,1)S(1)}, bf16[264,512]{1,0:T(8,128)(2,1)S(1)}, u32[]{:S(2)}, u32[]{:S(2)}) collective-permute-start(bf16[264,512]{1,0:T(8,128)(2,1)S(1)} %get-tuple-element.81), channel_id=1, source_target_pairs={{0,2},{1,3},{2,0},{3,1},{4,6},{5,7},{6,4},{7,5},{8,10},{9,11},{10,... | collective-permute-start | bytes 811016 | tf_op jit(solution)/shard_map/ppermute | solution.py:381
  11.6 1.2 %collective-permute-start.5 = (bf16[264,512]{1,0:T(8,128)(2,1)S(1)}, bf16[264,512]{1,0:T(8,128)(2,1)S(1)}, u32[]{:S(2)}, u32[]{:S(2)}) collective-permute-start(bf16[264,512]{1,0:T(8,128)(2,1)S(1)} %get-tuple-element.82), channel_id=1, source_target_pairs={{0,4},{1,5},{2,6},{3,7},{4,0},{5,1},{6,2},{7,3},{8,12},{9,13},{10,... | collective-permute-start | bytes 811016 | tf_op jit(solution)/shard_map/ppermute | solution.py:381
  12.9 0.2 collective-permute-start.6
  13.1 0.0 copy-done.2
  13.1 0.4 relayout.5
  13.5 1.2 %collective-permute-start.3 = (bf16[4,256,256]{2,1,0:T(8,128)(2,1)S(1)}, bf16[4,256,256]{2,1,0:T(8,128)(2,1)S(1)}, u32[]{:S(2)}, u32[]{:S(2)}) collective-permute-start(bf16[4,256,256]{2,1,0:T(8,128)(2,1)S(1)} %get-tuple-element.80), channel_id=1, source_target_pairs={{0,1},{1,0},{2,3},{3,2},{4,5},{5,4},{6,7},{7,6},{8,9},{9,8},{10,11... | collective-permute-start | bytes 1572872 | tf_op jit(solution)/shard_map/ppermute | solution.py:377
  14.7 3.5 %collective-permute-done.4.refs_1_ = bf16[264,512]{1,0:T(8,128)(2,1)S(1)} collective-permute-done((bf16[264,512]{1,0:T(8,128)(2,1)S(1)}, bf16[264,512]{1,0:T(8,128)(2,1)S(1)}, u32[]{:S(2)}, u32[]{:S(2)}) %collective-permute-start.4) | collective-permute-done | bytes 270368 | tf_op jit(solution)/shard_map/ppermute | solution.py:381
  18.2 0.9 %collective-permute-done.5.refs_2_ = bf16[264,512]{1,0:T(8,128)(2,1)S(1)} collective-permute-done((bf16[264,512]{1,0:T(8,128)(2,1)S(1)}, bf16[264,512]{1,0:T(8,128)(2,1)S(1)}, u32[]{:S(2)}, u32[]{:S(2)}) %collective-permute-start.5) | collective-permute-done | bytes 270368 | tf_op jit(solution)/shard_map/ppermute | solution.py:381
  19.1 5.9 %collective-permute-done.6.refs_3_ = bf16[264,512]{1,0:T(8,128)(2,1)S(1)} collective-permute-done((bf16[264,512]{1,0:T(8,128)(2,1)S(1)}, bf16[264,512]{1,0:T(8,128)(2,1)S(1)}, u32[]{:S(2)}, u32[]{:S(2)}) %collective-permute-start.6) | collective-permute-done | bytes 270368 | tf_op jit(solution)/shard_map/ppermute | solution.py:381
  25.0 0.8 %group_total.1 = bf16[264,512]{1,0:T(8,128)(2,1)S(1)} custom-call(s32[2]{0:T(128)S(1)} %pad_add_fusion.scalars, bf16[264,512]{1,0:T(8,128)(2,1)S(1)} %get-tuple-element.99.refs_0_, bf16[264,512]{1,0:T(8,128)(2,1)S(1)} %collective-permute-done.4.refs_1_, bf16[264,512]{1,0:T(8,128)(2,1)S(1)} %collective-permute-done.5.refs_2_, ...), custom_call_target="tpu_custom_call" | custom-call | tf_op jit(solution)/shard_map/group_total/pallas_call | solution.py:438
  25.8 1.3 %collective-permute-start.7 = (bf16[264,512]{1,0:T(8,128)(2,1)S(1)}, bf16[264,512]{1,0:T(8,128)(2,1)S(1)}, u32[]{:S(2)}, u32[]{:S(2)}) collective-permute-start(bf16[264,512]{1,0:T(8,128)(2,1)S(1)} %group_total.1), channel_id=1, source_target_pairs={{0,8},{1,9},{2,10},{3,11},{4,12},{5,13},{6,14},{7,15},{8,16},{9,17... | collective-permute-start | bytes 811016 | tf_op jit(solution)/shard_map/ppermute | solution.py:385
  27.1 0.0 collective-permute-done.3.refs_3_.q_oth
  27.1 2.2 %own_terms.2 = (f32[2,2,256,512]{3,2,1,0:T(8,128)S(1)}, f32[2,2,8,256]{3,2,1,0:T(8,128)S(1)}) custom-call(s32[2]{0:T(128)S(1)} %pad_add_fusion.scalars, bf16[4,256,256]{2,1,0:T(8,128)(2,1)S(1)} %get-tuple-element.94.refs_0_.q_own, bf16[4,256,256]{2,1,0:T(8,128)(2,1)S(1)} %get-tuple-element.65.refs_0_.refs_1_, ...), custom_call_target="tpu_custom_call" | custom-call | tf_op jit(solution)/shard_map/own_terms/pallas_call | solution.py:454
  29.3 5.1 %collective-permute-done.7.refs_4_ = bf16[264,512]{1,0:T(8,128)(2,1)S(1)} collective-permute-done((bf16[264,512]{1,0:T(8,128)(2,1)S(1)}, bf16[264,512]{1,0:T(8,128)(2,1)S(1)}, u32[]{:S(2)}, u32[]{:S(2)}) %collective-permute-start.7) | collective-permute-done | bytes 270368 | tf_op jit(solution)/shard_map/ppermute | solution.py:385
  34.4 1.3 %collective-permute-start.8 = (bf16[264,512]{1,0:T(8,128)(2,1)S(1)}, bf16[264,512]{1,0:T(8,128)(2,1)S(1)}, u32[]{:S(2)}, u32[]{:S(2)}) collective-permute-start(bf16[264,512]{1,0:T(8,128)(2,1)S(1)} %collective-permute-done.7.refs_4_), channel_id=1, source_target_pairs={{0,8},{1,9},{2,10},{3,11},{4,12},{5,13},{6,14},{7,15},{8,16},{9,17... | collective-permute-start | bytes 811016 | tf_op jit(solution)/shard_map/ppermute | solution.py:385
  35.7 2.2 %own_terms.3 = (f32[2,2,256,512]{3,2,1,0:T(8,128)S(1)}, f32[2,2,8,256]{3,2,1,0:T(8,128)S(1)}) custom-call(s32[2]{0:T(128)S(1)} %pad_add_fusion.scalars, bf16[4,256,256]{2,1,0:T(8,128)(2,1)S(1)} %get-tuple-element.94.refs_0_.q_own, bf16[4,256,256]{2,1,0:T(8,128)(2,1)S(1)} %get-tuple-element.65.refs_0_.refs_1_, ...), custom_call_target="tpu_custom_call" | custom-call | tf_op jit(solution)/shard_map/own_terms/pallas_call | solution.py:454
  37.9 4.3 %collective-permute-done.8.refs_5_ = bf16[264,512]{1,0:T(8,128)(2,1)S(1)} collective-permute-done((bf16[264,512]{1,0:T(8,128)(2,1)S(1)}, bf16[264,512]{1,0:T(8,128)(2,1)S(1)}, u32[]{:S(2)}, u32[]{:S(2)}) %collective-permute-start.8) | collective-permute-done | bytes 270368 | tf_op jit(solution)/shard_map/ppermute | solution.py:385
  42.2 1.4 %entering.1 = (bf16[264,512]{1,0:T(8,128)(2,1)S(1)}, bf16[264,512]{1,0:T(8,128)(2,1)S(1)}, bf16[264,512]{1,0:T(8,128)(2,1)S(1)}, bf16[264,512]{1,0:T(8,128)(2,1)S(1)}) custom-call(s32[2]{0:T(128)S(1)} %pad_add_fusion.scalars, bf16[264,512]{1,0:T(8,128)(2,1)S(1)} %get-tuple-element.99.refs_0_, bf16[264,512]{1,0:T(8,128)(2,1)S(1)} %collective-permute-done.4.refs_1_, ...), custom_call_target="tpu_custom_call" | custom-call | tf_op jit(solution)/shard_map/entering/pallas_call | solution.py:477
  43.6 1.6 %collective-permute-start.10 = (bf16[264,512]{1,0:T(8,128)(2,1)S(1)}, bf16[264,512]{1,0:T(8,128)(2,1)S(1)}, u32[]{:S(2)}, u32[]{:S(2)}) collective-permute-start(bf16[264,512]{1,0:T(8,128)(2,1)S(1)} %get-tuple-element.107), channel_id=1, source_target_pairs={{0,2},{1,3},{2,0},{3,1},{4,6},{5,7},{6,4},{7,5},{8,10},{9,11},{10,... | collective-permute-start | bytes 811016 | tf_op jit(solution)/shard_map/ppermute | solution.py:381
  45.2 0.0 collective-permute-start.11
  45.2 1.3 %collective-permute-start.12 = (bf16[264,512]{1,0:T(8,128)(2,1)S(1)}, bf16[264,512]{1,0:T(8,128)(2,1)S(1)}, u32[]{:S(2)}, u32[]{:S(2)}) collective-permute-start(bf16[264,512]{1,0:T(8,128)(2,1)S(1)} %get-tuple-element.121), channel_id=1, source_target_pairs={{0,6},{1,7},{2,4},{3,5},{4,2},{5,3},{6,0},{7,1},{8,14},{9,15},{10,... | collective-permute-start | bytes 811016 | tf_op jit(solution)/shard_map/ppermute | solution.py:381
  46.4 1.0 %outputs.4 = (bf16[1,256,512]{2,1,0:T(8,128)(2,1)S(1)}, bf16[1,256,512]{2,1,0:T(8,128)(2,1)S(1)}) custom-call(s32[2]{0:T(128)S(1)} %pad_add_fusion.scalars, bf16[4,256,256]{2,1,0:T(8,128)(2,1)S(1)} %get-tuple-element.94.refs_0_.q_own, bf16[4,256,256]{2,1,0:T(8,128)(2,1)S(1)} %collective-permute-done.3.refs_3_.q_oth, ...), custom_call_target="tpu_custom_call" | custom-call | tf_op jit(solution)/shard_map/outputs/pallas_call | solution.py:488
  47.4 3.8 %collective-permute-start.9 = (bf16[1,256,512]{2,1,0:T(8,128)(2,1)S(1)}, bf16[1,256,512]{2,1,0:T(8,128)(2,1)S(1)}, u32[]{:S(2)}, u32[]{:S(2)}) collective-permute-start(bf16[1,256,512]{2,1,0:T(8,128)(2,1)S(1)} %get-tuple-element.102), channel_id=1, source_target_pairs={{0,1},{1,0},{2,3},{3,2},{4,5},{5,4},{6,7},{7,6},{8,9},{9,8},{10,11... | collective-permute-start | bytes 786440 | tf_op jit(solution)/shard_map/ppermute | solution.py:377
  51.2 1.2 %collective-permute-done.9.refs_4_ = bf16[1,256,512]{2,1,0:T(8,128)(2,1)S(1)} collective-permute-done((bf16[1,256,512]{2,1,0:T(8,128)(2,1)S(1)}, bf16[1,256,512]{2,1,0:T(8,128)(2,1)S(1)}, u32[]{:S(2)}, u32[]{:S(2)}) %collective-permute-start.9) | collective-permute-done | bytes 262176 | tf_op jit(solution)/shard_map/ppermute | solution.py:377
  52.4 0.0 collective-permute-done.10.refs_4_
  52.4 1.0 %outputs.5 = (bf16[1,256,512]{2,1,0:T(8,128)(2,1)S(1)}, bf16[1,256,512]{2,1,0:T(8,128)(2,1)S(1)}) custom-call(s32[2]{0:T(128)S(1)} %pad_add_fusion.scalars, bf16[4,256,256]{2,1,0:T(8,128)(2,1)S(1)} %get-tuple-element.94.refs_0_.q_own, bf16[4,256,256]{2,1,0:T(8,128)(2,1)S(1)} %collective-permute-done.3.refs_3_.q_oth, ...), custom_call_target="tpu_custom_call" | custom-call | tf_op jit(solution)/shard_map/outputs/pallas_call | solution.py:488
  53.4 3.2 %collective-permute-start.13 = (bf16[1,256,512]{2,1,0:T(8,128)(2,1)S(1)}, bf16[1,256,512]{2,1,0:T(8,128)(2,1)S(1)}, u32[]{:S(2)}, u32[]{:S(2)}) collective-permute-start(bf16[1,256,512]{2,1,0:T(8,128)(2,1)S(1)} %get-tuple-element.109), channel_id=1, source_target_pairs={{0,1},{1,0},{2,3},{3,2},{4,5},{5,4},{6,7},{7,6},{8,9},{9,8},{10,11... | collective-permute-start | bytes 786440 | tf_op jit(solution)/shard_map/ppermute | solution.py:377
  56.6 0.0 collective-permute-done.11.refs_4_
  56.6 1.0 %outputs.6 = (bf16[1,256,512]{2,1,0:T(8,128)(2,1)S(1)}, bf16[1,256,512]{2,1,0:T(8,128)(2,1)S(1)}) custom-call(s32[2]{0:T(128)S(1)} %pad_add_fusion.scalars, bf16[4,256,256]{2,1,0:T(8,128)(2,1)S(1)} %get-tuple-element.94.refs_0_.q_own, bf16[4,256,256]{2,1,0:T(8,128)(2,1)S(1)} %collective-permute-done.3.refs_3_.q_oth, ...), custom_call_target="tpu_custom_call" | custom-call | tf_op jit(solution)/shard_map/outputs/pallas_call | solution.py:488
  57.6 3.4 %collective-permute-start.14 = (bf16[1,256,512]{2,1,0:T(8,128)(2,1)S(1)}, bf16[1,256,512]{2,1,0:T(8,128)(2,1)S(1)}, u32[]{:S(2)}, u32[]{:S(2)}) collective-permute-start(bf16[1,256,512]{2,1,0:T(8,128)(2,1)S(1)} %get-tuple-element.116), channel_id=1, source_target_pairs={{0,1},{1,0},{2,3},{3,2},{4,5},{5,4},{6,7},{7,6},{8,9},{9,8},{10,11... | collective-permute-start | bytes 786440 | tf_op jit(solution)/shard_map/ppermute | solution.py:377
  60.9 0.0 collective-permute-done.12.refs_4_
  60.9 1.0 %outputs.7 = (bf16[1,256,512]{2,1,0:T(8,128)(2,1)S(1)}, bf16[1,256,512]{2,1,0:T(8,128)(2,1)S(1)}) custom-call(s32[2]{0:T(128)S(1)} %pad_add_fusion.scalars, bf16[4,256,256]{2,1,0:T(8,128)(2,1)S(1)} %get-tuple-element.94.refs_0_.q_own, bf16[4,256,256]{2,1,0:T(8,128)(2,1)S(1)} %collective-permute-done.3.refs_3_.q_oth, ...), custom_call_target="tpu_custom_call" | custom-call | tf_op jit(solution)/shard_map/outputs/pallas_call | solution.py:488
  61.9 0.1 collective-permute-start.15
  62.0 0.0 collective-permute-done.13.refs_5_
  62.0 0.1 collective-permute-done.14.refs_6_
  62.1 1.4 %collective-permute-done.15.refs_7_ = bf16[1,256,512]{2,1,0:T(8,128)(2,1)S(1)} collective-permute-done((bf16[1,256,512]{2,1,0:T(8,128)(2,1)S(1)}, bf16[1,256,512]{2,1,0:T(8,128)(2,1)S(1)}, u32[]{:S(2)}, u32[]{:S(2)}) %collective-permute-start.15) | collective-permute-done | bytes 262176 | tf_op jit(solution)/shard_map/ppermute | solution.py:377
  63.5 2.1 %merge.1 = bf16[256,8,512]{2,1,0:T(8,128)(2,1)} custom-call(s32[2]{0:T(128)S(1)} %pad_add_fusion.scalars, bf16[1,256,512]{2,1,0:T(8,128)(2,1)S(1)} %get-tuple-element.101.refs_0_, bf16[1,256,512]{2,1,0:T(8,128)(2,1)S(1)} %get-tuple-element.108.refs_1_, bf16[1,256,512]{2,1,0:T(8,128)(2,1)S(1)} %get-tuple-element.115.refs_2_, ...), custom_call_target="tpu_custom_call" | custom-call | tf_op jit(solution)/shard_map/merge/pallas_call | solution.py:506
Async XLA Ops:
  0.0 6.5 %copy-start.3 = (s32[1024]{0:T(1024)S(1)}, s32[1024]{0:T(1024)}, u32[]{:S(2)}) copy-start(s32[1024]{0:T(1024)} %param.11) | copy-start | bytes 12292
  0.7 4.0 %collective-permute-start.1 = (bf16[16,256]{1,0:T(8,128)(2,1)S(1)}, bf16[16,256]{1,0:T(8,128)(2,1)S(1)}, u32[]{:S(2)}, u32[]{:S(2)}) collective-permute-start(bf16[16,256]{1,0:T(8,128)(2,1)S(1)} %pad_maximum_fusion.g_own), channel_id=1, source_target_pairs={{0,1},{1,0},{2,3},{3,2},{4,5},{5,4},{6,7},{7,6},{8,9},{9,8},{10,11... | collective-permute-start | bytes 24584 | tf_op jit(solution)/shard_map/ppermute | solution.py:377
  1.4 1.6 %copy-start = (bf16[256,8,512]{2,1,0:T(8,128)(2,1)S(1)}, bf16[256,8,512]{2,1,0:T(8,128)(2,1)}, u32[]{:S(2)}) copy-start(bf16[256,8,512]{2,1,0:T(8,128)(2,1)} %refs_0_.2) | copy-start | bytes 6291460
  3.0 1.7 %copy-start.1 = (bf16[256,8,256]{2,1,0:T(8,128)(2,1)S(1)}, bf16[256,8,256]{2,1,0:T(8,128)(2,1)}, u32[]{:S(2)}) copy-start(bf16[256,8,256]{2,1,0:T(8,128)(2,1)} %refs_0_.1) | copy-start | bytes 3145732
  4.7 3.6 %collective-permute-start.2 = (bf16[4,256,512]{2,1,0:T(8,128)(2,1)}, bf16[4,256,512]{2,1,0:T(8,128)(2,1)S(1)}, u32[]{:S(2)}, u32[]{:S(2)}) collective-permute-start(bf16[4,256,512]{2,1,0:T(8,128)(2,1)} %get-tuple-element.71), channel_id=1, source_target_pairs={{0,1},{1,0},{2,3},{3,2},{4,5},{5,4},{6,7},{7,6},{8,9},{9,8},{10,11... | collective-permute-start | bytes 3145736 | tf_op jit(solution)/shard_map/ppermute | solution.py:377
  6.0 2.4 %collective-permute-start = (bf16[4,256,256]{2,1,0:T(8,128)(2,1)}, bf16[4,256,256]{2,1,0:T(8,128)(2,1)S(1)}, u32[]{:S(2)}, u32[]{:S(2)}) collective-permute-start(bf16[4,256,256]{2,1,0:T(8,128)(2,1)} %get-tuple-element.68), channel_id=1, source_target_pairs={{0,1},{1,0},{2,3},{3,2},{4,5},{5,4},{6,7},{7,6},{8,9},{9,8},{10,11... | collective-permute-start | bytes 1572872 | tf_op jit(solution)/shard_map/ppermute | solution.py:377
  6.5 6.6 %copy-start.2 = (bf16[256,8,256]{2,1,0:T(8,128)(2,1)S(1)}, bf16[256,8,256]{2,1,0:T(8,128)(2,1)}, u32[]{:S(2)}) copy-start(bf16[256,8,256]{2,1,0:T(8,128)(2,1)} %refs_0_.3) | copy-start | bytes 3145732
  10.4 7.8 %collective-permute-start.4 = (bf16[264,512]{1,0:T(8,128)(2,1)S(1)}, bf16[264,512]{1,0:T(8,128)(2,1)S(1)}, u32[]{:S(2)}, u32[]{:S(2)}) collective-permute-start(bf16[264,512]{1,0:T(8,128)(2,1)S(1)} %get-tuple-element.81), channel_id=1, source_target_pairs={{0,2},{1,3},{2,0},{3,1},{4,6},{5,7},{6,4},{7,5},{8,10},{9,11},{10,... | collective-permute-start | bytes 811016 | tf_op jit(solution)/shard_map/ppermute | solution.py:381
  11.6 7.5 %collective-permute-start.5 = (bf16[264,512]{1,0:T(8,128)(2,1)S(1)}, bf16[264,512]{1,0:T(8,128)(2,1)S(1)}, u32[]{:S(2)}, u32[]{:S(2)}) collective-permute-start(bf16[264,512]{1,0:T(8,128)(2,1)S(1)} %get-tuple-element.82), channel_id=1, source_target_pairs={{0,4},{1,5},{2,6},{3,7},{4,0},{5,1},{6,2},{7,3},{8,12},{9,13},{10,... | collective-permute-start | bytes 811016 | tf_op jit(solution)/shard_map/ppermute | solution.py:381
  12.9 12.1 %collective-permute-start.6 = (bf16[264,512]{1,0:T(8,128)(2,1)S(1)}, bf16[264,512]{1,0:T(8,128)(2,1)S(1)}, u32[]{:S(2)}, u32[]{:S(2)}) collective-permute-start(bf16[264,512]{1,0:T(8,128)(2,1)S(1)} %get-tuple-element.83), channel_id=1, source_target_pairs={{0,6},{1,7},{2,4},{3,5},{4,2},{5,3},{6,0},{7,1},{8,14},{9,15},{10,... | collective-permute-start | bytes 811016 | tf_op jit(solution)/shard_map/ppermute | solution.py:381
  13.5 13.6 %collective-permute-start.3 = (bf16[4,256,256]{2,1,0:T(8,128)(2,1)S(1)}, bf16[4,256,256]{2,1,0:T(8,128)(2,1)S(1)}, u32[]{:S(2)}, u32[]{:S(2)}) collective-permute-start(bf16[4,256,256]{2,1,0:T(8,128)(2,1)S(1)} %get-tuple-element.80), channel_id=1, source_target_pairs={{0,1},{1,0},{2,3},{3,2},{4,5},{5,4},{6,7},{7,6},{8,9},{9,8},{10,11... | collective-permute-start | bytes 1572872 | tf_op jit(solution)/shard_map/ppermute | solution.py:377
  25.8 8.6 %collective-permute-start.7 = (bf16[264,512]{1,0:T(8,128)(2,1)S(1)}, bf16[264,512]{1,0:T(8,128)(2,1)S(1)}, u32[]{:S(2)}, u32[]{:S(2)}) collective-permute-start(bf16[264,512]{1,0:T(8,128)(2,1)S(1)} %group_total.1), channel_id=1, source_target_pairs={{0,8},{1,9},{2,10},{3,11},{4,12},{5,13},{6,14},{7,15},{8,16},{9,17... | collective-permute-start | bytes 811016 | tf_op jit(solution)/shard_map/ppermute | solution.py:385
  34.4 7.7 %collective-permute-start.8 = (bf16[264,512]{1,0:T(8,128)(2,1)S(1)}, bf16[264,512]{1,0:T(8,128)(2,1)S(1)}, u32[]{:S(2)}, u32[]{:S(2)}) collective-permute-start(bf16[264,512]{1,0:T(8,128)(2,1)S(1)} %collective-permute-done.7.refs_4_), channel_id=1, source_target_pairs={{0,8},{1,9},{2,10},{3,11},{4,12},{5,13},{6,14},{7,15},{8,16},{9,17... | collective-permute-start | bytes 811016 | tf_op jit(solution)/shard_map/ppermute | solution.py:385
  43.6 8.8 %collective-permute-start.10 = (bf16[264,512]{1,0:T(8,128)(2,1)S(1)}, bf16[264,512]{1,0:T(8,128)(2,1)S(1)}, u32[]{:S(2)}, u32[]{:S(2)}) collective-permute-start(bf16[264,512]{1,0:T(8,128)(2,1)S(1)} %get-tuple-element.107), channel_id=1, source_target_pairs={{0,2},{1,3},{2,0},{3,1},{4,6},{5,7},{6,4},{7,5},{8,10},{9,11},{10,... | collective-permute-start | bytes 811016 | tf_op jit(solution)/shard_map/ppermute | solution.py:381
  45.2 11.4 %collective-permute-start.11 = (bf16[264,512]{1,0:T(8,128)(2,1)S(1)}, bf16[264,512]{1,0:T(8,128)(2,1)S(1)}, u32[]{:S(2)}, u32[]{:S(2)}) collective-permute-start(bf16[264,512]{1,0:T(8,128)(2,1)S(1)} %get-tuple-element.114), channel_id=1, source_target_pairs={{0,4},{1,5},{2,6},{3,7},{4,0},{5,1},{6,2},{7,3},{8,12},{9,13},{10,... | collective-permute-start | bytes 811016 | tf_op jit(solution)/shard_map/ppermute | solution.py:381
  45.2 15.7 %collective-permute-start.12 = (bf16[264,512]{1,0:T(8,128)(2,1)S(1)}, bf16[264,512]{1,0:T(8,128)(2,1)S(1)}, u32[]{:S(2)}, u32[]{:S(2)}) collective-permute-start(bf16[264,512]{1,0:T(8,128)(2,1)S(1)} %get-tuple-element.121), channel_id=1, source_target_pairs={{0,6},{1,7},{2,4},{3,5},{4,2},{5,3},{6,0},{7,1},{8,14},{9,15},{10,... | collective-permute-start | bytes 811016 | tf_op jit(solution)/shard_map/ppermute | solution.py:381
  47.4 4.9 %collective-permute-start.9 = (bf16[1,256,512]{2,1,0:T(8,128)(2,1)S(1)}, bf16[1,256,512]{2,1,0:T(8,128)(2,1)S(1)}, u32[]{:S(2)}, u32[]{:S(2)}) collective-permute-start(bf16[1,256,512]{2,1,0:T(8,128)(2,1)S(1)} %get-tuple-element.102), channel_id=1, source_target_pairs={{0,1},{1,0},{2,3},{3,2},{4,5},{5,4},{6,7},{7,6},{8,9},{9,8},{10,11... | collective-permute-start | bytes 786440 | tf_op jit(solution)/shard_map/ppermute | solution.py:377
  53.4 8.6 %collective-permute-start.13 = (bf16[1,256,512]{2,1,0:T(8,128)(2,1)S(1)}, bf16[1,256,512]{2,1,0:T(8,128)(2,1)S(1)}, u32[]{:S(2)}, u32[]{:S(2)}) collective-permute-start(bf16[1,256,512]{2,1,0:T(8,128)(2,1)S(1)} %get-tuple-element.109), channel_id=1, source_target_pairs={{0,1},{1,0},{2,3},{3,2},{4,5},{5,4},{6,7},{7,6},{8,9},{9,8},{10,11... | collective-permute-start | bytes 786440 | tf_op jit(solution)/shard_map/ppermute | solution.py:377
  57.6 4.5 %collective-permute-start.14 = (bf16[1,256,512]{2,1,0:T(8,128)(2,1)S(1)}, bf16[1,256,512]{2,1,0:T(8,128)(2,1)S(1)}, u32[]{:S(2)}, u32[]{:S(2)}) collective-permute-start(bf16[1,256,512]{2,1,0:T(8,128)(2,1)S(1)} %get-tuple-element.116), channel_id=1, source_target_pairs={{0,1},{1,0},{2,3},{3,2},{4,5},{5,4},{6,7},{7,6},{8,9},{9,8},{10,11... | collective-permute-start | bytes 786440 | tf_op jit(solution)/shard_map/ppermute | solution.py:377
  61.9 1.6 %collective-permute-start.15 = (bf16[1,256,512]{2,1,0:T(8,128)(2,1)S(1)}, bf16[1,256,512]{2,1,0:T(8,128)(2,1)S(1)}, u32[]{:S(2)}, u32[]{:S(2)}) collective-permute-start(bf16[1,256,512]{2,1,0:T(8,128)(2,1)S(1)} %get-tuple-element.124), channel_id=1, source_target_pairs={{0,1},{1,0},{2,3},{3,2},{4,5},{5,4},{6,7},{7,6},{8,9},{9,8},{10,11... | collective-permute-start | bytes 786440 | tf_op jit(solution)/shard_map/ppermute | solution.py:377

commit v13 on v12

--- a/solution.py
+++ b/solution.py
@@ -129,15 +129,14 @@
     columns[...] = jnp.concatenate([decay, docs, filler], axis=0).T
 
 
-def state_kernel(heads, scalars, *refs):
+def state_kernel(heads, slots, scalars, *refs):
     k_own, v_own, k_oth, v_oth, factors, tops, decays, docs_ref = refs[:8]
     outs = refs[8:]
     mine, core = scalars[0], scalars[1]
     tokens, key_width = k_own.shape[1:]
     length = 2 * tokens
     doc = jnp.broadcast_to(docs_ref[:, length - 1 :], (1, LANES))
-    for slot in range(len(outs) - 1, -1, -1):
-        out = outs[slot]
+    for slot, out in zip(slots, outs, strict=True):
         local_head = jnp.bitwise_xor(mine, slot)
         head = (heads // 2) * core + local_head
         row = factors[pl.ds(head, 1), :]
@@ -426,14 +425,20 @@
     )(scalars, gates, gates_oth, ids)
 
     by_core = (k_keep, v_keep, k_oth, v_oth, factors, tops, decays, docs)
-    made = pl.pallas_call(
-        functools.partial(state_kernel, heads),
-        in_specs=[SMEM] + [VMEM] * len(by_core),
-        out_specs=[VMEM] * group,
-        out_shape=[shape_of(*state)] * group,
-        compiler_params=params(),
-        name="states",
-    )(scalars, *by_core)
+    def states_of(slots):
+        return pl.pallas_call(
+            functools.partial(state_kernel, heads, slots),
+            in_specs=[SMEM] + [VMEM] * len(by_core),
+            out_specs=[VMEM] * len(slots),
+            out_shape=[shape_of(*state)] * len(slots),
+            compiler_params=params(),
+            name="states",
+        )(scalars, *by_core)
+    made = [None] * group
+    for first in (1, 0):
+        slots = tuple(range(first, group, 2))
+        for slot, out in zip(slots, states_of(slots), strict=True):
+            made[slot] = out
     gathered = [made[0]] + [in_group(made[r], r) for r in range(1, group)]
     total = pl.pallas_call(
         functools.partial(total_kernel, group),

time: 65.9 us -> 66.6 us (1.011)
  Pallas kernels: 19 us -> 19.7 us
    ppermute x2, waiting for transfers between devices: 9.35 us -> 8.45 us  [to_next(): return lax.ppermute(x, AXES, [(d, d + jump) for d in range(devices - jump)])]
    ppermute x6, waiting for transfers between devices: 10.3 us -> 11.2 us  [in_group(): return lax.ppermute(x, AXES, pairs)]
    pallas_call x1 -> x2, Pallas kernels: 2.05 us -> 2.75 us  [states_of(): pl.pallas_call(functools.partial(state_kernel, heads, slots), in_specs=[S...]
  transfers between devices with their start and end apart: 16 -> 16, of which waited for: 9 -> 9; matrix products, arithmetic and copies ran while one was open for 0% -> 0% of each run, Pallas kernels for 20% -> 22%
where the time goes in v13:
time: 66.6 us; the launch traced here: 66.1 us
  waiting for transfers between devices  23.1 us (35%)
  starting transfers between devices  20.7 us (31%)
  Pallas kernels  19.7 us (30%)
  local copies, waits for them, and re-layouts  1.6 us (2%)
  other arithmetic  0.79 us (1%)
    ppermute x8, starting transfers between devices, swap_cores(): return lax.ppermute(x, AXES, [(d, d ^ 1) for d in range(devices)])  12.6 us
    ppermute x6, waiting for transfers between devices, in_group(): return lax.ppermute(x, AXES, pairs)  11.2 us
    ppermute x2, waiting for transfers between devices, to_next(): return lax.ppermute(x, AXES, [(d, d + jump) for d in range(devices - jump)])  8.45 us
    ppermute x6, starting transfers between devices, in_group(): return lax.ppermute(x, AXES, pairs)  5.49 us
    pallas_call x2, Pallas kernels, own_terms(): pl.pallas_call(functools.partial(local_kernel, first_slot, heads), in_spe...  4.39 us
    pallas_call x4, Pallas kernels, outputs(): pl.pallas_call(functools.partial(output_kernel, first, count), in_specs=[...  3.93 us
    ppermute x8, waiting for transfers between devices, swap_cores(): return lax.ppermute(x, AXES, [(d, d ^ 1) for d in range(devices)])  3.53 us
    pallas_call x3, Pallas kernels, relayout(): pl.pallas_call(functools.partial(relayout_kernel, half, len(sources)), in...  3.38 us
  transfers between devices with their start and end apart: 16, of which 9 were waited for; matrix products, arithmetic and copies ran while one was open for 0% of the time, Pallas kernels for 22%

profile of v13, /device:TPU:25, one launch (start us, length us, event | category | flops | bytes accessed | tf_op | source)
XLA Modules:
  0.0 66.1 jit_solution(3883031169755557950)
XLA Ops:
  0.0 0.0 copy-start.3
  0.0 0.7 %pad_maximum_fusion.g_own = bf16[16,256]{1,0:T(8,128)(2,1)S(1)} fusion(bf16[8,256]{1,0:T(8,128)(2,1)} %bitcast.6, bf16[8,256]{1,0:T(8,128)(2,1)} %bitcast.7), kind=kLoop, calls=%fused_computation | loop fusion | flops 16384 | bytes 16384 | tf_op jit(solution)/shard_map/concatenate | solution.py:401
  0.7 0.7 %collective-permute-start.1 = (bf16[16,256]{1,0:T(8,128)(2,1)S(1)}, bf16[16,256]{1,0:T(8,128)(2,1)S(1)}, u32[]{:S(2)}, u32[]{:S(2)}) collective-permute-start(bf16[16,256]{1,0:T(8,128)(2,1)S(1)} %pad_maximum_fusion.g_own), channel_id=1, source_target_pairs={{0,1},{1,0},{2,3},{3,2},{4,5},{5,4},{6,7},{7,6},{8,9},{9,8},{10,11... | collective-permute-start | bytes 24584 | tf_op jit(solution)/shard_map/ppermute | solution.py:376
  1.4 0.0 copy-start
  1.4 1.6 %copy-done = bf16[256,8,512]{2,1,0:T(8,128)(2,1)S(1)} copy-done((bf16[256,8,512]{2,1,0:T(8,128)(2,1)S(1)}, bf16[256,8,512]{2,1,0:T(8,128)(2,1)}, u32[]{:S(2)}) %copy-start) | copy-done | bytes 2097176
  3.0 0.0 copy-start.1
  3.0 1.7 %relayout.4 = (bf16[4,256,512]{2,1,0:T(8,128)(2,1)S(1)}, bf16[4,256,512]{2,1,0:T(8,128)(2,1)}) custom-call(bf16[256,8,512]{2,1,0:T(8,128)(2,1)S(1)} %copy-done), custom_call_target="tpu_custom_call" | custom-call | tf_op jit(solution)/shard_map/relayout/pallas_call | solution.py:392
  4.7 0.0 collective-permute-done.1.g_oth
  4.7 0.0 collective-permute-start.2
  4.7 0.0 copy-done.1
  4.7 1.3 %relayout.3 = (bf16[4,256,256]{2,1,0:T(8,128)(2,1)S(1)}, bf16[4,256,256]{2,1,0:T(8,128)(2,1)}) custom-call(bf16[256,8,256]{2,1,0:T(8,128)(2,1)S(1)} %copy-done.1), custom_call_target="tpu_custom_call" | custom-call | tf_op jit(solution)/shard_map/relayout/pallas_call | solution.py:392
  5.9 0.5 collective-permute-start
  6.4 0.1 pad_add_fusion.scalars
  6.5 0.0 copy-done.3
  6.5 0.9 %gates.1 = (f32[8,512]{1,0:T(8,128)S(1)}, f32[8,128]{1,0:T(8,128)S(1)}, f32[8,128]{1,0:T(8,128)S(1)}, f32[8,512]{1,0:T(8,128)S(1)}, f32[8,512]{1,0:T(8,128)S(1)}...) custom-call(s32[2]{0:T(128)S(1)} %pad_add_fusion.scalars, bf16[16,256]{1,0:T(8,128)(2,1)S(1)} %pad_maximum_fusion.g_own, ...), custom_call_target="tpu_custom_call" | custom-call | tf_op jit(solution)/shard_map/gates/pallas_call | solution.py:418
  7.5 0.8 %collective-permute-done.refs_2_.refs_4_ = bf16[4,256,256]{2,1,0:T(8,128)(2,1)S(1)} collective-permute-done((bf16[4,256,256]{2,1,0:T(8,128)(2,1)}, bf16[4,256,256]{2,1,0:T(8,128)(2,1)S(1)}, u32[]{:S(2)}, u32[]{:S(2)}) %collective-permute-start) | collective-permute-done | bytes 524320 | tf_op jit(solution)/shard_map/ppermute | solution.py:376
  8.3 0.0 collective-permute-done.2.refs_3_.refs_5_
  8.3 1.4 %states.3 = (bf16[264,512]{1,0:T(8,128)(2,1)S(1)}, bf16[264,512]{1,0:T(8,128)(2,1)S(1)}) custom-call(s32[2]{0:T(128)S(1)} %pad_add_fusion.scalars, bf16[4,256,256]{2,1,0:T(8,128)(2,1)S(1)} %get-tuple-element.65.refs_0_.refs_1_, bf16[4,256,512]{2,1,0:T(8,128)(2,1)S(1)} %get-tuple-element.67.refs_1_.refs_2_, ...), custom_call_target="tpu_custom_call" | custom-call | tf_op jit(solution)/shard_map/states/pallas_call | solution.py:429
  9.7 0.0 copy-start.2
  9.7 1.3 %collective-permute-start.4 = (bf16[264,512]{1,0:T(8,128)(2,1)S(1)}, bf16[264,512]{1,0:T(8,128)(2,1)S(1)}, u32[]{:S(2)}, u32[]{:S(2)}) collective-permute-start(bf16[264,512]{1,0:T(8,128)(2,1)S(1)} %get-tuple-element.81), channel_id=1, source_target_pairs={{0,2},{1,3},{2,0},{3,1},{4,6},{5,7},{6,4},{7,5},{8,10},{9,11},{10,... | collective-permute-start | bytes 811016 | tf_op jit(solution)/shard_map/ppermute | solution.py:380
  11.0 1.2 %collective-permute-start.6 = (bf16[264,512]{1,0:T(8,128)(2,1)S(1)}, bf16[264,512]{1,0:T(8,128)(2,1)S(1)}, u32[]{:S(2)}, u32[]{:S(2)}) collective-permute-start(bf16[264,512]{1,0:T(8,128)(2,1)S(1)} %get-tuple-element.83), channel_id=1, source_target_pairs={{0,6},{1,7},{2,4},{3,5},{4,2},{5,3},{6,0},{7,1},{8,14},{9,15},{10,... | collective-permute-start | bytes 811016 | tf_op jit(solution)/shard_map/ppermute | solution.py:380
  12.2 1.4 %states.2 = (bf16[264,512]{1,0:T(8,128)(2,1)S(1)}, bf16[264,512]{1,0:T(8,128)(2,1)S(1)}) custom-call(s32[2]{0:T(128)S(1)} %pad_add_fusion.scalars, bf16[4,256,256]{2,1,0:T(8,128)(2,1)S(1)} %get-tuple-element.65.refs_0_.refs_1_, bf16[4,256,512]{2,1,0:T(8,128)(2,1)S(1)} %get-tuple-element.67.refs_1_.refs_2_, ...), custom_call_target="tpu_custom_call" | custom-call | tf_op jit(solution)/shard_map/states/pallas_call | solution.py:429
  13.6 0.3 collective-permute-start.5
  13.9 0.0 copy-done.2
  13.9 0.4 relayout.5
  14.3 1.2 %collective-permute-start.3 = (bf16[4,256,256]{2,1,0:T(8,128)(2,1)S(1)}, bf16[4,256,256]{2,1,0:T(8,128)(2,1)S(1)}, u32[]{:S(2)}, u32[]{:S(2)}) collective-permute-start(bf16[4,256,256]{2,1,0:T(8,128)(2,1)S(1)} %get-tuple-element.80), channel_id=1, source_target_pairs={{0,1},{1,0},{2,3},{3,2},{4,5},{5,4},{6,7},{7,6},{8,9},{9,8},{10,11... | collective-permute-start | bytes 1572872 | tf_op jit(solution)/shard_map/ppermute | solution.py:376
  15.5 2.1 %collective-permute-done.4.refs_1_ = bf16[264,512]{1,0:T(8,128)(2,1)S(1)} collective-permute-done((bf16[264,512]{1,0:T(8,128)(2,1)S(1)}, bf16[264,512]{1,0:T(8,128)(2,1)S(1)}, u32[]{:S(2)}, u32[]{:S(2)}) %collective-permute-start.4) | collective-permute-done | bytes 270368 | tf_op jit(solution)/shard_map/ppermute | solution.py:380
  17.5 6.8 %collective-permute-done.6.refs_3_ = bf16[264,512]{1,0:T(8,128)(2,1)S(1)} collective-permute-done((bf16[264,512]{1,0:T(8,128)(2,1)S(1)}, bf16[264,512]{1,0:T(8,128)(2,1)S(1)}, u32[]{:S(2)}, u32[]{:S(2)}) %collective-permute-start.6) | collective-permute-done | bytes 270368 | tf_op jit(solution)/shard_map/ppermute | solution.py:380
  24.3 2.3 %collective-permute-done.5.refs_2_ = bf16[264,512]{1,0:T(8,128)(2,1)S(1)} collective-permute-done((bf16[264,512]{1,0:T(8,128)(2,1)S(1)}, bf16[264,512]{1,0:T(8,128)(2,1)S(1)}, u32[]{:S(2)}, u32[]{:S(2)}) %collective-permute-start.5) | collective-permute-done | bytes 270368 | tf_op jit(solution)/shard_map/ppermute | solution.py:380
  26.6 0.8 %group_total.1 = bf16[264,512]{1,0:T(8,128)(2,1)S(1)} custom-call(s32[2]{0:T(128)S(1)} %pad_add_fusion.scalars, bf16[264,512]{1,0:T(8,128)(2,1)S(1)} %get-tuple-element.99.refs_0_, bf16[264,512]{1,0:T(8,128)(2,1)S(1)} %collective-permute-done.4.refs_1_, bf16[264,512]{1,0:T(8,128)(2,1)S(1)} %collective-permute-done.5.refs_2_, ...), custom_call_target="tpu_custom_call" | custom-call | tf_op jit(solution)/shard_map/group_total/pallas_call | solution.py:443
  27.4 1.3 %collective-permute-start.7 = (bf16[264,512]{1,0:T(8,128)(2,1)S(1)}, bf16[264,512]{1,0:T(8,128)(2,1)S(1)}, u32[]{:S(2)}, u32[]{:S(2)}) collective-permute-start(bf16[264,512]{1,0:T(8,128)(2,1)S(1)} %group_total.1), channel_id=1, source_target_pairs={{0,8},{1,9},{2,10},{3,11},{4,12},{5,13},{6,14},{7,15},{8,16},{9,17... | collective-permute-start | bytes 811016 | tf_op jit(solution)/shard_map/ppermute | solution.py:384
  28.7 0.0 collective-permute-done.3.refs_3_.q_oth
  28.7 2.2 %own_terms.2 = (f32[2,2,256,512]{3,2,1,0:T(8,128)S(1)}, f32[2,2,8,256]{3,2,1,0:T(8,128)S(1)}) custom-call(s32[2]{0:T(128)S(1)} %pad_add_fusion.scalars, bf16[4,256,256]{2,1,0:T(8,128)(2,1)S(1)} %get-tuple-element.94.refs_0_.q_own, bf16[4,256,256]{2,1,0:T(8,128)(2,1)S(1)} %get-tuple-element.65.refs_0_.refs_1_, ...), custom_call_target="tpu_custom_call" | custom-call | tf_op jit(solution)/shard_map/own_terms/pallas_call | solution.py:459
  30.9 4.7 %collective-permute-done.7.refs_4_ = bf16[264,512]{1,0:T(8,128)(2,1)S(1)} collective-permute-done((bf16[264,512]{1,0:T(8,128)(2,1)S(1)}, bf16[264,512]{1,0:T(8,128)(2,1)S(1)}, u32[]{:S(2)}, u32[]{:S(2)}) %collective-permute-start.7) | collective-permute-done | bytes 270368 | tf_op jit(solution)/shard_map/ppermute | solution.py:384
  35.7 1.3 %collective-permute-start.8 = (bf16[264,512]{1,0:T(8,128)(2,1)S(1)}, bf16[264,512]{1,0:T(8,128)(2,1)S(1)}, u32[]{:S(2)}, u32[]{:S(2)}) collective-permute-start(bf16[264,512]{1,0:T(8,128)(2,1)S(1)} %collective-permute-done.7.refs_4_), channel_id=1, source_target_pairs={{0,8},{1,9},{2,10},{3,11},{4,12},{5,13},{6,14},{7,15},{8,16},{9,17... | collective-permute-start | bytes 811016 | tf_op jit(solution)/shard_map/ppermute | solution.py:384
  37.0 2.2 %own_terms.3 = (f32[2,2,256,512]{3,2,1,0:T(8,128)S(1)}, f32[2,2,8,256]{3,2,1,0:T(8,128)S(1)}) custom-call(s32[2]{0:T(128)S(1)} %pad_add_fusion.scalars, bf16[4,256,256]{2,1,0:T(8,128)(2,1)S(1)} %get-tuple-element.94.refs_0_.q_own, bf16[4,256,256]{2,1,0:T(8,128)(2,1)S(1)} %get-tuple-element.65.refs_0_.refs_1_, ...), custom_call_target="tpu_custom_call" | custom-call | tf_op jit(solution)/shard_map/own_terms/pallas_call | solution.py:459
  39.2 3.7 %collective-permute-done.8.refs_5_ = bf16[264,512]{1,0:T(8,128)(2,1)S(1)} collective-permute-done((bf16[264,512]{1,0:T(8,128)(2,1)S(1)}, bf16[264,512]{1,0:T(8,128)(2,1)S(1)}, u32[]{:S(2)}, u32[]{:S(2)}) %collective-permute-start.8) | collective-permute-done | bytes 270368 | tf_op jit(solution)/shard_map/ppermute | solution.py:384
  42.9 1.4 %entering.1 = (bf16[264,512]{1,0:T(8,128)(2,1)S(1)}, bf16[264,512]{1,0:T(8,128)(2,1)S(1)}, bf16[264,512]{1,0:T(8,128)(2,1)S(1)}, bf16[264,512]{1,0:T(8,128)(2,1)S(1)}) custom-call(s32[2]{0:T(128)S(1)} %pad_add_fusion.scalars, bf16[264,512]{1,0:T(8,128)(2,1)S(1)} %get-tuple-element.99.refs_0_, bf16[264,512]{1,0:T(8,128)(2,1)S(1)} %collective-permute-done.4.refs_1_, ...), custom_call_target="tpu_custom_call" | custom-call | tf_op jit(solution)/shard_map/entering/pallas_call | solution.py:482
  44.3 1.3 %collective-permute-start.10 = (bf16[264,512]{1,0:T(8,128)(2,1)S(1)}, bf16[264,512]{1,0:T(8,128)(2,1)S(1)}, u32[]{:S(2)}, u32[]{:S(2)}) collective-permute-start(bf16[264,512]{1,0:T(8,128)(2,1)S(1)} %get-tuple-element.107), channel_id=1, source_target_pairs={{0,2},{1,3},{2,0},{3,1},{4,6},{5,7},{6,4},{7,5},{8,10},{9,11},{10,... | collective-permute-start | bytes 811016 | tf_op jit(solution)/shard_map/ppermute | solution.py:380
  45.6 0.2 collective-permute-start.11
  45.8 1.2 %collective-permute-start.12 = (bf16[264,512]{1,0:T(8,128)(2,1)S(1)}, bf16[264,512]{1,0:T(8,128)(2,1)S(1)}, u32[]{:S(2)}, u32[]{:S(2)}) collective-permute-start(bf16[264,512]{1,0:T(8,128)(2,1)S(1)} %get-tuple-element.121), channel_id=1, source_target_pairs={{0,6},{1,7},{2,4},{3,5},{4,2},{5,3},{6,0},{7,1},{8,14},{9,15},{10,... | collective-permute-start | bytes 811016 | tf_op jit(solution)/shard_map/ppermute | solution.py:380
  47.0 1.0 %outputs.4 = (bf16[1,256,512]{2,1,0:T(8,128)(2,1)S(1)}, bf16[1,256,512]{2,1,0:T(8,128)(2,1)S(1)}) custom-call(s32[2]{0:T(128)S(1)} %pad_add_fusion.scalars, bf16[4,256,256]{2,1,0:T(8,128)(2,1)S(1)} %get-tuple-element.94.refs_0_.q_own, bf16[4,256,256]{2,1,0:T(8,128)(2,1)S(1)} %collective-permute-done.3.refs_3_.q_oth, ...), custom_call_target="tpu_custom_call" | custom-call | tf_op jit(solution)/shard_map/outputs/pallas_call | solution.py:493
  48.0 4.6 %collective-permute-start.9 = (bf16[1,256,512]{2,1,0:T(8,128)(2,1)S(1)}, bf16[1,256,512]{2,1,0:T(8,128)(2,1)S(1)}, u32[]{:S(2)}, u32[]{:S(2)}) collective-permute-start(bf16[1,256,512]{2,1,0:T(8,128)(2,1)S(1)} %get-tuple-element.102), channel_id=1, source_target_pairs={{0,1},{1,0},{2,3},{3,2},{4,5},{5,4},{6,7},{7,6},{8,9},{9,8},{10,11... | collective-permute-start | bytes 786440 | tf_op jit(solution)/shard_map/ppermute | solution.py:376
  52.6 1.2 %collective-permute-done.9.refs_4_ = bf16[1,256,512]{2,1,0:T(8,128)(2,1)S(1)} collective-permute-done((bf16[1,256,512]{2,1,0:T(8,128)(2,1)S(1)}, bf16[1,256,512]{2,1,0:T(8,128)(2,1)S(1)}, u32[]{:S(2)}, u32[]{:S(2)}) %collective-permute-start.9) | collective-permute-done | bytes 262176 | tf_op jit(solution)/shard_map/ppermute | solution.py:376
  53.7 0.0 collective-permute-done.10.refs_4_
  53.7 1.0 %outputs.5 = (bf16[1,256,512]{2,1,0:T(8,128)(2,1)S(1)}, bf16[1,256,512]{2,1,0:T(8,128)(2,1)S(1)}) custom-call(s32[2]{0:T(128)S(1)} %pad_add_fusion.scalars, bf16[4,256,256]{2,1,0:T(8,128)(2,1)S(1)} %get-tuple-element.94.refs_0_.q_own, bf16[4,256,256]{2,1,0:T(8,128)(2,1)S(1)} %collective-permute-done.3.refs_3_.q_oth, ...), custom_call_target="tpu_custom_call" | custom-call | tf_op jit(solution)/shard_map/outputs/pallas_call | solution.py:493
  54.7 2.5 %collective-permute-start.13 = (bf16[1,256,512]{2,1,0:T(8,128)(2,1)S(1)}, bf16[1,256,512]{2,1,0:T(8,128)(2,1)S(1)}, u32[]{:S(2)}, u32[]{:S(2)}) collective-permute-start(bf16[1,256,512]{2,1,0:T(8,128)(2,1)S(1)} %get-tuple-element.109), channel_id=1, source_target_pairs={{0,1},{1,0},{2,3},{3,2},{4,5},{5,4},{6,7},{7,6},{8,9},{9,8},{10,11... | collective-permute-start | bytes 786440 | tf_op jit(solution)/shard_map/ppermute | solution.py:376
  57.2 0.0 collective-permute-done.11.refs_4_
  57.2 1.0 %outputs.6 = (bf16[1,256,512]{2,1,0:T(8,128)(2,1)S(1)}, bf16[1,256,512]{2,1,0:T(8,128)(2,1)S(1)}) custom-call(s32[2]{0:T(128)S(1)} %pad_add_fusion.scalars, bf16[4,256,256]{2,1,0:T(8,128)(2,1)S(1)} %get-tuple-element.94.refs_0_.q_own, bf16[4,256,256]{2,1,0:T(8,128)(2,1)S(1)} %collective-permute-done.3.refs_3_.q_oth, ...), custom_call_target="tpu_custom_call" | custom-call | tf_op jit(solution)/shard_map/outputs/pallas_call | solution.py:493
  58.2 3.1 %collective-permute-start.14 = (bf16[1,256,512]{2,1,0:T(8,128)(2,1)S(1)}, bf16[1,256,512]{2,1,0:T(8,128)(2,1)S(1)}, u32[]{:S(2)}, u32[]{:S(2)}) collective-permute-start(bf16[1,256,512]{2,1,0:T(8,128)(2,1)S(1)} %get-tuple-element.116), channel_id=1, source_target_pairs={{0,1},{1,0},{2,3},{3,2},{4,5},{5,4},{6,7},{7,6},{8,9},{9,8},{10,11... | collective-permute-start | bytes 786440 | tf_op jit(solution)/shard_map/ppermute | solution.py:376
  61.3 0.0 collective-permute-done.12.refs_4_
  61.3 1.0 %outputs.7 = (bf16[1,256,512]{2,1,0:T(8,128)(2,1)S(1)}, bf16[1,256,512]{2,1,0:T(8,128)(2,1)S(1)}) custom-call(s32[2]{0:T(128)S(1)} %pad_add_fusion.scalars, bf16[4,256,256]{2,1,0:T(8,128)(2,1)S(1)} %get-tuple-element.94.refs_0_.q_own, bf16[4,256,256]{2,1,0:T(8,128)(2,1)S(1)} %collective-permute-done.3.refs_3_.q_oth, ...), custom_call_target="tpu_custom_call" | custom-call | tf_op jit(solution)/shard_map/outputs/pallas_call | solution.py:493
  62.3 0.1 collective-permute-start.15
  62.4 0.0 collective-permute-done.13.refs_5_
  62.4 0.1 collective-permute-done.14.refs_6_
  62.5 1.4 %collective-permute-done.15.refs_7_ = bf16[1,256,512]{2,1,0:T(8,128)(2,1)S(1)} collective-permute-done((bf16[1,256,512]{2,1,0:T(8,128)(2,1)S(1)}, bf16[1,256,512]{2,1,0:T(8,128)(2,1)S(1)}, u32[]{:S(2)}, u32[]{:S(2)}) %collective-permute-start.15) | collective-permute-done | bytes 262176 | tf_op jit(solution)/shard_map/ppermute | solution.py:376
  63.9 2.1 %merge.1 = bf16[256,8,512]{2,1,0:T(8,128)(2,1)} custom-call(s32[2]{0:T(128)S(1)} %pad_add_fusion.scalars, bf16[1,256,512]{2,1,0:T(8,128)(2,1)S(1)} %get-tuple-element.101.refs_0_, bf16[1,256,512]{2,1,0:T(8,128)(2,1)S(1)} %get-tuple-element.108.refs_1_, bf16[1,256,512]{2,1,0:T(8,128)(2,1)S(1)} %get-tuple-element.115.refs_2_, ...), custom_call_target="tpu_custom_call" | custom-call | tf_op jit(solution)/shard_map/merge/pallas_call | solution.py:511
Async XLA Ops:
  0.0 6.5 %copy-start.3 = (s32[1024]{0:T(1024)S(1)}, s32[1024]{0:T(1024)}, u32[]{:S(2)}) copy-start(s32[1024]{0:T(1024)} %param.11) | copy-start | bytes 12292
  0.7 4.0 %collective-permute-start.1 = (bf16[16,256]{1,0:T(8,128)(2,1)S(1)}, bf16[16,256]{1,0:T(8,128)(2,1)S(1)}, u32[]{:S(2)}, u32[]{:S(2)}) collective-permute-start(bf16[16,256]{1,0:T(8,128)(2,1)S(1)} %pad_maximum_fusion.g_own), channel_id=1, source_target_pairs={{0,1},{1,0},{2,3},{3,2},{4,5},{5,4},{6,7},{7,6},{8,9},{9,8},{10,11... | collective-permute-start | bytes 24584 | tf_op jit(solution)/shard_map/ppermute | solution.py:376
  1.4 1.6 %copy-start = (bf16[256,8,512]{2,1,0:T(8,128)(2,1)S(1)}, bf16[256,8,512]{2,1,0:T(8,128)(2,1)}, u32[]{:S(2)}) copy-start(bf16[256,8,512]{2,1,0:T(8,128)(2,1)} %refs_0_.2) | copy-start | bytes 6291460
  3.0 1.7 %copy-start.1 = (bf16[256,8,256]{2,1,0:T(8,128)(2,1)S(1)}, bf16[256,8,256]{2,1,0:T(8,128)(2,1)}, u32[]{:S(2)}) copy-start(bf16[256,8,256]{2,1,0:T(8,128)(2,1)} %refs_0_.1) | copy-start | bytes 3145732
  4.7 3.6 %collective-permute-start.2 = (bf16[4,256,512]{2,1,0:T(8,128)(2,1)}, bf16[4,256,512]{2,1,0:T(8,128)(2,1)S(1)}, u32[]{:S(2)}, u32[]{:S(2)}) collective-permute-start(bf16[4,256,512]{2,1,0:T(8,128)(2,1)} %get-tuple-element.71), channel_id=1, source_target_pairs={{0,1},{1,0},{2,3},{3,2},{4,5},{5,4},{6,7},{7,6},{8,9},{9,8},{10,11... | collective-permute-start | bytes 3145736 | tf_op jit(solution)/shard_map/ppermute | solution.py:376
  5.9 2.4 %collective-permute-start = (bf16[4,256,256]{2,1,0:T(8,128)(2,1)}, bf16[4,256,256]{2,1,0:T(8,128)(2,1)S(1)}, u32[]{:S(2)}, u32[]{:S(2)}) collective-permute-start(bf16[4,256,256]{2,1,0:T(8,128)(2,1)} %get-tuple-element.68), channel_id=1, source_target_pairs={{0,1},{1,0},{2,3},{3,2},{4,5},{5,4},{6,7},{7,6},{8,9},{9,8},{10,11... | collective-permute-start | bytes 1572872 | tf_op jit(solution)/shard_map/ppermute | solution.py:376
  9.7 4.2 %copy-start.2 = (bf16[256,8,256]{2,1,0:T(8,128)(2,1)S(1)}, bf16[256,8,256]{2,1,0:T(8,128)(2,1)}, u32[]{:S(2)}) copy-start(bf16[256,8,256]{2,1,0:T(8,128)(2,1)} %refs_0_.3) | copy-start | bytes 3145732
  9.7 7.8 %collective-permute-start.4 = (bf16[264,512]{1,0:T(8,128)(2,1)S(1)}, bf16[264,512]{1,0:T(8,128)(2,1)S(1)}, u32[]{:S(2)}, u32[]{:S(2)}) collective-permute-start(bf16[264,512]{1,0:T(8,128)(2,1)S(1)} %get-tuple-element.81), channel_id=1, source_target_pairs={{0,2},{1,3},{2,0},{3,1},{4,6},{5,7},{6,4},{7,5},{8,10},{9,11},{10,... | collective-permute-start | bytes 811016 | tf_op jit(solution)/shard_map/ppermute | solution.py:380
  11.0 13.3 %collective-permute-start.6 = (bf16[264,512]{1,0:T(8,128)(2,1)S(1)}, bf16[264,512]{1,0:T(8,128)(2,1)S(1)}, u32[]{:S(2)}, u32[]{:S(2)}) collective-permute-start(bf16[264,512]{1,0:T(8,128)(2,1)S(1)} %get-tuple-element.83), channel_id=1, source_target_pairs={{0,6},{1,7},{2,4},{3,5},{4,2},{5,3},{6,0},{7,1},{8,14},{9,15},{10,... | collective-permute-start | bytes 811016 | tf_op jit(solution)/shard_map/ppermute | solution.py:380
  13.6 13.1 %collective-permute-start.5 = (bf16[264,512]{1,0:T(8,128)(2,1)S(1)}, bf16[264,512]{1,0:T(8,128)(2,1)S(1)}, u32[]{:S(2)}, u32[]{:S(2)}) collective-permute-start(bf16[264,512]{1,0:T(8,128)(2,1)S(1)} %get-tuple-element.82), channel_id=1, source_target_pairs={{0,4},{1,5},{2,6},{3,7},{4,0},{5,1},{6,2},{7,3},{8,12},{9,13},{10,... | collective-permute-start | bytes 811016 | tf_op jit(solution)/shard_map/ppermute | solution.py:380
  14.3 14.4 %collective-permute-start.3 = (bf16[4,256,256]{2,1,0:T(8,128)(2,1)S(1)}, bf16[4,256,256]{2,1,0:T(8,128)(2,1)S(1)}, u32[]{:S(2)}, u32[]{:S(2)}) collective-permute-start(bf16[4,256,256]{2,1,0:T(8,128)(2,1)S(1)} %get-tuple-element.80), channel_id=1, source_target_pairs={{0,1},{1,0},{2,3},{3,2},{4,5},{5,4},{6,7},{7,6},{8,9},{9,8},{10,11... | collective-permute-start | bytes 1572872 | tf_op jit(solution)/shard_map/ppermute | solution.py:376
  27.4 8.3 %collective-permute-start.7 = (bf16[264,512]{1,0:T(8,128)(2,1)S(1)}, bf16[264,512]{1,0:T(8,128)(2,1)S(1)}, u32[]{:S(2)}, u32[]{:S(2)}) collective-permute-start(bf16[264,512]{1,0:T(8,128)(2,1)S(1)} %group_total.1), channel_id=1, source_target_pairs={{0,8},{1,9},{2,10},{3,11},{4,12},{5,13},{6,14},{7,15},{8,16},{9,17... | collective-permute-start | bytes 811016 | tf_op jit(solution)/shard_map/ppermute | solution.py:384
  35.7 7.2 %collective-permute-start.8 = (bf16[264,512]{1,0:T(8,128)(2,1)S(1)}, bf16[264,512]{1,0:T(8,128)(2,1)S(1)}, u32[]{:S(2)}, u32[]{:S(2)}) collective-permute-start(bf16[264,512]{1,0:T(8,128)(2,1)S(1)} %collective-permute-done.7.refs_4_), channel_id=1, source_target_pairs={{0,8},{1,9},{2,10},{3,11},{4,12},{5,13},{6,14},{7,15},{8,16},{9,17... | collective-permute-start | bytes 811016 | tf_op jit(solution)/shard_map/ppermute | solution.py:384
  44.3 9.5 %collective-permute-start.10 = (bf16[264,512]{1,0:T(8,128)(2,1)S(1)}, bf16[264,512]{1,0:T(8,128)(2,1)S(1)}, u32[]{:S(2)}, u32[]{:S(2)}) collective-permute-start(bf16[264,512]{1,0:T(8,128)(2,1)S(1)} %get-tuple-element.107), channel_id=1, source_target_pairs={{0,2},{1,3},{2,0},{3,1},{4,6},{5,7},{6,4},{7,5},{8,10},{9,11},{10,... | collective-permute-start | bytes 811016 | tf_op jit(solution)/shard_map/ppermute | solution.py:380
  45.6 11.7 %collective-permute-start.11 = (bf16[264,512]{1,0:T(8,128)(2,1)S(1)}, bf16[264,512]{1,0:T(8,128)(2,1)S(1)}, u32[]{:S(2)}, u32[]{:S(2)}) collective-permute-start(bf16[264,512]{1,0:T(8,128)(2,1)S(1)} %get-tuple-element.114), channel_id=1, source_target_pairs={{0,4},{1,5},{2,6},{3,7},{4,0},{5,1},{6,2},{7,3},{8,12},{9,13},{10,... | collective-permute-start | bytes 811016 | tf_op jit(solution)/shard_map/ppermute | solution.py:380
  45.8 15.5 %collective-permute-start.12 = (bf16[264,512]{1,0:T(8,128)(2,1)S(1)}, bf16[264,512]{1,0:T(8,128)(2,1)S(1)}, u32[]{:S(2)}, u32[]{:S(2)}) collective-permute-start(bf16[264,512]{1,0:T(8,128)(2,1)S(1)} %get-tuple-element.121), channel_id=1, source_target_pairs={{0,6},{1,7},{2,4},{3,5},{4,2},{5,3},{6,0},{7,1},{8,14},{9,15},{10,... | collective-permute-start | bytes 811016 | tf_op jit(solution)/shard_map/ppermute | solution.py:380
  48.0 5.8 %collective-permute-start.9 = (bf16[1,256,512]{2,1,0:T(8,128)(2,1)S(1)}, bf16[1,256,512]{2,1,0:T(8,128)(2,1)S(1)}, u32[]{:S(2)}, u32[]{:S(2)}) collective-permute-start(bf16[1,256,512]{2,1,0:T(8,128)(2,1)S(1)} %get-tuple-element.102), channel_id=1, source_target_pairs={{0,1},{1,0},{2,3},{3,2},{4,5},{5,4},{6,7},{7,6},{8,9},{9,8},{10,11... | collective-permute-start | bytes 786440 | tf_op jit(solution)/shard_map/ppermute | solution.py:376
  54.7 7.7 %collective-permute-start.13 = (bf16[1,256,512]{2,1,0:T(8,128)(2,1)S(1)}, bf16[1,256,512]{2,1,0:T(8,128)(2,1)S(1)}, u32[]{:S(2)}, u32[]{:S(2)}) collective-permute-start(bf16[1,256,512]{2,1,0:T(8,128)(2,1)S(1)} %get-tuple-element.109), channel_id=1, source_target_pairs={{0,1},{1,0},{2,3},{3,2},{4,5},{5,4},{6,7},{7,6},{8,9},{9,8},{10,11... | collective-permute-start | bytes 786440 | tf_op jit(solution)/shard_map/ppermute | solution.py:376
  58.2 4.3 %collective-permute-start.14 = (bf16[1,256,512]{2,1,0:T(8,128)(2,1)S(1)}, bf16[1,256,512]{2,1,0:T(8,128)(2,1)S(1)}, u32[]{:S(2)}, u32[]{:S(2)}) collective-permute-start(bf16[1,256,512]{2,1,0:T(8,128)(2,1)S(1)} %get-tuple-element.116), channel_id=1, source_target_pairs={{0,1},{1,0},{2,3},{3,2},{4,5},{5,4},{6,7},{7,6},{8,9},{9,8},{10,11... | collective-permute-start | bytes 786440 | tf_op jit(solution)/shard_map/ppermute | solution.py:376
  62.3 1.6 %collective-permute-start.15 = (bf16[1,256,512]{2,1,0:T(8,128)(2,1)S(1)}, bf16[1,256,512]{2,1,0:T(8,128)(2,1)S(1)}, u32[]{:S(2)}, u32[]{:S(2)}) collective-permute-start(bf16[1,256,512]{2,1,0:T(8,128)(2,1)S(1)} %get-tuple-element.124), channel_id=1, source_target_pairs={{0,1},{1,0},{2,3},{3,2},{4,5},{5,4},{6,7},{7,6},{8,9},{9,8},{10,11... | collective-permute-start | bytes 786440 | tf_op jit(solution)/shard_map/ppermute | solution.py:376
